TPU v7x, 32 devices: a whole 2x2x4 slice. The times are simulated.
32 devices in a mesh: dp: 4 (over y, core), seq: 2 (over x), tensor: 4 (over z).
Axes of the slice: x: 2, y: 2, z: 4, core: 2. Of those that a mesh axis runs over, the one named last changes fastest.
Arguments:
- tokens: bfloat16 [1024, 40, 1024], P(('seq', 'tensor'), 'dp'), may hold values from -6 to 6
- norm1_gain: float32 [1024], replicated, may hold values from 0.5 to 1.5
- norm1_bias: float32 [1024], replicated, may hold values from -0.12 to 0.12
- w_query: bfloat16 [1024, 1024], P(None, 'tensor'), may hold values from -0.1875 to 0.1875
- w_key: bfloat16 [1024, 1024], P(None, 'tensor'), may hold values from -0.1875 to 0.1875
- w_value: bfloat16 [1024, 1024], P(None, 'tensor'), may hold values from -0.1875 to 0.1875
- w_out: bfloat16 [1024, 1024], P('tensor'), may hold values from -3 to 3
- norm2_gain: float32 [1024], replicated, may hold values from 0.5 to 1.5
- norm2_bias: float32 [1024], replicated, may hold values from -1.8 to 1.8
- w_gate: bfloat16 [1024, 4096], P(None, 'tensor'), may hold values from -0.1875 to 0.1875
- w_up: bfloat16 [1024, 4096], P(None, 'tensor'), may hold values from -0.1875 to 0.1875
- w_down: bfloat16 [4096, 1024], P('tensor'), may hold values from -0.09375 to 0.09375
- out_grad: bfloat16 [40, 160, 1024], P('dp'), may hold values from -6 to 6
- masked_rows: int32 [40, 160], P('dp'), may hold values from 0 to 1024, as said below
- window_counts: int32 [4], P('dp'), may hold values from 1 to 10, as said below
Outputs:
- output: bfloat16 [1024, 40, 1024], P(('seq', 'tensor'), 'dp')
- grad_tokens: float32 [1024, 40, 1024], P(('seq', 'tensor'), 'dp')
- grad_norm1_gain: float32 [1024], P(('dp', 'seq', 'tensor'))
- grad_norm1_bias: float32 [1024], P(('dp', 'seq', 'tensor'))
- grad_w_query: float32 [1024, 1024], P(('dp', 'seq'), 'tensor')
- grad_w_key: float32 [1024, 1024], P(('dp', 'seq'), 'tensor')
- grad_w_value: float32 [1024, 1024], P(('dp', 'seq'), 'tensor')
- grad_w_out: float32 [1024, 1024], P('tensor', ('dp', 'seq'))
- grad_norm2_gain: float32 [1024], P(('dp', 'seq', 'tensor'))
- grad_norm2_bias: float32 [1024], P(('dp', 'seq', 'tensor'))
- grad_w_gate: float32 [1024, 4096], P(('dp', 'seq'), 'tensor')
- grad_w_up: float32 [1024, 4096], P(('dp', 'seq'), 'tensor')
- grad_w_down: float32 [4096, 1024], P('tensor', ('dp', 'seq'))
Inputs may be any that keep to these rules, and one draw needn't show every extreme that they name: Group d's live windows are its first window_counts[d] slots; some group has all 10 slots live. `masked_rows`: each row lists distinct positions of its window first, then padding entries equal to 1024; a row holds at least 120 positions, and some row holds 160.
All inputs are finite; a program needn't handle non-finite values.
Results may differ from a plain program's by a relative error of at most 0.02.
Values may be sent and summed in bfloat16 or wider, within the bound.
A program may use at most 512 MiB of HBM per device.

v0:
```python
import math

import jax
import jax.numpy as jnp
from jax import lax
from jax.sharding import PartitionSpec as P

HEAD_DIM = 64
L = 1024
LOSS_SCALE = 1024


epsilon = 1e-05


def layer_stats(inputs):
    row_mean = jnp.mean(inputs, axis=-1, keepdims=True)
    centred = inputs - row_mean
    inv_std = lax.rsqrt(jnp.mean(centred * centred, axis=-1, keepdims=True) + epsilon)
    return (centred * inv_std, inv_std)


def norm_back(grad_norm, normed, inv_std, gain_vec):
    scaled = grad_norm * gain_vec
    return inv_std * (
        scaled
        - jnp.mean(scaled, axis=-1, keepdims=True)
        - normed * jnp.mean(scaled * normed, axis=-1, keepdims=True)
    )


def rotary_tables(positions):
    half_dim = HEAD_DIM // 2
    inv_freq = 10000.0 ** (-jnp.arange(half_dim, dtype=jnp.float32) * 2.0 / HEAD_DIM)
    angles = positions.astype(jnp.float32)[:, None] * inv_freq[None, :]
    return (jnp.cos(angles), jnp.sin(angles))


def rotate(values, cosine, sine):
    half_dim = values.shape[-1] // 2
    first_half = values[..., :half_dim]
    second_half = values[..., half_dim:]
    cos_b = cosine[:, None, None, :]
    sin_b = sine[:, None, None, :]
    return jnp.concatenate(
        [first_half * cos_b - second_half * sin_b, second_half * cos_b + first_half * sin_b],
        axis=-1,
    )


def unrotate(grads, cosine, sine):
    half_dim = grads.shape[-1] // 2
    first_half = grads[..., :half_dim]
    second_half = grads[..., half_dim:]
    cos_b = cosine[:, None, None, :]
    sin_b = sine[:, None, None, :]
    return jnp.concatenate(
        [first_half * cos_b + second_half * sin_b, second_half * cos_b - first_half * sin_b],
        axis=-1,
    )


def shards(
    tokens,
    norm1_gain,
    norm1_bias,
    w_query,
    w_key,
    w_value,
    w_out,
    norm2_gain,
    norm2_bias,
    w_gate,
    w_up,
    w_down,
    out_grad,
    masked_rows,
    window_counts,
):
    rows_local, windows, model_width = tokens.shape
    span_rows = rows_local * lax.axis_size("tensor")
    seq_index = lax.axis_index("seq")
    tensor_index = lax.axis_index("tensor")
    head_width = w_query.shape[1]
    heads_local = head_width // HEAD_DIM
    score_scale = 1.0 / math.sqrt(HEAD_DIM)
    head_shape = (span_rows, windows, heads_local, HEAD_DIM)
    residual = tokens.astype(jnp.float32)
    normed1, inv_std1 = layer_stats(residual)
    first_low = (normed1 * norm1_gain + norm1_bias).astype(jnp.bfloat16)
    first_full = lax.all_gather(first_low, "tensor", axis=0, tiled=True)
    w_joined = jnp.concatenate([w_query, w_key, w_value], axis=1)
    projected = jnp.einsum("rwd,de->rwe", first_full, w_joined, preferred_element_type=jnp.float32)
    positions = seq_index * span_rows + jnp.arange(span_rows)
    cosine, sine = rotary_tables(positions)
    queries = rotate(projected[..., :head_width].reshape(head_shape), cosine, sine).astype(
        jnp.bfloat16
    )
    keys_rot = (
        rotate(projected[..., head_width : 2 * head_width].reshape(head_shape), cosine, sine)
        .astype(jnp.bfloat16)
        .reshape(span_rows, windows, head_width)
    )
    values_own = projected[..., 2 * head_width :].astype(jnp.bfloat16)
    keys_all, values_all = (
        lax.all_gather(keys_rot, "seq", axis=0, tiled=True),
        lax.all_gather(values_own, "seq", axis=0, tiled=True),
    )
    key_heads = keys_all.reshape(-1, windows, heads_local, HEAD_DIM)
    value_heads = values_all.reshape(-1, windows, heads_local, HEAD_DIM)
    scores = (
        jnp.einsum("qwhd,kwhd->whqk", queries, key_heads, preferred_element_type=jnp.float32)
        * score_scale
    )
    row_max = jnp.max(scores, axis=-1, keepdims=True)
    row_sum = jnp.sum(jnp.exp(scores - row_max), axis=-1, keepdims=True)
    log_norm = row_max + jnp.log(row_sum)
    attn_prob = jnp.exp(scores - log_norm)
    prob_low = attn_prob.astype(jnp.bfloat16)
    attended = (
        jnp.einsum("whqk,kwhd->qwhd", prob_low, value_heads, preferred_element_type=jnp.float32)
        .reshape(span_rows, windows, head_width)
        .astype(jnp.bfloat16)
    )
    block_part = attended
    attn_branch = lax.psum_scatter(
        jnp.einsum("rwe,ed->rwd", block_part, w_out, preferred_element_type=jnp.float32).astype(
            jnp.bfloat16
        ),
        "tensor",
        scatter_dimension=0,
        tiled=True,
    ).astype(jnp.float32)
    residual2 = residual + attn_branch
    normed2, inv_std2 = layer_stats(residual2)
    second_low = (normed2 * norm2_gain + norm2_bias).astype(jnp.bfloat16)
    second_full = lax.all_gather(second_low, "tensor", axis=0, tiled=True)
    gate_proj = jnp.einsum("rwd,df->rwf", second_full, w_gate, preferred_element_type=jnp.float32)
    up_proj = jnp.einsum("rwd,df->rwf", second_full, w_up, preferred_element_type=jnp.float32)
    hidden = (jax.nn.silu(gate_proj) * up_proj).astype(jnp.bfloat16)
    block_part = hidden
    ffn_branch = lax.psum_scatter(
        jnp.einsum("rwf,fd->rwd", block_part, w_down, preferred_element_type=jnp.float32).astype(
            jnp.bfloat16
        ),
        "tensor",
        scatter_dimension=0,
        tiled=True,
    ).astype(jnp.float32)
    output = (residual2 + ffn_branch).astype(jnp.bfloat16)
    live_slot = jnp.arange(windows) < window_counts[0]
    valid_slot = (masked_rows < L) & live_slot[:, None]
    local_masked = jnp.sum(jnp.where(valid_slot, 1, 0)).astype(jnp.int32)
    total_masked = lax.psum(local_masked, "dp")
    loss_weight = LOSS_SCALE / total_masked.astype(jnp.float32)
    own_positions = seq_index * span_rows + tensor_index * rows_local + jnp.arange(rows_local)
    matches = (masked_rows[:, None, :] == own_positions[None, :, None]) & live_slot[:, None, None]
    picked = jnp.einsum(
        "wrm,wmd->rwd", matches.astype(jnp.bfloat16), out_grad, preferred_element_type=jnp.float32
    )
    grad_out = picked * loss_weight
    grad_down_in = lax.all_gather(grad_out.astype(jnp.bfloat16), "tensor", axis=0, tiled=True)
    grad_w_down = jnp.einsum(
        "rwf,rwd->fd", hidden, grad_down_in, preferred_element_type=jnp.float32
    )
    grad_hidden = jnp.einsum(
        "rwd,fd->rwf", grad_down_in, w_down, preferred_element_type=jnp.float32
    )
    sigmoid_gate = jax.nn.sigmoid(gate_proj)
    silu_gate = gate_proj * sigmoid_gate
    grad_gate = (
        grad_hidden * up_proj * sigmoid_gate * (1.0 + gate_proj * (1.0 - sigmoid_gate))
    ).astype(jnp.bfloat16)
    grad_up = (grad_hidden * silu_gate).astype(jnp.bfloat16)
    grad_w_gate = jnp.einsum(
        "rwd,rwf->df", second_full, grad_gate, preferred_element_type=jnp.float32
    )
    grad_w_up = jnp.einsum("rwd,rwf->df", second_full, grad_up, preferred_element_type=jnp.float32)
    grad_second = lax.psum_scatter(
        (
            jnp.einsum("rwf,df->rwd", grad_gate, w_gate, preferred_element_type=jnp.float32)
            + jnp.einsum("rwf,df->rwd", grad_up, w_up, preferred_element_type=jnp.float32)
        ).astype(jnp.bfloat16),
        "tensor",
        scatter_dimension=0,
        tiled=True,
    ).astype(jnp.float32)
    grad_norm2_gain = jnp.sum(grad_second * normed2, axis=(0, 1))
    grad_norm2_bias = jnp.sum(grad_second, axis=(0, 1))
    grad_residual2 = grad_out + norm_back(grad_second, normed2, inv_std2, norm2_gain)
    grad_attn_in = lax.all_gather(grad_residual2.astype(jnp.bfloat16), "tensor", axis=0, tiled=True)
    grad_w_out = jnp.einsum(
        "rwe,rwd->ed", attended, grad_attn_in, preferred_element_type=jnp.float32
    )
    grad_attended = jnp.einsum(
        "rwd,ed->rwe", grad_attn_in, w_out, preferred_element_type=jnp.float32
    ).astype(jnp.bfloat16)
    grad_att_heads = grad_attended.reshape(head_shape)
    scores_again = (
        jnp.einsum("qwhd,kwhd->whqk", queries, key_heads, preferred_element_type=jnp.float32)
        * score_scale
    )
    probs_again = jnp.exp(scores_again - log_norm)
    grad_probs = jnp.einsum(
        "qwhd,kwhd->whqk", grad_att_heads, value_heads, preferred_element_type=jnp.float32
    )
    row_delta = jnp.sum(probs_again * grad_probs, axis=-1, keepdims=True)
    grad_scores = (probs_again * (grad_probs - row_delta)).astype(jnp.bfloat16)
    grad_queries = (
        jnp.einsum("whqk,kwhd->qwhd", grad_scores, key_heads, preferred_element_type=jnp.float32)
        * score_scale
    )
    grad_key_all = (
        jnp.einsum("whqk,qwhd->kwhd", grad_scores, queries, preferred_element_type=jnp.float32)
        * score_scale
    ).reshape(-1, windows, head_width)
    grad_value_all = jnp.einsum(
        "whqk,qwhd->kwhd",
        probs_again.astype(jnp.bfloat16),
        grad_att_heads,
        preferred_element_type=jnp.float32,
    ).reshape(-1, windows, head_width)
    grad_keys, grad_values = (
        lax.psum_scatter(
            grad_key_all.astype(jnp.bfloat16), "seq", scatter_dimension=0, tiled=True
        ).astype(jnp.float32),
        lax.psum_scatter(
            grad_value_all.astype(jnp.bfloat16), "seq", scatter_dimension=0, tiled=True
        ).astype(jnp.float32),
    )
    grad_query_lin = (
        unrotate(grad_queries, cosine, sine)
        .reshape(span_rows, windows, head_width)
        .astype(jnp.bfloat16)
    )
    grad_key_lin = (
        unrotate(grad_keys.reshape(head_shape), cosine, sine)
        .reshape(span_rows, windows, head_width)
        .astype(jnp.bfloat16)
    )
    grad_value_lin = grad_values.astype(jnp.bfloat16)
    grad_joined = jnp.concatenate([grad_query_lin, grad_key_lin, grad_value_lin], axis=-1)
    grad_w_joined = jnp.einsum(
        "rwd,rwe->de", first_full, grad_joined, preferred_element_type=jnp.float32
    )
    grad_w_query = grad_w_joined[:, :head_width]
    grad_w_key = grad_w_joined[:, head_width : 2 * head_width]
    grad_w_value = grad_w_joined[:, 2 * head_width :]
    block_part = grad_joined
    grad_first = lax.psum_scatter(
        jnp.einsum("rwe,de->rwd", block_part, w_joined, preferred_element_type=jnp.float32).astype(
            jnp.bfloat16
        ),
        "tensor",
        scatter_dimension=0,
        tiled=True,
    ).astype(jnp.float32)
    grad_norm1_gain = jnp.sum(grad_first * normed1, axis=(0, 1))
    grad_norm1_bias = jnp.sum(grad_first, axis=(0, 1))
    grad_tokens = grad_residual2 + norm_back(grad_first, normed1, inv_std1, norm1_gain)
    summed = (
        lax.psum_scatter(
            grad_w_query.astype(jnp.bfloat16), ("dp", "seq"), scatter_dimension=0, tiled=True
        ).astype(jnp.float32),
        lax.psum_scatter(
            grad_w_key.astype(jnp.bfloat16), ("dp", "seq"), scatter_dimension=0, tiled=True
        ).astype(jnp.float32),
        lax.psum_scatter(
            grad_w_value.astype(jnp.bfloat16), ("dp", "seq"), scatter_dimension=0, tiled=True
        ).astype(jnp.float32),
        lax.psum_scatter(
            grad_w_out.astype(jnp.bfloat16), ("dp", "seq"), scatter_dimension=1, tiled=True
        ).astype(jnp.float32),
        lax.psum_scatter(
            grad_w_gate.astype(jnp.bfloat16), ("dp", "seq"), scatter_dimension=0, tiled=True
        ).astype(jnp.float32),
        lax.psum_scatter(
            grad_w_up.astype(jnp.bfloat16), ("dp", "seq"), scatter_dimension=0, tiled=True
        ).astype(jnp.float32),
        lax.psum_scatter(
            grad_w_down.astype(jnp.bfloat16), ("dp", "seq"), scatter_dimension=1, tiled=True
        ).astype(jnp.float32),
    )
    norm_sums = (
        lax.psum_scatter(grad_norm1_gain, ("dp", "seq", "tensor"), scatter_dimension=0, tiled=True),
        lax.psum_scatter(grad_norm1_bias, ("dp", "seq", "tensor"), scatter_dimension=0, tiled=True),
        lax.psum_scatter(grad_norm2_gain, ("dp", "seq", "tensor"), scatter_dimension=0, tiled=True),
        lax.psum_scatter(grad_norm2_bias, ("dp", "seq", "tensor"), scatter_dimension=0, tiled=True),
    )
    return (
        output,
        grad_tokens,
        norm_sums[0],
        norm_sums[1],
        summed[0],
        summed[1],
        summed[2],
        summed[3],
        norm_sums[2],
        norm_sums[3],
        summed[4],
        summed[5],
        summed[6],
    )


def solution(mesh):
    return jax.shard_map(
        shards,
        mesh=mesh,
        in_specs=(
            P(("seq", "tensor"), "dp", None),
            P(),
            P(),
            P(None, "tensor"),
            P(None, "tensor"),
            P(None, "tensor"),
            P("tensor", None),
            P(),
            P(),
            P(None, "tensor"),
            P(None, "tensor"),
            P("tensor", None),
            P("dp", None, None),
            P("dp", None),
            P("dp"),
        ),
        out_specs=(
            P(("seq", "tensor"), "dp", None),
            P(("seq", "tensor"), "dp", None),
            P(("dp", "seq", "tensor")),
            P(("dp", "seq", "tensor")),
            P(("dp", "seq"), "tensor"),
            P(("dp", "seq"), "tensor"),
            P(("dp", "seq"), "tensor"),
            P("tensor", ("dp", "seq")),
            P(("dp", "seq", "tensor")),
            P(("dp", "seq", "tensor")),
            P(("dp", "seq"), "tensor"),
            P(("dp", "seq"), "tensor"),
            P("tensor", ("dp", "seq")),
        ),
        check_vma=False,
    )
```

profile of v0, /device:TPU:0, one launch (start us, length us, event | category | flops | bytes accessed | tf_op | source)
XLA Modules:
  0.0 2384.1 jit_solution(1912121650682582112)
XLA Ops:
  15.6 186.4 %all-gather.7.cloned.1.call-done = bf16[512,10,1024]{2,0,1:T(8,128)(2,1)} async-done(((bf16[128,10,1024]{2,0,1:T(8,128)(2,1)}), bf16[512,10,1024]{2,0,1:T(8,128)(2,1)}) %all-gather.7.cloned.1.call-update) | async-done | bytes 10485776 | tf_op jit(solution)/shard_map/all_gather | solution.py:91
  202.0 14.6 fusion.49
  216.5 9.1 fusion.66
  225.7 5.9 copy.54
  231.6 5.9 copy.55
  237.4 6.1 subtract_convert_fusion.3
  249.9 62.3 %all-gather.11.cloned.1.call-done = bf16[1024,10,256]{0,2,1:T(8,128)(2,1)} async-done(((bf16[512,10,256]{0,2,1:T(8,128)(2,1)}), bf16[1024,10,256]{0,2,1:T(8,128)(2,1)}) %all-gather.11.cloned.1.call-update) | async-done | bytes 5242896 | tf_op jit(solution)/shard_map/all_gather | solution.py:106
  312.2 34.6 %multiply_reduce_fusion.1 = (f32[10,4,512]{2,1,0:T(4,128)S(1)}, f32[10,4,512,1024]{3,2,1,0:T(8,128)}) fusion(bf16[1024,10,4,64]{0,3,2,1:T(8,128)(2,1)} %bitcast.107, bf16[512,10,4,32]{0,3,2,1:T(8,128)(2,1)} %get-tuple-element.35, bf16[512,10,4,32]{0,3,2,1:T(8,128)(2,1)} %get-tuple-element.34), kind=kOutput, calls=%fused_computation.4 | convolution fusion | flops 2731520000 | bytes 91832320 | tf_op jit(solution)/shard_map/qwhd,kwhd->whqk/dot_general | solution.py:112
  346.9 26.3 %exponential_reduce_fusion = f32[10,4,512]{2,1,0:T(4,128)S(1)} fusion(f32[10,4,512,1024]{3,2,1,0:T(8,128)} %get-tuple-element.52, f32[10,4,512]{2,1,0:T(4,128)S(1)} %get-tuple-element.51), kind=kLoop, calls=%fused_computation.3 | loop fusion | flops 62894080 | bytes 84049920 | tf_op jit(solution)/shard_map/reduce_sum | solution.py:116
  373.2 9.7 all-gather.9.cloned.1.call-done
  383.0 7.9 copy.53
  390.9 31.2 %fusion.44 = bf16[10,4,64,512]{3,2,1,0:T(8,128)(2,1)} fusion(bf16[1024,10,4,64]{0,3,2,1:T(8,128)(2,1)} %bitcast.102, f32[10,4,512,1024]{3,2,1,0:T(8,128)} %get-tuple-element.52, f32[10,4,512]{2,1,0:T(4,128)S(1)} %bitcast.120), kind=kOutput, calls=%fused_computation.87 | convolution fusion | flops 2748579840 | bytes 91832320 | tf_op jit(solution)/shard_map/whqk,kwhd->qwhd/dot_general | solution.py:121
  422.0 8.7 convolution_convert_fusion.2
  431.1 177.9 %reduce-scatter.18.cloned.1.call-done = bf16[128,10,1024]{2,0,1:T(8,128)(2,1)} async-done(((bf16[512,10,1024]{2,0,1:T(8,128)(2,1)}), bf16[128,10,1024]{2,0,1:T(8,128)(2,1)}) %reduce-scatter.18.cloned.1.call-update) | async-done | bytes 2621456 | tf_op jit(solution)/shard_map/reduce_scatter | solution.py:126
  629.7 172.7 %all-gather.13.cloned.1.call-done = bf16[512,10,1024]{2,0,1:T(8,128)(2,1)} async-done(((bf16[128,10,1024]{2,0,1:T(8,128)(2,1)}), bf16[512,10,1024]{2,0,1:T(8,128)(2,1)}) %all-gather.13.cloned.1.call-update) | async-done | bytes 10485776 | tf_op jit(solution)/shard_map/all_gather | solution.py:137
  802.4 18.5 fusion.38
  820.9 14.0 fusion.42
  834.8 151.1 %all-gather.15.cloned.1.call-done = bf16[512,10,1024]{2,0,1:T(8,128)(2,1)} async-done(((bf16[128,10,1024]{2,0,1:T(8,128)(2,1)}), bf16[512,10,1024]{2,0,1:T(8,128)(2,1)}) %all-gather.15.cloned.1.call-update) | async-done | bytes 10485776 | tf_op jit(solution)/shard_map/all_gather | solution.py:162
  986.0 34.1 %multiply_convert_fusion.1 = (bf16[512,10,1024]{2,0,1:T(8,128)(2,1)}, bf16[512,10,1024]{2,0,1:T(8,128)(2,1)}, bf16[512,10,1024]{2,0,1:T(8,128)(2,1)}) fusion(f32[512,10,1024]{2,0,1:T(8,128)} %fusion.42, f32[512,10,1024]{2,0,1:T(8,128)} %fusion.38, bf16[512,10,1024]{2,0,1:T(8,128)(2,1)} %all-gather.15.cloned.1.call-done, bf16[1024,1024]{1,0:T(8,128)(2,1)} %param.26), kind=kOutput, calls=%fused_computation.7 | convolution fusion | flops 10816061440 | bytes 85983232 | tf_op jit(solution)/shard_map/rwd,fd->rwf/dot_general | solution.py:166
  1020.1 17.7 fusion.40
  1037.8 21.2 add_convert_fusion
  1059.1 176.3 %reduce-scatter.22.cloned.1.call-done = bf16[128,10,1024]{2,0,1:T(8,128)(2,1)} async-done(((bf16[512,10,1024]{2,0,1:T(8,128)(2,1)}), bf16[128,10,1024]{2,0,1:T(8,128)(2,1)}) %reduce-scatter.22.cloned.1.call-update) | async-done | bytes 2621456 | tf_op jit(solution)/shard_map/reduce_scatter | solution.py:179
  1235.5 5.5 fusion.27
  1246.6 185.1 %all-gather.17.cloned.1.call-done = bf16[512,10,1024]{2,0,1:T(8,128)(2,1)} async-done(((bf16[128,10,1024]{2,0,1:T(8,128)(2,1)}), bf16[512,10,1024]{2,0,1:T(8,128)(2,1)}) %all-gather.17.cloned.1.call-update) | async-done | bytes 10485776 | tf_op jit(solution)/shard_map/all_gather | solution.py:191
  1431.7 11.3 convolution_convert_fusion.3
  1443.1 59.7 %multiply_reduce_fusion = (f32[10,4,512]{2,1,0:T(4,128)S(1)}, f32[10,4,512,1024]{3,2,1,0:T(8,128)}) fusion(f32[10,4,512,1024]{3,2,1,0:T(8,128)} %get-tuple-element.52, f32[10,4,512]{2,1,0:T(4,128)S(1)} %bitcast.121, bf16[512,10,4,64]{0,3,2,1:T(8,128)(2,1)S(1)} %bitcast.115, bf16[1024,10,4,64]{0,3,2,1:T(8,128)(2,1)} %bitcast.103), kind=kOutput, calls=%fused_computation.1 | convolution fusion | flops 2768220160 | bytes 175800320 | tf_op jit(solution)/shard_map/qwhd,kwhd->whqk/dot_general | solution.py:204
  1502.8 65.8 %multiply_convert_fusion = bf16[10,4,512,1024]{3,2,1,0:T(8,128)(2,1)} fusion(f32[10,4,512,1024]{3,2,1,0:T(8,128)} %get-tuple-element.54, f32[10,4,512,1024]{3,2,1,0:T(8,128)} %get-tuple-element.52, f32[10,4,512]{2,1,0:T(4,128)S(1)} %get-tuple-element.53, f32[10,4,512]{2,1,0:T(4,128)S(1)} %bitcast.122), kind=kLoop, calls=%fused_computation | loop fusion | flops 104857600 | bytes 209879040 | tf_op jit(solution)/shard_map/convert_element_type | solution.py:208
  1568.6 19.2 multiply_convert_fusion.4
  1589.5 33.5 %fusion.31 = bf16[10,4,64,1024]{3,2,1,0:T(8,128)(2,1)} fusion(bf16[512,10,4,64]{0,3,2,1:T(8,128)(2,1)S(1)} %bitcast.116, f32[10,4,512,1024]{3,2,1,0:T(8,128)} %get-tuple-element.52, f32[10,4,512]{2,1,0:T(4,128)S(1)} %bitcast.123), kind=kOutput, calls=%fused_computation.64 | convolution fusion | flops 2749890560 | bytes 91832320 | tf_op jit(solution)/shard_map/whqk,qwhd->kwhd/dot_general | solution.py:217
  1623.0 8.1 copy.57
  1631.2 15.7 bitcast_convert_fusion.1
  1649.6 18.1 bitcast_convert_fusion.2
  1667.7 18.3 bitcast_convert_fusion.3
  1686.1 6.8 fusion.48
  1694.0 22.1 multiply_bitcast_fusion
  1729.8 15.7 bitcast_convert_fusion.4
  1747.9 13.2 convolution_convert_fusion
  1762.7 17.4 convolution_convert_fusion.1
  1782.4 26.7 %reduce-scatter.38.cloned.1.call-done = bf16[128,1024]{1,0:T(8,128)(2,1)} async-done(((bf16[1024,1024]{1,0:T(8,128)(2,1)}), bf16[128,1024]{1,0:T(8,128)(2,1)}) %reduce-scatter.38.cloned.1.call-update) | async-done | bytes 262160 | tf_op jit(solution)/shard_map/reduce_scatter | solution.py:277
  1810.9 42.7 %reduce-scatter.36.cloned.1.call-done = bf16[128,1024]{1,0:T(8,128)(2,1)} async-done(((bf16[1024,1024]{1,0:T(8,128)(2,1)}), bf16[128,1024]{1,0:T(8,128)(2,1)}) %reduce-scatter.36.cloned.1.call-update) | async-done | bytes 262160 | tf_op jit(solution)/shard_map/reduce_scatter | solution.py:274
  1855.4 35.6 %reduce-scatter.40.cloned.1.call-done = bf16[128,256]{1,0:T(8,128)(2,1)} async-done(((bf16[1024,256]{1,0:T(8,128)(2,1)}), bf16[128,256]{1,0:T(8,128)(2,1)}) %reduce-scatter.40.cloned.1.call-update) | async-done | bytes 65552
  1892.7 35.4 %reduce-scatter.30.cloned.1.call-done = bf16[128,256]{1,0:T(8,128)(2,1)} async-done(((bf16[1024,256]{1,0:T(8,128)(2,1)}), bf16[128,256]{1,0:T(8,128)(2,1)}) %reduce-scatter.30.cloned.1.call-update) | async-done | bytes 65552 | tf_op jit(solution)/shard_map/reduce_scatter | solution.py:262
  1929.6 35.9 %reduce-scatter.32.cloned.1.call-done = bf16[128,256]{1,0:T(8,128)(2,1)} async-done(((bf16[1024,256]{1,0:T(8,128)(2,1)}), bf16[128,256]{1,0:T(8,128)(2,1)}) %reduce-scatter.32.cloned.1.call-update) | async-done | bytes 65552 | tf_op jit(solution)/shard_map/reduce_scatter | solution.py:265
  1967.0 35.6 %reduce-scatter.34.cloned.1.call-done = bf16[128,256]{1,0:T(8,128)(2,1)} async-done(((bf16[1024,256]{1,0:T(8,128)(2,1)}), bf16[128,256]{1,0:T(8,128)(2,1)}) %reduce-scatter.34.cloned.1.call-update) | async-done | bytes 65552 | tf_op jit(solution)/shard_map/reduce_scatter | solution.py:268
  2004.1 178.9 %reduce-scatter.28.cloned.1.call-done = bf16[128,10,1024]{2,0,1:T(8,128)(2,1)} async-done(((bf16[512,10,1024]{2,0,1:T(8,128)(2,1)}), bf16[128,10,1024]{2,0,1:T(8,128)(2,1)}) %reduce-scatter.28.cloned.1.call-update) | async-done | bytes 2621456 | tf_op jit(solution)/shard_map/reduce_scatter | solution.py:250
  2187.1 45.7 %all-reduce.4 = (f32[1024]{0:T(1024)S(1)}, f32[1024]{0:T(1024)S(1)}, f32[1024]{0:T(1024)S(1)}, f32[1024]{0:T(1024)S(1)}) all-reduce(f32[1024]{0:T(1024)S(1)} %get-tuple-element.15, f32[1024]{0:T(1024)S(1)} %get-tuple-element.20, f32[1024]{0:T(1024)S(1)} %copy-done.43, ...), channel_id=8, replica_groups=mesh['dp'=4,'seq'=2,'tensor'=4] {'dp','seq','tensor'}, use_global_device_ids=true, to_apply=%region_20.21.clone | all-reduce | flops 4096 | bytes 32768
  2235.1 130.4 %reduce-scatter.20.cloned.1.call-done = bf16[128,10,1024]{2,0,1:T(8,128)(2,1)} async-done(((bf16[512,10,1024]{2,0,1:T(8,128)(2,1)}), bf16[128,10,1024]{2,0,1:T(8,128)(2,1)}) %reduce-scatter.20.cloned.1.call-update) | async-done | bytes 2621456 | tf_op jit(solution)/shard_map/reduce_scatter | solution.py:142
  2365.6 11.5 fusion.20
  (191 shorter events, 81.4 us)
Async XLA Ops:
  7.2 617.8 %copy-start = (bf16[10,160,1024]{2,1,0:T(8,128)(2,1)S(1)}, bf16[10,160,1024]{2,1,0:T(8,128)(2,1)}, u32[]{:S(2)}) copy-start(bf16[10,160,1024]{2,1,0:T(8,128)(2,1)} %param.27) | copy-start | bytes 9830404
  7.2 194.8 %all-gather.7.cloned.1.call-start = ((), (), s32[]{:S(2)}) async-start(), calls=%async_computation.13 | async-start | bytes 13107200 | tf_op jit(solution)/shard_map/all_gather | solution.py:91
  15.2 297.0 %all-gather.11.cloned.1.call-start = ((), (), s32[]{:S(2)}) async-start(), calls=%async_computation.15 | async-start | bytes 7864320 | tf_op jit(solution)/shard_map/all_gather | solution.py:106
  15.6 221.8 %copy-start.18 = (f32[512,32]{0,1:T(8,128)}, f32[512,32]{0,1:T(8,128)S(1)}, u32[]{:S(2)}) copy-start(f32[512,32]{0,1:T(8,128)S(1)} %get-tuple-element.47) | copy-start | bytes 196612
  15.6 221.8 %copy-start.20 = (f32[512,32]{0,1:T(8,128)}, f32[512,32]{0,1:T(8,128)S(1)}, u32[]{:S(2)}) copy-start(f32[512,32]{0,1:T(8,128)S(1)} %get-tuple-element.48) | copy-start | bytes 196612
  245.3 137.6 %all-gather.9.cloned.1.call-start = ((), (), s32[]{:S(2)}) async-start(), calls=%async_computation.14 | async-start | bytes 7864320 | tf_op jit(solution)/shard_map/all_gather | solution.py:107
  249.7 359.3 %reduce-scatter.18.cloned.1.call-start = ((), (), s32[]{:S(2)}) async-start(), calls=%async_computation.16 | async-start | bytes 13107200 | tf_op jit(solution)/shard_map/reduce_scatter | solution.py:126
  430.8 184.0 %copy-start.38 = (f32[1024]{0:T(1024)S(1)}, f32[1024]{0:T(1024)}, u32[]{:S(2)}) copy-start(f32[1024]{0:T(1024)} %param.22) | copy-start | bytes 12292
  430.8 184.0 %copy-start.46 = (f32[1024]{0:T(1024)S(1)}, f32[1024]{0:T(1024)}, u32[]{:S(2)}) copy-start(f32[1024]{0:T(1024)} %param.23) | copy-start | bytes 12292
  430.8 371.6 %all-gather.13.cloned.1.call-start = ((), (), s32[]{:S(2)}) async-start(), calls=%async_computation.17 | async-start | bytes 13107200 | tf_op jit(solution)/shard_map/all_gather | solution.py:137
  617.3 368.7 %all-gather.15.cloned.1.call-start = ((), (), s32[]{:S(2)}) async-start(), calls=%async_computation.19 | async-start | bytes 13107200 | tf_op jit(solution)/shard_map/all_gather | solution.py:162
  629.6 191.2 %copy-start.48 = (bf16[1024,1024]{1,0:T(8,128)(2,1)S(1)}, bf16[1024,1024]{1,0:T(8,128)(2,1)}, u32[]{:S(2)}) copy-start(bf16[1024,1024]{1,0:T(8,128)(2,1)} %param.24) | copy-start | bytes 6291460
  629.7 605.8 %reduce-scatter.22.cloned.1.call-start = ((), (), s32[]{:S(2)}) async-start(), calls=%async_computation.20 | async-start | bytes 13107200 | tf_op jit(solution)/shard_map/reduce_scatter | solution.py:179
  802.4 18.5 copy-start.47
  1059.1 176.4 %copy-start.4 = (bf16[128,10,1024]{2,0,1:T(8,128)(2,1)S(1)}, bf16[128,10,1024]{2,0,1:T(8,128)(2,1)}, u32[]{:S(2)}) copy-start(bf16[128,10,1024]{2,0,1:T(8,128)(2,1)} %param.15) | copy-start | bytes 7864324
  1059.1 176.4 %copy-start.24 = (f32[128,10]{0,1:T(8,128)S(1)}, f32[128,10]{0,1:T(8,128)}, u32[]{:S(2)}) copy-start(f32[128,10]{0,1:T(8,128)} %copy-done.23) | copy-start | bytes 15364
  1059.1 176.4 %copy-start.29 = (f32[128,10]{0,1:T(8,128)S(1)}, f32[128,10]{0,1:T(8,128)}, u32[]{:S(2)}) copy-start(f32[128,10]{0,1:T(8,128)} %copy-done.28) | copy-start | bytes 15364
  1059.1 176.4 %copy-start.39 = (f32[1024]{0:T(1024)S(1)}, f32[1024]{0:T(1024)}, u32[]{:S(2)}) copy-start(f32[1024]{0:T(1024)} %param.22) | copy-start | bytes 12292
  1059.1 372.6 %all-gather.17.cloned.1.call-start = ((), (), s32[]{:S(2)}) async-start(), calls=%async_computation.21 | async-start | bytes 13107200 | tf_op jit(solution)/shard_map/all_gather | solution.py:191
  1241.0 190.6 %copy-start.22 = (bf16[256,1024]{1,0:T(8,128)(2,1)S(1)}, bf16[256,1024]{1,0:T(8,128)(2,1)}, u32[]{:S(2)}) copy-start(bf16[256,1024]{1,0:T(8,128)(2,1)} %param.21) | copy-start | bytes 1572868
  1246.6 196.5 %copy-start.17 = (f32[5,8,512]{2,1,0:T(8,128)S(1)}, f32[5,8,512]{2,1,0:T(8,128)}, u32[]{:S(2)}) copy-start(f32[5,8,512]{2,1,0:T(8,128)} %copy-done.16) | copy-start | bytes 245764
  1246.6 469.6 %reduce-scatter.24.cloned.1.call-start = ((), (), s32[]{:S(2)}) async-start(), calls=%async_computation.22 | async-start | bytes 7864320 | tf_op jit(solution)/shard_map/reduce_scatter | solution.py:224
  1443.0 59.8 %copy-start.13 = (bf16[512,10,256]{0,2,1:T(8,128)(2,1)}, bf16[512,10,256]{0,2,1:T(8,128)(2,1)S(1)}, u32[]{:S(2)}) copy-start(bf16[512,10,256]{0,2,1:T(8,128)(2,1)S(1)} %convolution_convert_fusion.3) | copy-start | bytes 7864324
  1502.8 65.8 %copy-start.10 = (bf16[512,10,4,32]{0,3,2,1:T(8,128)(2,1)S(1)}, bf16[512,10,4,32]{0,3,2,1:T(8,128)(2,1)}, u32[]{:S(2)}) copy-start(bf16[512,10,4,32]{0,3,2,1:T(8,128)(2,1)} %get-tuple-element.34) | copy-start | bytes 3932164
  1502.8 65.8 %copy-start.11 = (bf16[512,10,4,32]{0,3,2,1:T(8,128)(2,1)S(1)}, bf16[512,10,4,32]{0,3,2,1:T(8,128)(2,1)}, u32[]{:S(2)}) copy-start(bf16[512,10,4,32]{0,3,2,1:T(8,128)(2,1)} %get-tuple-element.35) | copy-start | bytes 3932164
  1587.8 141.9 %reduce-scatter.26.cloned.1.call-start = ((), (), s32[]{:S(2)}) async-start(), calls=%async_computation.23 | async-start | bytes 7864320 | tf_op jit(solution)/shard_map/reduce_scatter | solution.py:227
  1631.1 149.1 %reduce-scatter.42.cloned.1.call-start = ((), (), s32[]{:S(2)}) async-start(), calls=%async_computation.31 | async-start | bytes 2359296
  1649.5 159.6 %reduce-scatter.38.cloned.1.call-start = ((), (), s32[]{:S(2)}) async-start(), calls=%async_computation.29 | async-start | bytes 2359296 | tf_op jit(solution)/shard_map/reduce_scatter | solution.py:277
  1667.7 18.4 copy-start.12
  1667.7 185.9 %reduce-scatter.36.cloned.1.call-start = ((), (), s32[]{:S(2)}) async-start(), calls=%async_computation.28 | async-start | bytes 2359296 | tf_op jit(solution)/shard_map/reduce_scatter | solution.py:274
  1686.0 205.0 %reduce-scatter.40.cloned.1.call-start = ((), (), s32[]{:S(2)}) async-start(), calls=%async_computation.30 | async-start | bytes 589824
  1716.1 212.0 %reduce-scatter.30.cloned.1.call-start = ((), (), s32[]{:S(2)}) async-start(), calls=%async_computation.25 | async-start | bytes 589824 | tf_op jit(solution)/shard_map/reduce_scatter | solution.py:262
  1729.8 18.1 copy-start.50
  1746.7 218.8 %reduce-scatter.32.cloned.1.call-start = ((), (), s32[]{:S(2)}) async-start(), calls=%async_computation.26 | async-start | bytes 589824 | tf_op jit(solution)/shard_map/reduce_scatter | solution.py:265
  1747.3 255.3 %reduce-scatter.34.cloned.1.call-start = ((), (), s32[]{:S(2)}) async-start(), calls=%async_computation.27 | async-start | bytes 589824 | tf_op jit(solution)/shard_map/reduce_scatter | solution.py:268
  1747.8 435.1 %reduce-scatter.28.cloned.1.call-start = ((), (), s32[]{:S(2)}) async-start(), calls=%async_computation.24 | async-start | bytes 13107200 | tf_op jit(solution)/shard_map/reduce_scatter | solution.py:250
  1761.1 604.4 %reduce-scatter.20.cloned.1.call-start = ((), (), s32[]{:S(2)}) async-start(), calls=%async_computation.18 | async-start | bytes 13107200 | tf_op jit(solution)/shard_map/reduce_scatter | solution.py:142
  1780.1 402.8 %copy-start.5 = (bf16[128,10,1024]{2,0,1:T(8,128)(2,1)S(1)}, bf16[128,10,1024]{2,0,1:T(8,128)(2,1)}, u32[]{:S(2)}) copy-start(bf16[128,10,1024]{2,0,1:T(8,128)(2,1)} %param.15) | copy-start | bytes 7864324
  1780.1 402.8 %copy-start.27 = (f32[128,10]{0,1:T(8,128)S(1)}, f32[128,10]{0,1:T(8,128)}, u32[]{:S(2)}) copy-start(f32[128,10]{0,1:T(8,128)} %copy-done.26) | copy-start | bytes 15364
  1780.1 402.8 %copy-start.32 = (f32[128,10]{0,1:T(8,128)S(1)}, f32[128,10]{0,1:T(8,128)}, u32[]{:S(2)}) copy-start(f32[128,10]{0,1:T(8,128)} %copy-done.31) | copy-start | bytes 15364
  1780.1 402.8 %copy-start.42 = (f32[1024]{0:T(1024)S(1)}, f32[1024]{0:T(1024)}, u32[]{:S(2)}) copy-start(f32[1024]{0:T(1024)} %param.16) | copy-start | bytes 12292
  1780.2 406.9 %copy-start.43 = (f32[1024]{0:T(1024)S(1)}, f32[1024]{0:T(1024)}, u32[]{:S(2)}) copy-start(f32[1024]{0:T(1024)} %get-tuple-element.13) | copy-start | bytes 12292
  1780.2 406.9 %copy-start.44 = (f32[1024]{0:T(1024)S(1)}, f32[1024]{0:T(1024)}, u32[]{:S(2)}) copy-start(f32[1024]{0:T(1024)} %get-tuple-element.19) | copy-start | bytes 12292
  1780.2 585.4 %copy-start.25 = (f32[128,10]{0,1:T(8,128)S(1)}, f32[128,10]{0,1:T(8,128)}, u32[]{:S(2)}) copy-start(f32[128,10]{0,1:T(8,128)} %copy-done.23) | copy-start | bytes 15364
  1780.2 585.4 %copy-start.30 = (f32[128,10]{0,1:T(8,128)S(1)}, f32[128,10]{0,1:T(8,128)}, u32[]{:S(2)}) copy-start(f32[128,10]{0,1:T(8,128)} %copy-done.28) | copy-start | bytes 15364
  1780.2 585.4 %copy-start.34 = (f32[128,10]{0,1:T(8,128)S(1)}, f32[128,10]{0,1:T(8,128)}, u32[]{:S(2)}) copy-start(f32[128,10]{0,1:T(8,128)} %copy-done.33) | copy-start | bytes 15364
  1780.2 585.4 %copy-start.36 = (f32[128,10]{0,1:T(8,128)S(1)}, f32[128,10]{0,1:T(8,128)}, u32[]{:S(2)}) copy-start(f32[128,10]{0,1:T(8,128)} %copy-done.35) | copy-start | bytes 15364
  1780.2 585.4 %copy-start.40 = (f32[1024]{0:T(1024)S(1)}, f32[1024]{0:T(1024)}, u32[]{:S(2)}) copy-start(f32[1024]{0:T(1024)} %param.22) | copy-start | bytes 12292
  (22 other events, 114.6 us)
Sparse Core Ops, SparseCore 0:
  15.3 186.6 all-gather.6
  245.4 66.7 all-gather.10
  314.3 68.5 all-gather.8
  430.9 178.0 reduce-scatter.17
  617.4 184.9 all-gather.12
  803.8 182.0 all-gather.14
  1059.2 176.1 reduce-scatter.21
  1246.7 184.9 all-gather.16
  1587.9 63.8 reduce-scatter.23
  1654.1 65.6 reduce-scatter.25
  1723.1 41.1 reduce-scatter.41
  1767.8 41.2 reduce-scatter.37
  1812.4 41.1 reduce-scatter.35
  1856.9 34.1 reduce-scatter.39
  1894.0 34.0 reduce-scatter.29
  1931.3 34.1 reduce-scatter.31
  1968.4 34.1 reduce-scatter.33
  2004.9 177.9 reduce-scatter.27
  2185.4 180.0 reduce-scatter.19
where the time goes:
time: 2390 us; the launch traced here: 2380 us
  waiting for transfers between devices  1640 us (69%)
  matrix products  450 us (19%)
  other arithmetic  159 us (7%)
  local copies, waits for them, and re-layouts  61.5 us (3%)
  blocking collectives  51.2 us (2%)
    all_gather x1, waiting for transfers between devices, shards(): first_full = lax.all_gather(first_low, 'tensor', axis=0, tiled=True)  186 us
    all_gather x1, waiting for transfers between devices, shards(): lax.all_gather(grad_residual2.astype(jnp.bfloat16), 'tensor', axis=0, til...  185 us
    reduce_scatter x1, waiting for transfers between devices, shards(): lax.psum_scatter(jnp.einsum('rwe,de->rwd', block_part, w_joined, preferre...  179 us
    reduce_scatter x1, waiting for transfers between devices, shards(): lax.psum_scatter(jnp.einsum('rwe,ed->rwd', block_part, w_out, preferred_e...  178 us
    reduce_scatter x1, waiting for transfers between devices, shards(): lax.psum_scatter((jnp.einsum('rwf,df->rwd', grad_gate, w_gate, preferred_...  176 us
    all_gather x1, waiting for transfers between devices, shards(): second_full = lax.all_gather(second_low, 'tensor', axis=0, tiled=True)  173 us
    all_gather x1, waiting for transfers between devices, shards(): lax.all_gather(grad_out.astype(jnp.bfloat16), 'tensor', axis=0, tiled=True)  151 us
    reduce_scatter x1, waiting for transfers between devices, shards(): lax.psum_scatter(jnp.einsum('rwf,fd->rwd', block_part, w_down, preferred_...  130 us
  transfers between devices with their start and end apart: 19, of which 16 were waited for; matrix products, arithmetic and copies ran while one was open for 13% of the time, Pallas kernels for 0%

commit v1 on v0

--- a/solution.py
+++ b/solution.py
@@ -1,8 +1,12 @@
 import math
+
+import functools
 
 import jax
 import jax.numpy as jnp
 from jax import lax
+from jax.experimental import pallas as pl
+from jax.experimental.pallas import tpu as pltpu
 from jax.sharding import PartitionSpec as P
 
 HEAD_DIM = 64
@@ -60,7 +64,7 @@
     )
 
 
-def shards(
+def block_shards(
     tokens,
     norm1_gain,
     norm1_bias,
@@ -302,6 +306,416 @@
         summed[5],
         summed[6],
     )
+
+
+BF = jnp.bfloat16
+F32 = jnp.float32
+LANES = 128
+
+
+def dot_t(a, b):
+    return lax.dot_general(a, b, (((1,), (1,)), ((), ())), preferred_element_type=F32)
+
+
+def dot_n(a, b):
+    return lax.dot_general(a, b, (((1,), (0,)), ((), ())), preferred_element_type=F32)
+
+
+def t_dot(a, b):
+    return lax.dot_general(a, b, (((0,), (0,)), ((), ())), preferred_element_type=F32)
+
+
+def swap_halves(x):
+    half = HEAD_DIM // 2
+    lane = lax.broadcasted_iota(jnp.int32, x.shape, 1)
+    down = pltpu.roll(x, half, 1)
+    up = pltpu.roll(x, LANES - half, 1)
+    return jnp.where(lane % HEAD_DIM < half, up, down)
+
+
+def head_mask(h):
+    lane = lax.broadcasted_iota(jnp.int32, (1, LANES), 1)
+    return jnp.where(lane // HEAD_DIM == h, 1.0, 0.0).astype(BF)
+
+
+def qkv_kernel(x_ref, w_ref, cos_ref, sin_ref, out_ref):
+    acc = dot_n(x_ref[...], w_ref[...])
+    cos, sin = cos_ref[...], sin_ref[...]
+    chunks = acc.shape[1] // LANES
+    third = chunks // 3
+    for c in range(chunks):
+        part = acc[:, c * LANES : (c + 1) * LANES]
+        if c < 2 * third:
+            part = part * cos + swap_halves(part) * sin
+        if c < third:
+            part = part * (1.0 / math.sqrt(HEAD_DIM))
+        out_ref[:, c * LANES : (c + 1) * LANES] = part.astype(BF)
+
+
+def qkv_project(x, w, cos, sin, block):
+    rows, width = x.shape
+    tile = 256
+    return pl.pallas_call(
+        qkv_kernel,
+        grid=(w.shape[1] // block, rows // tile),
+        in_specs=[
+            pl.BlockSpec((tile, width), lambda t, r: (r, 0)),
+            pl.BlockSpec((width, block), lambda t, r: (0, t)),
+            pl.BlockSpec((tile, LANES), lambda t, r: (r, 0)),
+            pl.BlockSpec((tile, LANES), lambda t, r: (r, 0)),
+        ],
+        out_specs=pl.BlockSpec((tile, block), lambda t, r: (r, t)),
+        out_shape=jax.ShapeDtypeStruct((rows, w.shape[1]), BF),
+        cost_estimate=pl.CostEstimate(
+            flops=2 * rows * width * w.shape[1], bytes_accessed=2 * rows * (width + w.shape[1]), transcendentals=0
+        ),
+        name="qkv_project",
+    )(x, w, cos, sin)
+
+
+def attend_kernel(q_ref, k_ref, v_ref, o_ref):
+    q, k, v = q_ref[...], k_ref[...], v_ref[...]
+    outs = []
+    for h in range(LANES // HEAD_DIM):
+        s = dot_t(q * head_mask(h), k)
+        p = jnp.exp(s - jnp.max(s, axis=1, keepdims=True))
+        norm = jnp.sum(p, axis=1, keepdims=True)
+        outs.append(dot_n(p.astype(BF), v) / norm)
+    lane = lax.broadcasted_iota(jnp.int32, outs[0].shape, 1)
+    o_ref[...] = jnp.where(lane < HEAD_DIM, outs[0], outs[1]).astype(BF)
+
+
+def attend(qkv, block):
+    rows = qkv.shape[0]
+    per = block // 3 // LANES
+    pairs = qkv.shape[1] // block * per
+    tile = 512
+    spec = lambda which: lambda p, r: (0, p // per * 3 * per + which * per + p % per)
+    return pl.pallas_call(
+        attend_kernel,
+        grid=(pairs, rows // tile),
+        in_specs=[
+            pl.BlockSpec((tile, LANES), lambda p, r: (r, p // per * 3 * per + p % per)),
+            pl.BlockSpec((rows, LANES), spec(1)),
+            pl.BlockSpec((rows, LANES), spec(2)),
+        ],
+        out_specs=pl.BlockSpec((tile, LANES), lambda p, r: (r, p)),
+        out_shape=jax.ShapeDtypeStruct((rows, pairs * LANES), BF),
+        cost_estimate=pl.CostEstimate(
+            flops=16 * pairs * rows * rows * LANES, bytes_accessed=8 * rows * pairs * LANES, transcendentals=2 * pairs * rows * rows
+        ),
+        name="attend",
+    )(qkv, qkv, qkv)
+
+
+def attend_back_kernel(q_ref, g_ref, k_ref, v_ref, cos_ref, sin_ref, qcos_ref, qsin_ref, dq_ref, dk_ref, dv_ref):
+    q, g, k, v = q_ref[...], g_ref[...], k_ref[...], v_ref[...]
+    dq = []
+    all_p, all_ds, all_q, all_g = [], [], [], []
+    for h in range(LANES // HEAD_DIM):
+        mask = head_mask(h)
+        qh, gh = q * mask, g * mask
+        s = dot_t(qh, k)
+        p = jnp.exp(s - jnp.max(s, axis=1, keepdims=True))
+        p = p / jnp.sum(p, axis=1, keepdims=True)
+        dp = dot_t(gh, v)
+        ds = (p * (dp - jnp.sum(p * dp, axis=1, keepdims=True))).astype(BF)
+        dq.append(dot_n(ds, k))
+        all_p.append(p.astype(BF))
+        all_ds.append(ds)
+        all_q.append(qh)
+        all_g.append(gh)
+    lane = lax.broadcasted_iota(jnp.int32, dq[0].shape, 1)
+    dq = jnp.where(lane < HEAD_DIM, dq[0], dq[1]) * (1.0 / math.sqrt(HEAD_DIM))
+    dq_ref[...] = (dq * qcos_ref[...] - swap_halves(dq) * qsin_ref[...]).astype(BF)
+    dk = t_dot(jnp.concatenate(all_ds, axis=0), jnp.concatenate(all_q, axis=0))
+    dk_ref[...] = (dk * cos_ref[...] - swap_halves(dk) * sin_ref[...]).astype(BF)
+    dv_ref[...] = t_dot(jnp.concatenate(all_p, axis=0), jnp.concatenate(all_g, axis=0)).astype(BF)
+
+
+def attend_back(q_rows, grad_rows, qkv, block, cos, sin, row_cos, row_sin):
+    rows, masked = qkv.shape[0], q_rows.shape[0]
+    per = block // 3 // LANES
+    pairs = qkv.shape[1] // block * per
+    spec = lambda which: lambda p: (0, p // per * 3 * per + which * per + p % per)
+    pick = pl.BlockSpec((masked, LANES), lambda p: (0, p))
+    full = pl.BlockSpec((rows, LANES), lambda p: (0, p))
+    same = pl.BlockSpec((rows, LANES), lambda p: (0, 0))
+    row_same = pl.BlockSpec((masked, LANES), lambda p: (0, 0))
+    return pl.pallas_call(
+        attend_back_kernel,
+        grid=(pairs,),
+        in_specs=[
+            pick,
+            pick,
+            pl.BlockSpec((rows, LANES), spec(1)),
+            pl.BlockSpec((rows, LANES), spec(2)),
+            same,
+            same,
+            row_same,
+            row_same,
+        ],
+        out_specs=[pick, full, full],
+        out_shape=[
+            jax.ShapeDtypeStruct((masked, pairs * LANES), BF),
+            jax.ShapeDtypeStruct((rows, pairs * LANES), BF),
+            jax.ShapeDtypeStruct((rows, pairs * LANES), BF),
+        ],
+        cost_estimate=pl.CostEstimate(
+            flops=20 * pairs * rows * masked * LANES, bytes_accessed=10 * rows * pairs * LANES, transcendentals=2 * pairs * rows * masked
+        ),
+        name="attend_back",
+    )(q_rows, grad_rows, qkv, qkv, cos, sin, row_cos, row_sin)
+
+
+def rotary_lanes(positions):
+    cosine, sine = rotary_tables(positions)
+    reps = LANES // HEAD_DIM
+    return (
+        jnp.concatenate([cosine, cosine] * reps, axis=1),
+        jnp.concatenate([-sine, sine] * reps, axis=1),
+    )
+
+
+def window_shards(
+    tokens,
+    norm1_gain,
+    norm1_bias,
+    w_query,
+    w_key,
+    w_value,
+    w_out,
+    norm2_gain,
+    norm2_bias,
+    w_gate,
+    w_up,
+    w_down,
+    out_grad,
+    masked_rows,
+    window_counts,
+):
+    rows_local, windows, width = tokens.shape
+    n_seq, n_ten = lax.axis_size("seq"), lax.axis_size("tensor")
+    n_dp = lax.axis_size("dp")
+    seq_index, ten_index = lax.axis_index("seq"), lax.axis_index("tensor")
+    shard_index = lax.axis_index("dp") * n_seq + seq_index
+    half = windows // n_seq
+    length = rows_local * n_seq * n_ten
+    share = length // n_ten
+    hw = w_query.shape[1]
+    block = 3 * hw
+    slots = masked_rows.shape[1]
+    part = slots // n_ten
+
+    tok = jnp.swapaxes(tokens, 0, 1).reshape(n_seq, half, rows_local, width)
+    own_tok = lax.all_to_all(
+        tok[:, :n_ten].reshape(n_seq * n_ten, rows_local, width), ("seq", "tensor"), 0, 0, tiled=True
+    ).reshape(length, width)
+    left_x = lax.all_to_all(tok[:, n_ten], "seq", 0, 0, tiled=True)
+    left_tok = lax.all_gather(left_x, "tensor", axis=1, tiled=False).reshape(length, width)
+
+    def cut(w, count):
+        size = w.shape[0] // count
+        return lax.dynamic_slice_in_dim(w, shard_index * size, size, axis=0)
+
+    shards_xy = n_dp * n_seq
+
+    def gather_columns(w):
+        w = lax.all_gather(cut(w, shards_xy), "tensor", axis=1, tiled=True)
+        return lax.all_gather(w, ("dp", "seq"), axis=0, tiled=True)
+
+    def gather_rows(w):
+        own = cut(w, shards_xy)
+        w = lax.all_gather(own, "tensor", axis=0, tiled=False)
+        w = lax.all_gather(w, ("dp", "seq"), axis=0, tiled=False)
+        return jnp.swapaxes(w, 0, 1).reshape(-1, w.shape[-1])
+
+    w_joined = jnp.concatenate([w_query, w_key, w_value], axis=1)
+    all_joined = gather_columns(w_joined)
+    all_out = gather_rows(w_out)
+    all_gate = gather_columns(w_gate)
+    all_up = gather_columns(w_up)
+    all_down = gather_rows(w_down)
+
+    live = jnp.arange(windows) < window_counts[0]
+    valid = (masked_rows < length) & live[:, None]
+    total = lax.psum(jnp.sum(valid.astype(jnp.int32)), "dp")
+    loss_weight = LOSS_SCALE / total.astype(F32)
+    first_window = seq_index * half
+    my_rows = lax.dynamic_slice_in_dim(masked_rows, first_window, half, 0)
+    my_valid = lax.dynamic_slice_in_dim(valid, first_window, half, 0)
+    cot = lax.dynamic_slice_in_dim(out_grad, first_window, half, 0).astype(F32) * loss_weight
+    cot = jnp.where(my_valid[:, :, None], cot, 0.0)
+    cot_low = cot.astype(BF)
+    own_rows = lax.dynamic_index_in_dim(my_rows, ten_index, 0, keepdims=False)
+    own_valid = lax.dynamic_index_in_dim(my_valid, ten_index, 0, keepdims=False)
+    own_cot = lax.dynamic_index_in_dim(cot, ten_index, 0, keepdims=False)
+    left_rows, left_valid, left_cot = my_rows[n_ten], my_valid[n_ten], cot[n_ten]
+    every = jnp.arange(length)
+    own_pick = ((own_rows[:, None] == every[None, :]) & own_valid[:, None]).astype(BF)
+    left_pick = ((left_rows[:, None] == every[None, :]) & left_valid[:, None]).astype(BF)
+
+    cos, sin = rotary_lanes(every)
+    own_cos, own_sin = rotary_lanes(own_rows)
+    left_cos, left_sin = rotary_lanes(left_rows)
+
+    def norm(x, gain, bias):
+        normed, inv_std = layer_stats(x)
+        return normed, inv_std, (normed * gain + bias).astype(BF)
+
+    _, _, left_first = norm(left_tok.astype(F32), norm1_gain, norm1_bias)
+    left_qkv = qkv_project(left_first, w_joined, cos, sin, block)
+    left_att = attend(left_qkv, block)
+    _, _, own_first = norm(own_tok.astype(F32), norm1_gain, norm1_bias)
+    own_qkv = qkv_project(own_first, all_joined, cos, sin, block)
+    own_att = attend(own_qkv, block)
+
+    def spread(x):
+        x = x.reshape(n_seq, n_ten, rows_local, x.shape[-1])
+        x = lax.all_to_all(x, "tensor", 1, 1, tiled=True)
+        return jnp.swapaxes(x, 1, 2).reshape(n_seq * rows_local, -1)
+
+    def my_part(x):
+        x = x.reshape(n_seq, n_ten, rows_local, x.shape[-1])
+        return lax.dynamic_index_in_dim(x, ten_index, 1, keepdims=False).reshape(n_seq * rows_local, -1)
+
+    left_att_part = spread(left_att)
+
+    pick_rows = lambda pick, x: dot_n(pick, x).astype(BF)
+    own_att_m = pick_rows(own_pick, own_att)
+    left_att_m = pick_rows(left_pick, left_att)
+    own_res_m = pick_rows(own_pick, own_tok).astype(F32) + dot_n(own_att_m, all_out)
+    own_normed2, own_inv2, own_second = norm(own_res_m, norm2_gain, norm2_bias)
+    sent = lax.all_gather(jnp.concatenate([own_second, left_att_m], axis=1), "tensor", axis=0, tiled=False)
+    left_att_full = jnp.swapaxes(sent[:, :, width:], 0, 1).reshape(slots, -1)
+    left_res_m = pick_rows(left_pick, left_tok).astype(F32) + dot_n(left_att_full, all_out)
+    left_normed2, left_inv2, left_second = norm(left_res_m, norm2_gain, norm2_bias)
+    second = jnp.concatenate([sent[:, :, :width].reshape(n_ten * slots, width), left_second], axis=0)
+
+    gate = dot_n(second, w_gate)
+    up = dot_n(second, w_up)
+    down_in = cot_low.reshape(half * slots, width)
+    grad_hidden = dot_t(down_in, w_down)
+    sig = jax.nn.sigmoid(gate)
+    silu = gate * sig
+    hidden_m = (silu * up).astype(BF)
+    grad_gate = (grad_hidden * up * sig * (1.0 + gate * (1.0 - sig))).astype(BF)
+    grad_up = (grad_hidden * silu).astype(BF)
+    grad_second = (dot_t(grad_gate, w_gate) + dot_t(grad_up, w_up)).astype(BF)
+    grad_second = jnp.concatenate(
+        [
+            grad_second[: n_ten * slots].reshape(n_ten, slots, width),
+            grad_second[n_ten * slots :].reshape(n_ten, part, width),
+        ],
+        axis=1,
+    ).reshape(n_ten * (slots + part), width)
+    grad_second = lax.psum_scatter(grad_second, "tensor", scatter_dimension=0, tiled=True)
+    left_grad_second = lax.all_gather(grad_second[slots:], "tensor", axis=0, tiled=True).astype(F32)
+    own_grad_second = grad_second[:slots].astype(F32)
+    grad_w_down = t_dot(hidden_m, down_in).astype(BF)
+    grad_w_gate = t_dot(second, grad_gate).astype(BF)
+    grad_w_up = t_dot(second, grad_up).astype(BF)
+
+    mine = lambda x: lax.dynamic_slice_in_dim(x, ten_index * part, part, 0)
+    grad_norm2_gain = jnp.sum(own_grad_second * own_normed2, axis=0) + jnp.sum(
+        mine(left_grad_second * left_normed2), axis=0
+    )
+    grad_norm2_bias = jnp.sum(own_grad_second, axis=0) + jnp.sum(mine(left_grad_second), axis=0)
+    own_gr2 = (own_cot + norm_back(own_grad_second, own_normed2, own_inv2, norm2_gain)).astype(BF)
+    left_gr2 = (left_cot + norm_back(left_grad_second, left_normed2, left_inv2, norm2_gain)).astype(BF)
+
+    own_gatt = dot_t(own_gr2, all_out).astype(BF)
+    left_gatt = dot_t(left_gr2, w_out).astype(BF)
+    on_tensor = (jnp.arange(n_ten) == ten_index).astype(BF)
+    left_att_wide = (left_att_m[:, None, :] * on_tensor[None, :, None]).reshape(slots, width)
+    grad_w_out = t_dot(
+        jnp.concatenate([own_att_m, left_att_wide], axis=0), jnp.concatenate([own_gr2, left_gr2], axis=0)
+    ).astype(BF)
+
+    def queries_of(pick, qkv):
+        groups = qkv.shape[1] // block
+        q = qkv.reshape(length, groups, block)[:, :, :hw].reshape(length, groups * hw)
+        return pick_rows(pick, q)
+
+    own_dq, own_dk, own_dv = attend_back(
+        queries_of(own_pick, own_qkv), own_gatt, own_qkv, block, cos, sin, own_cos, own_sin
+    )
+    left_dq, left_dk, left_dv = attend_back(
+        queries_of(left_pick, left_qkv), left_gatt, left_qkv, block, cos, sin, left_cos, left_sin
+    )
+
+    def join(pick, dq, dk, dv):
+        groups = dk.shape[1] // hw
+        dense_q = t_dot(pick, dq).astype(BF)
+        parts = [x.reshape(length, groups, 1, hw) for x in (dense_q, dk, dv)]
+        return jnp.concatenate(parts, axis=2).reshape(length, groups * block)
+
+    own_grads = join(own_pick, own_dq, own_dk, own_dv)
+    left_grads = join(left_pick, left_dq, left_dk, left_dv)
+    left_grads_part = spread(left_grads)
+    grad_first = jnp.concatenate([dot_t(own_grads, all_joined), dot_t(left_grads_part, all_joined)], axis=0)
+    grad_w_all = t_dot(own_first, own_grads)
+    left_block = t_dot(left_first, left_grads)
+    grad_w_all = (grad_w_all.reshape(width, n_ten, block) + left_block[:, None, :] * on_tensor.astype(F32)[None, :, None]).reshape(
+        width, n_ten * block
+    ).astype(BF)
+
+    both_tok = jnp.concatenate([own_tok, my_part(left_tok)], axis=0)
+    normed1, inv_std1 = layer_stats(both_tok.astype(F32))
+    grad_norm1_gain = jnp.sum(grad_first * normed1, axis=0)
+    grad_norm1_bias = jnp.sum(grad_first, axis=0)
+    gr2_dense = jnp.concatenate([t_dot(own_pick, own_gr2), dot_n(my_part(left_pick.T), left_gr2)], axis=0)
+    grad_both = (gr2_dense + norm_back(grad_first, normed1, inv_std1, norm1_gain)).astype(BF)
+
+    att = jnp.concatenate([own_att, left_att_part], axis=0)
+    residual2 = both_tok.astype(F32) + dot_n(att, all_out)
+    _, _, second_low = norm(residual2, norm2_gain, norm2_bias)
+    hidden = (jax.nn.silu(dot_n(second_low, all_gate)) * dot_n(second_low, all_up)).astype(BF)
+    out_both = (residual2 + dot_n(hidden, all_down)).astype(BF)
+
+    def send_back(x):
+        own = lax.all_to_all(
+            x[:length].reshape(n_seq * n_ten, rows_local, width), ("seq", "tensor"), 0, 0, tiled=True
+        ).reshape(n_seq, n_ten, rows_local, width)
+        left = lax.all_to_all(x[length:].reshape(n_seq, rows_local, width), "seq", 0, 0, tiled=True)
+        both = jnp.concatenate([own, left[:, None]], axis=1).reshape(windows, rows_local, width)
+        return jnp.swapaxes(both, 0, 1)
+
+    output = send_back(out_both)
+    grad_tokens = send_back(grad_both).astype(F32)
+
+    def summed(x, dim):
+        return lax.psum_scatter(x, ("dp", "seq"), scatter_dimension=dim, tiled=True)
+
+    gw_all = lax.psum_scatter(summed(grad_w_all, 0), "tensor", scatter_dimension=1, tiled=True).astype(F32)
+    gw_out = lax.psum_scatter(summed(grad_w_out, 1), "tensor", scatter_dimension=0, tiled=True).astype(F32)
+    gw_gate, gw_up = summed(grad_w_gate, 0).astype(F32), summed(grad_w_up, 0).astype(F32)
+    gw_down = summed(grad_w_down, 1).astype(F32)
+    vectors = [
+        lax.psum_scatter(v, ("dp", "seq", "tensor"), scatter_dimension=0, tiled=True)
+        for v in (grad_norm1_gain, grad_norm1_bias, grad_norm2_gain, grad_norm2_bias)
+    ]
+    return (
+        output,
+        grad_tokens,
+        vectors[0],
+        vectors[1],
+        gw_all[:, :hw],
+        gw_all[:, hw : 2 * hw],
+        gw_all[:, 2 * hw :],
+        gw_out,
+        vectors[2],
+        vectors[3],
+        gw_gate,
+        gw_up,
+        gw_down,
+    )
+
+
+def shards(tokens, *rest):
+    n_seq, n_ten = lax.axis_size("seq"), lax.axis_size("tensor")
+    whole = tokens.shape[1] % n_seq == 0 and tokens.shape[1] // n_seq == n_ten + 1
+    return (window_shards if whole else block_shards)(tokens, *rest)
 
 
 def solution(mesh):

time: 2390 us -> 930 us (0.39)
  waiting for transfers between devices: 1640 us -> 342 us
  matrix products: 450 us -> 141 us
  Pallas kernels: 0 us -> 94.8 us
  other arithmetic: 159 us -> 73.5 us
  blocking collectives: 51.2 us -> 118 us
  local copies, waits for them, and re-layouts: 61.5 us -> 103 us
  starting transfers between devices: 1.17 us -> 32.4 us
    reduce_scatter x11 -> x6, waiting for transfers between devices: 840 us -> 96.3 us  [the longest x3 86 us: summed(): return lax.psum_scatter(x, ('dp', 'seq'), scatter_dimension=dim, tiled=True)]
    all_gather x6 -> x10, waiting for transfers between devices: 767 us -> 157 us  [the longest x2 57.8 us: gather_columns(): w = lax.all_gather(cut(w, shards_xy), 'tensor', axis=1, tiled=True)]
    dot_general x22 -> x30, matrix products: 450 us -> 141 us  [the longest x14 73.4 us: dot_n(): lax.dot_general(a, b, (((1,), (0,)), ((), ())), preferred_element_type=F32)]
    pallas_call x0 -> x6, Pallas kernels: none -> 94.8 us  [the longest x2 44.7 us: attend(): pl.pallas_call(attend_kernel, grid=(pairs, rows // tile), in_specs=[pl.Bl...]
    all_gather x0 -> x3, blocking collectives: none -> 59.9 us  [the longest x1 29.2 us: gather_columns(): w = lax.all_gather(cut(w, shards_xy), 'tensor', axis=1, tiled=True)]
    convert_element_type x11 -> x16, other arithmetic: 85.5 us -> 31.6 us  [the longest x5 10.8 us: norm(): return (normed, inv_std, (normed * gain + bias).astype(BF))]
    all_to_all x0 -> x7, waiting for transfers between devices: none -> 48.7 us  [the longest x2 37.8 us: send_back(): lax.all_to_all(x[:length].reshape(n_seq * n_ten, rows_local, width), ('se...]
    all_to_all x0 -> x7, starting transfers between devices: none -> 30.9 us  [the longest x2 9.58 us: send_back(): lax.all_to_all(x[:length].reshape(n_seq * n_ten, rows_local, width), ('se...]
  transfers between devices with their start and end apart: 19 -> 25, of which waited for: 16 -> 13; matrix products, arithmetic and copies ran while one was open for 13% -> 32% of each run, Pallas kernels for 0% -> 4%
where the time goes in v1:
time: 930 us; the launch traced here: 922 us
  waiting for transfers between devices  342 us (37%)
  matrix products  141 us (15%)
  blocking collectives  118 us (13%)
  local copies, waits for them, and re-layouts  103 us (11%)
  Pallas kernels  94.8 us (10%)
  other arithmetic  73.5 us (8%)
  starting transfers between devices  32.4 us (3%)
  between operations  17.2 us (2%)
    reduce_scatter x3, waiting for transfers between devices, summed(): return lax.psum_scatter(x, ('dp', 'seq'), scatter_dimension=dim, tiled=True)  86 us
    dot_general x14, matrix products, dot_n(): lax.dot_general(a, b, (((1,), (0,)), ((), ())), preferred_element_type=F32)  73.4 us
    all_gather x2, waiting for transfers between devices, gather_columns(): w = lax.all_gather(cut(w, shards_xy), 'tensor', axis=1, tiled=True)  57.8 us
    all_gather x2, waiting for transfers between devices, gather_rows(): w = lax.all_gather(w, ('dp', 'seq'), axis=0, tiled=False)  49.5 us
    pallas_call x2, Pallas kernels, attend(): pl.pallas_call(attend_kernel, grid=(pairs, rows // tile), in_specs=[pl.Bl...  44.7 us
    unnamed x20, waiting for transfers between devices  40.6 us
    unnamed x1, blocking collectives  39.8 us
    dot_general x9, matrix products, t_dot(): lax.dot_general(a, b, (((0,), (0,)), ((), ())), preferred_element_type=F32)  38.3 us
  transfers between devices with their start and end apart: 25, of which 13 were waited for; matrix products, arithmetic and copies ran while one was open for 32% of the time, Pallas kernels for 4%

profile of v1, /device:TPU:0, one launch (start us, length us, event | category | flops | bytes accessed | tf_op | source)
XLA Modules:
  0.0 922.0 jit_solution(16646068479631233765)
XLA Ops:
  8.5 12.6 %all_to_all.40 = bf16[2,128,1024]{2,1,0:T(8,128)(2,1)} all-to-all(bf16[2,128,1024]{2,1,0:T(8,128)(2,1)S(1)} %slice_bitcast_fusion.3), channel_id=1, replica_groups=mesh['dp'=4,'seq'=2,'tensor'=4] {'seq'}, dimensions={0} | all-to-all | bytes 1048576 | tf_op jit(solution)/shard_map/all_to_all | solution.py:514
  22.0 16.5 %all-gather.1 = bf16[128,1024]{1,0:T(8,128)(2,1)} all-gather(bf16[32,1024]{1,0:T(8,128)(2,1)S(1)} %constant_dynamic-slice_fusion.9), channel_id=3, replica_groups=mesh['dp'=4,'seq'=2,'tensor'=4] {'tensor'}, dimensions={0}, use_global_device_ids=true | all-gather | bytes 327680 | tf_op jit(solution)/shard_map/all_gather | solution.py:529
  40.9 29.2 %all_gather.59 = bf16[128,3072]{1,0:T(8,128)(2,1)} all-gather(bf16[128,768]{1,0:T(8,128)(2,1)S(1)} %constant_dynamic-slice_fusion.10), channel_id=1, replica_groups=mesh['dp'=4,'seq'=2,'tensor'=4] {'tensor'}, dimensions={1}, use_global_device_ids=true | all-gather | bytes 983040 | tf_op jit(solution)/shard_map/all_gather | solution.py:524
  73.3 5.4 all-to-all-start
  86.9 49.5 %all-gather.29.cloned.1.call-done = bf16[32,32,1024]{2,1,0:T(8,128)(2,1)} async-done(((bf16[4,32,1024]{2,1,0:T(8,128)(2,1)}), bf16[32,32,1024]{2,1,0:T(8,128)(2,1)}) %all-gather.29.cloned.1.call-update) | async-done | bytes 2097168 | tf_op jit(solution)/shard_map/all_gather | solution.py:530
  144.0 4.5 add_convert_fusion.4
  148.6 6.0 qkv_project.3.q_ref.k_ref.v_ref
  154.5 10.0 %attend.3 = bf16[1024,256]{1,0:T(8,128)(2,1)} custom-call(bf16[1024,768]{1,0:T(8,128)(2,1)} %qkv_project.3.q_ref.k_ref.v_ref, bf16[1024,768]{1,0:T(8,128)(2,1)} %qkv_project.3.q_ref.k_ref.v_ref, bf16[1024,768]{1,0:T(8,128)(2,1)} %qkv_project.3.q_ref.k_ref.v_ref), custom_call_target="tpu_custom_call" | custom-call | flops 4294967296 | bytes 2097152 | tf_op jit(solution)/shard_map/attend/pallas_call | solution.py:394
  168.0 15.8 %all-gather.17.cloned.1.call-done.w_ref = bf16[1024,3072]{1,0:T(8,128)(2,1)} async-done(((bf16[128,3072]{1,0:T(8,128)(2,1)}), bf16[1024,3072]{1,0:T(8,128)(2,1)}) %all-gather.17.cloned.1.call-update) | async-done | bytes 6291472 | tf_op jit(solution)/shard_map/all_gather | solution.py:525
  183.8 19.5 %qkv_project.2.q_ref.k_ref.v_ref = bf16[1024,3072]{1,0:T(8,128)(2,1)} custom-call(bf16[1024,1024]{1,0:T(8,128)(2,1)} %get-tuple-element.59.x_ref, bf16[1024,3072]{1,0:T(8,128)(2,1)} %all-gather.17.cloned.1.call-done.w_ref, f32[1024,128]{1,0:T(8,128)} %get-tuple-element.87.cos_ref, f32[1024,128]{1,0:T(8,128)} %get-tuple-element.88.sin_ref), custom_call_target="tpu_custom_call" | custom-call | flops 6442450944 | bytes 8388608 | tf_op jit(solution)/shard_map/qkv_project/pallas_call | solution.py:358
  203.3 34.8 %attend.2 = bf16[1024,1024]{1,0:T(8,128)(2,1)} custom-call(bf16[1024,3072]{1,0:T(8,128)(2,1)} %qkv_project.2.q_ref.k_ref.v_ref, bf16[1024,3072]{1,0:T(8,128)(2,1)} %qkv_project.2.q_ref.k_ref.v_ref, bf16[1024,3072]{1,0:T(8,128)(2,1)} %qkv_project.2.q_ref.k_ref.v_ref), custom_call_target="tpu_custom_call" | custom-call | flops 17179869184 | bytes 8388608 | tf_op jit(solution)/shard_map/attend/pallas_call | solution.py:394
  246.8 5.7 psum.7
  253.2 4.3 fusion.93
  258.0 22.6 %all-gather.35.cloned.1.call-done = bf16[640,1280]{1,0:T(8,128)(2,1)} async-done(((bf16[160,1280]{1,0:T(8,128)(2,1)}), bf16[640,1280]{1,0:T(8,128)(2,1)}) %all-gather.35.cloned.1.call-update) | async-done | bytes 1638416 | tf_op jit(solution)/shard_map/all_gather | solution.py:589
  298.2 10.7 %all-gather.31.cloned.1.call-done = bf16[512,1024]{1,0:T(8,128)(2,1)} async-done(((bf16[128,1024]{1,0:T(8,128)(2,1)}), bf16[512,1024]{1,0:T(8,128)(2,1)}) %all-gather.31.cloned.1.call-update) | async-done | bytes 1048592 | tf_op jit(solution)/shard_map/all_gather | solution.py:529
  309.0 28.8 %all-gather.19.cloned.1.call-done = bf16[128,4096]{1,0:T(8,128)(2,1)} async-done(((bf16[128,1024]{1,0:T(8,128)(2,1)}), bf16[128,4096]{1,0:T(8,128)(2,1)}) %all-gather.19.cloned.1.call-update) | async-done | bytes 1048592 | tf_op jit(solution)/shard_map/all_gather | solution.py:524
  337.9 29.0 %all-gather.23.cloned.1.call-done = bf16[128,4096]{1,0:T(8,128)(2,1)} async-done(((bf16[128,1024]{1,0:T(8,128)(2,1)}), bf16[128,4096]{1,0:T(8,128)(2,1)}) %all-gather.23.cloned.1.call-update) | async-done | bytes 1048592 | tf_op jit(solution)/shard_map/all_gather | solution.py:524
  378.8 12.3 %reshape.409 = bf16[1024,4,768]{2,1,0:T(4,128)(2,1)} reshape(bf16[1024,3072]{1,0:T(8,128)(2,1)} %qkv_project.2.q_ref.k_ref.v_ref) | data formatting | bytes 12582912 | tf_op jit(solution)/shard_map/reshape | solution.py:637
  394.6 10.3 %reduce-scatter.13.cloned.1.call-done = bf16[200,1024]{1,0:T(8,128)(2,1)} async-done(((bf16[800,1024]{1,0:T(8,128)(2,1)}), bf16[200,1024]{1,0:T(8,128)(2,1)}) %reduce-scatter.13.cloned.1.call-update) | async-done | bytes 409616 | tf_op jit(solution)/shard_map/reduce_scatter | solution.py:612
  405.9 14.2 %all_gather.75 = bf16[160,1024]{1,0:T(8,128)(2,1)S(1)} all-gather(bf16[40,1024]{1,0:T(8,128)(2,1)S(1)} %slice.90), channel_id=1, replica_groups=mesh['dp'=4,'seq'=2,'tensor'=4] {'tensor'}, dimensions={0}, use_global_device_ids=true | all-gather | bytes 409600 | tf_op jit(solution)/shard_map/all_gather | solution.py:613
  427.6 4.0 copy.113
  434.8 18.4 %attend_back.2 = (bf16[160,1024]{1,0:T(8,128)(2,1)}, bf16[1024,1024]{1,0:T(8,128)(2,1)}, bf16[1024,1024]{1,0:T(8,128)(2,1)}) custom-call(bf16[160,1024]{1,0:T(8,128)(2,1)} %convolution_convert_fusion.7.q_ref, bf16[160,1024]{1,0:T(8,128)(2,1)} %convolution_convert_fusion.6.g_ref, bf16[1024,3072]{1,0:T(8,128)(2,1)} %qkv_project.2.q_ref.k_ref.v_ref, ...), custom_call_target="tpu_custom_call" | custom-call | flops 3355443200 | bytes 10485760 | tf_op jit(solution)/shard_map/attend_back/pallas_call | solution.py:445
  453.2 4.1 copy.110
  462.2 6.2 attend_back.3
  479.7 4.2 pad_maximum_fusion
  487.2 8.9 add_convert_fusion
  496.1 8.4 copy.107
  504.7 7.2 convolution_convert_fusion.2
  511.8 4.0 copy.115
  517.8 4.1 all-to-all-start.2
  527.1 7.0 all-to-all-done.2
  535.6 5.3 fusion.110
  548.5 8.2 copy.94
  556.7 19.8 %fusion.29 = f32[1280,4096]{1,0:T(8,128)} fusion(bf16[1024,4096]{1,0:T(8,128)(2,1)} %all-gather.21.cloned.1.call-done, f32[1280,1024]{1,0:T(8,128)} %copy-done.18, f32[1024]{0:T(1024)S(1)} %copy-done.48, f32[1024]{0:T(1024)S(1)} %copy-done.43, f32[1280]{0:T(1024)S(1)} %add_rsqrt_fusion.1, f32[1280]{0:T(1024)S(1)} %broadcast_multiply_fusion.4), kind=kOutput, calls=%fused_computation.56 | convolution fusion | flops 10743971840 | bytes 34621440 | tf_op jit(solution)/shard_map/dot_general | solution.py:321
  582.6 4.6 all-to-all-start.5
  587.2 33.3 %add_convert_fusion.1 = bf16[1280,1024]{1,0:T(8,128)(2,1)} fusion(f32[1280,1024]{1,0:T(8,128)} %copy-done.18, bf16[4096,1024]{1,0:T(8,128)(2,1)} %bitcast.185, f32[1280,4096]{1,0:T(8,128)} %fusion.29, bf16[1024,4096]{1,0:T(8,128)(2,1)} %all-gather.25.cloned.1.call-done, f32[1024]{0:T(1024)S(1)} %copy-done.48, f32[1024]{0:T(1024)S(1)} %copy-done.43, ...), kind=kOutput, calls=%fused_computation.25 | convolution fusion | flops 21515468800 | bytes 45631488 | tf_op jit(solution)/shard_map/dot_general | solution.py:321
  625.6 13.1 %fusion.113 = (f32[1024]{0:T(1024)S(1)}, f32[1024,1024]{1,0:T(8,128)}) fusion(bf16[1024,3072]{0,1:T(8,128)(2,1)} %bitcast.197, bf16[1024,3072]{1,0:T(8,128)(2,1)} %all-gather.17.cloned.1.call-done.w_ref), kind=kOutput, calls=%fused_computation.220 | convolution fusion | flops 6443498496 | bytes 16781312 | tf_op jit(solution)/shard_map/dot_general | solution.py:317
  642.5 5.9 fusion.114
  648.4 5.1 fusion.11
  653.6 5.0 fusion.10
  671.5 5.2 all-to-all-start.3
  676.7 5.5 convolution_convert_fusion.4
  685.5 37.8 %all-to-all-done.3 = bf16[8,128,1024]{2,1,0:T(8,128)(2,1)S(1)} async-done(((bf16[8,128,1024]{2,1,0:T(8,128)(2,1)}), bf16[8,128,1024]{2,1,0:T(8,128)(2,1)S(1)}, u32[]{:S(2)}, u32[]{:S(2)}) %all-to-all-start.3) | async-done | bytes 2097184 | tf_op jit(solution)/shard_map/all_to_all | solution.py:677
  723.3 4.4 all-to-all-start.6
  730.2 39.8 %reduce-scatter.27.cloned.1.call-done = bf16[128,1024]{1,0:T(8,128)(2,1)} async-done(((bf16[1024,1024]{1,0:T(8,128)(2,1)}), bf16[128,1024]{1,0:T(8,128)(2,1)}) %reduce-scatter.27.cloned.1.call-update) | async-done | bytes 262160
  771.9 42.4 %reduce-scatter.23.cloned.1.call-done = bf16[128,1024]{1,0:T(8,128)(2,1)} async-done(((bf16[1024,1024]{1,0:T(8,128)(2,1)}), bf16[128,1024]{1,0:T(8,128)(2,1)}) %reduce-scatter.23.cloned.1.call-update) | async-done | bytes 262160 | tf_op jit(solution)/shard_map/reduce_scatter | solution.py:688
  816.1 43.5 %reduce-scatter.21.cloned.1.call-done = bf16[128,1024]{1,0:T(8,128)(2,1)} async-done(((bf16[1024,1024]{1,0:T(8,128)(2,1)}), bf16[128,1024]{1,0:T(8,128)(2,1)}) %reduce-scatter.21.cloned.1.call-update) | async-done | bytes 262160 | tf_op jit(solution)/shard_map/reduce_scatter | solution.py:688
  862.6 39.8 %all-reduce.4 = (f32[1024]{0:T(1024)S(1)}, f32[1024]{0:T(1024)S(1)}, f32[1024]{0:T(1024)S(1)}, f32[1024]{0:T(1024)S(1)}) all-reduce(f32[1024]{0:T(1024)S(1)} %get-tuple-element.25, f32[1024]{0:T(1024)S(1)} %reduce_sum.255, f32[1024]{0:T(1024)S(1)} %add.251, ...), channel_id=9, replica_groups=mesh['dp'=4,'seq'=2,'tensor'=4] {'dp','seq','tensor'}, use_global_device_ids=true, to_apply=%region_22.23.clone | all-reduce | flops 4096 | bytes 32768
  (299 shorter events, 167.7 us)
Async XLA Ops:
  7.2 235.2 %copy-start = (bf16[1024,1024]{1,0:T(8,128)(2,1)S(1)}, bf16[1024,1024]{1,0:T(8,128)(2,1)}, u32[]{:S(2)}) copy-start(bf16[1024,1024]{1,0:T(8,128)(2,1)} %param.26) | copy-start | bytes 6291460
  7.2 31.4 %copy-start.32 = (bf16[1024,256]{1,0:T(8,128)(2,1)S(1)}, bf16[1024,256]{1,0:T(8,128)(2,1)}, u32[]{:S(2)}) copy-start(bf16[1024,256]{1,0:T(8,128)(2,1)} %param.18) | copy-start | bytes 1572868
  7.2 31.4 %copy-start.33 = (bf16[1024,256]{1,0:T(8,128)(2,1)S(1)}, bf16[1024,256]{1,0:T(8,128)(2,1)}, u32[]{:S(2)}) copy-start(bf16[1024,256]{1,0:T(8,128)(2,1)} %param.19) | copy-start | bytes 1572868
  7.2 76.7 %all-gather.27.cloned.1.call-start = ((), (), s32[]{:S(2)}) async-start(), calls=%async_computation.27 | async-start | bytes 2621440 | tf_op jit(solution)/shard_map/all_gather | solution.py:515
  21.1 115.2 %all-gather.29.cloned.1.call-start = ((), (), s32[]{:S(2)}) async-start(), calls=%async_computation.28 | async-start | bytes 2359296 | tf_op jit(solution)/shard_map/all_gather | solution.py:530
  38.5 145.3 %all-gather.17.cloned.1.call-start = ((), (), s32[]{:S(2)}) async-start(), calls=%async_computation.16 | async-start | bytes 7077888 | tf_op jit(solution)/shard_map/all_gather | solution.py:525
  70.1 9.2 %copy-start.47 = (s32[10,160]{1,0:T(8,128)S(1)}, s32[10,160]{1,0:T(8,128)}, u32[]{:S(2)}) copy-start(s32[10,160]{1,0:T(8,128)} %param.28) | copy-start | bytes 19204
  73.3 66.3 %all-to-all-start = ((bf16[8,128,1024]{2,1,0:T(8,128)(2,1)}), bf16[8,128,1024]{2,1,0:T(8,128)(2,1)}, u32[]{:S(2)}, u32[]{:S(2)}) async-start(bf16[8,128,1024]{2,1,0:T(8,128)(2,1)} %bitcast.190), calls=%async_computation | async-start | bytes 4194304 | tf_op jit(solution)/shard_map/all_to_all | solution.py:511
  78.6 202.0 %all-gather.35.cloned.1.call-start = ((), (), s32[]{:S(2)}) async-start(), calls=%async_computation.31 | async-start | bytes 2048000 | tf_op jit(solution)/shard_map/all_gather | solution.py:589
  136.4 7.6 copy-start.41
  136.4 7.6 copy-start.44
  242.3 66.6 %all-gather.31.cloned.1.call-start = ((), (), s32[]{:S(2)}) async-start(), calls=%async_computation.29 | async-start | bytes 1310720 | tf_op jit(solution)/shard_map/all_gather | solution.py:529
  243.2 94.6 %all-gather.19.cloned.1.call-start = ((), (), s32[]{:S(2)}) async-start(), calls=%async_computation.17 | async-start | bytes 1310720 | tf_op jit(solution)/shard_map/all_gather | solution.py:524
  244.9 121.9 %all-gather.23.cloned.1.call-start = ((), (), s32[]{:S(2)}) async-start(), calls=%async_computation.19 | async-start | bytes 1310720 | tf_op jit(solution)/shard_map/all_gather | solution.py:524
  246.7 158.3 %reduce-scatter.13.cloned.1.call-start = ((), (), s32[]{:S(2)}) async-start(), calls=%async_computation.21 | async-start | bytes 2048000 | tf_op jit(solution)/shard_map/reduce_scatter | solution.py:612
  284.7 137.7 %copy-start.12 = (f32[160,1024]{1,0:T(8,128)}, f32[160,1024]{1,0:T(8,128)S(1)}, u32[]{:S(2)}) copy-start(f32[160,1024]{1,0:T(8,128)S(1)} %get-tuple-element.45) | copy-start | bytes 1966084
  298.1 71.9 %copy-start.5 = (bf16[2,512,1024]{2,1,0:T(8,128)(2,1)S(1)}, bf16[2,512,1024]{2,1,0:T(8,128)(2,1)}, u32[]{:S(2)}) copy-start(bf16[2,512,1024]{2,1,0:T(8,128)(2,1)} %all-gather.27.cloned.1.call-done) | copy-start | bytes 6291460
  298.2 250.3 %all-gather.33.cloned.1.call-start = ((), (), s32[]{:S(2)}) async-start(), calls=%async_computation.30 | async-start | bytes 9437184 | tf_op jit(solution)/shard_map/all_gather | solution.py:530
  308.9 247.8 %all-gather.21.cloned.1.call-start = ((), (), s32[]{:S(2)}) async-start(), calls=%async_computation.18 | async-start | bytes 9437184 | tf_op jit(solution)/shard_map/all_gather | solution.py:525
  337.8 249.4 %all-gather.25.cloned.1.call-start = ((), (), s32[]{:S(2)}) async-start(), calls=%async_computation.20 | async-start | bytes 9437184 | tf_op jit(solution)/shard_map/all_gather | solution.py:525
  366.8 360.9 %reduce-scatter.25.cloned.1.call-start = ((), (), s32[]{:S(2)}) async-start(), calls=%async_computation.32 | async-start | bytes 2359296
  405.0 20.1 %copy-start.35 = (bf16[160,1024]{1,0:T(8,128)(2,1)S(1)}, bf16[160,1024]{1,0:T(8,128)(2,1)}, u32[]{:S(2)}) copy-start(bf16[160,1024]{1,0:T(8,128)(2,1)} %broadcast_multiply_fusion) | copy-start | bytes 983044
  405.0 20.1 %copy-start.40 = (bf16[160,1024]{1,0:T(8,128)(2,1)S(1)}, bf16[160,1024]{1,0:T(8,128)(2,1)}, u32[]{:S(2)}) copy-start(bf16[160,1024]{1,0:T(8,128)(2,1)} %copy-done.39) | copy-start | bytes 983044
  453.2 8.1 copy-start.21
  453.2 8.1 copy-start.31
  468.5 6.1 copy-start.34
  474.1 255.5 %reduce-scatter.15.cloned.1.call-start = ((), (), s32[]{:S(2)}) async-start(), calls=%async_computation.22 | async-start | bytes 7077888 | tf_op jit(solution)/shard_map/reduce_scatter | solution.py:688
  504.6 265.4 %reduce-scatter.27.cloned.1.call-start = ((), (), s32[]{:S(2)}) async-start(), calls=%async_computation.33 | async-start | bytes 2359296
  517.8 16.2 %all-to-all-start.2 = ((bf16[2,4,128,256]{3,2,0,1:T(8,128)(2,1)}), bf16[2,4,128,256]{3,2,0,1:T(8,128)(2,1)}, u32[]{:S(2)}, u32[]{:S(2)}) async-start(bf16[2,4,128,256]{3,2,0,1:T(8,128)(2,1)} %copy.91), calls=%async_computation.2 | async-start | bytes 1048576 | tf_op jit(solution)/shard_map/all_to_all | solution.py:575
  522.0 292.3 %reduce-scatter.23.cloned.1.call-start = ((), (), s32[]{:S(2)}) async-start(), calls=%async_computation.26 | async-start | bytes 2359296 | tf_op jit(solution)/shard_map/reduce_scatter | solution.py:688
  522.2 13.4 %copy-start.8 = (bf16[4,8,32,1024]{3,2,1,0:T(8,128)(2,1)S(1)}, bf16[4,8,32,1024]{3,2,1,0:T(8,128)(2,1)}, u32[]{:S(2)}) copy-start(bf16[4,8,32,1024]{3,2,1,0:T(8,128)(2,1)} %copy.93) | copy-start | bytes 6291460
  556.7 19.8 %copy-start.15 = (bf16[1024,1,3,256]{0,3,2,1:T(8,128)(2,1)S(1)}, bf16[1024,1,3,256]{0,3,2,1:T(8,128)(2,1)}, u32[]{:S(2)}) copy-start(bf16[1024,1,3,256]{0,3,2,1:T(8,128)(2,1)} %copy.101) | copy-start | bytes 4718596
  582.6 56.1 %all-to-all-start.5 = ((bf16[2,4,128,768]{2,0,3,1:T(2,128)(2,1)}), bf16[2,4,128,768]{2,0,3,1:T(2,128)(2,1)}, u32[]{:S(2)}, u32[]{:S(2)}) async-start(bf16[2,4,128,768]{2,0,3,1:T(2,128)(2,1)} %copy.102), calls=%async_computation.6 | async-start | bytes 3145728 | tf_op jit(solution)/shard_map/all_to_all | solution.py:575
  638.7 22.2 %all-to-all-start.4 = ((bf16[2,128,1024]{2,1,0:T(8,128)(2,1)}), bf16[2,128,1024]{2,1,0:T(8,128)(2,1)S(1)}, u32[]{:S(2)}, u32[]{:S(2)}) async-start(bf16[2,128,1024]{2,1,0:T(8,128)(2,1)} %bitcast.25), calls=%async_computation.4 | async-start | bytes 1048576 | tf_op jit(solution)/shard_map/all_to_all | solution.py:680
  642.4 5.9 copy-start.10
  660.9 10.5 %all-to-all-start.7 = ((bf16[2,128,1024]{2,1,0:T(8,128)(2,1)}), bf16[2,128,1024]{2,1,0:T(8,128)(2,1)S(1)}, u32[]{:S(2)}, u32[]{:S(2)}) async-start(bf16[2,128,1024]{2,1,0:T(8,128)(2,1)} %bitcast.56), calls=%async_computation.8 | async-start | bytes 1048576 | tf_op jit(solution)/shard_map/all_to_all | solution.py:680
  664.4 12.3 %copy-start.38 = (bf16[160,1024]{1,0:T(8,128)(2,1)S(1)}, bf16[160,1024]{1,0:T(8,128)(2,1)}, u32[]{:S(2)}) copy-start(bf16[160,1024]{1,0:T(8,128)(2,1)} %copy-done.36) | copy-start | bytes 983044
  671.5 10.8 %copy-start.24 = (bf16[2,128,1024]{2,1,0:T(8,128)(2,1)}, bf16[2,128,1024]{2,1,0:T(8,128)(2,1)S(1)}, u32[]{:S(2)}) copy-start(bf16[2,128,1024]{2,1,0:T(8,128)(2,1)S(1)} %all-to-all-done.7) | copy-start | bytes 1572868
  671.5 51.8 %all-to-all-start.3 = ((bf16[8,128,1024]{2,1,0:T(8,128)(2,1)}), bf16[8,128,1024]{2,1,0:T(8,128)(2,1)S(1)}, u32[]{:S(2)}, u32[]{:S(2)}) async-start(bf16[8,128,1024]{2,1,0:T(8,128)(2,1)} %bitcast.191), calls=%async_computation.3 | async-start | bytes 4194304 | tf_op jit(solution)/shard_map/all_to_all | solution.py:677
  676.7 183.0 %reduce-scatter.21.cloned.1.call-start = ((), (), s32[]{:S(2)}) async-start(), calls=%async_computation.25 | async-start | bytes 2359296 | tf_op jit(solution)/shard_map/reduce_scatter | solution.py:688
  723.3 184.6 %all-to-all-start.6 = ((bf16[8,128,1024]{2,1,0:T(8,128)(2,1)}), bf16[8,128,1024]{2,1,0:T(8,128)(2,1)}, u32[]{:S(2)}, u32[]{:S(2)}) async-start(bf16[8,128,1024]{2,1,0:T(8,128)(2,1)} %bitcast.189), calls=%async_computation.7 | async-start | bytes 4194304 | tf_op jit(solution)/shard_map/all_to_all | solution.py:677
  727.7 133.8 %copy-start.17 = (bf16[160,1024]{1,0:T(8,128)(2,1)S(1)}, bf16[160,1024]{1,0:T(8,128)(2,1)}, u32[]{:S(2)}) copy-start(bf16[160,1024]{1,0:T(8,128)(2,1)} %copy-done.16) | copy-start | bytes 983044
  727.7 134.9 %copy-start.50 = (f32[1024]{0:T(1024)S(1)}, f32[1024]{0:T(1024)}, u32[]{:S(2)}) copy-start(f32[1024]{0:T(1024)} %get-tuple-element.33) | copy-start | bytes 12292
  727.7 134.9 %copy-start.49 = (f32[1024]{0:T(1024)S(1)}, f32[1024]{0:T(1024)}, u32[]{:S(2)}) copy-start(f32[1024]{0:T(1024)} %get-tuple-element.28) | copy-start | bytes 12292
  727.7 178.7 %reduce-scatter.19.cloned.1.call-start = ((), (), s32[]{:S(2)}) async-start(), calls=%async_computation.24 | async-start | bytes 327680 | tf_op jit(solution)/shard_map/reduce_scatter | solution.py:691
  729.6 183.5 %reduce-scatter.17.cloned.1.call-start = ((), (), s32[]{:S(2)}) async-start(), calls=%async_computation.23 | async-start | bytes 983040 | tf_op jit(solution)/shard_map/reduce_scatter | solution.py:690
  861.5 46.4 %copy-start.25 = (bf16[2,128,1024]{2,1,0:T(8,128)(2,1)S(1)}, bf16[2,128,1024]{2,1,0:T(8,128)(2,1)}, u32[]{:S(2)}) copy-start(bf16[2,128,1024]{2,1,0:T(8,128)(2,1)} %copy-done.24) | copy-start | bytes 1572868
  907.9 6.8 copy-start.1
  (35 other events, 101.5 us)
Sparse Core Ops, SparseCore 0:
  21.2 61.1 all-gather.26
  84.3 51.9 all-gather.28
  138.2 45.5 all-gather.16
  242.5 38.1 all-gather.34
  282.1 26.7 all-gather.30
  310.3 27.4 all-gather.18
  339.4 27.4 all-gather.22
  369.1 35.7 reduce-scatter.12
  407.0 53.3 all-gather.32
  462.3 54.3 all-gather.20
  518.8 54.3 all-gather.24
  576.7 41.2 reduce-scatter.24
  621.4 76.0 reduce-scatter.14
  701.0 68.9 reduce-scatter.26
  773.1 41.2 reduce-scatter.22
  818.4 41.2 reduce-scatter.20
  862.4 19.6 reduce-scatter.18
  884.3 21.6 reduce-scatter.16

commit v2 on v1

--- a/solution.py
+++ b/solution.py
@@ -338,42 +338,185 @@
     return jnp.where(lane // HEAD_DIM == h, 1.0, 0.0).astype(BF)
 
 
-def qkv_kernel(x_ref, w_ref, cos_ref, sin_ref, out_ref):
-    acc = dot_n(x_ref[...], w_ref[...])
+MESH = pl.DeviceIdType.MESH
+
+
+def any_spec():
+    return pl.BlockSpec(memory_space=pl.ANY)
+
+
+def greet(peers):
+    barrier = pltpu.get_barrier_semaphore()
+    for peer in peers:
+        pl.semaphore_signal(barrier, inc=1, device_id=peer, device_id_type=MESH)
+    pl.semaphore_wait(barrier, len(peers))
+
+
+def remote(src, dst, send, recv, peer):
+    return pltpu.make_async_remote_copy(
+        src_ref=src, dst_ref=dst, send_sem=send, recv_sem=recv, device_id=peer, device_id_type=MESH
+    )
+
+
+def start_all(copies):
+    for copy in copies:
+        copy.start()
+
+
+def wait_all(copies):
+    for copy in copies:
+        copy.wait()
+
+
+def exchange_in_kernel(
+    sizes, tok_ref, wq_ref, wk_ref, wv_ref, wo_ref, x_ref, q_ref, k_ref, v_ref, o_ref,
+    tok_send, tok_recv, w_send, w_recv, local_sem,
+):
+    n_seq, n_ten, half, rows, slices = sizes
+    dp, sx, t = lax.axis_index("dp"), lax.axis_index("seq"), lax.axis_index("tensor")
+    y, c = dp // 2, dp % 2
+    me = sx * n_ten + t
+    group = n_seq * n_ten
+    others = []
+    for i in range(1, group):
+        g = (me + i) % group
+        others.append((g // n_ten, g % n_ten))
+    y_peer, c_peer, x_peer = {"dp": (dp + 2) % 4}, {"dp": 2 * y + 1 - c}, {"seq": 1 - sx}
+    greet([{"seq": a, "tensor": b} for a, b in others] + [y_peer, c_peer])
+
+    hw = wq_ref.shape[1]
+    srow, orow = wq_ref.shape[0] // slices, hw // slices
+    s_xy, s_yx = c * 4 + y * 2 + sx, c * 4 + sx * 2 + y
+    weights = ((wq_ref, q_ref, s_xy, 0), (wk_ref, k_ref, s_xy, 0), (wv_ref, v_ref, s_yx, 0), (wo_ref, o_ref, s_yx, 1))
+
+    def block(out, by_rows, base, count, which):
+        if by_rows:
+            return out.at[pl.ds(pl.multiple_of(which * hw + base * orow, orow), count * orow), :]
+        return out.at[
+            pl.ds(pl.multiple_of(base * srow, srow), count * srow), pl.ds(pl.multiple_of(which * hw, hw), hw)
+        ]
+
+    stage = [[], [], [], []]
+    n = 0
+    for j in range(1, n_ten):
+        peer = {"tensor": (t + j) % n_ten}
+        for w_ref, out, s, by_rows in weights:
+            size = orow if by_rows else srow
+            src = w_ref.at[pl.ds(pl.multiple_of(s * size, size), size), :]
+            stage[0].append(remote(src, block(out, by_rows, s, 1, t), w_send.at[0, n], w_recv.at[0, n], peer))
+            n += 1
+    n = 0
+    for j in range(1, n_ten):
+        which = (t + j) % n_ten
+        for w_ref, out, s, by_rows in weights:
+            xy = s is s_xy
+            hops = (
+                (1, x_peer if xy else y_peer, s, 1),
+                (2, y_peer if xy else x_peer, s // 2 * 2, 2),
+                (3, c_peer, c * 4, 4),
+            )
+            for k, peer, base, count in hops:
+                ref = block(out, by_rows, base, count, which)
+                stage[k].append(remote(ref, ref, w_send.at[k, n], w_recv.at[k, n], peer))
+            n += 1
+    start_all(stage[0])
+
+    tokens = []
+    for i, (a, b) in enumerate(others):
+        tokens.append(
+            remote(
+                tok_ref.at[a * half + b],
+                x_ref.at[pl.ds(pl.multiple_of(me * rows, rows), rows), :],
+                tok_send.at[i], tok_recv.at[i], {"seq": a, "tensor": b},
+            )
+        )
+    tokens.append(
+        remote(
+            tok_ref.at[(1 - sx) * half + n_ten],
+            x_ref.at[pl.ds(pl.multiple_of((group + sx) * rows, rows), rows), :],
+            tok_send.at[group - 1], tok_recv.at[group - 1], x_peer,
+        )
+    )
+    start_all(tokens)
+    local = [
+        pltpu.make_async_copy(
+            tok_ref.at[sx * half + t], x_ref.at[pl.ds(pl.multiple_of(me * rows, rows), rows), :], local_sem.at[0]
+        ),
+        pltpu.make_async_copy(
+            tok_ref.at[sx * half + n_ten],
+            x_ref.at[pl.ds(pl.multiple_of((group + sx) * rows, rows), rows), :],
+            local_sem.at[1],
+        ),
+    ]
+    for i, (w_ref, out, s, by_rows) in enumerate(weights):
+        local.append(pltpu.make_async_copy(w_ref, block(out, by_rows, 0, slices, t), local_sem.at[2 + i]))
+    start_all(local)
+    for k in range(1, 4):
+        for earlier in stage[k - 1]:
+            earlier.wait_recv()
+        start_all(stage[k])
+    for copy in stage[3]:
+        copy.wait_recv()
+    for copies in stage:
+        for copy in copies:
+            copy.wait_send()
+    wait_all(local)
+    wait_all(tokens)
+
+
+def exchange_in(tok, w_query, w_key, w_value, w_out, n_dp, n_seq, n_ten):
+    windows, rows, width = tok.shape
+    slices = n_dp * n_seq
+    vmem = pl.BlockSpec(memory_space=pltpu.VMEM)
+    square = jax.ShapeDtypeStruct((width, width), BF)
+    group = n_seq * n_ten
+    return pl.pallas_call(
+        functools.partial(exchange_in_kernel, (n_seq, n_ten, windows // n_seq, rows, slices)),
+        in_specs=[vmem] * 5,
+        out_specs=[any_spec()] * 5,
+        out_shape=[jax.ShapeDtypeStruct(((group + n_seq) * rows, width), BF)] + [square] * 4,
+        scratch_shapes=[
+            pltpu.SemaphoreType.DMA((group,)),
+            pltpu.SemaphoreType.DMA((group,)),
+            pltpu.SemaphoreType.DMA((4, 4 * (n_ten - 1))),
+            pltpu.SemaphoreType.DMA((4, 4 * (n_ten - 1))),
+            pltpu.SemaphoreType.DMA((6,)),
+        ],
+        compiler_params=pltpu.CompilerParams(collective_id=0, has_side_effects=True),
+        name="exchange_in",
+    )(tok, w_query, w_key, w_value, w_out)
+
+
+def qkv_kernel(x_ref, wq_ref, wk_ref, wv_ref, cos_ref, sin_ref, q_ref, k_ref, v_ref):
+    x = x_ref[...]
     cos, sin = cos_ref[...], sin_ref[...]
-    chunks = acc.shape[1] // LANES
-    third = chunks // 3
-    for c in range(chunks):
-        part = acc[:, c * LANES : (c + 1) * LANES]
-        if c < 2 * third:
-            part = part * cos + swap_halves(part) * sin
-        if c < third:
-            part = part * (1.0 / math.sqrt(HEAD_DIM))
-        out_ref[:, c * LANES : (c + 1) * LANES] = part.astype(BF)
-
-
-def qkv_project(x, w, cos, sin, block):
+    for w_ref, out_ref, scale in ((wq_ref, q_ref, 1.0 / math.sqrt(HEAD_DIM)), (wk_ref, k_ref, 1.0), (wv_ref, v_ref, None)):
+        acc = dot_n(x, w_ref[...])
+        for c in range(acc.shape[1] // LANES):
+            part = acc[:, c * LANES : (c + 1) * LANES]
+            if scale is not None:
+                part = (part * cos + swap_halves(part) * sin) * scale
+            out_ref[:, c * LANES : (c + 1) * LANES] = part.astype(BF)
+
+
+def qkv_project(x, w_query, w_key, w_value, cos, sin):
     rows, width = x.shape
-    tile = 256
+    tile, cols = 256, 512
+    w_spec = pl.BlockSpec((width, cols), lambda t, r: (0, t))
+    out_spec = pl.BlockSpec((tile, cols), lambda t, r: (r, t))
+    table = pl.BlockSpec((tile, LANES), lambda t, r: (r, 0))
     return pl.pallas_call(
         qkv_kernel,
-        grid=(w.shape[1] // block, rows // tile),
-        in_specs=[
-            pl.BlockSpec((tile, width), lambda t, r: (r, 0)),
-            pl.BlockSpec((width, block), lambda t, r: (0, t)),
-            pl.BlockSpec((tile, LANES), lambda t, r: (r, 0)),
-            pl.BlockSpec((tile, LANES), lambda t, r: (r, 0)),
-        ],
-        out_specs=pl.BlockSpec((tile, block), lambda t, r: (r, t)),
-        out_shape=jax.ShapeDtypeStruct((rows, w.shape[1]), BF),
-        cost_estimate=pl.CostEstimate(
-            flops=2 * rows * width * w.shape[1], bytes_accessed=2 * rows * (width + w.shape[1]), transcendentals=0
-        ),
+        grid=(width // cols, rows // tile),
+        in_specs=[pl.BlockSpec((tile, width), lambda t, r: (r, 0)), w_spec, w_spec, w_spec, table, table],
+        out_specs=[out_spec] * 3,
+        out_shape=[jax.ShapeDtypeStruct((rows, width), BF)] * 3,
+        cost_estimate=pl.CostEstimate(flops=6 * rows * width * width, bytes_accessed=8 * rows * width, transcendentals=0),
         name="qkv_project",
-    )(x, w, cos, sin)
-
-
-def attend_kernel(q_ref, k_ref, v_ref, o_ref):
+    )(x, w_query, w_key, w_value, cos, sin)
+
+
+def attend_body(q_ref, k_ref, v_ref, o_ref):
     q, k, v = q_ref[...], k_ref[...], v_ref[...]
     outs = []
     for h in range(LANES // HEAD_DIM):
@@ -385,31 +528,95 @@
     o_ref[...] = jnp.where(lane < HEAD_DIM, outs[0], outs[1]).astype(BF)
 
 
-def attend(qkv, block):
-    rows = qkv.shape[0]
-    per = block // 3 // LANES
-    pairs = qkv.shape[1] // block * per
-    tile = 512
-    spec = lambda which: lambda p, r: (0, p // per * 3 * per + which * per + p % per)
+def attend_specs(rows, tile):
+    return [
+        pl.BlockSpec((tile, LANES), lambda p, r: (r, p)),
+        pl.BlockSpec((rows, LANES), lambda p, r: (0, p)),
+        pl.BlockSpec((rows, LANES), lambda p, r: (0, p)),
+    ]
+
+
+def attend_cost(rows, pairs):
+    return pl.CostEstimate(
+        flops=16 * pairs * rows * rows * LANES, bytes_accessed=8 * rows * pairs * LANES, transcendentals=2 * pairs * rows * rows
+    )
+
+
+def attend(q, k, v):
+    rows, width = q.shape
+    tile, pairs = 512, width // LANES
     return pl.pallas_call(
-        attend_kernel,
+        attend_body,
         grid=(pairs, rows // tile),
-        in_specs=[
-            pl.BlockSpec((tile, LANES), lambda p, r: (r, p // per * 3 * per + p % per)),
-            pl.BlockSpec((rows, LANES), spec(1)),
-            pl.BlockSpec((rows, LANES), spec(2)),
+        in_specs=attend_specs(rows, tile),
+        out_specs=pl.BlockSpec((tile, LANES), lambda p, r: (r, p)),
+        out_shape=jax.ShapeDtypeStruct((rows, width), BF),
+        cost_estimate=attend_cost(rows, pairs),
+        name="attend",
+    )(q, k, v)
+
+
+def swap_part(refs, outs, send, recv, local_sem, n_ten, base):
+    t = lax.axis_index("tensor")
+    share, hw = outs[0].shape[0] // n_ten, outs[0].shape[1]
+    copies, local = [], []
+    rows = pl.ds(base, share)
+    mine = pl.ds(pl.multiple_of(t * share, share), share)
+    for i, (ref, out) in enumerate(zip(refs, outs, strict=True)):
+        for j in range(1, n_ten):
+            to = (t + j) % n_ten
+            src = ref.at[rows, pl.ds(pl.multiple_of(to * hw, hw), hw)]
+            copies.append(remote(src, out.at[mine, :], send.at[i, j - 1], recv.at[i, j - 1], {"tensor": to}))
+        src = ref.at[rows, pl.ds(pl.multiple_of(t * hw, hw), hw)]
+        local.append(pltpu.make_async_copy(src, out.at[mine, :], local_sem.at[i]))
+    return copies, local
+
+
+def attend_swap_kernel(
+    n_ten, length, q_ref, k_ref, v_ref, q_all, k_all, v_all, o_ref, lq_ref, lk_ref, lv_ref, send, recv, local_sem
+):
+    t = lax.axis_index("tensor")
+    step = pl.program_id(0) * pl.num_programs(1) + pl.program_id(1)
+    copies, local = swap_part(
+        (q_all, k_all, v_all), (lq_ref, lk_ref, lv_ref), send, recv, local_sem, n_ten, length
+    )
+
+    @pl.when(step == 0)
+    def _():
+        greet([{"tensor": (t + j) % n_ten} for j in range(1, n_ten)])
+        start_all(copies + local)
+
+    attend_body(q_ref, k_ref, v_ref, o_ref)
+
+    @pl.when(step == pl.num_programs(0) * pl.num_programs(1) - 1)
+    def _():
+        wait_all(copies + local)
+
+
+def attend_swap(q, k, v, length, n_ten):
+    width = q.shape[1]
+    tile, pairs, hw = 512, width // LANES, width // n_ten
+    left = jax.ShapeDtypeStruct((length, hw), BF)
+    return pl.pallas_call(
+        functools.partial(attend_swap_kernel, n_ten, length),
+        grid=(pairs, length // tile),
+        in_specs=attend_specs(length, tile) + [any_spec()] * 3,
+        out_specs=[pl.BlockSpec((tile, LANES), lambda p, r: (r, p))] + [any_spec()] * 3,
+        out_shape=[jax.ShapeDtypeStruct((length, width), BF), left, left, left],
+        scratch_shapes=[
+            pltpu.SemaphoreType.DMA((3, n_ten - 1)),
+            pltpu.SemaphoreType.DMA((3, n_ten - 1)),
+            pltpu.SemaphoreType.DMA((3,)),
         ],
-        out_specs=pl.BlockSpec((tile, LANES), lambda p, r: (r, p)),
-        out_shape=jax.ShapeDtypeStruct((rows, pairs * LANES), BF),
-        cost_estimate=pl.CostEstimate(
-            flops=16 * pairs * rows * rows * LANES, bytes_accessed=8 * rows * pairs * LANES, transcendentals=2 * pairs * rows * rows
-        ),
-        name="attend",
-    )(qkv, qkv, qkv)
-
-
-def attend_back_kernel(q_ref, g_ref, k_ref, v_ref, cos_ref, sin_ref, qcos_ref, qsin_ref, dq_ref, dk_ref, dv_ref):
-    q, g, k, v = q_ref[...], g_ref[...], k_ref[...], v_ref[...]
+        compiler_params=pltpu.CompilerParams(collective_id=1, has_side_effects=True),
+        cost_estimate=attend_cost(length, pairs),
+        name="attend_swap",
+    )(q, k, v, q, k, v)
+
+
+def back_body(q_ref, g_ref, k_ref, v_ref, pick_ref, cos_ref, sin_ref, qcos_ref, qsin_ref):
+    g, k, v, pick = g_ref[...], k_ref[...], v_ref[...], pick_ref[...]
+    q = dot_n(pick, q_ref[...]).astype(BF)
     dq = []
     all_p, all_ds, all_q, all_g = [], [], [], []
     for h in range(LANES // HEAD_DIM):
@@ -427,45 +634,170 @@
         all_g.append(gh)
     lane = lax.broadcasted_iota(jnp.int32, dq[0].shape, 1)
     dq = jnp.where(lane < HEAD_DIM, dq[0], dq[1]) * (1.0 / math.sqrt(HEAD_DIM))
-    dq_ref[...] = (dq * qcos_ref[...] - swap_halves(dq) * qsin_ref[...]).astype(BF)
+    dq = (dq * qcos_ref[...] - swap_halves(dq) * qsin_ref[...]).astype(BF)
+    dq = t_dot(pick, dq).astype(BF)
     dk = t_dot(jnp.concatenate(all_ds, axis=0), jnp.concatenate(all_q, axis=0))
-    dk_ref[...] = (dk * cos_ref[...] - swap_halves(dk) * sin_ref[...]).astype(BF)
-    dv_ref[...] = t_dot(jnp.concatenate(all_p, axis=0), jnp.concatenate(all_g, axis=0)).astype(BF)
-
-
-def attend_back(q_rows, grad_rows, qkv, block, cos, sin, row_cos, row_sin):
-    rows, masked = qkv.shape[0], q_rows.shape[0]
-    per = block // 3 // LANES
-    pairs = qkv.shape[1] // block * per
-    spec = lambda which: lambda p: (0, p // per * 3 * per + which * per + p % per)
-    pick = pl.BlockSpec((masked, LANES), lambda p: (0, p))
-    full = pl.BlockSpec((rows, LANES), lambda p: (0, p))
-    same = pl.BlockSpec((rows, LANES), lambda p: (0, 0))
+    dk = (dk * cos_ref[...] - swap_halves(dk) * sin_ref[...]).astype(BF)
+    dv = t_dot(jnp.concatenate(all_p, axis=0), jnp.concatenate(all_g, axis=0)).astype(BF)
+    return dq, dk, dv
+
+
+def back_kernel(q_ref, g_ref, k_ref, v_ref, pick_ref, cos_ref, sin_ref, qcos_ref, qsin_ref, dq_ref, dk_ref, dv_ref):
+    dq_ref[...], dk_ref[...], dv_ref[...] = back_body(
+        q_ref, g_ref, k_ref, v_ref, pick_ref, cos_ref, sin_ref, qcos_ref, qsin_ref
+    )
+
+
+def back_specs(length, masked):
+    full = pl.BlockSpec((length, LANES), lambda p: (0, p))
+    same = pl.BlockSpec((length, LANES), lambda p: (0, 0))
     row_same = pl.BlockSpec((masked, LANES), lambda p: (0, 0))
+    return [
+        full, pl.BlockSpec((masked, LANES), lambda p: (0, p)), full, full,
+        pl.BlockSpec((masked, length), lambda p: (0, 0)), same, same, row_same, row_same,
+    ]
+
+
+def back_cost(length, masked, pairs):
+    return pl.CostEstimate(
+        flops=24 * pairs * length * masked * LANES, bytes_accessed=12 * length * pairs * LANES, transcendentals=2 * pairs * length * masked
+    )
+
+
+def attend_back(q, grad_rows, k, v, pick, tables):
+    masked, length = pick.shape
+    width = q.shape[1]
+    full = pl.BlockSpec((length, LANES), lambda p: (0, p))
     return pl.pallas_call(
-        attend_back_kernel,
-        grid=(pairs,),
+        back_kernel,
+        grid=(width // LANES,),
+        in_specs=back_specs(length, masked),
+        out_specs=[full] * 3,
+        out_shape=[jax.ShapeDtypeStruct((length, width), BF)] * 3,
+        cost_estimate=back_cost(length, masked, width // LANES),
+        name="attend_back",
+    )(q, grad_rows, k, v, pick, *tables)
+
+
+def back_swap_kernel(
+    n_ten, q_ref, g_ref, k_ref, v_ref, pick_ref, cos_ref, sin_ref, qcos_ref, qsin_ref, lq_ref, lk_ref, lv_ref,
+    dq_ref, dk_ref, dv_ref, buf, out_sem, send, recv, local_sem,
+):
+    t = lax.axis_index("tensor")
+    step, steps = pl.program_id(0), pl.num_programs(0)
+    length = q_ref.shape[0]
+    share, hw = lq_ref.shape[0] // n_ten, lq_ref.shape[1]
+    outs = (dq_ref, dk_ref, dv_ref)
+    copies, local = [], []
+    mine = pl.ds(pl.multiple_of(t * hw, hw), hw)
+    for i, (ref, out) in enumerate(zip((lq_ref, lk_ref, lv_ref), outs, strict=True)):
+        dst = out.at[pl.ds(length, share), mine]
+        for j in range(1, n_ten):
+            to = (t + j) % n_ten
+            src = ref.at[pl.ds(pl.multiple_of(to * share, share), share), :]
+            copies.append(remote(src, dst, send.at[i, j - 1], recv.at[i, j - 1], {"tensor": to}))
+        src = ref.at[pl.ds(pl.multiple_of(t * share, share), share), :]
+        local.append(pltpu.make_async_copy(src, dst, local_sem.at[i]))
+
+    def out_copy(at, i):
+        slot = at % 2
+        columns = pl.ds(pl.multiple_of(at * LANES, LANES), LANES)
+        return pltpu.make_async_copy(buf.at[slot, i], outs[i].at[pl.ds(0, length), columns], out_sem.at[slot, i])
+
+    @pl.when(step == 0)
+    def _():
+        greet([{"tensor": (t + j) % n_ten} for j in range(1, n_ten)])
+        start_all(copies + local)
+
+    @pl.when(step >= 2)
+    def _():
+        for i in range(3):
+            out_copy(step - 2, i).wait()
+
+    results = back_body(q_ref, g_ref, k_ref, v_ref, pick_ref, cos_ref, sin_ref, qcos_ref, qsin_ref)
+    for i in range(3):
+        buf[step % 2, i] = results[i]
+        out_copy(step, i).start()
+
+    @pl.when(step == steps - 1)
+    def _():
+        for i in range(3):
+            out_copy(step - 1, i).wait()
+            out_copy(step, i).wait()
+        wait_all(copies + local)
+
+
+def back_swap(q, grad_rows, k, v, pick, tables, left, n_ten):
+    masked, length = pick.shape
+    width = q.shape[1]
+    share = left[0].shape[0] // n_ten
+    return pl.pallas_call(
+        functools.partial(back_swap_kernel, n_ten),
+        grid=(width // LANES,),
+        in_specs=back_specs(length, masked) + [any_spec()] * 3,
+        out_specs=[any_spec()] * 3,
+        out_shape=[jax.ShapeDtypeStruct((length + share, width), BF)] * 3,
+        scratch_shapes=[
+            pltpu.VMEM((2, 3, length, LANES), BF),
+            pltpu.SemaphoreType.DMA((2, 3)),
+            pltpu.SemaphoreType.DMA((3, n_ten - 1)),
+            pltpu.SemaphoreType.DMA((3, n_ten - 1)),
+            pltpu.SemaphoreType.DMA((3,)),
+        ],
+        compiler_params=pltpu.CompilerParams(collective_id=2, has_side_effects=True),
+        cost_estimate=back_cost(length, masked, width // LANES),
+        name="back_swap",
+    )(q, grad_rows, k, v, pick, *tables, *left)
+
+
+def feed_kernel(x_ref, res_ref, gu_ref, down_ref, out_ref, acc_ref):
+    step = pl.program_id(0)
+    x = x_ref[...]
+    unit = down_ref.shape[1]
+    parts = []
+    for p in range(gu_ref.shape[0]):
+        both = dot_n(x, gu_ref[p])
+        gate, up = both[:, :unit], both[:, unit:]
+        parts.append((gate * jax.nn.sigmoid(gate) * up).astype(BF))
+    hidden = jnp.concatenate(parts, axis=1)
+    down = down_ref[...].reshape(-1, down_ref.shape[2])
+    new = dot_n(hidden, down)
+
+    @pl.when(step == 0)
+    def _():
+        acc_ref[...] = res_ref[...] + new
+
+    @pl.when(step > 0)
+    def _():
+        acc_ref[...] += new
+
+    @pl.when(step == pl.num_programs(0) - 1)
+    def _():
+        out_ref[...] = acc_ref[...].astype(BF)
+
+
+def feed_forward(x, res, gate_up, down):
+    rows, width = x.shape
+    pieces, unit = down.shape[:2]
+    per = 2
+    whole = lambda i: (0, 0)
+    return pl.pallas_call(
+        feed_kernel,
+        grid=(pieces // per,),
         in_specs=[
-            pick,
-            pick,
-            pl.BlockSpec((rows, LANES), spec(1)),
-            pl.BlockSpec((rows, LANES), spec(2)),
-            same,
-            same,
-            row_same,
-            row_same,
+            pl.BlockSpec((rows, width), whole, pipeline_mode=pl.Buffered(1)),
+            pl.BlockSpec((rows, width), whole, pipeline_mode=pl.Buffered(1)),
+            pl.BlockSpec((per, width, 2 * unit), lambda i: (i, 0, 0)),
+            pl.BlockSpec((per, unit, width), lambda i: (i, 0, 0)),
         ],
-        out_specs=[pick, full, full],
-        out_shape=[
-            jax.ShapeDtypeStruct((masked, pairs * LANES), BF),
-            jax.ShapeDtypeStruct((rows, pairs * LANES), BF),
-            jax.ShapeDtypeStruct((rows, pairs * LANES), BF),
-        ],
+        out_specs=pl.BlockSpec((rows, width), whole),
+        out_shape=jax.ShapeDtypeStruct((rows, width), BF),
+        scratch_shapes=[pltpu.VMEM((rows, width), F32)],
         cost_estimate=pl.CostEstimate(
-            flops=20 * pairs * rows * masked * LANES, bytes_accessed=10 * rows * pairs * LANES, transcendentals=2 * pairs * rows * masked
+            flops=6 * rows * width * pieces * unit, bytes_accessed=6 * width * pieces * unit, transcendentals=rows * pieces * unit
         ),
-        name="attend_back",
-    )(q_rows, grad_rows, qkv, qkv, cos, sin, row_cos, row_sin)
+        name="feed_forward",
+    )(x, res, gate_up, down)
 
 
 def rotary_lanes(positions):
@@ -495,47 +827,25 @@
     window_counts,
 ):
     rows_local, windows, width = tokens.shape
-    n_seq, n_ten = lax.axis_size("seq"), lax.axis_size("tensor")
-    n_dp = lax.axis_size("dp")
+    n_dp, n_seq, n_ten = lax.axis_size("dp"), lax.axis_size("seq"), lax.axis_size("tensor")
     seq_index, ten_index = lax.axis_index("seq"), lax.axis_index("tensor")
     shard_index = lax.axis_index("dp") * n_seq + seq_index
     half = windows // n_seq
     length = rows_local * n_seq * n_ten
     share = length // n_ten
     hw = w_query.shape[1]
-    block = 3 * hw
     slots = masked_rows.shape[1]
     part = slots // n_ten
-
-    tok = jnp.swapaxes(tokens, 0, 1).reshape(n_seq, half, rows_local, width)
-    own_tok = lax.all_to_all(
-        tok[:, :n_ten].reshape(n_seq * n_ten, rows_local, width), ("seq", "tensor"), 0, 0, tiled=True
-    ).reshape(length, width)
-    left_x = lax.all_to_all(tok[:, n_ten], "seq", 0, 0, tiled=True)
-    left_tok = lax.all_gather(left_x, "tensor", axis=1, tiled=False).reshape(length, width)
-
-    def cut(w, count):
-        size = w.shape[0] // count
-        return lax.dynamic_slice_in_dim(w, shard_index * size, size, axis=0)
-
-    shards_xy = n_dp * n_seq
-
-    def gather_columns(w):
-        w = lax.all_gather(cut(w, shards_xy), "tensor", axis=1, tiled=True)
-        return lax.all_gather(w, ("dp", "seq"), axis=0, tiled=True)
-
-    def gather_rows(w):
-        own = cut(w, shards_xy)
-        w = lax.all_gather(own, "tensor", axis=0, tiled=False)
-        w = lax.all_gather(w, ("dp", "seq"), axis=0, tiled=False)
-        return jnp.swapaxes(w, 0, 1).reshape(-1, w.shape[-1])
-
-    w_joined = jnp.concatenate([w_query, w_key, w_value], axis=1)
-    all_joined = gather_columns(w_joined)
-    all_out = gather_rows(w_out)
-    all_gate = gather_columns(w_gate)
-    all_up = gather_columns(w_up)
-    all_down = gather_rows(w_down)
+    units = w_down.shape[0] // (n_dp * n_seq)
+
+    cut = lambda w, axis: lax.dynamic_slice_in_dim(w, shard_index * units, units, axis)
+    everywhere = ("dp", "seq", "tensor")
+    gate_up = lax.all_gather(jnp.concatenate([cut(w_gate, 1), cut(w_up, 1)], axis=1), everywhere, axis=0, tiled=False)
+    down = lax.all_gather(cut(w_down, 0), everywhere, axis=0, tiled=False)
+
+    both_tok, all_q, all_k, all_v, all_out = exchange_in(
+        jnp.swapaxes(tokens, 0, 1), w_query, w_key, w_value, w_out, n_dp, n_seq, n_ten
+    )
 
     live = jnp.arange(windows) < window_counts[0]
     valid = (masked_rows < length) & live[:, None]
@@ -552,43 +862,39 @@
     own_cot = lax.dynamic_index_in_dim(cot, ten_index, 0, keepdims=False)
     left_rows, left_valid, left_cot = my_rows[n_ten], my_valid[n_ten], cot[n_ten]
     every = jnp.arange(length)
+    left_every = jnp.swapaxes(every.reshape(n_seq, n_ten, rows_local), 0, 1).reshape(n_ten, share)
+    my_left = lax.dynamic_index_in_dim(left_every, ten_index, 0, keepdims=False)
+    left_every = left_every.reshape(length)
     own_pick = ((own_rows[:, None] == every[None, :]) & own_valid[:, None]).astype(BF)
-    left_pick = ((left_rows[:, None] == every[None, :]) & left_valid[:, None]).astype(BF)
-
-    cos, sin = rotary_lanes(every)
-    own_cos, own_sin = rotary_lanes(own_rows)
-    left_cos, left_sin = rotary_lanes(left_rows)
+    left_pick = ((left_rows[:, None] == left_every[None, :]) & left_valid[:, None]).astype(BF)
+    part_pick = ((left_rows[:, None] == my_left[None, :]) & left_valid[:, None]).astype(BF)
+
+    own_tables = rotary_lanes(every) + rotary_lanes(own_rows)
+    left_tables = rotary_lanes(left_every) + rotary_lanes(left_rows)
+    part_tables = rotary_lanes(my_left)
+    cos, sin = [jnp.concatenate([a, b], axis=0) for a, b in zip(own_tables[:2], part_tables, strict=True)]
 
     def norm(x, gain, bias):
         normed, inv_std = layer_stats(x)
         return normed, inv_std, (normed * gain + bias).astype(BF)
 
-    _, _, left_first = norm(left_tok.astype(F32), norm1_gain, norm1_bias)
-    left_qkv = qkv_project(left_first, w_joined, cos, sin, block)
-    left_att = attend(left_qkv, block)
-    _, _, own_first = norm(own_tok.astype(F32), norm1_gain, norm1_bias)
-    own_qkv = qkv_project(own_first, all_joined, cos, sin, block)
-    own_att = attend(own_qkv, block)
-
-    def spread(x):
-        x = x.reshape(n_seq, n_ten, rows_local, x.shape[-1])
-        x = lax.all_to_all(x, "tensor", 1, 1, tiled=True)
-        return jnp.swapaxes(x, 1, 2).reshape(n_seq * rows_local, -1)
-
-    def my_part(x):
-        x = x.reshape(n_seq, n_ten, rows_local, x.shape[-1])
-        return lax.dynamic_index_in_dim(x, ten_index, 1, keepdims=False).reshape(n_seq * rows_local, -1)
-
-    left_att_part = spread(left_att)
-
     pick_rows = lambda pick, x: dot_n(pick, x).astype(BF)
+    left_tok_m = lax.all_gather(pick_rows(part_pick, both_tok[length:]), "tensor", axis=0, tiled=False)
+    _, _, first = norm(both_tok.astype(F32), norm1_gain, norm1_bias)
+    q, k, v = qkv_project(first, all_q, all_k, all_v, cos, sin)
+    own_att, left_q, left_k, left_v = attend_swap(q, k, v, length, n_ten)
+    left_att = attend(left_q, left_k, left_v)
+    left_att_part = lax.all_to_all(left_att.reshape(n_ten, share, hw), "tensor", 0, 0, tiled=True)
+    left_att_part = jnp.swapaxes(left_att_part, 0, 1).reshape(share, width)
+
     own_att_m = pick_rows(own_pick, own_att)
     left_att_m = pick_rows(left_pick, left_att)
-    own_res_m = pick_rows(own_pick, own_tok).astype(F32) + dot_n(own_att_m, all_out)
+    own_res_m = pick_rows(own_pick, both_tok[:length]).astype(F32) + dot_n(own_att_m, all_out)
     own_normed2, own_inv2, own_second = norm(own_res_m, norm2_gain, norm2_bias)
     sent = lax.all_gather(jnp.concatenate([own_second, left_att_m], axis=1), "tensor", axis=0, tiled=False)
-    left_att_full = jnp.swapaxes(sent[:, :, width:], 0, 1).reshape(slots, -1)
-    left_res_m = pick_rows(left_pick, left_tok).astype(F32) + dot_n(left_att_full, all_out)
+    left_att_full = jnp.swapaxes(sent[:, :, width:], 0, 1).reshape(slots, width)
+    left_tok_full = jnp.sum(left_tok_m.astype(F32), axis=0)
+    left_res_m = left_tok_full + dot_n(left_att_full, all_out)
     left_normed2, left_inv2, left_second = norm(left_res_m, norm2_gain, norm2_bias)
     second = jnp.concatenate([sent[:, :, :width].reshape(n_ten * slots, width), left_second], axis=0)
 
@@ -612,9 +918,9 @@
     grad_second = lax.psum_scatter(grad_second, "tensor", scatter_dimension=0, tiled=True)
     left_grad_second = lax.all_gather(grad_second[slots:], "tensor", axis=0, tiled=True).astype(F32)
     own_grad_second = grad_second[:slots].astype(F32)
-    grad_w_down = t_dot(hidden_m, down_in).astype(BF)
-    grad_w_gate = t_dot(second, grad_gate).astype(BF)
-    grad_w_up = t_dot(second, grad_up).astype(BF)
+    grad_w_ffn = jnp.concatenate(
+        [t_dot(second, grad_gate).astype(BF), t_dot(second, grad_up).astype(BF), t_dot(down_in, hidden_m).astype(BF)], axis=1
+    )
 
     mine = lambda x: lax.dynamic_slice_in_dim(x, ten_index * part, part, 0)
     grad_norm2_gain = jnp.sum(own_grad_second * own_normed2, axis=0) + jnp.sum(
@@ -631,47 +937,21 @@
     grad_w_out = t_dot(
         jnp.concatenate([own_att_m, left_att_wide], axis=0), jnp.concatenate([own_gr2, left_gr2], axis=0)
     ).astype(BF)
-
-    def queries_of(pick, qkv):
-        groups = qkv.shape[1] // block
-        q = qkv.reshape(length, groups, block)[:, :, :hw].reshape(length, groups * hw)
-        return pick_rows(pick, q)
-
-    own_dq, own_dk, own_dv = attend_back(
-        queries_of(own_pick, own_qkv), own_gatt, own_qkv, block, cos, sin, own_cos, own_sin
-    )
-    left_dq, left_dk, left_dv = attend_back(
-        queries_of(left_pick, left_qkv), left_gatt, left_qkv, block, cos, sin, left_cos, left_sin
-    )
-
-    def join(pick, dq, dk, dv):
-        groups = dk.shape[1] // hw
-        dense_q = t_dot(pick, dq).astype(BF)
-        parts = [x.reshape(length, groups, 1, hw) for x in (dense_q, dk, dv)]
-        return jnp.concatenate(parts, axis=2).reshape(length, groups * block)
-
-    own_grads = join(own_pick, own_dq, own_dk, own_dv)
-    left_grads = join(left_pick, left_dq, left_dk, left_dv)
-    left_grads_part = spread(left_grads)
-    grad_first = jnp.concatenate([dot_t(own_grads, all_joined), dot_t(left_grads_part, all_joined)], axis=0)
-    grad_w_all = t_dot(own_first, own_grads)
-    left_block = t_dot(left_first, left_grads)
-    grad_w_all = (grad_w_all.reshape(width, n_ten, block) + left_block[:, None, :] * on_tensor.astype(F32)[None, :, None]).reshape(
-        width, n_ten * block
-    ).astype(BF)
-
-    both_tok = jnp.concatenate([own_tok, my_part(left_tok)], axis=0)
+    left_back = attend_back(left_q, left_gatt, left_k, left_v, left_pick, left_tables)
+    dq, dk, dv = back_swap(q, own_gatt, k, v, own_pick, own_tables, left_back, n_ten)
+    grad_first = dot_t(dq, all_q) + dot_t(dk, all_k) + dot_t(dv, all_v)
+    grad_w_query, grad_w_key, grad_w_value = [t_dot(first, d).astype(BF) for d in (dq, dk, dv)]
+
     normed1, inv_std1 = layer_stats(both_tok.astype(F32))
     grad_norm1_gain = jnp.sum(grad_first * normed1, axis=0)
     grad_norm1_bias = jnp.sum(grad_first, axis=0)
-    gr2_dense = jnp.concatenate([t_dot(own_pick, own_gr2), dot_n(my_part(left_pick.T), left_gr2)], axis=0)
+    gr2_dense = jnp.concatenate([t_dot(own_pick, own_gr2), t_dot(part_pick, left_gr2)], axis=0)
     grad_both = (gr2_dense + norm_back(grad_first, normed1, inv_std1, norm1_gain)).astype(BF)
 
     att = jnp.concatenate([own_att, left_att_part], axis=0)
     residual2 = both_tok.astype(F32) + dot_n(att, all_out)
     _, _, second_low = norm(residual2, norm2_gain, norm2_bias)
-    hidden = (jax.nn.silu(dot_n(second_low, all_gate)) * dot_n(second_low, all_up)).astype(BF)
-    out_both = (residual2 + dot_n(hidden, all_down)).astype(BF)
+    out_both = feed_forward(second_low, residual2, gate_up, down)
 
     def send_back(x):
         own = lax.all_to_all(
@@ -687,10 +967,16 @@
     def summed(x, dim):
         return lax.psum_scatter(x, ("dp", "seq"), scatter_dimension=dim, tiled=True)
 
-    gw_all = lax.psum_scatter(summed(grad_w_all, 0), "tensor", scatter_dimension=1, tiled=True).astype(F32)
+    gw_all = summed(jnp.concatenate([grad_w_query, grad_w_key, grad_w_value], axis=1), 0)
+    gw_q, gw_k, gw_v = [
+        lax.psum_scatter(gw_all[:, i * width : (i + 1) * width], "tensor", scatter_dimension=1, tiled=True).astype(F32)
+        for i in range(3)
+    ]
     gw_out = lax.psum_scatter(summed(grad_w_out, 1), "tensor", scatter_dimension=0, tiled=True).astype(F32)
-    gw_gate, gw_up = summed(grad_w_gate, 0).astype(F32), summed(grad_w_up, 0).astype(F32)
-    gw_down = summed(grad_w_down, 1).astype(F32)
+    gw_ffn = summed(grad_w_ffn, 0).astype(F32)
+    hidden_units = w_gate.shape[1]
+    gw_gate, gw_up = gw_ffn[:, :hidden_units], gw_ffn[:, hidden_units : 2 * hidden_units]
+    gw_down = gw_ffn[:, 2 * hidden_units :].T
     vectors = [
         lax.psum_scatter(v, ("dp", "seq", "tensor"), scatter_dimension=0, tiled=True)
         for v in (grad_norm1_gain, grad_norm1_bias, grad_norm2_gain, grad_norm2_bias)
@@ -700,9 +986,9 @@
         grad_tokens,
         vectors[0],
         vectors[1],
-        gw_all[:, :hw],
-        gw_all[:, hw : 2 * hw],
-        gw_all[:, 2 * hw :],
+        gw_q,
+        gw_k,
+        gw_v,
         gw_out,
         vectors[2],
         vectors[3],
@@ -713,8 +999,8 @@
 
 
 def shards(tokens, *rest):
-    n_seq, n_ten = lax.axis_size("seq"), lax.axis_size("tensor")
-    whole = tokens.shape[1] % n_seq == 0 and tokens.shape[1] // n_seq == n_ten + 1
+    n_dp, n_seq, n_ten = lax.axis_size("dp"), lax.axis_size("seq"), lax.axis_size("tensor")
+    whole = n_dp == 4 and n_seq == 2 and tokens.shape[1] == n_seq * (n_ten + 1)
     return (window_shards if whole else block_shards)(tokens, *rest)
 
 

time: 930 us -> 761 us (0.82)
  waiting for transfers between devices: 342 us -> 102 us
  Pallas kernels: 94.8 us -> 255 us
  matrix products: 141 us -> 67.9 us
  local copies, waits for them, and re-layouts: 103 us -> 62.7 us
  other arithmetic: 73.5 us -> 87.3 us
    pallas_call x6 -> x7, Pallas kernels: 94.8 us -> 255 us  [the longest x1 76.8 us: exchange_in(): pl.pallas_call(functools.partial(exchange_in_kernel, (n_seq, n_ten, windo...]
    all_gather x9 -> x3, waiting for transfers between devices: 134 us -> 26.2 us  [the longest x1 26.2 us: window_shards(): lax.all_gather(jnp.concatenate([cut(w_gate, 1), cut(w_up, 1)], axis=1), e...]
    reduce_scatter x4 -> x3, waiting for transfers between devices: 86 us -> 3.68 us  [window_shards(): lax.psum_scatter(gw_all[:, i * width:(i + 1) * width], 'tensor', scatter_...]
    dot_general x14 -> x9, matrix products: 73.4 us -> 18.1 us  [dot_n(): lax.dot_general(a, b, (((1,), (0,)), ((), ())), preferred_element_type=F32)]
    all_gather x2 -> x0, blocking collectives: 45.7 us -> none  [the longest x1 29.2 us: gather_columns(): w = lax.all_gather(cut(w, shards_xy), 'tensor', axis=1, tiled=True)]
    unnamed x20 -> x15, waiting for transfers between devices: 40.6 us -> 0.22 us
    all_to_all x2, waiting for transfers between devices: 37.8 us -> 0.01 us  [send_back(): lax.all_to_all(x[:length].reshape(n_seq * n_ten, rows_local, width), ('se...]
    unnamed x1, blocking collectives: 39.8 us -> 73.3 us
  transfers between devices with their start and end apart: 25 -> 16, of which waited for: 13 -> 6; matrix products, arithmetic and copies ran while one was open for 32% -> 24% of each run, Pallas kernels for 4% -> 24%
where the time goes in v2:
time: 761 us; the launch traced here: 750 us
  Pallas kernels  255 us (34%)
  blocking collectives  123 us (16%)
  waiting for transfers between devices  102 us (13%)
  other arithmetic  87.3 us (11%)
  matrix products  67.9 us (9%)
  local copies, waits for them, and re-layouts  62.7 us (8%)
  starting transfers between devices  33.1 us (4%)
  between operations  18.5 us (2%)
    pallas_call x1, Pallas kernels, exchange_in(): pl.pallas_call(functools.partial(exchange_in_kernel, (n_seq, n_ten, windo...  76.8 us
    unnamed x1, blocking collectives  73.3 us
    pallas_call x1, Pallas kernels, feed_forward(): pl.pallas_call(feed_kernel, grid=(pieces // per,), in_specs=[pl.BlockSpec...  50.1 us
    pallas_call x1, Pallas kernels, attend_swap(): pl.pallas_call(functools.partial(attend_swap_kernel, n_ten, length), grid...  49 us
    pallas_call x1, Pallas kernels, back_swap(): pl.pallas_call(functools.partial(back_swap_kernel, n_ten), grid=(width //...  46.2 us
    unnamed x146, local copies, waits for them, and re-layouts  44.9 us
    reduce_scatter x1, waiting for transfers between devices, window_shards(): lax.psum_scatter(grad_second, 'tensor', scatter_dimension=0, tiled=True)  34.3 us
    all_to_all x1, blocking collectives, window_shards(): lax.all_to_all(left_att.reshape(n_ten, share, hw), 'tensor', 0, 0, tiled=...  29.3 us
  transfers between devices with their start and end apart: 16, of which 6 were waited for; matrix products, arithmetic and copies ran while one was open for 24% of the time, Pallas kernels for 24%

profile of v2, /device:TPU:0, one launch (start us, length us, event | category | flops | bytes accessed | tf_op | source)
XLA Modules:
  0.0 749.8 jit_solution(2025465169347553997)
XLA Ops:
  11.2 76.8 %exchange_in.1 = (bf16[1280,1024]{1,0:T(8,128)(2,1)}, bf16[1024,1024]{1,0:T(8,128)(2,1)}, bf16[1024,1024]{1,0:T(8,128)(2,1)}, bf16[1024,1024]{1,0:T(8,128)(2,1)}, bf16[1024,1024]{1,0:T(8,128)(2,1)}) custom-call(bf16[10,128,1024]{2,1,0:T(8,128)(2,1)} %bitcast.108, bf16[1024,256]{1,0:T(8,128)(2,1)} %wq_ref.1, bf16[1024,256]{1,0:T(8,128)(2,1)} %wk_ref.1, ...), custom_call_target="tpu_custom_call" | custom-call | tf_op jit(solution)/shard_map/exchange_in/pallas_call | solution.py:473
  94.1 5.0 fusion.64
  101.1 2.3 fusion.7.x_ref
  104.9 15.6 %qkv_project.1 = (bf16[1280,1024]{1,0:T(8,128)(2,1)}, bf16[1280,1024]{1,0:T(8,128)(2,1)}, bf16[1280,1024]{1,0:T(8,128)(2,1)}) custom-call(bf16[1280,1024]{1,0:T(8,128)(2,1)} %fusion.7.x_ref, bf16[1024,1024]{1,0:T(8,128)(2,1)} %get-tuple-element.32.wq_ref, bf16[1024,1024]{1,0:T(8,128)(2,1)} %get-tuple-element.33.wk_ref, ...), custom_call_target="tpu_custom_call" | custom-call | flops 8053063680 | bytes 10485760 | tf_op jit(solution)/shard_map/qkv_project/pallas_call | solution.py:508
  120.4 49.0 %attend_swap.1 = (bf16[1024,1024]{1,0:T(8,128)(2,1)}, bf16[1024,256]{1,0:T(8,128)(2,1)}, bf16[1024,256]{1,0:T(8,128)(2,1)}, bf16[1024,256]{1,0:T(8,128)(2,1)}) custom-call(bf16[1280,1024]{1,0:T(8,128)(2,1)} %get-tuple-element.35.q_ref.q_all, bf16[1280,1024]{1,0:T(8,128)(2,1)} %get-tuple-element.36.k_ref.k_all, ...), custom_call_target="tpu_custom_call" | custom-call | flops 17179869184 | bytes 8388608 | tf_op jit(solution)/shard_map/attend_swap/pallas_call | solution.py:600
  172.8 9.8 %attend.1 = bf16[1024,256]{1,0:T(8,128)(2,1)} custom-call(bf16[1024,256]{1,0:T(8,128)(2,1)} %get-tuple-element.39.q_ref, bf16[1024,256]{1,0:T(8,128)(2,1)} %get-tuple-element.40.k_ref, bf16[1024,256]{1,0:T(8,128)(2,1)} %get-tuple-element.41.v_ref), custom_call_target="tpu_custom_call" | custom-call | flops 4294967296 | bytes 2097152 | tf_op jit(solution)/shard_map/attend/pallas_call | solution.py:548
  185.1 6.2 psum.7
  192.0 4.3 fusion.62
  197.9 25.9 %all-gather.13.cloned.1.call-done = bf16[640,1280]{1,0:T(8,128)(2,1)} async-done(((bf16[160,1280]{1,0:T(8,128)(2,1)}), bf16[640,1280]{1,0:T(8,128)(2,1)}) %all-gather.13.cloned.1.call-update) | async-done | bytes 1638416 | tf_op jit(solution)/shard_map/all_gather | solution.py:894
  232.9 2.9 multiply_convert_fusion.1
  242.2 34.3 %reduce-scatter.15.cloned.1.call-done = bf16[200,1024]{1,0:T(8,128)(2,1)} async-done(((bf16[800,1024]{1,0:T(8,128)(2,1)}), bf16[200,1024]{1,0:T(8,128)(2,1)}) %reduce-scatter.15.cloned.1.call-update) | async-done | bytes 409616 | tf_op jit(solution)/shard_map/reduce_scatter | solution.py:918
  277.4 14.4 %all_gather.35 = bf16[160,1024]{1,0:T(8,128)(2,1)S(1)} all-gather(bf16[40,1024]{1,0:T(8,128)(2,1)S(1)} %slice.92), channel_id=1, replica_groups=mesh['dp'=4,'seq'=2,'tensor'=4] {'tensor'}, dimensions={0}, use_global_device_ids=true | all-gather | bytes 409600 | tf_op jit(solution)/shard_map/all_gather | solution.py:919
  296.1 2.6 convolution_convert_fusion.3
  298.7 3.9 copy.73
  313.9 7.4 attend_back.1
  322.9 46.2 %back_swap.1 = (bf16[1280,1024]{1,0:T(8,128)(2,1)}, bf16[1280,1024]{1,0:T(8,128)(2,1)}, bf16[1280,1024]{1,0:T(8,128)(2,1)}) custom-call(bf16[1280,1024]{1,0:T(8,128)(2,1)} %get-tuple-element.35.q_ref.q_all, bf16[160,1024]{1,0:T(8,128)(2,1)} %convolution_convert_fusion.7.g_ref, bf16[1280,1024]{1,0:T(8,128)(2,1)} %get-tuple-element.36.k_ref.k_all, ...), custom_call_target="tpu_custom_call" | custom-call | flops 4026531840 | bytes 12582912 | tf_op jit(solution)/shard_map/back_swap/pallas_call | solution.py:734
  369.1 6.8 convolution_convert_fusion
  375.9 3.2 convolution_convert_fusion.1
  379.1 3.2 convolution_convert_fusion.2
  382.3 13.4 %pad_maximum_fusion = bf16[1024,3072]{0,1:T(8,128)(2,1)} fusion(bf16[1024,1024]{0,1:T(8,128)(2,1)S(1)} %convolution_convert_fusion, bf16[1024,1024]{0,1:T(8,128)(2,1)S(1)} %convolution_convert_fusion.1, bf16[1024,1024]{0,1:T(8,128)(2,1)S(1)} %convolution_convert_fusion.2), kind=kLoop, calls=%fused_computation.3 | loop fusion | flops 18874368 | bytes 12582912 | tf_op jit(solution)/shard_map/concatenate | solution.py:970
  395.7 8.7 %copy.71 = bf16[1024,3072]{1,0:T(8,128)(2,1)} copy(bf16[1024,3072]{0,1:T(8,128)(2,1)} %pad_maximum_fusion) | data formatting | bytes 12582912
  404.4 29.3 %all_to_all.25 = bf16[4,256,256]{2,1,0:T(8,128)(2,1)S(1)} all-to-all(bf16[4,256,256]{2,1,0:T(8,128)(2,1)} %bitcast.128), channel_id=1, replica_groups=mesh['dp'=4,'seq'=2,'tensor'=4] {'tensor'}, dimensions={0} | all-to-all | bytes 1048576 | tf_op jit(solution)/shard_map/all_to_all | solution.py:887
  433.7 6.8 fusion.85
  440.6 2.4 convolution_convert_fusion.6
  444.1 3.8 convolution_convert_fusion.4
  450.2 4.4 convolution_convert_fusion.5
  454.6 13.2 %pad_maximum_fusion.1 = bf16[1024,3072]{0,1:T(8,128)(2,1)} fusion(bf16[1024,1024]{0,1:T(8,128)(2,1)S(1)} %copy-done.30, bf16[1024,1024]{0,1:T(8,128)(2,1)S(1)} %convolution_convert_fusion.5, bf16[1024,1024]{0,1:T(8,128)(2,1)S(1)} %convolution_convert_fusion.6), kind=kLoop, calls=%fused_computation.4 | loop fusion | flops 18874368 | bytes 12582912 | tf_op jit(solution)/shard_map/concatenate | solution.py:921
  467.9 8.8 %copy.75 = bf16[1024,3072]{1,0:T(8,128)(2,1)} copy(bf16[1024,3072]{0,1:T(8,128)(2,1)} %pad_maximum_fusion.1) | data formatting | bytes 12582912
  476.7 5.7 fusion.90
  482.5 2.9 fusion.89
  485.6 4.3 fusion.13
  491.4 2.6 fusion.12
  496.3 3.7 all-to-all-start.4
  500.0 3.3 multiply_reduce_fusion
  504.9 7.3 all-to-all-done.4
  512.1 4.8 all-to-all-start.3
  516.9 4.6 add_convert_fusion.x_ref
  521.5 26.2 %all-gather.9.cloned.1.call-done = bf16[32768,256]{1,0:T(8,128)(2,1)} async-done(((bf16[1024,256]{1,0:T(8,128)(2,1)}), bf16[32768,256]{1,0:T(8,128)(2,1)}) %all-gather.9.cloned.1.call-update) | async-done | bytes 16777232 | tf_op jit(solution)/shard_map/all_gather | solution.py:843
  547.7 50.1 %feed_forward.1 = bf16[1280,1024]{1,0:T(8,128)(2,1)} custom-call(bf16[1280,1024]{1,0:T(8,128)(2,1)} %add_convert_fusion.x_ref, f32[1280,1024]{1,0:T(8,128)} %get-tuple-element.160.res_ref, bf16[32,1024,256]{2,1,0:T(8,128)(2,1)} %bitcast.148, bf16[32,128,1024]{2,1,0:T(8,128)(2,1)} %bitcast.149), custom_call_target="tpu_custom_call" | custom-call | flops 32212254720 | bytes 25165824 | tf_op jit(solution)/shard_map/feed_forward/pallas_call | solution.py:784
  599.6 3.5 all-to-all-start.2
  603.1 3.2 slice.84
  606.3 4.7 all-to-all-done.2
  611.8 20.3 %all-to-all-start.1 = ((bf16[8,128,1024]{2,1,0:T(8,128)(2,1)}), bf16[8,128,1024]{2,1,0:T(8,128)(2,1)}, u32[]{:S(2)}, u32[]{:S(2)}) async-start(bf16[8,128,1024]{2,1,0:T(8,128)(2,1)} %bitcast.8), calls=%async_computation.1 | async-start | bytes 4194304 | tf_op jit(solution)/shard_map/all_to_all | solution.py:957
  638.0 73.3 %all-reduce.4 = (f32[1024]{0:T(1024)S(1)}, f32[1024]{0:T(1024)S(1)}, f32[1024]{0:T(1024)S(1)}, f32[1024]{0:T(1024)S(1)}) all-reduce(f32[1024]{0:T(1024)S(1)} %get-tuple-element.101, f32[1024]{0:T(1024)S(1)} %get-tuple-element.104, f32[1024]{0:T(1024)S(1)} %add.215, ...), channel_id=7, replica_groups=mesh['dp'=4,'seq'=2,'tensor'=4] {'dp','seq','tensor'}, use_global_device_ids=true, to_apply=%region_19.20.clone | all-reduce | flops 4096 | bytes 32768
  713.6 2.8 pad_maximum_fusion.3
  717.3 4.8 convert_bitcast_fusion
  733.4 3.7 reduce-scatter.21.cloned.1.call-done
  738.7 3.5 pad_maximum_fusion.2
  (263 shorter events, 85.9 us)
Async XLA Ops:
  8.0 224.2 %copy-start = (bf16[1024,1024]{1,0:T(8,128)(2,1)S(1)}, bf16[1024,1024]{1,0:T(8,128)(2,1)}, u32[]{:S(2)}) copy-start(bf16[1024,1024]{1,0:T(8,128)(2,1)} %param.26) | copy-start | bytes 6291460
  8.0 188.2 %all-gather.15.cloned.1.call-start = ((), (), s32[]{:S(2)}) async-start(), calls=%async_computation.21 | async-start | bytes 1638400 | tf_op jit(solution)/shard_map/all_gather | solution.py:882
  11.1 79.0 %copy-start.46 = (s32[1,256]{1,0:T(1,128)}, s32[1,256]{1,0:T(1,128)S(1)}, u32[]{:S(2)}) copy-start(s32[1,256]{1,0:T(1,128)S(1)} %fusion.77) | copy-start | bytes 3076
  90.1 133.7 %all-gather.13.cloned.1.call-start = ((), (), s32[]{:S(2)}) async-start(), calls=%async_computation.20 | async-start | bytes 2048000 | tf_op jit(solution)/shard_map/all_gather | solution.py:894
  99.1 4.4 copy-start.11
  99.1 4.4 copy-start.13
  99.1 4.4 copy-start.15
  172.7 11.2 %copy-start.41 = (f32[1024]{0:T(1024)S(1)}, f32[1024]{0:T(1024)}, u32[]{:S(2)}) copy-start(f32[1024]{0:T(1024)} %param.22) | copy-start | bytes 12292
  172.8 11.2 %copy-start.42 = (f32[1024]{0:T(1024)S(1)}, f32[1024]{0:T(1024)}, u32[]{:S(2)}) copy-start(f32[1024]{0:T(1024)} %param.23) | copy-start | bytes 12292
  185.0 91.4 %reduce-scatter.15.cloned.1.call-start = ((), (), s32[]{:S(2)}) async-start(), calls=%async_computation.13 | async-start | bytes 2048000 | tf_op jit(solution)/shard_map/reduce_scatter | solution.py:918
  241.1 206.8 %reduce-scatter.27.cloned.1.call-start = ((), (), s32[]{:S(2)}) async-start(), calls=%async_computation.23 | async-start | bytes 2359296
  276.4 17.0 %copy-start.33 = (bf16[200,1024]{1,0:T(8,128)(2,1)S(1)}, bf16[200,1024]{1,0:T(8,128)(2,1)}, u32[]{:S(2)}) copy-start(bf16[200,1024]{1,0:T(8,128)(2,1)} %reduce-scatter.15.cloned.1.call-done) | copy-start | bytes 1228804
  291.8 4.3 copy-start.40
  302.7 5.4 copy-start.12
  302.7 218.8 %all-gather.11.cloned.1.call-start = ((), (), s32[]{:S(2)}) async-start(), calls=%async_computation.19 | async-start | bytes 8650752 | tf_op jit(solution)/shard_map/all_gather | solution.py:844
  303.5 4.6 copy-start.14
  303.5 4.6 copy-start.16
  303.5 244.1 %all-gather.9.cloned.1.call-start = ((), (), s32[]{:S(2)}) async-start(), calls=%async_computation.18 | async-start | bytes 17301504 | tf_op jit(solution)/shard_map/all_gather | solution.py:843
  304.7 5.2 copy-start.27
  304.7 5.2 copy-start.28
  305.6 326.5 %reduce-scatter.25.cloned.1.call-start = ((), (), s32[]{:S(2)}) async-start(), calls=%async_computation.22 | async-start | bytes 7077888
  305.7 4.3 copy-start.29
  308.1 4.8 copy-start.18
  308.1 4.8 copy-start.23
  311.8 9.5 %copy-start.6 = (bf16[1024,1024]{1,0:T(8,128)(2,1)S(1)}, bf16[1024,1024]{1,0:T(8,128)(2,1)}, u32[]{:S(2)}) copy-start(bf16[1024,1024]{1,0:T(8,128)(2,1)} %get-tuple-element.42) | copy-start | bytes 6291460
  311.8 9.5 %copy-start.21 = (bf16[160,1024]{1,0:T(8,128)(2,1)S(1)}, bf16[160,1024]{1,0:T(8,128)(2,1)}, u32[]{:S(2)}) copy-start(bf16[160,1024]{1,0:T(8,128)(2,1)} %copy-done.20) | copy-start | bytes 983044
  369.1 6.8 copy-start.22
  369.1 6.8 copy-start.54
  404.3 317.7 %reduce-scatter.23.cloned.1.call-start = ((), (), s32[]{:S(2)}) async-start(), calls=%async_computation.17 | async-start | bytes 327680 | tf_op jit(solution)/shard_map/reduce_scatter | solution.py:975
  433.7 6.8 copy-start.35
  433.7 6.8 copy-start.38
  433.7 6.8 copy-start.60
  449.8 273.7 %reduce-scatter.29.cloned.1.call-start = ((), (), s32[]{:S(2)}) async-start(), calls=%async_computation.24 | async-start | bytes 7077888
  450.2 4.4 copy-start.30
  476.7 5.7 copy-start.50
  476.7 5.7 copy-start.53
  485.6 4.4 copy-start.19
  485.6 4.4 copy-start.47
  496.3 15.9 %all-to-all-start.4 = ((bf16[2,128,1024]{2,1,0:T(8,128)(2,1)}), bf16[2,128,1024]{2,1,0:T(8,128)(2,1)S(1)}, u32[]{:S(2)}, u32[]{:S(2)}) async-start(bf16[2,128,1024]{2,1,0:T(8,128)(2,1)} %bitcast.31), calls=%async_computation.5 | async-start | bytes 1048576 | tf_op jit(solution)/shard_map/all_to_all | solution.py:960
  512.1 9.4 %copy-start.26 = (bf16[2,128,1024]{2,1,0:T(8,128)(2,1)}, bf16[2,128,1024]{2,1,0:T(8,128)(2,1)S(1)}, u32[]{:S(2)}) copy-start(bf16[2,128,1024]{2,1,0:T(8,128)(2,1)S(1)} %all-to-all-done.4) | copy-start | bytes 1572868
  512.1 87.5 %all-to-all-start.3 = ((bf16[8,128,1024]{2,1,0:T(8,128)(2,1)}), bf16[8,128,1024]{2,1,0:T(8,128)(2,1)S(1)}, u32[]{:S(2)}, u32[]{:S(2)}) async-start(bf16[8,128,1024]{2,1,0:T(8,128)(2,1)} %bitcast.105), calls=%async_computation.4 | async-start | bytes 4194304 | tf_op jit(solution)/shard_map/all_to_all | solution.py:957
  599.6 11.4 %all-to-all-start.2 = ((bf16[2,128,1024]{2,1,0:T(8,128)(2,1)}), bf16[2,128,1024]{2,1,0:T(8,128)(2,1)S(1)}, u32[]{:S(2)}, u32[]{:S(2)}) async-start(bf16[2,128,1024]{2,1,0:T(8,128)(2,1)} %bitcast.112), calls=%async_computation.2 | async-start | bytes 1048576 | tf_op jit(solution)/shard_map/all_to_all | solution.py:960
  611.8 126.9 %all-to-all-start.1 = ((bf16[8,128,1024]{2,1,0:T(8,128)(2,1)}), bf16[8,128,1024]{2,1,0:T(8,128)(2,1)}, u32[]{:S(2)}, u32[]{:S(2)}) async-start(bf16[8,128,1024]{2,1,0:T(8,128)(2,1)} %bitcast.8), calls=%async_computation.1 | async-start | bytes 4194304 | tf_op jit(solution)/shard_map/all_to_all | solution.py:957
  632.1 5.8 copy-start.10
  632.1 98.1 %reduce-scatter.17.cloned.1.call-start = ((), (), s32[]{:S(2)}) async-start(), calls=%async_computation.14 | async-start | bytes 327680 | tf_op jit(solution)/shard_map/reduce_scatter | solution.py:972
  636.0 95.9 %reduce-scatter.19.cloned.1.call-start = ((), (), s32[]{:S(2)}) async-start(), calls=%async_computation.15 | async-start | bytes 327680 | tf_op jit(solution)/shard_map/reduce_scatter | solution.py:972
  637.8 99.3 %reduce-scatter.21.cloned.1.call-start = ((), (), s32[]{:S(2)}) async-start(), calls=%async_computation.16 | async-start | bytes 327680 | tf_op jit(solution)/shard_map/reduce_scatter | solution.py:972
  726.3 12.4 %copy-start.25 = (bf16[2,128,1024]{2,1,0:T(8,128)(2,1)S(1)}, bf16[2,128,1024]{2,1,0:T(8,128)(2,1)}, u32[]{:S(2)}) copy-start(bf16[2,128,1024]{2,1,0:T(8,128)(2,1)} %copy-done.24) | copy-start | bytes 1572868
  (30 other events, 73.8 us)
Sparse Core Ops, SparseCore 0:
  90.2 42.4 all-gather.14
  185.1 38.5 all-gather.12
  241.2 35.1 reduce-scatter.14
  302.8 43.3 reduce-scatter.26
  404.5 68.8 reduce-scatter.24
  475.6 42.5 reduce-scatter.22
  521.5 82.5 reduce-scatter.28
  636.1 49.8 reduce-scatter.16
  688.3 24.1 reduce-scatter.18
  717.4 19.6 reduce-scatter.20
Sparse Core Ops, SparseCore 1:
  306.1 93.7 all-gather.10
  402.7 144.9 all-gather.8

commit v3 on v2

--- a/solution.py
+++ b/solution.py
@@ -4,6 +4,7 @@
 
 import jax
 import jax.numpy as jnp
+import numpy as np
 from jax import lax
 from jax.experimental import pallas as pl
 from jax.experimental.pallas import tpu as pltpu
@@ -369,8 +370,8 @@
 
 
 def exchange_in_kernel(
-    sizes, tok_ref, wq_ref, wk_ref, wv_ref, wo_ref, x_ref, q_ref, k_ref, v_ref, o_ref,
-    tok_send, tok_recv, w_send, w_recv, local_sem,
+    sizes, tok_ref, wq_ref, wk_ref, wv_ref, wo_ref, count_ref, x_ref, q_ref, k_ref, v_ref, o_ref, counts_ref,
+    tok_send, tok_recv, w_send, w_recv, count_send, count_recv, local_sem,
 ):
     n_seq, n_ten, half, rows, slices = sizes
     dp, sx, t = lax.axis_index("dp"), lax.axis_index("seq"), lax.axis_index("tensor")
@@ -382,7 +383,12 @@
         g = (me + i) % group
         others.append((g // n_ten, g % n_ten))
     y_peer, c_peer, x_peer = {"dp": (dp + 2) % 4}, {"dp": 2 * y + 1 - c}, {"seq": 1 - sx}
-    greet([{"seq": a, "tensor": b} for a, b in others] + [y_peer, c_peer])
+    dp_peers = [{"dp": (dp + i) % 4} for i in range(1, 4)]
+    greet([{"seq": a, "tensor": b} for a, b in others] + dp_peers)
+    counts = [
+        remote(count_ref, counts_ref.at[dp], count_send.at[i], count_recv.at[i], peer) for i, peer in enumerate(dp_peers)
+    ]
+    start_all(counts)
 
     hw = wq_ref.shape[1]
     srow, orow = wq_ref.shape[0] // slices, hw // slices
@@ -450,6 +456,7 @@
     ]
     for i, (w_ref, out, s, by_rows) in enumerate(weights):
         local.append(pltpu.make_async_copy(w_ref, block(out, by_rows, 0, slices, t), local_sem.at[2 + i]))
+    local.append(pltpu.make_async_copy(count_ref, counts_ref.at[dp], local_sem.at[6]))
     start_all(local)
     for k in range(1, 4):
         for earlier in stage[k - 1]:
@@ -461,10 +468,11 @@
         for copy in copies:
             copy.wait_send()
     wait_all(local)
+    wait_all(counts)
     wait_all(tokens)
 
 
-def exchange_in(tok, w_query, w_key, w_value, w_out, n_dp, n_seq, n_ten):
+def exchange_in(tok, w_query, w_key, w_value, w_out, count, n_dp, n_seq, n_ten):
     windows, rows, width = tok.shape
     slices = n_dp * n_seq
     vmem = pl.BlockSpec(memory_space=pltpu.VMEM)
@@ -472,51 +480,67 @@
     group = n_seq * n_ten
     return pl.pallas_call(
         functools.partial(exchange_in_kernel, (n_seq, n_ten, windows // n_seq, rows, slices)),
-        in_specs=[vmem] * 5,
-        out_specs=[any_spec()] * 5,
-        out_shape=[jax.ShapeDtypeStruct(((group + n_seq) * rows, width), BF)] + [square] * 4,
+        in_specs=[vmem] * 6,
+        out_specs=[any_spec()] * 6,
+        out_shape=[jax.ShapeDtypeStruct(((group + n_seq) * rows, width), BF)]
+        + [square] * 4
+        + [jax.ShapeDtypeStruct((n_dp,) + count.shape, count.dtype)],
         scratch_shapes=[
             pltpu.SemaphoreType.DMA((group,)),
             pltpu.SemaphoreType.DMA((group,)),
             pltpu.SemaphoreType.DMA((4, 4 * (n_ten - 1))),
             pltpu.SemaphoreType.DMA((4, 4 * (n_ten - 1))),
-            pltpu.SemaphoreType.DMA((6,)),
+            pltpu.SemaphoreType.DMA((3,)),
+            pltpu.SemaphoreType.DMA((3,)),
+            pltpu.SemaphoreType.DMA((7,)),
         ],
         compiler_params=pltpu.CompilerParams(collective_id=0, has_side_effects=True),
         name="exchange_in",
-    )(tok, w_query, w_key, w_value, w_out)
-
-
-def qkv_kernel(x_ref, wq_ref, wk_ref, wv_ref, cos_ref, sin_ref, q_ref, k_ref, v_ref):
-    x = x_ref[...]
-    cos, sin = cos_ref[...], sin_ref[...]
+    )(tok, w_query, w_key, w_value, w_out, count)
+
+
+def qkv_kernel(
+    x_ref, gain_ref, bias_ref, wq_ref, wk_ref, wv_ref, cos_ref, sin_ref, part_cos_ref, part_sin_ref,
+    first_ref, q_ref, k_ref, v_ref,
+):
+    shared = pl.program_id(0) == pl.num_programs(0) - 1
+    normed, _ = layer_stats(x_ref[...].astype(F32))
+    first_ref[...] = (normed * gain_ref[...] + bias_ref[...]).astype(BF)
+    cos = jnp.where(shared, part_cos_ref[...], cos_ref[...])
+    sin = jnp.where(shared, part_sin_ref[...], sin_ref[...])
+    wide = 256
     for w_ref, out_ref, scale in ((wq_ref, q_ref, 1.0 / math.sqrt(HEAD_DIM)), (wk_ref, k_ref, 1.0), (wv_ref, v_ref, None)):
-        acc = dot_n(x, w_ref[...])
-        for c in range(acc.shape[1] // LANES):
-            part = acc[:, c * LANES : (c + 1) * LANES]
-            if scale is not None:
-                part = (part * cos + swap_halves(part) * sin) * scale
-            out_ref[:, c * LANES : (c + 1) * LANES] = part.astype(BF)
-
-
-def qkv_project(x, w_query, w_key, w_value, cos, sin):
+        for at in range(0, w_ref.shape[1], wide):
+            acc = dot_n(first_ref[...], w_ref[:, at : at + wide])
+            for c in range(0, wide, LANES):
+                part = acc[:, c : c + LANES]
+                if scale is not None:
+                    part = (part * cos + swap_halves(part) * sin) * scale
+                out_ref[:, at + c : at + c + LANES] = part.astype(BF)
+
+
+def once(shape):
+    return pl.BlockSpec(shape, lambda *_: (0,) * len(shape), pipeline_mode=pl.Buffered(1))
+
+
+def norm_qkv(x, gain, bias, w_query, w_key, w_value, tables, part_tables):
     rows, width = x.shape
-    tile, cols = 256, 512
-    w_spec = pl.BlockSpec((width, cols), lambda t, r: (0, t))
-    out_spec = pl.BlockSpec((tile, cols), lambda t, r: (r, t))
-    table = pl.BlockSpec((tile, LANES), lambda t, r: (r, 0))
+    tile = 256
+    row = pl.BlockSpec((tile, width), lambda r: (r, 0))
+    own = tables[0].shape[0] // tile
+    table = pl.BlockSpec((tile, LANES), lambda r: (jnp.minimum(r, own - 1), 0))
     return pl.pallas_call(
         qkv_kernel,
-        grid=(width // cols, rows // tile),
-        in_specs=[pl.BlockSpec((tile, width), lambda t, r: (r, 0)), w_spec, w_spec, w_spec, table, table],
-        out_specs=[out_spec] * 3,
-        out_shape=[jax.ShapeDtypeStruct((rows, width), BF)] * 3,
-        cost_estimate=pl.CostEstimate(flops=6 * rows * width * width, bytes_accessed=8 * rows * width, transcendentals=0),
-        name="qkv_project",
-    )(x, w_query, w_key, w_value, cos, sin)
-
-
-def attend_body(q_ref, k_ref, v_ref, o_ref):
+        grid=(rows // tile,),
+        in_specs=[row, once((1, width)), once((1, width))] + [once((width, width))] * 3 + [table, table] + [once((tile, LANES))] * 2,
+        out_specs=[row] * 4,
+        out_shape=[jax.ShapeDtypeStruct((rows, width), BF)] * 4,
+        cost_estimate=pl.CostEstimate(flops=6 * rows * width * width, bytes_accessed=16 * rows * width, transcendentals=0),
+        name="norm_qkv",
+    )(x, gain.reshape(1, width), bias.reshape(1, width), w_query, w_key, w_value, *tables, *part_tables)
+
+
+def attend_body(q_ref, k_ref, v_ref):
     q, k, v = q_ref[...], k_ref[...], v_ref[...]
     outs = []
     for h in range(LANES // HEAD_DIM):
@@ -525,7 +549,7 @@
         norm = jnp.sum(p, axis=1, keepdims=True)
         outs.append(dot_n(p.astype(BF), v) / norm)
     lane = lax.broadcasted_iota(jnp.int32, outs[0].shape, 1)
-    o_ref[...] = jnp.where(lane < HEAD_DIM, outs[0], outs[1]).astype(BF)
+    return jnp.where(lane < HEAD_DIM, outs[0], outs[1]).astype(BF)
 
 
 def attend_specs(rows, tile):
@@ -542,17 +566,57 @@
     )
 
 
-def attend(q, k, v):
-    rows, width = q.shape
-    tile, pairs = 512, width // LANES
+def attend_left_kernel(n_ten, q_ref, k_ref, v_ref, part_ref, buf, send, recv, local_sem):
+    t = lax.axis_index("tensor")
+    r, p = pl.program_id(0), pl.program_id(1)
+    last_pair = p == pl.num_programs(1) - 1
+    hw = buf.shape[2]
+    heads = pl.ds(pl.multiple_of(t * hw, hw), hw)
+    dst = part_ref.at[:, heads]
+
+    @pl.when((p == 0) & (r == 0))
+    def _():
+        greet([{"tensor": (t + j) % n_ten} for j in range(1, n_ten)])
+
+    buf[r, :, pl.ds(pl.multiple_of(p * LANES, LANES), LANES)] = attend_body(q_ref, k_ref, v_ref)
+
+    def copy_to(j):
+        to = (t + j) % n_ten
+        return remote(buf.at[to], dst, send.at[j - 1], recv.at[j - 1], {"tensor": to})
+
+    own = pltpu.make_async_copy(buf.at[t], dst, local_sem.at[0])
+    for j in range(1, n_ten):
+
+        @pl.when(last_pair & (r == (t + j) % n_ten))
+        def _(j=j):
+            copy_to(j).start()
+
+    @pl.when(last_pair & (r == t))
+    def _():
+        own.start()
+
+    @pl.when(last_pair & (r == n_ten - 1))
+    def _():
+        wait_all([copy_to(j) for j in range(1, n_ten)])
+        own.wait()
+
+
+def attend_left(q, k, v, n_ten):
+    rows, hw = q.shape
+    tile, pairs = rows // n_ten, hw // LANES
+    column = pl.BlockSpec((rows, LANES), lambda r, p: (0, p))
     return pl.pallas_call(
-        attend_body,
-        grid=(pairs, rows // tile),
-        in_specs=attend_specs(rows, tile),
-        out_specs=pl.BlockSpec((tile, LANES), lambda p, r: (r, p)),
-        out_shape=jax.ShapeDtypeStruct((rows, width), BF),
+        functools.partial(attend_left_kernel, n_ten),
+        grid=(n_ten, pairs),
+        in_specs=[pl.BlockSpec((tile, LANES), lambda r, p: (r, p)), column, column],
+        out_specs=any_spec(),
+        out_shape=jax.ShapeDtypeStruct((tile, n_ten * hw), BF),
+        scratch_shapes=[pltpu.VMEM((n_ten, tile, hw), BF)]
+        + [pltpu.SemaphoreType.DMA((n_ten - 1,))] * 2
+        + [pltpu.SemaphoreType.DMA((1,))],
+        compiler_params=pltpu.CompilerParams(collective_id=3, has_side_effects=True),
         cost_estimate=attend_cost(rows, pairs),
-        name="attend",
+        name="attend_left",
     )(q, k, v)
 
 
@@ -586,7 +650,7 @@
         greet([{"tensor": (t + j) % n_ten} for j in range(1, n_ten)])
         start_all(copies + local)
 
-    attend_body(q_ref, k_ref, v_ref, o_ref)
+    o_ref[...] = attend_body(q_ref, k_ref, v_ref)
 
     @pl.when(step == pl.num_programs(0) * pl.num_programs(1) - 1)
     def _():
@@ -642,9 +706,34 @@
     return dq, dk, dv
 
 
-def back_kernel(q_ref, g_ref, k_ref, v_ref, pick_ref, cos_ref, sin_ref, qcos_ref, qsin_ref, dq_ref, dk_ref, dv_ref):
+def back_left_kernel(
+    n_ten, q_ref, g_ref, k_ref, v_ref, pick_ref, cos_ref, sin_ref, qcos_ref, qsin_ref, dq_ref, dk_ref, dv_ref,
+    parts, total, send, recv,
+):
+    t = lax.axis_index("tensor")
+    p = pl.program_id(0)
+    hw = total.shape[1]
+
+    @pl.when(p == 0)
+    def _():
+        peers = [(t + j) % n_ten for j in range(1, n_ten)]
+        greet([{"tensor": to} for to in peers])
+        copies = [
+            remote(
+                g_ref.at[:, pl.ds(pl.multiple_of(to * hw, hw), hw)], parts.at[j], send.at[j], recv.at[j], {"tensor": to}
+            )
+            for j, to in enumerate(peers)
+        ]
+        start_all(copies)
+        wait_all(copies)
+        whole = g_ref[:, pl.ds(pl.multiple_of(t * hw, hw), hw)].astype(F32)
+        for j in range(n_ten - 1):
+            whole = whole + parts[j].astype(F32)
+        total[...] = whole.astype(BF)
+
+    g_view = total.at[:, pl.ds(pl.multiple_of(p * LANES, LANES), LANES)]
     dq_ref[...], dk_ref[...], dv_ref[...] = back_body(
-        q_ref, g_ref, k_ref, v_ref, pick_ref, cos_ref, sin_ref, qcos_ref, qsin_ref
+        q_ref, g_view, k_ref, v_ref, pick_ref, cos_ref, sin_ref, qcos_ref, qsin_ref
     )
 
 
@@ -664,18 +753,27 @@
     )
 
 
-def attend_back(q, grad_rows, k, v, pick, tables):
+def back_left(q, grad_rows, k, v, pick, tables, n_ten):
     masked, length = pick.shape
     width = q.shape[1]
     full = pl.BlockSpec((length, LANES), lambda p: (0, p))
+    specs = back_specs(length, masked)
+    specs[1] = once(grad_rows.shape)
     return pl.pallas_call(
-        back_kernel,
+        functools.partial(back_left_kernel, n_ten),
         grid=(width // LANES,),
-        in_specs=back_specs(length, masked),
+        in_specs=specs,
         out_specs=[full] * 3,
         out_shape=[jax.ShapeDtypeStruct((length, width), BF)] * 3,
+        scratch_shapes=[
+            pltpu.VMEM((n_ten - 1, masked, width), BF),
+            pltpu.VMEM((masked, width), BF),
+            pltpu.SemaphoreType.DMA((n_ten - 1,)),
+            pltpu.SemaphoreType.DMA((n_ten - 1,)),
+        ],
+        compiler_params=pltpu.CompilerParams(collective_id=6, has_side_effects=True),
         cost_estimate=back_cost(length, masked, width // LANES),
-        name="attend_back",
+        name="back_left",
     )(q, grad_rows, k, v, pick, *tables)
 
 
@@ -750,63 +848,545 @@
     )(q, grad_rows, k, v, pick, *tables, *left)
 
 
-def feed_kernel(x_ref, res_ref, gu_ref, down_ref, out_ref, acc_ref):
-    step = pl.program_id(0)
+def weight_hops(gathered, n_ten, sems):
+    dp, sx, t = lax.axis_index("dp"), lax.axis_index("seq"), lax.axis_index("tensor")
+    y, c = dp // 2, dp % 2
+    gate_ref, up_ref, down_ref = gathered
+    width, units = gate_ref.shape[0], gate_ref.shape[1] // n_ten
+    size, cols = width // 8, width // 2
+    s_xy, s_yx = c * 4 + y * 2 + sx, c * 4 + sx * 2 + y
+    x_peer, y_peer, c_peer = {"seq": 1 - sx}, {"dp": (dp + 2) % 4}, {"dp": 2 * y + 1 - c}
+    send, recv = sems
+
+    def shard(ref, k, first, count, which):
+        rows = pl.multiple_of(first * (size if k < 2 else units // 8), 16)
+        if k < 2:
+            at = 0 if which is None else pl.multiple_of(which * units, units)
+            return ref.at[pl.ds(rows, count * size), pl.ds(at, units)]
+        at = rows if which is None else pl.multiple_of(which * units + rows, 16)
+        return ref.at[pl.ds(at, count * (units // 8)), pl.ds((k - 2) * cols, cols)]
+
+    refs = (gate_ref, up_ref, down_ref, down_ref)
+    slices = (s_xy, s_yx, s_xy, s_yx)
+
+    def along(which, peer_t, slot, number, own=None):
+        copies = []
+        for k in range(4):
+            dst = shard(refs[k], k, slices[k], 1, which)
+            src = dst if own is None else shard(own[min(k, 2)], k, slices[k], 1, None)
+            copies.append(remote(src, dst, send.at[number, k], recv.at[slot, k], {"tensor": peer_t}))
+        return copies
+
+    def across(hop, which, order):
+        copies = []
+        for k in range(4):
+            xy = k % 2 == 0
+            peer, first, count = (
+                (x_peer if xy else y_peer, slices[k], 1),
+                (y_peer if xy else x_peer, slices[k] // 2 * 2, 2),
+                (c_peer, c * 4, 4),
+            )[hop]
+            ref = shard(refs[k], k, first, count, which)
+            copies.append(remote(ref, ref, send.at[5 + 3 * order + hop, k], recv.at[4 + 3 * order + hop, k], peer))
+        return copies
+
+    return along, across
+
+
+def feed_kernel(
+    n_ten, tok_ref, att_ref, left_ref, wo_ref, gain_ref, bias_ref, pick_ref, part_pick_ref, cot_ref, wg_ref, wu_ref, wd_ref,
+    out_ref, att_m_ref, gr2_ref, gatt_ref, vec_ref, x_m_ref, ag_ref, au_ref, ad_ref,
+    x_ref, acc_ref, normed_ref, inv_ref, grad_ref, g_buf, u_buf, d_buf, buf_sem, send, recv,
+):
+    dp, sx, t = lax.axis_index("dp"), lax.axis_index("seq"), lax.axis_index("tensor")
+    step, steps = pl.program_id(0), pl.num_programs(0)
+    rows, width = tok_ref.shape
+    length = att_ref.shape[0]
+    masked = cot_ref.shape[0]
+    slots = masked // 2
+    unit = g_buf.shape[2]
+    units = wg_ref.shape[1]
+    per = units // unit
+    gain = gain_ref[...]
+    own = (wg_ref, wu_ref, wd_ref)
+
+    side = t // 2
+    middle = jnp.minimum(t, n_ten - 1 - t)
+    mirror = lambda k: k + side * (n_ten - 1 - 2 * k)
+    order = [mirror(k) for k in (middle, 1 - middle, 2, 3)]
+    inward, outward = mirror(middle + 1), mirror(0)
+    along, across = weight_hops((ag_ref, au_ref, ad_ref), n_ten, (send, recv))
+    to_in = along(t, inward, 1 + middle, 0, own)
+    to_out = along(t, outward, 1, 1, own)
+    in_far = along(mirror(0), inward, 3, 2)
+    out_two = along(mirror(2), outward, 2, 3)
+    out_three = along(mirror(3), outward, 3, 4)
+    is_middle, is_end = middle == 1, middle == 0
+    hop = [[across(h, order[i], i - 1) for h in range(3)] for i in (1, 2, 3)]
+
+    def arrived(i):
+        for copy in along(order[i], inward, i, 0):
+            copy.wait_recv()
+
+    def got(copies):
+        for copy in copies:
+            copy.wait_recv()
+
+    def fetch(at):
+        slot, i, b = at % 2, at // per, at % per
+
+        def make(refs, shard_at):
+            base = pl.multiple_of(shard_at * units + b * unit, unit)
+            return [
+                pltpu.make_async_copy(refs[0].at[:, pl.ds(base, unit)], g_buf.at[slot], buf_sem.at[slot, 0]),
+                pltpu.make_async_copy(refs[1].at[:, pl.ds(base, unit)], u_buf.at[slot], buf_sem.at[slot, 1]),
+                pltpu.make_async_copy(refs[2].at[pl.ds(base, unit), :], d_buf.at[slot], buf_sem.at[slot, 2]),
+            ]
+
+        @pl.when(i == 0)
+        def _():
+            start_all(make(own, 0))
+
+        @pl.when(i > 0)
+        def _():
+            which = order[1] * (i == 1) + order[2] * (i == 2) + order[3] * (i == 3)
+            start_all(make((ag_ref, au_ref, ad_ref), which))
+
+    def fetched(at):
+        slot = at % 2
+        wait_all(
+            [
+                pltpu.make_async_copy(wg_ref.at[:, pl.ds(0, unit)], g_buf.at[slot], buf_sem.at[slot, 0]),
+                pltpu.make_async_copy(wu_ref.at[:, pl.ds(0, unit)], u_buf.at[slot], buf_sem.at[slot, 1]),
+                pltpu.make_async_copy(wd_ref.at[pl.ds(0, unit), :], d_buf.at[slot], buf_sem.at[slot, 2]),
+            ]
+        )
+
+    def norm(res):
+        normed, inv_std = layer_stats(res)
+        return normed, inv_std, (normed * gain + bias_ref[...]).astype(BF)
+
+    @pl.when(step == 0)
+    def _():
+        peers = [{"tensor": (t + j) % n_ten} for j in range(1, n_ten)]
+        greet(peers + [{"seq": 1 - sx}] + [{"dp": (dp + 2) % 4}, {"dp": dp // 2 * 2 + 1 - dp % 2}])
+        start_all(to_in)
+
+        @pl.when(is_middle)
+        def _():
+            start_all(to_out)
+
+        fetch(0)
+        tile = rows - length
+        for i, (pick, att, tok) in enumerate(
+            ((pick_ref[...], att_ref[...], tok_ref[:length, :]), (part_pick_ref[...], left_ref[...], tok_ref[length:, :]))
+        ):
+            here = slice(i * slots, (i + 1) * slots)
+            att_m = dot_n(pick, att).astype(BF)
+            att_m_ref[here, :] = att_m
+            normed, inv_std, low = norm(dot_n(pick, tok) + dot_n(att_m, wo_ref[...]))
+            normed_ref[here, :] = normed
+            inv_ref[here, :] = jnp.broadcast_to(inv_std, (slots, LANES))
+            here_too = jnp.sum(pick.astype(F32), axis=1, keepdims=True) > 0.0
+            low = jnp.where(here_too, low.astype(F32), 0.0).astype(BF)
+            x_ref[rows + i * slots : rows + (i + 1) * slots, :] = low
+            x_m_ref[here, :] = low
+        for at in range(0, rows, tile):
+            att = att_ref[at : at + tile, :] if at < length else left_ref[...]
+            res = tok_ref[at : at + tile, :].astype(F32) + dot_n(att, wo_ref[...])
+            x_ref[at : at + tile, :] = norm(res)[2]
+            acc_ref[at : at + tile, :] = res
+        grad_ref[...] = jnp.zeros_like(grad_ref)
+
+    fetched(step)
+
+    @pl.when((step + 1 < steps) & ((step + 1) % per != 0))
+    def _():
+        fetch(step + 1)
+
+    slot = step % 2
     x = x_ref[...]
-    unit = down_ref.shape[1]
-    parts = []
-    for p in range(gu_ref.shape[0]):
-        both = dot_n(x, gu_ref[p])
-        gate, up = both[:, :unit], both[:, unit:]
-        parts.append((gate * jax.nn.sigmoid(gate) * up).astype(BF))
-    hidden = jnp.concatenate(parts, axis=1)
-    down = down_ref[...].reshape(-1, down_ref.shape[2])
-    new = dot_n(hidden, down)
-
-    @pl.when(step == 0)
-    def _():
-        acc_ref[...] = res_ref[...] + new
-
-    @pl.when(step > 0)
-    def _():
-        acc_ref[...] += new
-
-    @pl.when(step == pl.num_programs(0) - 1)
+    w_g, w_u, w_d = g_buf[slot], u_buf[slot], d_buf[slot]
+    gate, up = dot_n(x, w_g), dot_n(x, w_u)
+    sig = jax.nn.sigmoid(gate)
+    act = gate * sig
+    hidden = (act[:rows] * up[:rows]).astype(BF)
+    for at in range(0, width, unit):
+        acc_ref[:, at : at + unit] += dot_n(hidden, w_d[:, at : at + unit])
+    back = dot_t(cot_ref[...].astype(BF), w_d)
+    gate, up, sig, act = gate[rows:], up[rows:], sig[rows:], act[rows:]
+    grad_gate = (back * up * sig * (1.0 + gate * (1.0 - sig))).astype(BF)
+    grad_up = (back * act).astype(BF)
+    grad_ref[...] += dot_t(grad_gate, w_g) + dot_t(grad_up, w_u)
+
+    @pl.when(step == per - 1)
+    def _():
+        arrived(1)
+        start_all(hop[0][0])
+
+        @pl.when(is_middle)
+        def _():
+            arrived(2)
+            start_all(in_far)
+            start_all(out_two)
+
+        got(hop[0][0])
+        start_all(hop[0][1])
+
+        @pl.when(is_end)
+        def _():
+            arrived(2)
+
+        @pl.when(is_middle)
+        def _():
+            arrived(3)
+            start_all(out_three)
+
+        start_all(hop[1][0])
+        got(hop[0][1])
+        start_all(hop[0][2])
+        got(hop[0][2])
+
+    @pl.when(step == per)
+    def _():
+        got(hop[1][0])
+        start_all(hop[1][1])
+
+    @pl.when(step == per + 1)
+    def _():
+        @pl.when(is_end)
+        def _():
+            arrived(3)
+
+        start_all(hop[2][0])
+
+    @pl.when(step == 2 * per - 1)
+    def _():
+        got(hop[1][1])
+        start_all(hop[1][2])
+        got(hop[2][0])
+        start_all(hop[2][1])
+        got(hop[1][2])
+
+    @pl.when(step == 3 * per - 1)
+    def _():
+        got(hop[2][1])
+        start_all(hop[2][2])
+        got(hop[2][2])
+
+    @pl.when((step + 1 < steps) & ((step + 1) % per == 0))
+    def _():
+        fetch(step + 1)
+
+    @pl.when(step == steps - 1)
     def _():
         out_ref[...] = acc_ref[...].astype(BF)
-
-
-def feed_forward(x, res, gate_up, down):
-    rows, width = x.shape
-    pieces, unit = down.shape[:2]
-    per = 2
-    whole = lambda i: (0, 0)
+        grad, normed = grad_ref[...], normed_ref[...]
+        vec_ref[...] = jnp.concatenate(
+            [jnp.sum(grad * normed, axis=0, keepdims=True), jnp.sum(grad, axis=0, keepdims=True)], axis=0
+        )
+        gr2 = (cot_ref[...] + norm_back(grad, normed, inv_ref[:, :1], gain)).astype(BF)
+        gr2_ref[...] = gr2
+        gatt_ref[...] = dot_t(gr2, wo_ref[...]).astype(BF)
+        for copy in to_in:
+            copy.wait_send()
+
+        @pl.when(is_middle)
+        def _():
+            for copy in to_out + in_far + out_two + out_three:
+                copy.wait_send()
+
+        for shard_hops in hop:
+            for copies in shard_hops:
+                for copy in copies:
+                    copy.wait_send()
+
+
+def feed_forward(tok, att, left_att, w_out, gain, bias, pick, part_pick, cot, w_gate, w_up, w_down, n_ten):
+    rows, width = tok.shape
+    units = w_gate.shape[1]
+    masked = cot.shape[0]
+    unit = 256
+    whole = lambda *shape: pl.BlockSpec(shape, lambda i: (0,) * len(shape))
+    low = jax.ShapeDtypeStruct((masked, width), BF)
     return pl.pallas_call(
-        feed_kernel,
-        grid=(pieces // per,),
-        in_specs=[
-            pl.BlockSpec((rows, width), whole, pipeline_mode=pl.Buffered(1)),
-            pl.BlockSpec((rows, width), whole, pipeline_mode=pl.Buffered(1)),
-            pl.BlockSpec((per, width, 2 * unit), lambda i: (i, 0, 0)),
-            pl.BlockSpec((per, unit, width), lambda i: (i, 0, 0)),
+        functools.partial(feed_kernel, n_ten),
+        grid=(n_ten * units // unit,),
+        in_specs=[once(x.shape) for x in (tok, att, left_att, w_out)]
+        + [once((1, width)), once((1, width)), once(pick.shape), once(part_pick.shape), once(cot.shape)]
+        + [any_spec()] * 3,
+        out_specs=[whole(rows, width)] + [whole(masked, width)] * 3 + [whole(2, width), whole(masked, width)] + [any_spec()] * 3,
+        out_shape=[
+            jax.ShapeDtypeStruct((rows, width), BF), low, low, low,
+            jax.ShapeDtypeStruct((2, width), F32), low,
+            jax.ShapeDtypeStruct((width, n_ten * units), BF),
+            jax.ShapeDtypeStruct((width, n_ten * units), BF),
+            jax.ShapeDtypeStruct((n_ten * units, width), BF),
         ],
-        out_specs=pl.BlockSpec((rows, width), whole),
-        out_shape=jax.ShapeDtypeStruct((rows, width), BF),
-        scratch_shapes=[pltpu.VMEM((rows, width), F32)],
+        scratch_shapes=[
+            pltpu.VMEM((rows + masked, width), BF),
+            pltpu.VMEM((rows, width), F32),
+            pltpu.VMEM((masked, width), F32),
+            pltpu.VMEM((masked, LANES), F32),
+            pltpu.VMEM((masked, width), F32),
+            pltpu.VMEM((2, width, unit), BF),
+            pltpu.VMEM((2, width, unit), BF),
+            pltpu.VMEM((2, unit, width), BF),
+            pltpu.SemaphoreType.DMA((2, 3)),
+            pltpu.SemaphoreType.DMA((14, 4)),
+            pltpu.SemaphoreType.DMA((13, 4)),
+        ],
+        compiler_params=pltpu.CompilerParams(collective_id=5, has_side_effects=True),
         cost_estimate=pl.CostEstimate(
-            flops=6 * rows * width * pieces * unit, bytes_accessed=6 * width * pieces * unit, transcendentals=rows * pieces * unit
+            flops=8 * rows * width * n_ten * units, bytes_accessed=6 * width * n_ten * units, transcendentals=rows * n_ten * units
         ),
         name="feed_forward",
-    )(x, res, gate_up, down)
-
-
-def rotary_lanes(positions):
-    cosine, sine = rotary_tables(positions)
+    )(tok, att, left_att, w_out, gain.reshape(1, width), bias.reshape(1, width), pick, part_pick, cot, w_gate, w_up, w_down)[:6]
+
+
+def token_back_kernel(
+    tok_ref, dq_ref, dk_ref, dv_ref, wq_ref, wk_ref, wv_ref, gain_ref, pick_ref, rows_ref, out_ref, vec_ref
+):
+    acc = dot_t(dq_ref[...], wq_ref[...]) + dot_t(dk_ref[...], wk_ref[...]) + dot_t(dv_ref[...], wv_ref[...])
+    normed, inv_std = layer_stats(tok_ref[...].astype(F32))
+    direct = t_dot(pick_ref[...], rows_ref[0])
+    out_ref[...] = (direct + norm_back(acc, normed, inv_std, gain_ref[...])).astype(BF)
+    sums = jnp.concatenate([jnp.sum(acc * normed, axis=0, keepdims=True), jnp.sum(acc, axis=0, keepdims=True)], axis=0)
+
+    @pl.when(pl.program_id(0) == 0)
+    def _():
+        vec_ref[...] = sums
+
+    @pl.when(pl.program_id(0) > 0)
+    def _():
+        vec_ref[...] += sums
+
+
+def token_back(tok, grads, weights, gain, pick, rows_m):
+    rows, width = tok.shape
+    slots = pick.shape[0]
+    tile = 256
+    row = pl.BlockSpec((tile, width), lambda r: (r, 0))
+    own = rows // tile - 1
+    return pl.pallas_call(
+        token_back_kernel,
+        grid=(rows // tile,),
+        in_specs=[row] * 4
+        + [once((width, width))] * 3
+        + [
+            once((1, width)),
+            pl.BlockSpec((slots, tile), lambda r: (0, r)),
+            pl.BlockSpec((1, slots, width), lambda r: (r // own, 0, 0)),
+        ],
+        out_specs=[row, pl.BlockSpec((2, width), lambda r: (0, 0))],
+        out_shape=[jax.ShapeDtypeStruct((rows, width), BF), jax.ShapeDtypeStruct((2, width), F32)],
+        cost_estimate=pl.CostEstimate(flops=6 * rows * width * width, bytes_accessed=16 * rows * width, transcendentals=0),
+        name="token_back",
+    )(tok, *grads, *weights, gain.reshape(1, width), pick, rows_m)
+
+
+def exchange_out_kernel(
+    sizes, gq_ref, gk_ref, gv_ref, go_ref, grad_ref, vec_ref, w_ref, tok_ref, vec_out,
+    buf1, sum1, buf2, sum2, buf3, sum3, buf4, vec_buf, vec_sum,
+    tok_send, tok_recv, send1, recv1, send2, recv2, send3, recv3, send4, recv4, vec_send, vec_recv, local_sem,
+):
+    n_seq, n_ten, half, rows = sizes
+    dp, sx, t = lax.axis_index("dp"), lax.axis_index("seq"), lax.axis_index("tensor")
+    y, c = dp // 2, dp % 2
+    me = sx * n_ten + t
+    group = n_seq * n_ten
+    others = []
+    for i in range(1, group):
+        g = (me + i) % group
+        others.append((g // n_ten, g % n_ten))
+    y_peer, c_peer, x_peer = {"dp": (dp + 2) % 4}, {"dp": 2 * y + 1 - c}, {"seq": 1 - sx}
+    z_peers = [{"tensor": (t + j) % n_ten} for j in range(1, n_ten)]
+    greet([{"seq": a, "tensor": b} for a, b in others] + [y_peer, c_peer])
+    grads = (gq_ref, gk_ref, gv_ref, go_ref)
+    count = len(grads)
+    height = gq_ref.shape[0]
+    hw = height // n_ten
+
+    def columns(b_y, b_c, b_x):
+        return pl.ds(pl.multiple_of((b_y * 4 + b_c * 2 + b_x) * LANES, LANES), LANES)
+
+    def add_rows(out, first, second):
+        def body(i, carry):
+            at = pl.ds(pl.multiple_of(i * hw, hw), hw)
+            out[at, :] = (first[at, :].astype(F32) + second[at, :].astype(F32)).astype(BF)
+            return carry
+
+        lax.fori_loop(0, height // hw, body, 0)
+
+    stage1 = []
+    for a in range(count):
+        stage1.append(
+            [
+                remote(
+                    grads[a].at[:, columns(b_y, 1 - c, b_x)], buf1.at[a, b_y, b_x],
+                    send1.at[a, 2 * b_y + b_x], recv1.at[a, 2 * b_y + b_x], c_peer,
+                )
+                for b_y in range(2)
+                for b_x in range(2)
+            ]
+        )
+    for copies in stage1:
+        start_all(copies)
+
+    vec_hops = []
+    hops = [c_peer, x_peer, y_peer]
+    vec_sum[0] = vec_ref[...]
+    for i, peer in enumerate(hops):
+        vec_hops.append([remote(vec_sum.at[i], vec_buf.at[i], vec_send.at[i], vec_recv.at[i], peer)])
+    vec_hops.append(
+        [
+            remote(vec_sum.at[3], vec_buf.at[3 + j], vec_send.at[3 + j], vec_recv.at[3 + j], peer)
+            for j, peer in enumerate(z_peers)
+        ]
+    )
+    start_all(vec_hops[0])
+
+    tokens = []
+    for i, (a, b) in enumerate(others):
+        tokens.append(
+            remote(
+                grad_ref.at[pl.ds(pl.multiple_of((a * n_ten + b) * rows, rows), rows), :],
+                tok_ref.at[sx * half + t],
+                tok_send.at[i], tok_recv.at[i], {"seq": a, "tensor": b},
+            )
+        )
+    tokens.append(
+        remote(
+            grad_ref.at[pl.ds(pl.multiple_of((group + 1 - sx) * rows, rows), rows), :],
+            tok_ref.at[sx * half + n_ten],
+            tok_send.at[group - 1], tok_recv.at[group - 1], x_peer,
+        )
+    )
+    start_all(tokens)
+    local = [
+        pltpu.make_async_copy(
+            grad_ref.at[pl.ds(pl.multiple_of(me * rows, rows), rows), :], tok_ref.at[sx * half + t], local_sem.at[0]
+        ),
+        pltpu.make_async_copy(
+            grad_ref.at[pl.ds(pl.multiple_of((group + sx) * rows, rows), rows), :],
+            tok_ref.at[sx * half + n_ten],
+            local_sem.at[1],
+        ),
+    ]
+    start_all(local)
+
+    stage2 = []
+    for a in range(count):
+        for copy in stage1[a]:
+            copy.wait_recv()
+        for b_y in range(2):
+            for b_x in range(2):
+                add_rows(sum1.at[a, b_y, b_x], grads[a].at[:, columns(b_y, c, b_x)], buf1.at[a, b_y, b_x])
+        copies = []
+        for b in range(2):
+            src, peer = (sum1.at[a, b, 1 - sx], x_peer) if a % 2 == 0 else (sum1.at[a, 1 - y, b], y_peer)
+            copies.append(remote(src, buf2.at[a, b], send2.at[a, b], recv2.at[a, b], peer))
+        start_all(copies)
+        stage2.append(copies)
+    vec_hops[0][0].wait_recv()
+    vec_sum[1] = vec_sum[0] + vec_buf[0]
+    start_all(vec_hops[1])
+    stage3 = []
+    for a in range(count):
+        for copy in stage2[a]:
+            copy.wait_recv()
+        for b in range(2):
+            own = sum1.at[a, b, sx] if a % 2 == 0 else sum1.at[a, y, b]
+            add_rows(sum2.at[a, b], own, buf2.at[a, b])
+        src, peer = (sum2.at[a, 1 - y], y_peer) if a % 2 == 0 else (sum2.at[a, 1 - sx], x_peer)
+        copy = remote(src, buf3.at[a], send3.at[a], recv3.at[a], peer)
+        copy.start()
+        stage3.append(copy)
+    vec_hops[1][0].wait_recv()
+    vec_sum[2] = vec_sum[1] + vec_buf[1]
+    start_all(vec_hops[2])
+    stage4 = []
+    for a in range(count):
+        stage3[a].wait_recv()
+        add_rows(sum3.at[a], sum2.at[a, y] if a % 2 == 0 else sum2.at[a, sx], buf3.at[a])
+        copies = []
+        for j, peer in enumerate(z_peers):
+            to = (t + 1 + j) % n_ten
+            src = sum3.at[a, pl.ds(pl.multiple_of(to * hw, hw), hw), :]
+            copies.append(remote(src, buf4.at[a, j], send4.at[a, j], recv4.at[a, j], peer))
+        start_all(copies)
+        stage4.append(copies)
+    vec_hops[2][0].wait_recv()
+    vec_sum[3] = vec_sum[2] + vec_buf[2]
+    start_all(vec_hops[3])
+    for a in range(count):
+        total = sum3[a, pl.ds(pl.multiple_of(t * hw, hw), hw), :].astype(F32)
+        for j, copy in enumerate(stage4[a]):
+            copy.wait_recv()
+            total = total + buf4[a, j].astype(F32)
+        w_ref[a] = total
+    total = vec_sum[3]
+    for j, copy in enumerate(vec_hops[3]):
+        copy.wait_recv()
+        total = total + vec_buf[3 + j]
+    vec_out[...] = total
+    for copies in stage1 + stage2 + stage4 + [stage3] + vec_hops:
+        for copy in copies:
+            copy.wait_send()
+    wait_all(local)
+    wait_all(tokens)
+
+
+def exchange_out(grads, grad_tok, vectors, n_seq, n_ten, half, rows):
+    height, width = grads[0].shape
+    hw, count, group = height // n_ten, len(grads), n_seq * n_ten
+    vmem = pl.BlockSpec(memory_space=pltpu.VMEM)
+    dma = pltpu.SemaphoreType.DMA
+    hops = 3 + n_ten - 1
+    return pl.pallas_call(
+        functools.partial(exchange_out_kernel, (n_seq, n_ten, half, rows)),
+        in_specs=[vmem] * 6,
+        out_specs=[vmem, any_spec(), vmem],
+        out_shape=[
+            jax.ShapeDtypeStruct((count, hw, LANES), F32),
+            jax.ShapeDtypeStruct((n_seq * half, rows, width), BF),
+            jax.ShapeDtypeStruct(vectors.shape, F32),
+        ],
+        scratch_shapes=[
+            pltpu.VMEM((count, 2, 2, height, LANES), BF),
+            pltpu.VMEM((count, 2, 2, height, LANES), BF),
+            pltpu.VMEM((count, 2, height, LANES), BF),
+            pltpu.VMEM((count, 2, height, LANES), BF),
+            pltpu.VMEM((count, height, LANES), BF),
+            pltpu.VMEM((count, height, LANES), BF),
+            pltpu.VMEM((count, n_ten - 1, hw, LANES), BF),
+            pltpu.VMEM((hops,) + vectors.shape, F32),
+            pltpu.VMEM((4,) + vectors.shape, F32),
+            dma((group,)), dma((group,)),
+            dma((count, 4)), dma((count, 4)),
+            dma((count, 2)), dma((count, 2)),
+            dma((count,)), dma((count,)),
+            dma((count, n_ten - 1)), dma((count, n_ten - 1)),
+            dma((hops,)), dma((hops,)),
+            dma((2,)),
+        ],
+        compiler_params=pltpu.CompilerParams(collective_id=4, has_side_effects=True),
+        name="exchange_out",
+    )(*grads, grad_tok, vectors)
+
+
+def rotary_lanes(cosine, sine):
     reps = LANES // HEAD_DIM
-    return (
-        jnp.concatenate([cosine, cosine] * reps, axis=1),
-        jnp.concatenate([-sine, sine] * reps, axis=1),
-    )
+    return jnp.concatenate([cosine, cosine] * reps, axis=1), jnp.concatenate([-sine, sine] * reps, axis=1)
+
+
+def position_tables(length):
+    half_dim = HEAD_DIM // 2
+    inv_freq = np.float32(10000.0) ** (-np.arange(half_dim, dtype=np.float32) * np.float32(2.0 / HEAD_DIM))
+    angles = (np.arange(length, dtype=np.float32)[:, None] * inv_freq[None, :]).astype(np.float64)
+    cosine, sine = np.cos(angles).astype(np.float32), np.sin(angles).astype(np.float32)
+    reps = LANES // HEAD_DIM
+    return np.concatenate([cosine, cosine] * reps, axis=1), np.concatenate([-sine, sine] * reps, axis=1)
 
 
 def window_shards(
@@ -836,122 +1416,78 @@
     hw = w_query.shape[1]
     slots = masked_rows.shape[1]
     part = slots // n_ten
-    units = w_down.shape[0] // (n_dp * n_seq)
-
-    cut = lambda w, axis: lax.dynamic_slice_in_dim(w, shard_index * units, units, axis)
-    everywhere = ("dp", "seq", "tensor")
-    gate_up = lax.all_gather(jnp.concatenate([cut(w_gate, 1), cut(w_up, 1)], axis=1), everywhere, axis=0, tiled=False)
-    down = lax.all_gather(cut(w_down, 0), everywhere, axis=0, tiled=False)
-
-    both_tok, all_q, all_k, all_v, all_out = exchange_in(
-        jnp.swapaxes(tokens, 0, 1), w_query, w_key, w_value, w_out, n_dp, n_seq, n_ten
-    )
 
     live = jnp.arange(windows) < window_counts[0]
     valid = (masked_rows < length) & live[:, None]
-    total = lax.psum(jnp.sum(valid.astype(jnp.int32)), "dp")
-    loss_weight = LOSS_SCALE / total.astype(F32)
+    count = jnp.full((8, LANES), jnp.sum(valid.astype(jnp.int32)))
+    both_tok, all_q, all_k, all_v, all_out, counts = exchange_in(
+        jnp.swapaxes(tokens, 0, 1), w_query, w_key, w_value, w_out, count, n_dp, n_seq, n_ten
+    )
+    loss_weight = LOSS_SCALE / jnp.sum(counts[:, 0, 0]).astype(F32)
     first_window = seq_index * half
     my_rows = lax.dynamic_slice_in_dim(masked_rows, first_window, half, 0)
     my_valid = lax.dynamic_slice_in_dim(valid, first_window, half, 0)
     cot = lax.dynamic_slice_in_dim(out_grad, first_window, half, 0).astype(F32) * loss_weight
     cot = jnp.where(my_valid[:, :, None], cot, 0.0)
-    cot_low = cot.astype(BF)
     own_rows = lax.dynamic_index_in_dim(my_rows, ten_index, 0, keepdims=False)
     own_valid = lax.dynamic_index_in_dim(my_valid, ten_index, 0, keepdims=False)
-    own_cot = lax.dynamic_index_in_dim(cot, ten_index, 0, keepdims=False)
-    left_rows, left_valid, left_cot = my_rows[n_ten], my_valid[n_ten], cot[n_ten]
+    left_rows, left_valid = my_rows[n_ten], my_valid[n_ten]
     every = jnp.arange(length)
     left_every = jnp.swapaxes(every.reshape(n_seq, n_ten, rows_local), 0, 1).reshape(n_ten, share)
     my_left = lax.dynamic_index_in_dim(left_every, ten_index, 0, keepdims=False)
     left_every = left_every.reshape(length)
     own_pick = ((own_rows[:, None] == every[None, :]) & own_valid[:, None]).astype(BF)
     left_pick = ((left_rows[:, None] == left_every[None, :]) & left_valid[:, None]).astype(BF)
-    part_pick = ((left_rows[:, None] == my_left[None, :]) & left_valid[:, None]).astype(BF)
-
-    own_tables = rotary_lanes(every) + rotary_lanes(own_rows)
-    left_tables = rotary_lanes(left_every) + rotary_lanes(left_rows)
-    part_tables = rotary_lanes(my_left)
-    cos, sin = [jnp.concatenate([a, b], axis=0) for a, b in zip(own_tables[:2], part_tables, strict=True)]
-
-    def norm(x, gain, bias):
-        normed, inv_std = layer_stats(x)
-        return normed, inv_std, (normed * gain + bias).astype(BF)
-
-    pick_rows = lambda pick, x: dot_n(pick, x).astype(BF)
-    left_tok_m = lax.all_gather(pick_rows(part_pick, both_tok[length:]), "tensor", axis=0, tiled=False)
-    _, _, first = norm(both_tok.astype(F32), norm1_gain, norm1_bias)
-    q, k, v = qkv_project(first, all_q, all_k, all_v, cos, sin)
+    part_match = (left_rows[:, None] == my_left[None, :]) & left_valid[:, None]
+    part_pick = part_match.astype(BF)
+    my_cot = jnp.concatenate(
+        [
+            lax.dynamic_index_in_dim(cot, ten_index, 0, keepdims=False),
+            jnp.where(jnp.any(part_match, axis=1, keepdims=True), cot[n_ten], 0.0),
+        ],
+        axis=0,
+    )
+
+    tables = [jnp.asarray(x) for x in position_tables(length)]
+    by_block = [x.reshape(n_seq, n_ten, rows_local, LANES) for x in tables]
+    part_tables = [lax.dynamic_index_in_dim(x, ten_index, 1, keepdims=False).reshape(share, LANES) for x in by_block]
+    left_tables = [jnp.swapaxes(x, 0, 1).reshape(length, LANES) for x in by_block]
+    own_tables = tables + list(rotary_lanes(*rotary_tables(own_rows)))
+    left_tables = left_tables + list(rotary_lanes(*rotary_tables(left_rows)))
+
+    first, q, k, v = norm_qkv(both_tok, norm1_gain, norm1_bias, all_q, all_k, all_v, tables, part_tables)
     own_att, left_q, left_k, left_v = attend_swap(q, k, v, length, n_ten)
-    left_att = attend(left_q, left_k, left_v)
-    left_att_part = lax.all_to_all(left_att.reshape(n_ten, share, hw), "tensor", 0, 0, tiled=True)
-    left_att_part = jnp.swapaxes(left_att_part, 0, 1).reshape(share, width)
-
-    own_att_m = pick_rows(own_pick, own_att)
-    left_att_m = pick_rows(left_pick, left_att)
-    own_res_m = pick_rows(own_pick, both_tok[:length]).astype(F32) + dot_n(own_att_m, all_out)
-    own_normed2, own_inv2, own_second = norm(own_res_m, norm2_gain, norm2_bias)
-    sent = lax.all_gather(jnp.concatenate([own_second, left_att_m], axis=1), "tensor", axis=0, tiled=False)
-    left_att_full = jnp.swapaxes(sent[:, :, width:], 0, 1).reshape(slots, width)
-    left_tok_full = jnp.sum(left_tok_m.astype(F32), axis=0)
-    left_res_m = left_tok_full + dot_n(left_att_full, all_out)
-    left_normed2, left_inv2, left_second = norm(left_res_m, norm2_gain, norm2_bias)
-    second = jnp.concatenate([sent[:, :, :width].reshape(n_ten * slots, width), left_second], axis=0)
-
+    left_att_part = attend_left(left_q, left_k, left_v, n_ten)
+    out_both, att_m, gr2, gatt, grad_norm2, second_m = feed_forward(
+        both_tok, own_att, left_att_part, all_out, norm2_gain, norm2_bias, own_pick, part_pick, my_cot,
+        w_gate, w_up, w_down, n_ten,
+    )
+    sent = lax.all_gather(second_m, "tensor", axis=0, tiled=False)
+
+    second = jnp.concatenate(
+        [sent[:, :slots].reshape(n_ten * slots, width), jnp.sum(sent[:, slots:].astype(F32), axis=0).astype(BF)], axis=0
+    )
     gate = dot_n(second, w_gate)
     up = dot_n(second, w_up)
-    down_in = cot_low.reshape(half * slots, width)
+    down_in = cot.astype(BF).reshape(half * slots, width)
     grad_hidden = dot_t(down_in, w_down)
     sig = jax.nn.sigmoid(gate)
     silu = gate * sig
     hidden_m = (silu * up).astype(BF)
     grad_gate = (grad_hidden * up * sig * (1.0 + gate * (1.0 - sig))).astype(BF)
     grad_up = (grad_hidden * silu).astype(BF)
-    grad_second = (dot_t(grad_gate, w_gate) + dot_t(grad_up, w_up)).astype(BF)
-    grad_second = jnp.concatenate(
-        [
-            grad_second[: n_ten * slots].reshape(n_ten, slots, width),
-            grad_second[n_ten * slots :].reshape(n_ten, part, width),
-        ],
-        axis=1,
-    ).reshape(n_ten * (slots + part), width)
-    grad_second = lax.psum_scatter(grad_second, "tensor", scatter_dimension=0, tiled=True)
-    left_grad_second = lax.all_gather(grad_second[slots:], "tensor", axis=0, tiled=True).astype(F32)
-    own_grad_second = grad_second[:slots].astype(F32)
-    grad_w_ffn = jnp.concatenate(
-        [t_dot(second, grad_gate).astype(BF), t_dot(second, grad_up).astype(BF), t_dot(down_in, hidden_m).astype(BF)], axis=1
-    )
-
-    mine = lambda x: lax.dynamic_slice_in_dim(x, ten_index * part, part, 0)
-    grad_norm2_gain = jnp.sum(own_grad_second * own_normed2, axis=0) + jnp.sum(
-        mine(left_grad_second * left_normed2), axis=0
-    )
-    grad_norm2_bias = jnp.sum(own_grad_second, axis=0) + jnp.sum(mine(left_grad_second), axis=0)
-    own_gr2 = (own_cot + norm_back(own_grad_second, own_normed2, own_inv2, norm2_gain)).astype(BF)
-    left_gr2 = (left_cot + norm_back(left_grad_second, left_normed2, left_inv2, norm2_gain)).astype(BF)
-
-    own_gatt = dot_t(own_gr2, all_out).astype(BF)
-    left_gatt = dot_t(left_gr2, w_out).astype(BF)
-    on_tensor = (jnp.arange(n_ten) == ten_index).astype(BF)
-    left_att_wide = (left_att_m[:, None, :] * on_tensor[None, :, None]).reshape(slots, width)
-    grad_w_out = t_dot(
-        jnp.concatenate([own_att_m, left_att_wide], axis=0), jnp.concatenate([own_gr2, left_gr2], axis=0)
-    ).astype(BF)
-    left_back = attend_back(left_q, left_gatt, left_k, left_v, left_pick, left_tables)
-    dq, dk, dv = back_swap(q, own_gatt, k, v, own_pick, own_tables, left_back, n_ten)
-    grad_first = dot_t(dq, all_q) + dot_t(dk, all_k) + dot_t(dv, all_v)
-    grad_w_query, grad_w_key, grad_w_value = [t_dot(first, d).astype(BF) for d in (dq, dk, dv)]
-
-    normed1, inv_std1 = layer_stats(both_tok.astype(F32))
-    grad_norm1_gain = jnp.sum(grad_first * normed1, axis=0)
-    grad_norm1_bias = jnp.sum(grad_first, axis=0)
-    gr2_dense = jnp.concatenate([t_dot(own_pick, own_gr2), t_dot(part_pick, left_gr2)], axis=0)
-    grad_both = (gr2_dense + norm_back(grad_first, normed1, inv_std1, norm1_gain)).astype(BF)
-
-    att = jnp.concatenate([own_att, left_att_part], axis=0)
-    residual2 = both_tok.astype(F32) + dot_n(att, all_out)
-    _, _, second_low = norm(residual2, norm2_gain, norm2_bias)
-    out_both = feed_forward(second_low, residual2, gate_up, down)
+    grad_w_ffn = [
+        t_dot(second, grad_gate).astype(BF), t_dot(second, grad_up).astype(BF), t_dot(down_in, hidden_m).astype(BF)
+    ]
+
+    grad_w_out = t_dot(att_m, gr2).astype(BF)
+    left_back = back_left(left_q, gatt[slots:], left_k, left_v, left_pick, left_tables, n_ten)
+    dq, dk, dv = back_swap(q, gatt[:slots], k, v, own_pick, own_tables, left_back, n_ten)
+    grad_w_attn = [t_dot(d, first).astype(BF) for d in (dq, dk, dv)] + [grad_w_out]
+    grad_both, grad_norm1 = token_back(
+        both_tok, (dq, dk, dv), (all_q, all_k, all_v), norm1_gain,
+        jnp.concatenate([own_pick, part_pick], axis=1), gr2.reshape(2, slots, width),
+    )
 
     def send_back(x):
         own = lax.all_to_all(
@@ -962,39 +1498,31 @@
         return jnp.swapaxes(both, 0, 1)
 
     output = send_back(out_both)
-    grad_tokens = send_back(grad_both).astype(F32)
-
-    def summed(x, dim):
-        return lax.psum_scatter(x, ("dp", "seq"), scatter_dimension=dim, tiled=True)
-
-    gw_all = summed(jnp.concatenate([grad_w_query, grad_w_key, grad_w_value], axis=1), 0)
-    gw_q, gw_k, gw_v = [
-        lax.psum_scatter(gw_all[:, i * width : (i + 1) * width], "tensor", scatter_dimension=1, tiled=True).astype(F32)
-        for i in range(3)
-    ]
-    gw_out = lax.psum_scatter(summed(grad_w_out, 1), "tensor", scatter_dimension=0, tiled=True).astype(F32)
-    gw_ffn = summed(grad_w_ffn, 0).astype(F32)
-    hidden_units = w_gate.shape[1]
-    gw_gate, gw_up = gw_ffn[:, :hidden_units], gw_ffn[:, hidden_units : 2 * hidden_units]
-    gw_down = gw_ffn[:, 2 * hidden_units :].T
-    vectors = [
-        lax.psum_scatter(v, ("dp", "seq", "tensor"), scatter_dimension=0, tiled=True)
-        for v in (grad_norm1_gain, grad_norm1_bias, grad_norm2_gain, grad_norm2_bias)
+    vectors = jnp.concatenate(
+        [grad_norm1, grad_norm2, jnp.zeros((4, width), F32)], axis=0
+    )
+    gw_attn, grad_tokens, vectors = exchange_out(grad_w_attn, grad_both, vectors, n_seq, n_ten, half, rows_local)
+    grad_tokens = jnp.swapaxes(grad_tokens, 0, 1).astype(F32)
+    small = width // (n_dp * n_seq * n_ten)
+    vectors = lax.dynamic_slice_in_dim(vectors, (shard_index * n_ten + ten_index) * small, small, 1)
+
+    gw_gate, gw_up, gw_down = [
+        lax.psum_scatter(x, ("dp", "seq"), scatter_dimension=0, tiled=True).astype(F32) for x in grad_w_ffn
     ]
     return (
         output,
         grad_tokens,
         vectors[0],
         vectors[1],
-        gw_q,
-        gw_k,
-        gw_v,
-        gw_out,
+        gw_attn[0].T,
+        gw_attn[1].T,
+        gw_attn[2].T,
+        gw_attn[3],
         vectors[2],
         vectors[3],
         gw_gate,
         gw_up,
-        gw_down,
+        gw_down.T,
     )
 
 

time: 761 us -> 649 us (0.85)
  Pallas kernels: 255 us -> 476 us
  blocking collectives: 123 us -> 0 us
  other arithmetic: 87.3 us -> 24.7 us
  waiting for transfers between devices: 102 us -> 56.4 us
  local copies, waits for them, and re-layouts: 62.7 us -> 18.3 us
  matrix products: 67.9 us -> 42.4 us
  starting transfers between devices: 33.1 us -> 9.47 us
    pallas_call x4 -> x6, Pallas kernels: 82.8 us -> 313 us  [the longest x1 146 us: feed_forward(): pl.pallas_call(functools.partial(feed_kernel, n_ten), grid=(n_ten * units...]
    unnamed x1 -> x0, blocking collectives: 73.3 us -> none
    reduce_scatter x5 -> x3, waiting for transfers between devices: 38 us -> 0.01 us  [window_shards(): lax.psum_scatter(x, ('dp', 'seq'), scatter_dimension=0, tiled=True)]
    unnamed x146 -> x46, local copies, waits for them, and re-layouts: 44.9 us -> 7.02 us
    concatenate x7 -> x3, other arithmetic: 32.4 us -> 2.67 us  [the longest x1 1.21 us: window_shards(): jnp.concatenate([lax.dynamic_index_in_dim(cot, ten_index, 0, keepdims=Fal...]
    all_to_all x1 -> x0, blocking collectives: 29.3 us -> none  [window_shards(): lax.all_to_all(left_att.reshape(n_ten, share, hw), 'tensor', 0, 0, tiled=...]
    all_to_all x2 -> x1, starting transfers between devices: 25 us -> 5.39 us  [send_back(): lax.all_to_all(x[:length].reshape(n_seq * n_ten, rows_local, width), ('se...]
    dot_general x8 -> x1, matrix products: 22.2 us -> 3.72 us  [dot_t(): lax.dot_general(a, b, (((1,), (1,)), ((), ())), preferred_element_type=F32)]
  transfers between devices with their start and end apart: 16 -> 6, of which waited for: 6 -> 1; matrix products, arithmetic and copies ran while one was open for 24% -> 9% of each run, Pallas kernels for 24% -> 27%
where the time goes in v3:
time: 649 us; the launch traced here: 643 us
  Pallas kernels  476 us (73%)
  waiting for transfers between devices  56.4 us (9%)
  matrix products  42.4 us (7%)
  other arithmetic  24.7 us (4%)
  local copies, waits for them, and re-layouts  18.3 us (3%)
  between operations  16.1 us (2%)
  starting transfers between devices  9.47 us (1%)
    pallas_call x1, Pallas kernels, feed_forward(): pl.pallas_call(functools.partial(feed_kernel, n_ten), grid=(n_ten * units...  146 us
    pallas_call x1, Pallas kernels, exchange_out(): pl.pallas_call(functools.partial(exchange_out_kernel, (n_seq, n_ten, half...  100 us
    pallas_call x1, Pallas kernels, exchange_in(): pl.pallas_call(functools.partial(exchange_in_kernel, (n_seq, n_ten, windo...  75.2 us
    all_gather x1, waiting for transfers between devices, window_shards(): sent = lax.all_gather(second_m, 'tensor', axis=0, tiled=False)  56.4 us
    pallas_call x1, Pallas kernels, attend_swap(): pl.pallas_call(functools.partial(attend_swap_kernel, n_ten, length), grid...  50.6 us
    pallas_call x1, Pallas kernels, back_swap(): pl.pallas_call(functools.partial(back_swap_kernel, n_ten), grid=(width //...  36.5 us
    dot_general x7, matrix products, t_dot(): lax.dot_general(a, b, (((0,), (0,)), ((), ())), preferred_element_type=F32)  34.9 us
    pallas_call x1, Pallas kernels, attend_left(): pl.pallas_call(functools.partial(attend_left_kernel, n_ten), grid=(n_ten,...  17.8 us
  transfers between devices with their start and end apart: 6, of which 1 were waited for; matrix products, arithmetic and copies ran while one was open for 9% of the time, Pallas kernels for 27%

profile of v3, /device:TPU:0, one launch (start us, length us, event | category | flops | bytes accessed | tf_op | source)
XLA Modules:
  0.0 642.9 jit_solution(573178249207100637)
XLA Ops:
  8.1 1.5 convert_reduce_fusion
  9.6 0.8 constant_dynamic-slice_fusion.2
  10.5 1.2 broadcast_in_dim.44.count_ref
  11.7 75.2 %exchange_in.1 = (bf16[1280,1024]{1,0:T(8,128)(2,1)}, bf16[1024,1024]{1,0:T(8,128)(2,1)}, bf16[1024,1024]{1,0:T(8,128)(2,1)}, bf16[1024,1024]{1,0:T(8,128)(2,1)}...) custom-call(bf16[10,128,1024]{2,1,0:T(8,128)(2,1)} %bitcast.77, bf16[1024,256]{1,0:T(8,128)(2,1)} %wq_ref.1, ...), custom_call_target="tpu_custom_call" | custom-call | tf_op jit(solution)/shard_map/exchange_in/pallas_call | solution.py:481
  86.9 1.4 slice_reduce_fusion.1
  88.9 1.7 fusion.6
  91.6 1.2 pad_maximum_fusion.2.cot_ref
  92.8 1.7 constant_dynamic-slice_fusion.4
  94.4 14.8 %norm_qkv.1 = (bf16[1280,1024]{1,0:T(8,128)(2,1)}, bf16[1280,1024]{1,0:T(8,128)(2,1)}, bf16[1280,1024]{1,0:T(8,128)(2,1)}, bf16[1280,1024]{1,0:T(8,128)(2,1)}) custom-call(bf16[1280,1024]{1,0:T(8,128)(2,1)} %get-tuple-element.44.x_ref.tok_ref, f32[1,1024]{1,0:T(1,128)} %bitcast.99, f32[1,1024]{1,0:T(1,128)} %bitcast.96, ...), custom_call_target="tpu_custom_call" | custom-call | flops 8053063680 | bytes 20971520 | tf_op jit(solution)/shard_map/norm_qkv/pallas_call | solution.py:532
  109.3 50.6 %attend_swap.1 = (bf16[1024,1024]{1,0:T(8,128)(2,1)}, bf16[1024,256]{1,0:T(8,128)(2,1)}, bf16[1024,256]{1,0:T(8,128)(2,1)}, bf16[1024,256]{1,0:T(8,128)(2,1)}) custom-call(bf16[1280,1024]{1,0:T(8,128)(2,1)} %get-tuple-element.48.q_ref.q_all, bf16[1280,1024]{1,0:T(8,128)(2,1)} %get-tuple-element.49.k_ref.k_all, ...), custom_call_target="tpu_custom_call" | custom-call | flops 17179869184 | bytes 8388608 | tf_op jit(solution)/shard_map/attend_swap/pallas_call | solution.py:664
  159.9 17.8 %attend_left.1.left_ref = bf16[256,1024]{1,0:T(8,128)(2,1)} custom-call(bf16[1024,256]{1,0:T(8,128)(2,1)} %get-tuple-element.52.q_ref, bf16[1024,256]{1,0:T(8,128)(2,1)} %get-tuple-element.53.k_ref, bf16[1024,256]{1,0:T(8,128)(2,1)} %get-tuple-element.54.v_ref), custom_call_target="tpu_custom_call" | custom-call | flops 4294967296 | bytes 2097152 | tf_op jit(solution)/shard_map/attend_left/pallas_call | solution.py:608
  177.7 1.1 fusion.3
  178.8 146.2 %feed_forward.1 = (bf16[1280,1024]{1,0:T(8,128)(2,1)}, bf16[320,1024]{1,0:T(8,128)(2,1)}, bf16[320,1024]{1,0:T(8,128)(2,1)}, bf16[320,1024]{1,0:T(8,128)(2,1)}, ...) custom-call(bf16[1280,1024]{1,0:T(8,128)(2,1)} %get-tuple-element.44, ...), custom_call_target="tpu_custom_call" | custom-call | flops 42949672960 | bytes 25165824 | tf_op jit(solution)/shard_map/feed_forward/pallas_call | solution.py:1112
  325.3 56.4 %all-gather.3.cloned.1.call-done = bf16[1280,1024]{1,0:T(8,128)(2,1)} async-done(((bf16[320,1024]{1,0:T(8,128)(2,1)}), bf16[1280,1024]{1,0:T(8,128)(2,1)}) %all-gather.3.cloned.1.call-update) | async-done | bytes 2621456 | tf_op jit(solution)/shard_map/all_gather | solution.py:1465
  381.6 2.1 fusion.18
  383.8 1.9 fusion.17
  385.9 1.9 fusion.16
  387.8 1.7 copy-done.18
  389.5 3.8 convolution_convert_fusion.4
  393.4 0.8 slice.59
  394.2 3.5 all-to-all-start.1
  398.4 0.9 pad_maximum_fusion.6
  399.3 0.9 pad_maximum_fusion.4
  400.2 2.0 fusion.19
  402.2 3.7 fusion.20
  405.9 1.7 copy-done.16
  407.6 3.9 convolution_convert_fusion.5
  411.5 17.3 %back_left.1 = (bf16[1024,256]{1,0:T(8,128)(2,1)}, bf16[1024,256]{1,0:T(8,128)(2,1)}, bf16[1024,256]{1,0:T(8,128)(2,1)}) custom-call(bf16[1024,256]{1,0:T(8,128)(2,1)} %get-tuple-element.52.q_ref, bf16[160,1024]{1,0:T(8,128)(2,1)} %get-tuple-element.96.g_ref, bf16[1024,256]{1,0:T(8,128)(2,1)} %get-tuple-element.53.k_ref, ...), custom_call_target="tpu_custom_call" | custom-call | flops 1006632960 | bytes 3145728 | tf_op jit(solution)/shard_map/back_left/pallas_call | solution.py:762
  428.8 0.8 pad_maximum_fusion.3.pick_ref
  429.6 36.5 %back_swap.1 = (bf16[1280,1024]{1,0:T(8,128)(2,1)}, bf16[1280,1024]{1,0:T(8,128)(2,1)}, bf16[1280,1024]{1,0:T(8,128)(2,1)}) custom-call(bf16[1280,1024]{1,0:T(8,128)(2,1)} %get-tuple-element.48.q_ref.q_all, bf16[160,1024]{1,0:T(8,128)(2,1)} %get-tuple-element.97.g_ref, bf16[1280,1024]{1,0:T(8,128)(2,1)} %get-tuple-element.49.k_ref.k_all, ...), custom_call_target="tpu_custom_call" | custom-call | flops 4026531840 | bytes 12582912 | tf_op jit(solution)/shard_map/back_swap/pallas_call | solution.py:832
  466.1 16.9 %token_back.1 = (bf16[1280,1024]{1,0:T(8,128)(2,1)}, f32[2,1024]{1,0:T(2,128)}) custom-call(bf16[1280,1024]{1,0:T(8,128)(2,1)} %get-tuple-element.44.x_ref.tok_ref, bf16[1280,1024]{1,0:T(8,128)(2,1)} %get-tuple-element.62.dq_ref, bf16[1280,1024]{1,0:T(8,128)(2,1)} %get-tuple-element.64.dk_ref, bf16[1280,1024]{1,0:T(8,128)(2,1)} %get-tuple-element.65.dv_ref, ...), custom_call_target="tpu_custom_call" | custom-call | flops 8053063680 | bytes 20971520 | tf_op jit(solution)/shard_map/token_back/pallas_call | solution.py:1171
  483.0 6.8 %convolution_convert_fusion.gv_ref = bf16[1024,1024]{1,0:T(8,128)(2,1)} fusion(bf16[1280,1024]{1,0:T(8,128)(2,1)} %get-tuple-element.65.dv_ref, bf16[1280,1024]{1,0:T(8,128)(2,1)} %get-tuple-element.63), kind=kOutput, calls=%fused_computation.8 | convolution fusion | flops 2685403136 | bytes 7340032 | tf_op jit(solution)/shard_map/dot_general | solution.py:326
  489.8 1.5 slice.58
  491.4 5.4 all-to-all-start
  497.1 8.1 %convolution_convert_fusion.6 = bf16[1024,1024]{1,0:T(8,128)(2,1)} fusion(f32[800,1024]{1,0:T(8,128)} %copy-done.18, f32[800,1024]{1,0:T(8,128)} %copy-done.16, f32[800,1024]{1,0:T(8,128)} %copy-done.17, bf16[160,1024]{1,0:T(8,128)(2,1)S(1)} %copy-done.8, bf16[640,1024]{1,0:T(8,128)(2,1)} %bitcast.85), kind=kOutput, calls=%fused_computation.14 | convolution fusion | flops 1690238976 | bytes 13565952 | tf_op jit(solution)/shard_map/dot_general | solution.py:326
  506.0 4.1 convolution_convert_fusion.3.go_ref
  510.1 4.1 convolution_convert_fusion.1.gk_ref
  514.2 4.1 convolution_convert_fusion.2.gq_ref
  518.3 100.3 %exchange_out.1 = (f32[4,256,128]{2,1,0:T(8,128)}, bf16[10,128,1024]{2,1,0:T(8,128)(2,1)}, f32[8,1024]{1,0:T(8,128)}) custom-call(bf16[1024,1024]{1,0:T(8,128)(2,1)} %convolution_convert_fusion.2.gq_ref, bf16[1024,1024]{1,0:T(8,128)(2,1)} %convolution_convert_fusion.1.gk_ref, bf16[1024,1024]{1,0:T(8,128)(2,1)} %convolution_convert_fusion.gv_ref, ...), custom_call_target="tpu_custom_call" | custom-call | tf_op jit(solution)/shard_map/exchange_out/pallas_call | solution.py:1346
  618.6 1.8 slice_bitcast_fusion.1
  620.4 0.8 copy.31
  621.9 0.8 copy.33
  623.9 4.8 convert_bitcast_fusion
  628.7 1.7 pad_maximum_fusion
  630.4 1.0 convert_bitcast_fusion.1
  631.4 1.0 copy.34
  632.4 1.8 convert_element_type.100
  634.2 1.8 convert_element_type.97
  (72 shorter events, 5.5 us)
Async XLA Ops:
  7.2 81.7 %copy-start.6 = (bf16[10,160,1024]{2,1,0:T(8,128)(2,1)S(1)}, bf16[10,160,1024]{2,1,0:T(8,128)(2,1)}, u32[]{:S(2)}) copy-start(bf16[10,160,1024]{2,1,0:T(8,128)(2,1)} %param.29) | copy-start | bytes 9830404
  7.2 374.4 %all-gather.3.cloned.1.call-start = ((), (), s32[]{:S(2)}) async-start(), calls=%async_computation.8 | async-start | bytes 3276800 | tf_op jit(solution)/shard_map/all_gather | solution.py:1465
  325.0 58.7 %copy-start.12 = (bf16[1024,1024]{1,0:T(8,128)(2,1)S(1)}, bf16[1024,1024]{1,0:T(8,128)(2,1)}, u32[]{:S(2)}) copy-start(bf16[1024,1024]{1,0:T(8,128)(2,1)} %wu_ref.1) | copy-start | bytes 6291460
  325.1 305.3 %reduce-scatter.8.cloned.1.call-start = ((), (), s32[]{:S(2)}) async-start(), calls=%async_computation.7 | async-start | bytes 2359296 | tf_op jit(solution)/shard_map/reduce_scatter | solution.py:1510
  383.7 1.9 copy-start.3
  383.7 22.2 %copy-start.7 = (bf16[160,1024]{1,0:T(8,128)(2,1)}, bf16[160,1024]{1,0:T(8,128)(2,1)S(1)}, u32[]{:S(2)}) copy-start(bf16[160,1024]{1,0:T(8,128)(2,1)S(1)} %get-tuple-element.95) | copy-start | bytes 983044
  383.7 2.2 copy-start.13
  385.9 1.9 copy-start.17
  385.9 3.6 copy-start.1
  387.8 1.7 copy-start.18
  389.5 3.8 copy-start
  394.2 97.2 %all-to-all-start.1 = ((bf16[2,128,1024]{2,1,0:T(8,128)(2,1)}), bf16[2,128,1024]{2,1,0:T(8,128)(2,1)S(1)}, u32[]{:S(2)}, u32[]{:S(2)}) async-start(bf16[2,128,1024]{2,1,0:T(8,128)(2,1)} %bitcast.80), calls=%async_computation.1 | async-start | bytes 1048576 | tf_op jit(solution)/shard_map/all_to_all | solution.py:1496
  397.7 234.7 %reduce-scatter.6.cloned.1.call-start = ((), (), s32[]{:S(2)}) async-start(), calls=%async_computation.6 | async-start | bytes 2359296 | tf_op jit(solution)/shard_map/reduce_scatter | solution.py:1510
  397.7 4.4 copy-start.2
  402.2 5.5 copy-start.4
  402.2 5.5 copy-start.19
  405.9 1.7 copy-start.16
  411.5 17.3 %copy-start.5 = (bf16[160,1024]{1,0:T(8,128)(2,1)S(1)}, bf16[160,1024]{1,0:T(8,128)(2,1)}, u32[]{:S(2)}) copy-start(bf16[160,1024]{1,0:T(8,128)(2,1)} %get-tuple-element.121.pick_ref) | copy-start | bytes 983044
  411.5 17.3 %copy-start.9 = (bf16[160,256]{1,0:T(8,128)(2,1)S(1)}, bf16[160,256]{1,0:T(8,128)(2,1)}, u32[]{:S(2)}) copy-start(bf16[160,256]{1,0:T(8,128)(2,1)} %get-tuple-element.109.part_pick_ref) | copy-start | bytes 245764
  491.3 5.8 copy-start.8
  491.4 137.3 %all-to-all-start = ((bf16[8,128,1024]{2,1,0:T(8,128)(2,1)}), bf16[8,128,1024]{2,1,0:T(8,128)(2,1)S(1)}, u32[]{:S(2)}, u32[]{:S(2)}) async-start(bf16[8,128,1024]{2,1,0:T(8,128)(2,1)} %bitcast.15), calls=%async_computation | async-start | bytes 4194304 | tf_op jit(solution)/shard_map/all_to_all | solution.py:1493
  496.8 8.5 %copy-start.10 = (f32[2,1024]{1,0:T(2,128)S(1)}, f32[2,1024]{1,0:T(2,128)}, u32[]{:S(2)}) copy-start(f32[2,1024]{1,0:T(2,128)} %get-tuple-element.70) | copy-start | bytes 24580
  496.8 8.5 %copy-start.11 = (f32[2,1024]{1,0:T(2,128)S(1)}, f32[2,1024]{1,0:T(2,128)}, u32[]{:S(2)}) copy-start(f32[2,1024]{1,0:T(2,128)} %get-tuple-element.69) | copy-start | bytes 24580
  496.8 137.4 %reduce-scatter.4.cloned.1.call-start = ((), (), s32[]{:S(2)}) async-start(), calls=%async_computation.5 | async-start | bytes 2359296 | tf_op jit(solution)/shard_map/reduce_scatter | solution.py:1510
  506.0 4.1 copy-start.15
  506.0 4.1 copy-start.20
  510.1 4.1 copy-start.14
Sparse Core Ops, SparseCore 0:
  325.2 56.4 all-gather.2
  393.5 39.9 reduce-scatter.7
  437.2 41.2 reduce-scatter.5
  505.4 73.1 reduce-scatter.3

commit v4 on v3

--- a/solution.py
+++ b/solution.py
@@ -312,6 +312,7 @@
 BF = jnp.bfloat16
 F32 = jnp.float32
 LANES = 128
+QUAD = 4
 
 
 def dot_t(a, b):
@@ -369,9 +370,102 @@
         copy.wait()
 
 
+def quad_place():
+    dp, sx = lax.axis_index("dp"), lax.axis_index("seq")
+    place = sx * 2 + dp % 2
+    return place, lambda to: {"dp": dp // 2 * 2 + to % 2, "seq": to // 2}
+
+
+def quad_peers():
+    place, device = quad_place()
+    return [device((place + j) % QUAD) for j in range(1, QUAD)]
+
+
+class WeightRoute:
+    def __init__(self, gathered, own, n_ten, send, recv):
+        dp, sx, t = lax.axis_index("dp"), lax.axis_index("seq"), lax.axis_index("tensor")
+        y, c = dp // 2, dp % 2
+        gate_ref, up_ref, down_ref = gathered
+        self.refs, self.own = (gate_ref, up_ref, down_ref), own
+        self.width, self.units = gate_ref.shape[0], gate_ref.shape[1] // n_ten
+        self.send, self.recv, self.c = send, recv, c
+        s_xy, s_yx = c * 4 + y * 2 + sx, c * 4 + sx * 2 + y
+        self.slices = (s_xy, s_yx, s_xy)
+        self.x_peer, self.y_peer, self.c_peer = {"seq": 1 - sx}, {"dp": (dp + 2) % 4}, {"dp": 2 * y + 1 - c}
+        side = t // 2
+        middle = jnp.minimum(t, n_ten - 1 - t)
+        mirror = lambda k: k + side * (n_ten - 1 - 2 * k)
+        self.order = [mirror(k) for k in (middle, 1 - middle, 2, 3)]
+        self.inward, self.outward = mirror(middle + 1), mirror(0)
+        self.is_middle, self.is_end = middle == 1, middle == 0
+        self.t, self.middle, self.mirror = t, middle, mirror
+
+    def shard(self, ref, k, first, count, which):
+        size, units = self.width // 8, self.units
+        rows = pl.multiple_of(first * (size if k < 2 else units // 8), 16)
+        if k < 2:
+            at = 0 if which is None else pl.multiple_of(which * units, units)
+            return ref.at[pl.ds(rows, count * size), pl.ds(at, units)]
+        at = rows if which is None else pl.multiple_of(which * units + rows, 16)
+        return ref.at[pl.ds(at, count * (units // 8)), :]
+
+    def along(self, which, to, slot, number, own=False):
+        copies = []
+        for k in range(3):
+            dst = self.shard(self.refs[k], k, self.slices[k], 1, which)
+            src = self.shard(self.own[k], k, self.slices[k], 1, None) if own else dst
+            copies.append(remote(src, dst, self.send.at[number, k], self.recv.at[slot, k], {"tensor": to}))
+        return copies
+
+    def to_in(self):
+        return self.along(self.t, self.inward, 1 + self.middle, 0, True)
+
+    def to_out(self):
+        return self.along(self.t, self.outward, 1, 1, True)
+
+    def in_far(self):
+        return self.along(self.mirror(0), self.inward, 3, 2)
+
+    def out_two(self):
+        return self.along(self.mirror(2), self.outward, 2, 3)
+
+    def out_three(self):
+        return self.along(self.mirror(3), self.outward, 3, 4)
+
+    def arrived(self, i):
+        received(self.along(self.order[i], self.inward, i, 0))
+
+    def hop(self, i, h):
+        copies = []
+        for k in range(3):
+            xy = k != 1
+            peer, first, count = (
+                (self.x_peer if xy else self.y_peer, self.slices[k], 1),
+                (self.y_peer if xy else self.x_peer, self.slices[k] // 2 * 2, 2),
+                (self.c_peer, self.c * 4, 4),
+            )[h]
+            ref = self.shard(self.refs[k], k, first, count, self.order[i])
+            copies.append(remote(ref, ref, self.send.at[2 + 3 * i + h, k], self.recv.at[1 + 3 * i + h, k], peer))
+        return copies
+
+
+def received(copies):
+    for copy in copies:
+        copy.wait_recv()
+
+
+def sent_all(copies):
+    for copy in copies:
+        copy.wait_send()
+
+
+def route_sems():
+    return [pltpu.SemaphoreType.DMA((14, 3)), pltpu.SemaphoreType.DMA((13, 3))]
+
+
 def exchange_in_kernel(
-    sizes, tok_ref, wq_ref, wk_ref, wv_ref, wo_ref, count_ref, x_ref, q_ref, k_ref, v_ref, o_ref, counts_ref,
-    tok_send, tok_recv, w_send, w_recv, count_send, count_recv, local_sem,
+    sizes, tok_ref, wq_ref, wk_ref, wv_ref, wo_ref, count_ref, rows_ref, x_ref, q_ref, k_ref, v_ref, o_ref, counts_ref,
+    peer_rows_ref, tok_send, tok_recv, w_send, w_recv, count_send, count_recv, rows_send, rows_recv, local_sem,
 ):
     n_seq, n_ten, half, rows, slices = sizes
     dp, sx, t = lax.axis_index("dp"), lax.axis_index("seq"), lax.axis_index("tensor")
@@ -384,7 +478,8 @@
         others.append((g // n_ten, g % n_ten))
     y_peer, c_peer, x_peer = {"dp": (dp + 2) % 4}, {"dp": 2 * y + 1 - c}, {"seq": 1 - sx}
     dp_peers = [{"dp": (dp + i) % 4} for i in range(1, 4)]
-    greet([{"seq": a, "tensor": b} for a, b in others] + dp_peers)
+    beside = [{"dp": 2 * y + 1 - c, "tensor": (t + j) % n_ten} for j in range(1, n_ten)]
+    greet([{"seq": a, "tensor": b} for a, b in others] + dp_peers + beside)
     counts = [
         remote(count_ref, counts_ref.at[dp], count_send.at[i], count_recv.at[i], peer) for i, peer in enumerate(dp_peers)
     ]
@@ -436,22 +531,38 @@
                 tok_send.at[i], tok_recv.at[i], {"seq": a, "tensor": b},
             )
         )
-    tokens.append(
+    shared = []
+    for i in range(n_seq):
+        src, dst = tok_ref.at[i * half + n_ten], x_ref.at[pl.ds(pl.multiple_of((group + t % 2) * rows, rows), rows), :]
+        shared.append(
+            (
+                2 * c + i == t,
+                remote(
+                    src, dst, tok_send.at[group - 1 + i], tok_recv.at[group - 1 + t % 2],
+                    {"dp": 2 * y + t // 2, "tensor": 2 * c + i},
+                ),
+                pltpu.make_async_copy(src, dst, local_sem.at[1]),
+            )
+        )
+    arriving = [
         remote(
-            tok_ref.at[(1 - sx) * half + n_ten],
-            x_ref.at[pl.ds(pl.multiple_of((group + sx) * rows, rows), rows), :],
-            tok_send.at[group - 1], tok_recv.at[group - 1], x_peer,
+            tok_ref.at[n_ten], x_ref.at[pl.ds((group + i) * rows, rows), :],
+            tok_send.at[group - 1], tok_recv.at[group - 1 + i], c_peer,
         )
-    )
+        for i in range(n_seq)
+    ]
     start_all(tokens)
+    for here, away, near in shared:
+        pl.when(here)(near.start)
+        pl.when(jnp.logical_not(here))(away.start)
+    peer_rows = [
+        remote(rows_ref.at[i * half + n_ten], peer_rows_ref.at[i], rows_send.at[i], rows_recv.at[i], c_peer)
+        for i in range(n_seq)
+    ]
+    start_all(peer_rows)
     local = [
         pltpu.make_async_copy(
             tok_ref.at[sx * half + t], x_ref.at[pl.ds(pl.multiple_of(me * rows, rows), rows), :], local_sem.at[0]
-        ),
-        pltpu.make_async_copy(
-            tok_ref.at[sx * half + n_ten],
-            x_ref.at[pl.ds(pl.multiple_of((group + sx) * rows, rows), rows), :],
-            local_sem.at[1],
         ),
     ]
     for i, (w_ref, out, s, by_rows) in enumerate(weights):
@@ -469,10 +580,16 @@
             copy.wait_send()
     wait_all(local)
     wait_all(counts)
+    wait_all(peer_rows)
     wait_all(tokens)
-
-
-def exchange_in(tok, w_query, w_key, w_value, w_out, count, n_dp, n_seq, n_ten):
+    for here, away, near in shared:
+        pl.when(here)(near.wait)
+        pl.when(jnp.logical_not(here))(away.wait_send)
+    for i in range(n_seq):
+        pl.when(jnp.logical_not((t // 2 == c) & (t % 2 == i)))(arriving[i].wait_recv)
+
+
+def exchange_in(tok, w_query, w_key, w_value, w_out, count, out_grad, n_dp, n_seq, n_ten):
     windows, rows, width = tok.shape
     slices = n_dp * n_seq
     vmem = pl.BlockSpec(memory_space=pltpu.VMEM)
@@ -480,29 +597,43 @@
     group = n_seq * n_ten
     return pl.pallas_call(
         functools.partial(exchange_in_kernel, (n_seq, n_ten, windows // n_seq, rows, slices)),
-        in_specs=[vmem] * 6,
-        out_specs=[any_spec()] * 6,
+        in_specs=[vmem] * 6 + [any_spec()],
+        out_specs=[any_spec()] * 7,
         out_shape=[jax.ShapeDtypeStruct(((group + n_seq) * rows, width), BF)]
         + [square] * 4
-        + [jax.ShapeDtypeStruct((n_dp,) + count.shape, count.dtype)],
+        + [jax.ShapeDtypeStruct((n_dp,) + count.shape, count.dtype)]
+        + [jax.ShapeDtypeStruct((n_seq,) + out_grad.shape[1:], BF)],
         scratch_shapes=[
-            pltpu.SemaphoreType.DMA((group,)),
-            pltpu.SemaphoreType.DMA((group,)),
+            pltpu.SemaphoreType.DMA((group + 1,)),
+            pltpu.SemaphoreType.DMA((group + 1,)),
             pltpu.SemaphoreType.DMA((4, 4 * (n_ten - 1))),
             pltpu.SemaphoreType.DMA((4, 4 * (n_ten - 1))),
             pltpu.SemaphoreType.DMA((3,)),
             pltpu.SemaphoreType.DMA((3,)),
+            pltpu.SemaphoreType.DMA((2,)),
+            pltpu.SemaphoreType.DMA((2,)),
             pltpu.SemaphoreType.DMA((7,)),
         ],
         compiler_params=pltpu.CompilerParams(collective_id=0, has_side_effects=True),
         name="exchange_in",
-    )(tok, w_query, w_key, w_value, w_out, count)
+    )(tok, w_query, w_key, w_value, w_out, count, out_grad)
 
 
 def qkv_kernel(
-    x_ref, gain_ref, bias_ref, wq_ref, wk_ref, wv_ref, cos_ref, sin_ref, part_cos_ref, part_sin_ref,
-    first_ref, q_ref, k_ref, v_ref,
+    n_ten, x_ref, gain_ref, bias_ref, wq_ref, wk_ref, wv_ref, cos_ref, sin_ref, part_cos_ref, part_sin_ref,
+    wg_ref, wu_ref, wd_ref, first_ref, q_ref, k_ref, v_ref, ag_ref, au_ref, ad_ref, send, recv,
 ):
+    route = WeightRoute((ag_ref, au_ref, ad_ref), (wg_ref, wu_ref, wd_ref), n_ten, send, recv)
+
+    @pl.when(pl.program_id(0) == 0)
+    def _():
+        greet([{"tensor": (route.t + j) % n_ten} for j in range(1, n_ten)])
+        start_all(route.to_in())
+
+        @pl.when(route.is_middle)
+        def _():
+            start_all(route.to_out())
+
     shared = pl.program_id(0) == pl.num_programs(0) - 1
     normed, _ = layer_stats(x_ref[...].astype(F32))
     first_ref[...] = (normed * gain_ref[...] + bias_ref[...]).astype(BF)
@@ -518,26 +649,43 @@
                     part = (part * cos + swap_halves(part) * sin) * scale
                 out_ref[:, at + c : at + c + LANES] = part.astype(BF)
 
+    @pl.when(shared)
+    def _():
+        route.arrived(1)
+        sent_all(route.to_in())
+
+        @pl.when(route.is_middle)
+        def _():
+            route.arrived(2)
+            sent_all(route.to_out())
+
 
 def once(shape):
     return pl.BlockSpec(shape, lambda *_: (0,) * len(shape), pipeline_mode=pl.Buffered(1))
 
 
-def norm_qkv(x, gain, bias, w_query, w_key, w_value, tables, part_tables):
+def norm_qkv(x, gain, bias, w_query, w_key, w_value, tables, part_tables, ffn, n_ten):
     rows, width = x.shape
     tile = 256
     row = pl.BlockSpec((tile, width), lambda r: (r, 0))
     own = tables[0].shape[0] // tile
     table = pl.BlockSpec((tile, LANES), lambda r: (jnp.minimum(r, own - 1), 0))
     return pl.pallas_call(
-        qkv_kernel,
+        functools.partial(qkv_kernel, n_ten),
         grid=(rows // tile,),
-        in_specs=[row, once((1, width)), once((1, width))] + [once((width, width))] * 3 + [table, table] + [once((tile, LANES))] * 2,
-        out_specs=[row] * 4,
-        out_shape=[jax.ShapeDtypeStruct((rows, width), BF)] * 4,
+        in_specs=[row, once((1, width)), once((1, width))] + [once((width, width))] * 3 + [table, table] + [once((tile, LANES))] * 2 + [any_spec()] * 3,
+        out_specs=[row] * 4 + [any_spec()] * 3,
+        out_shape=[jax.ShapeDtypeStruct((rows, width), BF)] * 4
+        + [
+            jax.ShapeDtypeStruct((width, n_ten * ffn[0].shape[1]), BF),
+            jax.ShapeDtypeStruct((width, n_ten * ffn[1].shape[1]), BF),
+            jax.ShapeDtypeStruct((n_ten * ffn[2].shape[0], width), BF),
+        ],
+        scratch_shapes=route_sems(),
+        compiler_params=pltpu.CompilerParams(collective_id=7, has_side_effects=True),
         cost_estimate=pl.CostEstimate(flops=6 * rows * width * width, bytes_accessed=16 * rows * width, transcendentals=0),
         name="norm_qkv",
-    )(x, gain.reshape(1, width), bias.reshape(1, width), w_query, w_key, w_value, *tables, *part_tables)
+    )(x, gain.reshape(1, width), bias.reshape(1, width), w_query, w_key, w_value, *tables, *part_tables, *ffn)
 
 
 def attend_body(q_ref, k_ref, v_ref):
@@ -566,116 +714,151 @@
     )
 
 
-def attend_left_kernel(n_ten, q_ref, k_ref, v_ref, part_ref, buf, send, recv, local_sem):
-    t = lax.axis_index("tensor")
+def attend_left_kernel(
+    n_ten, q_ref, k_ref, v_ref, ag_in, au_in, ad_in, part_ref, ag_ref, au_ref, ad_ref, buf, send, recv, local_sem,
+    route_send, route_recv,
+):
+    place, device = quad_place()
     r, p = pl.program_id(0), pl.program_id(1)
     last_pair = p == pl.num_programs(1) - 1
     hw = buf.shape[2]
-    heads = pl.ds(pl.multiple_of(t * hw, hw), hw)
-    dst = part_ref.at[:, heads]
+    dst = part_ref.at[:, pl.ds(pl.multiple_of(place * hw, hw), hw)]
+    route = WeightRoute((ag_ref, au_ref, ad_ref), None, n_ten, route_send, route_recv)
+    hops = route.hop(1, 2) + route.hop(2, 0)
 
     @pl.when((p == 0) & (r == 0))
     def _():
-        greet([{"tensor": (t + j) % n_ten} for j in range(1, n_ten)])
+        greet(quad_peers() + [route.y_peer])
+        start_all(hops)
 
     buf[r, :, pl.ds(pl.multiple_of(p * LANES, LANES), LANES)] = attend_body(q_ref, k_ref, v_ref)
 
     def copy_to(j):
-        to = (t + j) % n_ten
-        return remote(buf.at[to], dst, send.at[j - 1], recv.at[j - 1], {"tensor": to})
-
-    own = pltpu.make_async_copy(buf.at[t], dst, local_sem.at[0])
-    for j in range(1, n_ten):
-
-        @pl.when(last_pair & (r == (t + j) % n_ten))
-        def _(j=j):
-            copy_to(j).start()
-
-    @pl.when(last_pair & (r == t))
-    def _():
-        own.start()
-
-    @pl.when(last_pair & (r == n_ten - 1))
-    def _():
-        wait_all([copy_to(j) for j in range(1, n_ten)])
+        to = (place + j) % QUAD
+        return remote(buf.at[to], dst, send.at[j - 1], recv.at[j - 1], device(to))
+
+    own = pltpu.make_async_copy(buf.at[place], dst, local_sem.at[0])
+    for j in range(1, QUAD):
+        pl.when(last_pair & (r == (place + j) % QUAD))(copy_to(j).start)
+    pl.when(last_pair & (r == place))(own.start)
+
+    @pl.when(last_pair & (r == QUAD - 1))
+    def _():
+        wait_all([copy_to(j) for j in range(1, QUAD)])
         own.wait()
-
-
-def attend_left(q, k, v, n_ten):
+        wait_all(hops)
+
+
+def attend_left(q, k, v, gathered, n_ten):
     rows, hw = q.shape
-    tile, pairs = rows // n_ten, hw // LANES
+    tile, pairs = rows // QUAD, hw // LANES
     column = pl.BlockSpec((rows, LANES), lambda r, p: (0, p))
     return pl.pallas_call(
         functools.partial(attend_left_kernel, n_ten),
-        grid=(n_ten, pairs),
-        in_specs=[pl.BlockSpec((tile, LANES), lambda r, p: (r, p)), column, column],
-        out_specs=any_spec(),
-        out_shape=jax.ShapeDtypeStruct((tile, n_ten * hw), BF),
-        scratch_shapes=[pltpu.VMEM((n_ten, tile, hw), BF)]
-        + [pltpu.SemaphoreType.DMA((n_ten - 1,))] * 2
-        + [pltpu.SemaphoreType.DMA((1,))],
+        grid=(QUAD, pairs),
+        in_specs=[pl.BlockSpec((tile, LANES), lambda r, p: (r, p)), column, column] + [any_spec()] * 3,
+        out_specs=[any_spec()] * 4,
+        out_shape=[jax.ShapeDtypeStruct((tile, QUAD * hw), BF)] + [jax.ShapeDtypeStruct(w.shape, BF) for w in gathered],
+        input_output_aliases={3: 1, 4: 2, 5: 3},
+        scratch_shapes=[pltpu.VMEM((QUAD, tile, hw), BF)]
+        + [pltpu.SemaphoreType.DMA((QUAD - 1,))] * 2
+        + [pltpu.SemaphoreType.DMA((1,))]
+        + route_sems(),
         compiler_params=pltpu.CompilerParams(collective_id=3, has_side_effects=True),
         cost_estimate=attend_cost(rows, pairs),
         name="attend_left",
-    )(q, k, v)
-
-
-def swap_part(refs, outs, send, recv, local_sem, n_ten, base):
-    t = lax.axis_index("tensor")
-    share, hw = outs[0].shape[0] // n_ten, outs[0].shape[1]
+    )(q, k, v, *gathered)
+
+
+def swap_part(refs, outs, send, recv, local_sem, base):
+    place, device = quad_place()
+    share, hw = outs[0].shape[0] // QUAD, outs[0].shape[1]
     copies, local = [], []
     rows = pl.ds(base, share)
-    mine = pl.ds(pl.multiple_of(t * share, share), share)
+    mine = pl.ds(pl.multiple_of(place * share, share), share)
     for i, (ref, out) in enumerate(zip(refs, outs, strict=True)):
-        for j in range(1, n_ten):
-            to = (t + j) % n_ten
+        for j in range(1, QUAD):
+            to = (place + j) % QUAD
             src = ref.at[rows, pl.ds(pl.multiple_of(to * hw, hw), hw)]
-            copies.append(remote(src, out.at[mine, :], send.at[i, j - 1], recv.at[i, j - 1], {"tensor": to}))
-        src = ref.at[rows, pl.ds(pl.multiple_of(t * hw, hw), hw)]
+            copies.append(remote(src, out.at[mine, :], send.at[i, j - 1], recv.at[i, j - 1], device(to)))
+        src = ref.at[rows, pl.ds(pl.multiple_of(place * hw, hw), hw)]
         local.append(pltpu.make_async_copy(src, out.at[mine, :], local_sem.at[i]))
     return copies, local
 
 
 def attend_swap_kernel(
-    n_ten, length, q_ref, k_ref, v_ref, q_all, k_all, v_all, o_ref, lq_ref, lk_ref, lv_ref, send, recv, local_sem
+    n_ten, length, q_ref, k_ref, v_ref, q_all, k_all, v_all, ag_in, au_in, ad_in, o_ref, lq_ref, lk_ref, lv_ref,
+    ag_ref, au_ref, ad_ref, send, recv, local_sem, route_send, route_recv,
 ):
-    t = lax.axis_index("tensor")
     step = pl.program_id(0) * pl.num_programs(1) + pl.program_id(1)
-    copies, local = swap_part(
-        (q_all, k_all, v_all), (lq_ref, lk_ref, lv_ref), send, recv, local_sem, n_ten, length
-    )
+    steps = pl.num_programs(0) * pl.num_programs(1)
+    copies, local = swap_part((q_all, k_all, v_all), (lq_ref, lk_ref, lv_ref), send, recv, local_sem, length)
+    route = WeightRoute((ag_ref, au_ref, ad_ref), None, n_ten, route_send, route_recv)
 
     @pl.when(step == 0)
     def _():
-        greet([{"tensor": (t + j) % n_ten} for j in range(1, n_ten)])
+        greet(quad_peers() + [route.y_peer] + [{"tensor": (route.t + j) % n_ten} for j in range(1, n_ten)])
+        start_all(route.hop(1, 0))
+
+        @pl.when(route.is_middle)
+        def _():
+            start_all(route.in_far())
+            start_all(route.out_two())
+
         start_all(copies + local)
 
     o_ref[...] = attend_body(q_ref, k_ref, v_ref)
 
-    @pl.when(step == pl.num_programs(0) * pl.num_programs(1) - 1)
+    @pl.when(step == steps // 4)
+    def _():
+        received(route.hop(1, 0))
+        start_all(route.hop(1, 1))
+
+    @pl.when(step == steps // 2)
+    def _():
+        @pl.when(route.is_middle)
+        def _():
+            route.arrived(3)
+            start_all(route.out_three())
+
+    @pl.when(step == steps - 1)
     def _():
         wait_all(copies + local)
-
-
-def attend_swap(q, k, v, length, n_ten):
+        received(route.hop(1, 1))
+        sent_all(route.hop(1, 0) + route.hop(1, 1))
+
+        @pl.when(route.is_middle)
+        def _():
+            sent_all(route.in_far() + route.out_two() + route.out_three())
+
+        @pl.when(route.is_end)
+        def _():
+            route.arrived(2)
+            route.arrived(3)
+
+
+def attend_swap(q, k, v, gathered, length, n_ten):
     width = q.shape[1]
-    tile, pairs, hw = 512, width // LANES, width // n_ten
+    tile, pairs, hw = 512, width // LANES, width // QUAD
     left = jax.ShapeDtypeStruct((length, hw), BF)
     return pl.pallas_call(
         functools.partial(attend_swap_kernel, n_ten, length),
         grid=(pairs, length // tile),
-        in_specs=attend_specs(length, tile) + [any_spec()] * 3,
-        out_specs=[pl.BlockSpec((tile, LANES), lambda p, r: (r, p))] + [any_spec()] * 3,
-        out_shape=[jax.ShapeDtypeStruct((length, width), BF), left, left, left],
+        in_specs=attend_specs(length, tile) + [any_spec()] * 6,
+        out_specs=[pl.BlockSpec((tile, LANES), lambda p, r: (r, p))] + [any_spec()] * 6,
+        out_shape=[jax.ShapeDtypeStruct((length, width), BF), left, left, left]
+        + [jax.ShapeDtypeStruct(w.shape, BF) for w in gathered],
+        input_output_aliases={6: 4, 7: 5, 8: 6},
         scratch_shapes=[
-            pltpu.SemaphoreType.DMA((3, n_ten - 1)),
-            pltpu.SemaphoreType.DMA((3, n_ten - 1)),
+            pltpu.SemaphoreType.DMA((3, QUAD - 1)),
+            pltpu.SemaphoreType.DMA((3, QUAD - 1)),
             pltpu.SemaphoreType.DMA((3,)),
-        ],
+        ]
+        + route_sems(),
         compiler_params=pltpu.CompilerParams(collective_id=1, has_side_effects=True),
         cost_estimate=attend_cost(length, pairs),
         name="attend_swap",
-    )(q, k, v, q, k, v)
+    )(q, k, v, q, k, v, *gathered)
 
 
 def back_body(q_ref, g_ref, k_ref, v_ref, pick_ref, cos_ref, sin_ref, qcos_ref, qsin_ref):
@@ -706,34 +889,9 @@
     return dq, dk, dv
 
 
-def back_left_kernel(
-    n_ten, q_ref, g_ref, k_ref, v_ref, pick_ref, cos_ref, sin_ref, qcos_ref, qsin_ref, dq_ref, dk_ref, dv_ref,
-    parts, total, send, recv,
-):
-    t = lax.axis_index("tensor")
-    p = pl.program_id(0)
-    hw = total.shape[1]
-
-    @pl.when(p == 0)
-    def _():
-        peers = [(t + j) % n_ten for j in range(1, n_ten)]
-        greet([{"tensor": to} for to in peers])
-        copies = [
-            remote(
-                g_ref.at[:, pl.ds(pl.multiple_of(to * hw, hw), hw)], parts.at[j], send.at[j], recv.at[j], {"tensor": to}
-            )
-            for j, to in enumerate(peers)
-        ]
-        start_all(copies)
-        wait_all(copies)
-        whole = g_ref[:, pl.ds(pl.multiple_of(t * hw, hw), hw)].astype(F32)
-        for j in range(n_ten - 1):
-            whole = whole + parts[j].astype(F32)
-        total[...] = whole.astype(BF)
-
-    g_view = total.at[:, pl.ds(pl.multiple_of(p * LANES, LANES), LANES)]
+def back_kernel(q_ref, g_ref, k_ref, v_ref, pick_ref, cos_ref, sin_ref, qcos_ref, qsin_ref, dq_ref, dk_ref, dv_ref):
     dq_ref[...], dk_ref[...], dv_ref[...] = back_body(
-        q_ref, g_view, k_ref, v_ref, pick_ref, cos_ref, sin_ref, qcos_ref, qsin_ref
+        q_ref, g_ref, k_ref, v_ref, pick_ref, cos_ref, sin_ref, qcos_ref, qsin_ref
     )
 
 
@@ -753,48 +911,39 @@
     )
 
 
-def back_left(q, grad_rows, k, v, pick, tables, n_ten):
+def back_left(q, grad_rows, k, v, pick, tables):
     masked, length = pick.shape
     width = q.shape[1]
     full = pl.BlockSpec((length, LANES), lambda p: (0, p))
-    specs = back_specs(length, masked)
-    specs[1] = once(grad_rows.shape)
     return pl.pallas_call(
-        functools.partial(back_left_kernel, n_ten),
+        back_kernel,
         grid=(width // LANES,),
-        in_specs=specs,
+        in_specs=back_specs(length, masked),
         out_specs=[full] * 3,
         out_shape=[jax.ShapeDtypeStruct((length, width), BF)] * 3,
-        scratch_shapes=[
-            pltpu.VMEM((n_ten - 1, masked, width), BF),
-            pltpu.VMEM((masked, width), BF),
-            pltpu.SemaphoreType.DMA((n_ten - 1,)),
-            pltpu.SemaphoreType.DMA((n_ten - 1,)),
-        ],
-        compiler_params=pltpu.CompilerParams(collective_id=6, has_side_effects=True),
         cost_estimate=back_cost(length, masked, width // LANES),
         name="back_left",
     )(q, grad_rows, k, v, pick, *tables)
 
 
 def back_swap_kernel(
-    n_ten, q_ref, g_ref, k_ref, v_ref, pick_ref, cos_ref, sin_ref, qcos_ref, qsin_ref, lq_ref, lk_ref, lv_ref,
+    q_ref, g_ref, k_ref, v_ref, pick_ref, cos_ref, sin_ref, qcos_ref, qsin_ref, lq_ref, lk_ref, lv_ref,
     dq_ref, dk_ref, dv_ref, buf, out_sem, send, recv, local_sem,
 ):
-    t = lax.axis_index("tensor")
+    place, device = quad_place()
     step, steps = pl.program_id(0), pl.num_programs(0)
     length = q_ref.shape[0]
-    share, hw = lq_ref.shape[0] // n_ten, lq_ref.shape[1]
+    share, hw = lq_ref.shape[0] // QUAD, lq_ref.shape[1]
     outs = (dq_ref, dk_ref, dv_ref)
     copies, local = [], []
-    mine = pl.ds(pl.multiple_of(t * hw, hw), hw)
+    mine = pl.ds(pl.multiple_of(place * hw, hw), hw)
     for i, (ref, out) in enumerate(zip((lq_ref, lk_ref, lv_ref), outs, strict=True)):
         dst = out.at[pl.ds(length, share), mine]
-        for j in range(1, n_ten):
-            to = (t + j) % n_ten
+        for j in range(1, QUAD):
+            to = (place + j) % QUAD
             src = ref.at[pl.ds(pl.multiple_of(to * share, share), share), :]
-            copies.append(remote(src, dst, send.at[i, j - 1], recv.at[i, j - 1], {"tensor": to}))
-        src = ref.at[pl.ds(pl.multiple_of(t * share, share), share), :]
+            copies.append(remote(src, dst, send.at[i, j - 1], recv.at[i, j - 1], device(to)))
+        src = ref.at[pl.ds(pl.multiple_of(place * share, share), share), :]
         local.append(pltpu.make_async_copy(src, dst, local_sem.at[i]))
 
     def out_copy(at, i):
@@ -804,7 +953,7 @@
 
     @pl.when(step == 0)
     def _():
-        greet([{"tensor": (t + j) % n_ten} for j in range(1, n_ten)])
+        greet(quad_peers())
         start_all(copies + local)
 
     @pl.when(step >= 2)
@@ -825,12 +974,12 @@
         wait_all(copies + local)
 
 
-def back_swap(q, grad_rows, k, v, pick, tables, left, n_ten):
+def back_swap(q, grad_rows, k, v, pick, tables, left):
     masked, length = pick.shape
     width = q.shape[1]
-    share = left[0].shape[0] // n_ten
+    share = left[0].shape[0] // QUAD
     return pl.pallas_call(
-        functools.partial(back_swap_kernel, n_ten),
+        back_swap_kernel,
         grid=(width // LANES,),
         in_specs=back_specs(length, masked) + [any_spec()] * 3,
         out_specs=[any_spec()] * 3,
@@ -838,8 +987,8 @@
         scratch_shapes=[
             pltpu.VMEM((2, 3, length, LANES), BF),
             pltpu.SemaphoreType.DMA((2, 3)),
-            pltpu.SemaphoreType.DMA((3, n_ten - 1)),
-            pltpu.SemaphoreType.DMA((3, n_ten - 1)),
+            pltpu.SemaphoreType.DMA((3, QUAD - 1)),
+            pltpu.SemaphoreType.DMA((3, QUAD - 1)),
             pltpu.SemaphoreType.DMA((3,)),
         ],
         compiler_params=pltpu.CompilerParams(collective_id=2, has_side_effects=True),
@@ -848,57 +997,13 @@
     )(q, grad_rows, k, v, pick, *tables, *left)
 
 
-def weight_hops(gathered, n_ten, sems):
-    dp, sx, t = lax.axis_index("dp"), lax.axis_index("seq"), lax.axis_index("tensor")
-    y, c = dp // 2, dp % 2
-    gate_ref, up_ref, down_ref = gathered
-    width, units = gate_ref.shape[0], gate_ref.shape[1] // n_ten
-    size, cols = width // 8, width // 2
-    s_xy, s_yx = c * 4 + y * 2 + sx, c * 4 + sx * 2 + y
-    x_peer, y_peer, c_peer = {"seq": 1 - sx}, {"dp": (dp + 2) % 4}, {"dp": 2 * y + 1 - c}
-    send, recv = sems
-
-    def shard(ref, k, first, count, which):
-        rows = pl.multiple_of(first * (size if k < 2 else units // 8), 16)
-        if k < 2:
-            at = 0 if which is None else pl.multiple_of(which * units, units)
-            return ref.at[pl.ds(rows, count * size), pl.ds(at, units)]
-        at = rows if which is None else pl.multiple_of(which * units + rows, 16)
-        return ref.at[pl.ds(at, count * (units // 8)), pl.ds((k - 2) * cols, cols)]
-
-    refs = (gate_ref, up_ref, down_ref, down_ref)
-    slices = (s_xy, s_yx, s_xy, s_yx)
-
-    def along(which, peer_t, slot, number, own=None):
-        copies = []
-        for k in range(4):
-            dst = shard(refs[k], k, slices[k], 1, which)
-            src = dst if own is None else shard(own[min(k, 2)], k, slices[k], 1, None)
-            copies.append(remote(src, dst, send.at[number, k], recv.at[slot, k], {"tensor": peer_t}))
-        return copies
-
-    def across(hop, which, order):
-        copies = []
-        for k in range(4):
-            xy = k % 2 == 0
-            peer, first, count = (
-                (x_peer if xy else y_peer, slices[k], 1),
-                (y_peer if xy else x_peer, slices[k] // 2 * 2, 2),
-                (c_peer, c * 4, 4),
-            )[hop]
-            ref = shard(refs[k], k, first, count, which)
-            copies.append(remote(ref, ref, send.at[5 + 3 * order + hop, k], recv.at[4 + 3 * order + hop, k], peer))
-        return copies
-
-    return along, across
-
-
 def feed_kernel(
     n_ten, tok_ref, att_ref, left_ref, wo_ref, gain_ref, bias_ref, pick_ref, part_pick_ref, cot_ref, wg_ref, wu_ref, wd_ref,
-    out_ref, att_m_ref, gr2_ref, gatt_ref, vec_ref, x_m_ref, ag_ref, au_ref, ad_ref,
-    x_ref, acc_ref, normed_ref, inv_ref, grad_ref, g_buf, u_buf, d_buf, buf_sem, send, recv,
+    ag_in, au_in, ad_in, out_ref, att_m_ref, gr2_ref, gatt_ref, left_gatt_ref, vec_ref, all_own_ref, all_left_ref,
+    ag_ref, au_ref, ad_ref,
+    x_ref, acc_ref, normed_ref, inv_ref, grad_ref, g_buf, u_buf, d_buf, rows_buf, rows_parts, own_m, left_m, gatt_buf, gatt_parts,
+    buf_sem, small_send, small_recv, line_send, line_recv, local_sem, send, recv,
 ):
-    dp, sx, t = lax.axis_index("dp"), lax.axis_index("seq"), lax.axis_index("tensor")
     step, steps = pl.program_id(0), pl.num_programs(0)
     rows, width = tok_ref.shape
     length = att_ref.shape[0]
@@ -907,30 +1012,32 @@
     unit = g_buf.shape[2]
     units = wg_ref.shape[1]
     per = units // unit
+    part, hw = rows_buf.shape[1], gatt_parts.shape[2]
     gain = gain_ref[...]
     own = (wg_ref, wu_ref, wd_ref)
-
-    side = t // 2
-    middle = jnp.minimum(t, n_ten - 1 - t)
-    mirror = lambda k: k + side * (n_ten - 1 - 2 * k)
-    order = [mirror(k) for k in (middle, 1 - middle, 2, 3)]
-    inward, outward = mirror(middle + 1), mirror(0)
-    along, across = weight_hops((ag_ref, au_ref, ad_ref), n_ten, (send, recv))
-    to_in = along(t, inward, 1 + middle, 0, own)
-    to_out = along(t, outward, 1, 1, own)
-    in_far = along(mirror(0), inward, 3, 2)
-    out_two = along(mirror(2), outward, 2, 3)
-    out_three = along(mirror(3), outward, 3, 4)
-    is_middle, is_end = middle == 1, middle == 0
-    hop = [[across(h, order[i], i - 1) for h in range(3)] for i in (1, 2, 3)]
-
-    def arrived(i):
-        for copy in along(order[i], inward, i, 0):
-            copy.wait_recv()
-
-    def got(copies):
-        for copy in copies:
-            copy.wait_recv()
+    route = WeightRoute((ag_ref, au_ref, ad_ref), own, n_ten, send, recv)
+    order = route.order
+    place, device = quad_place()
+    rows_copies, gatt_copies = [], []
+    for j in range(1, QUAD):
+        to = (place + j) % QUAD
+        rows_copies.append(
+            remote(rows_buf.at[to], rows_parts.at[j - 1], small_send.at[0, j - 1], small_recv.at[0, j - 1], device(to))
+        )
+        src = gatt_buf.at[:, pl.ds(pl.multiple_of(to * hw, hw), hw)]
+        gatt_copies.append(
+            remote(src, gatt_parts.at[j - 1], small_send.at[1, j - 1], small_recv.at[1, j - 1], device(to))
+        )
+
+    line_copies = [[], []]
+    local = []
+    for n, (src, out) in enumerate(((own_m, all_own_ref), (left_m, all_left_ref))):
+        for j in range(1, n_ten):
+            to = (route.t + j) % n_ten
+            line_copies[n].append(
+                remote(src, out.at[route.t], line_send.at[n, j - 1], line_recv.at[n, j - 1], {"tensor": to})
+            )
+        local.append(pltpu.make_async_copy(src, out.at[route.t], local_sem.at[n]))
 
     def fetch(at):
         slot, i, b = at % 2, at // per, at % per
@@ -968,14 +1075,9 @@
 
     @pl.when(step == 0)
     def _():
-        peers = [{"tensor": (t + j) % n_ten} for j in range(1, n_ten)]
-        greet(peers + [{"seq": 1 - sx}] + [{"dp": (dp + 2) % 4}, {"dp": dp // 2 * 2 + 1 - dp % 2}])
-        start_all(to_in)
-
-        @pl.when(is_middle)
-        def _():
-            start_all(to_out)
-
+        greet(quad_peers() + [route.y_peer] + [{"tensor": (route.t + j) % n_ten} for j in range(1, n_ten)])
+        start_all(route.hop(2, 1))
+        start_all(route.hop(3, 0))
         fetch(0)
         tile = rows - length
         for i, (pick, att, tok) in enumerate(
@@ -988,9 +1090,13 @@
             normed_ref[here, :] = normed
             inv_ref[here, :] = jnp.broadcast_to(inv_std, (slots, LANES))
             here_too = jnp.sum(pick.astype(F32), axis=1, keepdims=True) > 0.0
-            low = jnp.where(here_too, low.astype(F32), 0.0).astype(BF)
-            x_ref[rows + i * slots : rows + (i + 1) * slots, :] = low
-            x_m_ref[here, :] = low
+            low = jnp.where(here_too, low.astype(F32), 0.0)
+            x_ref[rows + i * slots : rows + (i + 1) * slots, :] = low.astype(BF)
+            if i == 0:
+                own_m[...] = low.astype(BF)
+            else:
+                for k in range(QUAD):
+                    rows_buf[k] = low[k * part : (k + 1) * part, :].astype(BF)
         for at in range(0, rows, tile):
             att = att_ref[at : at + tile, :] if at < length else left_ref[...]
             res = tok_ref[at : at + tile, :].astype(F32) + dot_n(att, wo_ref[...])
@@ -1019,60 +1125,44 @@
     grad_up = (back * act).astype(BF)
     grad_ref[...] += dot_t(grad_gate, w_g) + dot_t(grad_up, w_u)
 
-    @pl.when(step == per - 1)
-    def _():
-        arrived(1)
-        start_all(hop[0][0])
-
-        @pl.when(is_middle)
-        def _():
-            arrived(2)
-            start_all(in_far)
-            start_all(out_two)
-
-        got(hop[0][0])
-        start_all(hop[0][1])
-
-        @pl.when(is_end)
-        def _():
-            arrived(2)
-
-        @pl.when(is_middle)
-        def _():
-            arrived(3)
-            start_all(out_three)
-
-        start_all(hop[1][0])
-        got(hop[0][1])
-        start_all(hop[0][2])
-        got(hop[0][2])
-
-    @pl.when(step == per)
-    def _():
-        got(hop[1][0])
-        start_all(hop[1][1])
+    @pl.when(step == 1)
+    def _():
+        start_all(rows_copies)
+        start_all(line_copies[0])
+        local[0].start()
+
+    @pl.when(step == 3)
+    def _():
+        wait_all(rows_copies)
+        whole = rows_buf[place].astype(F32)
+        for j in range(QUAD - 1):
+            whole = whole + rows_parts[j].astype(F32)
+        left_m[...] = whole.astype(BF)
+
+    @pl.when(step == 4)
+    def _():
+        start_all(line_copies[1])
+        local[1].start()
 
     @pl.when(step == per + 1)
     def _():
-        @pl.when(is_end)
-        def _():
-            arrived(3)
-
-        start_all(hop[2][0])
+        received(route.hop(2, 1))
+        start_all(route.hop(2, 2))
+        received(route.hop(3, 0))
+        start_all(route.hop(3, 1))
 
     @pl.when(step == 2 * per - 1)
     def _():
-        got(hop[1][1])
-        start_all(hop[1][2])
-        got(hop[2][0])
-        start_all(hop[2][1])
-        got(hop[1][2])
+        received(route.hop(2, 2))
+
+    @pl.when(step == 2 * per + 2)
+    def _():
+        received(route.hop(3, 1))
+        start_all(route.hop(3, 2))
 
     @pl.when(step == 3 * per - 1)
     def _():
-        got(hop[2][1])
-        start_all(hop[2][2])
-        got(hop[2][2])
+        received(route.hop(3, 2))
 
     @pl.when((step + 1 < steps) & ((step + 1) % per == 0))
     def _():
@@ -1080,32 +1170,32 @@
 
     @pl.when(step == steps - 1)
     def _():
-        out_ref[...] = acc_ref[...].astype(BF)
         grad, normed = grad_ref[...], normed_ref[...]
+        gr2 = (cot_ref[...] + norm_back(grad, normed, inv_ref[:, :1], gain)).astype(BF)
+        gr2_ref[...] = gr2
+        gatt = dot_t(gr2, wo_ref[...]).astype(BF)
+        gatt_ref[...] = gatt[:slots]
+        gatt_buf[...] = gatt[slots:]
         vec_ref[...] = jnp.concatenate(
             [jnp.sum(grad * normed, axis=0, keepdims=True), jnp.sum(grad, axis=0, keepdims=True)], axis=0
         )
-        gr2 = (cot_ref[...] + norm_back(grad, normed, inv_ref[:, :1], gain)).astype(BF)
-        gr2_ref[...] = gr2
-        gatt_ref[...] = dot_t(gr2, wo_ref[...]).astype(BF)
-        for copy in to_in:
-            copy.wait_send()
-
-        @pl.when(is_middle)
-        def _():
-            for copy in to_out + in_far + out_two + out_three:
-                copy.wait_send()
-
-        for shard_hops in hop:
-            for copies in shard_hops:
-                for copy in copies:
-                    copy.wait_send()
-
-
-def feed_forward(tok, att, left_att, w_out, gain, bias, pick, part_pick, cot, w_gate, w_up, w_down, n_ten):
+        start_all(gatt_copies)
+        out_ref[...] = acc_ref[...].astype(BF)
+        sent_all(route.hop(2, 1) + route.hop(2, 2) + route.hop(3, 0) + route.hop(3, 1) + route.hop(3, 2))
+        wait_all(gatt_copies)
+        whole = gatt_buf[:, pl.ds(pl.multiple_of(place * hw, hw), hw)].astype(F32)
+        for j in range(QUAD - 1):
+            whole = whole + gatt_parts[j].astype(F32)
+        left_gatt_ref[...] = whole.astype(BF)
+        wait_all(line_copies[0] + line_copies[1])
+        wait_all(local)
+
+
+def feed_forward(tok, att, left_att, w_out, gain, bias, pick, part_pick, cot, ffn, gathered, n_ten):
     rows, width = tok.shape
-    units = w_gate.shape[1]
+    units = ffn[0].shape[1]
     masked = cot.shape[0]
+    slots, hw = masked // 2, width // QUAD
     unit = 256
     whole = lambda *shape: pl.BlockSpec(shape, lambda i: (0,) * len(shape))
     low = jax.ShapeDtypeStruct((masked, width), BF)
@@ -1114,15 +1204,18 @@
         grid=(n_ten * units // unit,),
         in_specs=[once(x.shape) for x in (tok, att, left_att, w_out)]
         + [once((1, width)), once((1, width)), once(pick.shape), once(part_pick.shape), once(cot.shape)]
-        + [any_spec()] * 3,
-        out_specs=[whole(rows, width)] + [whole(masked, width)] * 3 + [whole(2, width), whole(masked, width)] + [any_spec()] * 3,
+        + [any_spec()] * 6,
+        out_specs=[whole(rows, width), whole(masked, width), whole(masked, width), whole(slots, width), whole(slots, hw)]
+        + [whole(2, width)]
+        + [any_spec()] * 5,
         out_shape=[
-            jax.ShapeDtypeStruct((rows, width), BF), low, low, low,
-            jax.ShapeDtypeStruct((2, width), F32), low,
-            jax.ShapeDtypeStruct((width, n_ten * units), BF),
-            jax.ShapeDtypeStruct((width, n_ten * units), BF),
-            jax.ShapeDtypeStruct((n_ten * units, width), BF),
-        ],
+            jax.ShapeDtypeStruct((rows, width), BF), low, low,
+            jax.ShapeDtypeStruct((slots, width), BF), jax.ShapeDtypeStruct((slots, hw), BF),
+            jax.ShapeDtypeStruct((2, width), F32),
+            jax.ShapeDtypeStruct((n_ten, slots, width), BF), jax.ShapeDtypeStruct((n_ten, slots // QUAD, width), BF),
+        ]
+        + [jax.ShapeDtypeStruct(w.shape, BF) for w in gathered],
+        input_output_aliases={12: 8, 13: 9, 14: 10},
         scratch_shapes=[
             pltpu.VMEM((rows + masked, width), BF),
             pltpu.VMEM((rows, width), F32),
@@ -1132,16 +1225,26 @@
             pltpu.VMEM((2, width, unit), BF),
             pltpu.VMEM((2, width, unit), BF),
             pltpu.VMEM((2, unit, width), BF),
+            pltpu.VMEM((QUAD, slots // QUAD, width), BF),
+            pltpu.VMEM((QUAD - 1, slots // QUAD, width), BF),
+            pltpu.VMEM((slots, width), BF),
+            pltpu.VMEM((slots // QUAD, width), BF),
+            pltpu.VMEM((slots, width), BF),
+            pltpu.VMEM((QUAD - 1, slots, hw), BF),
             pltpu.SemaphoreType.DMA((2, 3)),
-            pltpu.SemaphoreType.DMA((14, 4)),
-            pltpu.SemaphoreType.DMA((13, 4)),
-        ],
+            pltpu.SemaphoreType.DMA((2, QUAD - 1)),
+            pltpu.SemaphoreType.DMA((2, QUAD - 1)),
+            pltpu.SemaphoreType.DMA((2, n_ten - 1)),
+            pltpu.SemaphoreType.DMA((2, n_ten - 1)),
+            pltpu.SemaphoreType.DMA((2,)),
+        ]
+        + route_sems(),
         compiler_params=pltpu.CompilerParams(collective_id=5, has_side_effects=True),
         cost_estimate=pl.CostEstimate(
             flops=8 * rows * width * n_ten * units, bytes_accessed=6 * width * n_ten * units, transcendentals=rows * n_ten * units
         ),
         name="feed_forward",
-    )(tok, att, left_att, w_out, gain.reshape(1, width), bias.reshape(1, width), pick, part_pick, cot, w_gate, w_up, w_down)[:6]
+    )(tok, att, left_att, w_out, gain.reshape(1, width), bias.reshape(1, width), pick, part_pick, cot, *ffn, *gathered)[:8]
 
 
 def token_back_kernel(
@@ -1186,8 +1289,8 @@
 
 
 def exchange_out_kernel(
-    sizes, gq_ref, gk_ref, gv_ref, go_ref, grad_ref, vec_ref, w_ref, tok_ref, vec_out,
-    buf1, sum1, buf2, sum2, buf3, sum3, buf4, vec_buf, vec_sum,
+    sizes, go_ref, gq_ref, gk_ref, gv_ref, gg_ref, gu_ref, gd_ref, grad_ref, vec_ref, w_ref, ffn_ref, tok_ref, vec_out,
+    buf1, buf2, buf3, buf4, vec_buf, vec_sum,
     tok_send, tok_recv, send1, recv1, send2, recv2, send3, recv3, send4, recv4, vec_send, vec_recv, local_sem,
 ):
     n_seq, n_ten, half, rows = sizes
@@ -1201,9 +1304,11 @@
         others.append((g // n_ten, g % n_ten))
     y_peer, c_peer, x_peer = {"dp": (dp + 2) % 4}, {"dp": 2 * y + 1 - c}, {"seq": 1 - sx}
     z_peers = [{"tensor": (t + j) % n_ten} for j in range(1, n_ten)]
-    greet([{"seq": a, "tensor": b} for a, b in others] + [y_peer, c_peer])
-    grads = (gq_ref, gk_ref, gv_ref, go_ref)
-    count = len(grads)
+    beside = [{"dp": 2 * y + 1 - c, "tensor": (t + j) % n_ten} for j in range(1, n_ten)]
+    greet([{"seq": a, "tensor": b} for a, b in others] + [y_peer, c_peer] + beside)
+    grads = (go_ref, gq_ref, gk_ref, gv_ref, gg_ref, gu_ref, gd_ref)
+    count, attn = len(grads), w_ref.shape[0]
+    x_first = (True, False, False, False, True, False, False)
     height = gq_ref.shape[0]
     hw = height // n_ten
 
@@ -1255,22 +1360,33 @@
                 tok_send.at[i], tok_recv.at[i], {"seq": a, "tensor": b},
             )
         )
-    tokens.append(
+    shared = []
+    for i in range(n_seq):
+        src, dst = grad_ref.at[pl.ds((group + i) * rows, rows), :], tok_ref.at[t % 2 * half + n_ten]
+        shared.append(
+            (
+                2 * c + i == t,
+                remote(
+                    src, dst, tok_send.at[group - 1 + i], tok_recv.at[group - 1 + t % 2],
+                    {"dp": 2 * y + t // 2, "tensor": 2 * c + i},
+                ),
+                pltpu.make_async_copy(src, dst, local_sem.at[1]),
+            )
+        )
+    arriving = [
         remote(
-            grad_ref.at[pl.ds(pl.multiple_of((group + 1 - sx) * rows, rows), rows), :],
-            tok_ref.at[sx * half + n_ten],
-            tok_send.at[group - 1], tok_recv.at[group - 1], x_peer,
+            grad_ref.at[pl.ds(0, rows), :], tok_ref.at[i * half + n_ten],
+            tok_send.at[group - 1], tok_recv.at[group - 1 + i], c_peer,
         )
-    )
+        for i in range(n_seq)
+    ]
     start_all(tokens)
+    for here, away, near in shared:
+        pl.when(here)(near.start)
+        pl.when(jnp.logical_not(here))(away.start)
     local = [
         pltpu.make_async_copy(
             grad_ref.at[pl.ds(pl.multiple_of(me * rows, rows), rows), :], tok_ref.at[sx * half + t], local_sem.at[0]
-        ),
-        pltpu.make_async_copy(
-            grad_ref.at[pl.ds(pl.multiple_of((group + sx) * rows, rows), rows), :],
-            tok_ref.at[sx * half + n_ten],
-            local_sem.at[1],
         ),
     ]
     start_all(local)
@@ -1281,10 +1397,10 @@
             copy.wait_recv()
         for b_y in range(2):
             for b_x in range(2):
-                add_rows(sum1.at[a, b_y, b_x], grads[a].at[:, columns(b_y, c, b_x)], buf1.at[a, b_y, b_x])
+                add_rows(buf1.at[a, b_y, b_x], grads[a].at[:, columns(b_y, c, b_x)], buf1.at[a, b_y, b_x])
         copies = []
         for b in range(2):
-            src, peer = (sum1.at[a, b, 1 - sx], x_peer) if a % 2 == 0 else (sum1.at[a, 1 - y, b], y_peer)
+            src, peer = (buf1.at[a, b, 1 - sx], x_peer) if x_first[a] else (buf1.at[a, 1 - y, b], y_peer)
             copies.append(remote(src, buf2.at[a, b], send2.at[a, b], recv2.at[a, b], peer))
         start_all(copies)
         stage2.append(copies)
@@ -1296,9 +1412,9 @@
         for copy in stage2[a]:
             copy.wait_recv()
         for b in range(2):
-            own = sum1.at[a, b, sx] if a % 2 == 0 else sum1.at[a, y, b]
-            add_rows(sum2.at[a, b], own, buf2.at[a, b])
-        src, peer = (sum2.at[a, 1 - y], y_peer) if a % 2 == 0 else (sum2.at[a, 1 - sx], x_peer)
+            own = buf1.at[a, b, sx] if x_first[a] else buf1.at[a, y, b]
+            add_rows(buf2.at[a, b], own, buf2.at[a, b])
+        src, peer = (buf2.at[a, 1 - y], y_peer) if x_first[a] else (buf2.at[a, 1 - sx], x_peer)
         copy = remote(src, buf3.at[a], send3.at[a], recv3.at[a], peer)
         copy.start()
         stage3.append(copy)
@@ -1308,23 +1424,33 @@
     stage4 = []
     for a in range(count):
         stage3[a].wait_recv()
-        add_rows(sum3.at[a], sum2.at[a, y] if a % 2 == 0 else sum2.at[a, sx], buf3.at[a])
+        own = buf2.at[a, y] if x_first[a] else buf2.at[a, sx]
+        if a >= attn:
+
+            def final(i, carry, a=a, own=own):
+                at = pl.ds(pl.multiple_of(i * hw, hw), hw)
+                ffn_ref[a - attn, at, :] = own[at, :].astype(F32) + buf3[a, at, :].astype(F32)
+                return carry
+
+            lax.fori_loop(0, height // hw, final, 0)
+            continue
+        add_rows(buf3.at[a], own, buf3.at[a])
         copies = []
         for j, peer in enumerate(z_peers):
             to = (t + 1 + j) % n_ten
-            src = sum3.at[a, pl.ds(pl.multiple_of(to * hw, hw), hw), :]
+            src = buf3.at[a, pl.ds(pl.multiple_of(to * hw, hw), hw), :]
             copies.append(remote(src, buf4.at[a, j], send4.at[a, j], recv4.at[a, j], peer))
         start_all(copies)
         stage4.append(copies)
     vec_hops[2][0].wait_recv()
     vec_sum[3] = vec_sum[2] + vec_buf[2]
     start_all(vec_hops[3])
-    for a in range(count):
-        total = sum3[a, pl.ds(pl.multiple_of(t * hw, hw), hw), :].astype(F32)
-        for j, copy in enumerate(stage4[a]):
+    for n, copies in enumerate(stage4):
+        total = buf3[n, pl.ds(pl.multiple_of(t * hw, hw), hw), :].astype(F32)
+        for j, copy in enumerate(copies):
             copy.wait_recv()
-            total = total + buf4[a, j].astype(F32)
-        w_ref[a] = total
+            total = total + buf4[n, j].astype(F32)
+        w_ref[n] = total
     total = vec_sum[3]
     for j, copy in enumerate(vec_hops[3]):
         copy.wait_recv()
@@ -1335,9 +1461,16 @@
             copy.wait_send()
     wait_all(local)
     wait_all(tokens)
-
-
-def exchange_out(grads, grad_tok, vectors, n_seq, n_ten, half, rows):
+    for here, away, near in shared:
+        pl.when(here)(near.wait)
+        pl.when(jnp.logical_not(here))(away.wait_send)
+    for i in range(n_seq):
+        pl.when(jnp.logical_not(2 * c + i == t))(arriving[i].wait_recv)
+
+
+def exchange_out(ffn_grads, attn_grads, grad_tok, vectors, n_seq, n_ten, half, rows):
+    grads = (*attn_grads, *ffn_grads)
+    ffn, attn = len(ffn_grads), len(attn_grads)
     height, width = grads[0].shape
     hw, count, group = height // n_ten, len(grads), n_seq * n_ten
     vmem = pl.BlockSpec(memory_space=pltpu.VMEM)
@@ -1345,28 +1478,26 @@
     hops = 3 + n_ten - 1
     return pl.pallas_call(
         functools.partial(exchange_out_kernel, (n_seq, n_ten, half, rows)),
-        in_specs=[vmem] * 6,
-        out_specs=[vmem, any_spec(), vmem],
+        in_specs=[vmem] * (count + 2),
+        out_specs=[vmem, vmem, any_spec(), vmem],
         out_shape=[
-            jax.ShapeDtypeStruct((count, hw, LANES), F32),
+            jax.ShapeDtypeStruct((attn, hw, LANES), F32),
+            jax.ShapeDtypeStruct((ffn, height, LANES), F32),
             jax.ShapeDtypeStruct((n_seq * half, rows, width), BF),
             jax.ShapeDtypeStruct(vectors.shape, F32),
         ],
         scratch_shapes=[
             pltpu.VMEM((count, 2, 2, height, LANES), BF),
-            pltpu.VMEM((count, 2, 2, height, LANES), BF),
-            pltpu.VMEM((count, 2, height, LANES), BF),
             pltpu.VMEM((count, 2, height, LANES), BF),
             pltpu.VMEM((count, height, LANES), BF),
-            pltpu.VMEM((count, height, LANES), BF),
-            pltpu.VMEM((count, n_ten - 1, hw, LANES), BF),
+            pltpu.VMEM((attn, n_ten - 1, hw, LANES), BF),
             pltpu.VMEM((hops,) + vectors.shape, F32),
             pltpu.VMEM((4,) + vectors.shape, F32),
-            dma((group,)), dma((group,)),
+            dma((group + 1,)), dma((group + 1,)),
             dma((count, 4)), dma((count, 4)),
             dma((count, 2)), dma((count, 2)),
             dma((count,)), dma((count,)),
-            dma((count, n_ten - 1)), dma((count, n_ten - 1)),
+            dma((attn, n_ten - 1)), dma((attn, n_ten - 1)),
             dma((hops,)), dma((hops,)),
             dma((2,)),
         ],
@@ -1408,68 +1539,79 @@
 ):
     rows_local, windows, width = tokens.shape
     n_dp, n_seq, n_ten = lax.axis_size("dp"), lax.axis_size("seq"), lax.axis_size("tensor")
-    seq_index, ten_index = lax.axis_index("seq"), lax.axis_index("tensor")
-    shard_index = lax.axis_index("dp") * n_seq + seq_index
+    dp_index, seq_index, ten_index = lax.axis_index("dp"), lax.axis_index("seq"), lax.axis_index("tensor")
+    shard_index = dp_index * n_seq + seq_index
+    core = dp_index % 2
+    place = seq_index * 2 + core
     half = windows // n_seq
     length = rows_local * n_seq * n_ten
-    share = length // n_ten
-    hw = w_query.shape[1]
+    share = length // QUAD
+    hw = width // QUAD
     slots = masked_rows.shape[1]
-    part = slots // n_ten
+    part = slots // QUAD
 
     live = jnp.arange(windows) < window_counts[0]
     valid = (masked_rows < length) & live[:, None]
-    count = jnp.full((8, LANES), jnp.sum(valid.astype(jnp.int32)))
-    both_tok, all_q, all_k, all_v, all_out, counts = exchange_in(
-        jnp.swapaxes(tokens, 0, 1), w_query, w_key, w_value, w_out, count, n_dp, n_seq, n_ten
-    )
-    loss_weight = LOSS_SCALE / jnp.sum(counts[:, 0, 0]).astype(F32)
+    coded = jnp.where(valid, masked_rows, length)
+    info = jnp.concatenate([coded, jnp.full((1, slots), jnp.sum(valid.astype(jnp.int32)))], axis=0)
+    info = jnp.pad(info, ((0, -(windows + 1) % 8), (0, -slots % LANES)))
+    both_tok, all_q, all_k, all_v, all_out, infos, peer_grad = exchange_in(
+        jnp.swapaxes(tokens, 0, 1), w_query, w_key, w_value, w_out, info, out_grad, n_dp, n_seq, n_ten
+    )
+    loss_weight = LOSS_SCALE / jnp.sum(infos[:, windows, 0]).astype(F32)
+    pick_one = lambda x, at: lax.dynamic_index_in_dim(x, at, 0, keepdims=False)
     first_window = seq_index * half
-    my_rows = lax.dynamic_slice_in_dim(masked_rows, first_window, half, 0)
-    my_valid = lax.dynamic_slice_in_dim(valid, first_window, half, 0)
-    cot = lax.dynamic_slice_in_dim(out_grad, first_window, half, 0).astype(F32) * loss_weight
-    cot = jnp.where(my_valid[:, :, None], cot, 0.0)
-    own_rows = lax.dynamic_index_in_dim(my_rows, ten_index, 0, keepdims=False)
-    own_valid = lax.dynamic_index_in_dim(my_valid, ten_index, 0, keepdims=False)
-    left_rows, left_valid = my_rows[n_ten], my_valid[n_ten]
+    my_coded = lax.dynamic_slice_in_dim(coded, first_window, n_ten, 0)
+    my_grad = lax.dynamic_slice_in_dim(out_grad, first_window, n_ten, 0)
+    pair_infos = lax.dynamic_slice_in_dim(infos, dp_index - core, 2, 0)
+    left_coded = jnp.stack([pair_infos[i // n_seq, i % n_seq * half + n_ten, :slots] for i in range(n_ten)])
+    own_left = jnp.stack([out_grad[i * half + n_ten] for i in range(n_seq)])
+    left_grad = jnp.where(core == 0, jnp.concatenate([own_left, peer_grad]), jnp.concatenate([peer_grad, own_left]))
+    weigh = lambda grad, rows: jnp.where((rows < length)[..., None], grad.astype(F32) * loss_weight, 0.0)
+
+    own_rows, left_rows = pick_one(my_coded, ten_index), pick_one(left_coded, ten_index)
     every = jnp.arange(length)
-    left_every = jnp.swapaxes(every.reshape(n_seq, n_ten, rows_local), 0, 1).reshape(n_ten, share)
-    my_left = lax.dynamic_index_in_dim(left_every, ten_index, 0, keepdims=False)
-    left_every = left_every.reshape(length)
-    own_pick = ((own_rows[:, None] == every[None, :]) & own_valid[:, None]).astype(BF)
-    left_pick = ((left_rows[:, None] == left_every[None, :]) & left_valid[:, None]).astype(BF)
-    part_match = (left_rows[:, None] == my_left[None, :]) & left_valid[:, None]
+    my_left = place * share + jnp.arange(share)
+    own_pick = (own_rows[:, None] == every[None, :]).astype(BF)
+    left_pick = (left_rows[:, None] == every[None, :]).astype(BF)
+    part_match = left_rows[:, None] == my_left[None, :]
     part_pick = part_match.astype(BF)
+    left_here = jnp.where(jnp.any(part_match, axis=1), left_rows, length)
     my_cot = jnp.concatenate(
+        [weigh(pick_one(my_grad, ten_index), own_rows), weigh(pick_one(left_grad, ten_index), left_here)], axis=0
+    )
+
+    tables = [jnp.asarray(x) for x in position_tables(length)]
+    part_tables = [lax.dynamic_slice_in_dim(x, place * share, share, 0) for x in tables]
+    own_tables = tables + list(rotary_lanes(*rotary_tables(own_rows)))
+    left_tables = tables + list(rotary_lanes(*rotary_tables(left_rows)))
+
+    ffn = (w_gate, w_up, w_down)
+    first, q, k, v, *gathered = norm_qkv(
+        both_tok, norm1_gain, norm1_bias, all_q, all_k, all_v, tables, part_tables, ffn, n_ten
+    )
+    own_att, left_q, left_k, left_v, *gathered = attend_swap(q, k, v, gathered, length, n_ten)
+    left_att_part, *gathered = attend_left(left_q, left_k, left_v, gathered, n_ten)
+    out_both, att_m, gr2, own_gatt, left_gatt, grad_norm2, all_own, all_left = feed_forward(
+        both_tok, own_att, left_att_part, all_out, norm2_gain, norm2_bias, own_pick, part_pick, my_cot, ffn, gathered, n_ten
+    )
+
+    grad_w_out = t_dot(att_m, gr2).astype(BF)
+    left_back = back_left(left_q, left_gatt, left_k, left_v, left_pick, left_tables)
+    dq, dk, dv = back_swap(q, own_gatt, k, v, own_pick, own_tables, left_back)
+    all_own, dq, dk, dv = lax.optimization_barrier((all_own, dq, dk, dv))
+
+    second = jnp.concatenate([all_own.reshape(-1, width), all_left.reshape(-1, width)], axis=0)
+    part_of = lambda x: lax.dynamic_slice_in_dim(x, place * part, part, 1)
+    down_in = jnp.concatenate(
         [
-            lax.dynamic_index_in_dim(cot, ten_index, 0, keepdims=False),
-            jnp.where(jnp.any(part_match, axis=1, keepdims=True), cot[n_ten], 0.0),
+            weigh(my_grad, my_coded).reshape(n_ten * slots, width),
+            weigh(part_of(left_grad), part_of(left_coded)).reshape(n_ten * part, width),
         ],
         axis=0,
-    )
-
-    tables = [jnp.asarray(x) for x in position_tables(length)]
-    by_block = [x.reshape(n_seq, n_ten, rows_local, LANES) for x in tables]
-    part_tables = [lax.dynamic_index_in_dim(x, ten_index, 1, keepdims=False).reshape(share, LANES) for x in by_block]
-    left_tables = [jnp.swapaxes(x, 0, 1).reshape(length, LANES) for x in by_block]
-    own_tables = tables + list(rotary_lanes(*rotary_tables(own_rows)))
-    left_tables = left_tables + list(rotary_lanes(*rotary_tables(left_rows)))
-
-    first, q, k, v = norm_qkv(both_tok, norm1_gain, norm1_bias, all_q, all_k, all_v, tables, part_tables)
-    own_att, left_q, left_k, left_v = attend_swap(q, k, v, length, n_ten)
-    left_att_part = attend_left(left_q, left_k, left_v, n_ten)
-    out_both, att_m, gr2, gatt, grad_norm2, second_m = feed_forward(
-        both_tok, own_att, left_att_part, all_out, norm2_gain, norm2_bias, own_pick, part_pick, my_cot,
-        w_gate, w_up, w_down, n_ten,
-    )
-    sent = lax.all_gather(second_m, "tensor", axis=0, tiled=False)
-
-    second = jnp.concatenate(
-        [sent[:, :slots].reshape(n_ten * slots, width), jnp.sum(sent[:, slots:].astype(F32), axis=0).astype(BF)], axis=0
-    )
+    ).astype(BF)
     gate = dot_n(second, w_gate)
     up = dot_n(second, w_up)
-    down_in = cot.astype(BF).reshape(half * slots, width)
     grad_hidden = dot_t(down_in, w_down)
     sig = jax.nn.sigmoid(gate)
     silu = gate * sig
@@ -1477,58 +1619,61 @@
     grad_gate = (grad_hidden * up * sig * (1.0 + gate * (1.0 - sig))).astype(BF)
     grad_up = (grad_hidden * silu).astype(BF)
     grad_w_ffn = [
-        t_dot(second, grad_gate).astype(BF), t_dot(second, grad_up).astype(BF), t_dot(down_in, hidden_m).astype(BF)
+        t_dot(grad_gate, second).astype(BF), t_dot(grad_up, second).astype(BF), t_dot(hidden_m, down_in).astype(BF)
     ]
-
-    grad_w_out = t_dot(att_m, gr2).astype(BF)
-    left_back = back_left(left_q, gatt[slots:], left_k, left_v, left_pick, left_tables, n_ten)
-    dq, dk, dv = back_swap(q, gatt[:slots], k, v, own_pick, own_tables, left_back, n_ten)
-    grad_w_attn = [t_dot(d, first).astype(BF) for d in (dq, dk, dv)] + [grad_w_out]
+    grad_w_attn = [grad_w_out] + [t_dot(d, first).astype(BF) for d in (dq, dk, dv)]
     grad_both, grad_norm1 = token_back(
         both_tok, (dq, dk, dv), (all_q, all_k, all_v), norm1_gain,
         jnp.concatenate([own_pick, part_pick], axis=1), gr2.reshape(2, slots, width),
     )
 
-    def send_back(x):
-        own = lax.all_to_all(
-            x[:length].reshape(n_seq * n_ten, rows_local, width), ("seq", "tensor"), 0, 0, tiled=True
-        ).reshape(n_seq, n_ten, rows_local, width)
-        left = lax.all_to_all(x[length:].reshape(n_seq, rows_local, width), "seq", 0, 0, tiled=True)
-        both = jnp.concatenate([own, left[:, None]], axis=1).reshape(windows, rows_local, width)
-        return jnp.swapaxes(both, 0, 1)
-
-    output = send_back(out_both)
+    own_out = lax.all_to_all(
+        out_both[:length].reshape(n_seq * n_ten, rows_local, width), ("seq", "tensor"), 0, 0, tiled=True
+    ).reshape(n_seq, n_ten, rows_local, width)
+    left_chunks = out_both[length:].reshape(n_seq, rows_local, width)
+    left_out = []
+    for turn in range(2):
+        perm = []
+        for d in range(n_dp):
+            for sx in range(n_seq):
+                for p in range(n_ten):
+                    to = d // 2 * 2 + p // 2, sx, d % 2 * 2 + (p % 2 ^ turn)
+                    perm.append(((d * n_seq + sx) * n_ten + p, (to[0] * n_seq + to[1]) * n_ten + to[2]))
+        left_out.append(lax.ppermute(pick_one(left_chunks, (ten_index + turn) % 2), ("dp", "seq", "tensor"), perm))
+    even = ten_index % 2 == 0
+    left_out = jnp.stack([jnp.where(even, left_out[0], left_out[1]), jnp.where(even, left_out[1], left_out[0])])
+    output = jnp.concatenate([own_out, left_out[:, None]], axis=1).reshape(windows, rows_local, width)
+    output = jnp.swapaxes(output, 0, 1)
     vectors = jnp.concatenate(
         [grad_norm1, grad_norm2, jnp.zeros((4, width), F32)], axis=0
     )
-    gw_attn, grad_tokens, vectors = exchange_out(grad_w_attn, grad_both, vectors, n_seq, n_ten, half, rows_local)
+    gw_attn, gw_ffn, grad_tokens, vectors = exchange_out(
+        grad_w_ffn, grad_w_attn, grad_both, vectors, n_seq, n_ten, half, rows_local
+    )
     grad_tokens = jnp.swapaxes(grad_tokens, 0, 1).astype(F32)
     small = width // (n_dp * n_seq * n_ten)
     vectors = lax.dynamic_slice_in_dim(vectors, (shard_index * n_ten + ten_index) * small, small, 1)
 
-    gw_gate, gw_up, gw_down = [
-        lax.psum_scatter(x, ("dp", "seq"), scatter_dimension=0, tiled=True).astype(F32) for x in grad_w_ffn
-    ]
     return (
         output,
         grad_tokens,
         vectors[0],
         vectors[1],
-        gw_attn[0].T,
         gw_attn[1].T,
         gw_attn[2].T,
-        gw_attn[3],
+        gw_attn[3].T,
+        gw_attn[0],
         vectors[2],
         vectors[3],
-        gw_gate,
-        gw_up,
-        gw_down.T,
+        gw_ffn[0].T,
+        gw_ffn[1].T,
+        gw_ffn[2],
     )
 
 
 def shards(tokens, *rest):
     n_dp, n_seq, n_ten = lax.axis_size("dp"), lax.axis_size("seq"), lax.axis_size("tensor")
-    whole = n_dp == 4 and n_seq == 2 and tokens.shape[1] == n_seq * (n_ten + 1)
+    whole = n_dp == 4 and n_seq == 2 and n_ten == 4 and tokens.shape[1] == n_seq * (n_ten + 1)
     return (window_shards if whole else block_shards)(tokens, *rest)
 
 

time: 649 us -> 554 us (0.85)
  waiting for transfers between devices: 56.4 us -> 0.01 us
  Pallas kernels: 476 us -> 443 us
  between operations: 16.1 us -> 2.91 us
    all_gather x1 -> x0, waiting for transfers between devices: 56.4 us -> none  [window_shards(): sent = lax.all_gather(second_m, 'tensor', axis=0, tiled=False)]
    pallas_call x1, Pallas kernels: 146 us -> 100 us  [feed_forward(): pl.pallas_call(functools.partial(feed_kernel, n_ten), grid=(n_ten * units...]
    pallas_call x1, Pallas kernels: 100 us -> 110 us  [exchange_out(): pl.pallas_call(functools.partial(exchange_out_kernel, (n_seq, n_ten, half...]
  transfers between devices with their start and end apart: 6 -> 3, of which waited for: 1 -> 0; matrix products, arithmetic and copies ran while one was open for 9% -> 13% of each run, Pallas kernels for 27% -> 30%
where the time goes in v4:
time: 554 us; the launch traced here: 546 us
  Pallas kernels  443 us (80%)
  matrix products  42.2 us (8%)
  other arithmetic  26 us (5%)
  local copies, waits for them, and re-layouts  22.5 us (4%)
  starting transfers between devices  9.1 us (2%)
    pallas_call x1, Pallas kernels, exchange_out(): pl.pallas_call(functools.partial(exchange_out_kernel, (n_seq, n_ten, half...  110 us
    pallas_call x1, Pallas kernels, feed_forward(): pl.pallas_call(functools.partial(feed_kernel, n_ten), grid=(n_ten * units...  100 us
    pallas_call x1, Pallas kernels, exchange_in(): pl.pallas_call(functools.partial(exchange_in_kernel, (n_seq, n_ten, windo...  79 us
    pallas_call x1, Pallas kernels, attend_swap(): pl.pallas_call(functools.partial(attend_swap_kernel, n_ten, length), grid...  46.8 us
    pallas_call x1, Pallas kernels, norm_qkv(): pl.pallas_call(functools.partial(qkv_kernel, n_ten), grid=(rows // tile,)...  34.8 us
    dot_general x7, matrix products, t_dot(): lax.dot_general(a, b, (((0,), (0,)), ((), ())), preferred_element_type=F32)  31 us
    pallas_call x1, Pallas kernels, back_swap(): pl.pallas_call(back_swap_kernel, grid=(width // LANES,), in_specs=back_sp...  27.4 us
    pallas_call x1, Pallas kernels, attend_left(): pl.pallas_call(functools.partial(attend_left_kernel, n_ten), grid=(QUAD,...  20.6 us
  transfers between devices with their start and end apart: 3, of which 0 were waited for; matrix products, arithmetic and copies ran while one was open for 13% of the time, Pallas kernels for 30%

profile of v4, /device:TPU:0, one launch (start us, length us, event | category | flops | bytes accessed | tf_op | source)
XLA Modules:
  0.0 546.3 jit_solution(3606770477911872872)
XLA Ops:
  1.3 1.4 convert_reduce_fusion
  2.8 0.8 fusion.2.pick_ref
  3.6 1.3 select_select_fusion.count_ref
  4.9 1.9 fusion.23
  6.8 79.0 %exchange_in.1 = (bf16[1280,1024]{1,0:T(8,128)(2,1)}, bf16[1024,1024]{1,0:T(8,128)(2,1)}, bf16[1024,1024]{1,0:T(8,128)(2,1)}, bf16[1024,1024]{1,0:T(8,128)(2,1)}...) custom-call(bf16[10,128,1024]{2,1,0:T(8,128)(2,1)} %bitcast.88, ...), custom_call_target="tpu_custom_call" | custom-call | tf_op jit(solution)/shard_map/exchange_in/pallas_call | solution.py:598
  85.8 1.4 slice_reduce_fusion
  89.4 2.0 maximum_select_fusion
  91.4 1.0 copy-done.1
  92.6 1.2 pad_maximum_fusion.3.cot_ref
  93.8 1.7 constant_dynamic-slice_fusion.8
  95.5 34.8 %norm_qkv.1 = (bf16[1280,1024]{1,0:T(8,128)(2,1)}, bf16[1280,1024]{1,0:T(8,128)(2,1)}, bf16[1280,1024]{1,0:T(8,128)(2,1)}, bf16[1280,1024]{1,0:T(8,128)(2,1)}, b...) custom-call(bf16[1280,1024]{1,0:T(8,128)(2,1)} %get-tuple-element.62.x_ref.tok_ref, ...), custom_call_target="tpu_custom_call" | custom-call | flops 8053063680 | bytes 20971520 | tf_op jit(solution)/shard_map/norm_qkv/pallas_call | solution.py:673
  130.3 46.8 %attend_swap.1 = (bf16[1024,1024]{1,0:T(8,128)(2,1)}, bf16[1024,256]{1,0:T(8,128)(2,1)}, bf16[1024,256]{1,0:T(8,128)(2,1)}, bf16[1024,256]{1,0:T(8,128)(2,1)}, b...) custom-call(bf16[1280,1024]{1,0:T(8,128)(2,1)} %get-tuple-element.66, ...), custom_call_target="tpu_custom_call", output_to_operand_aliasing={{4}: (6, {}), {5}: (7, {}), {6}: (8, {})} | custom-call | flops 17179869184 | bytes 8388608 | tf_op jit(solution)/shard_map/attend_swap/pallas_call | solution.py:844
  177.1 20.6 %attend_left.1 = (bf16[256,1024]{1,0:T(8,128)(2,1)}, bf16[1024,4096]{1,0:T(8,128)(2,1)}, bf16[1024,4096]{1,0:T(8,128)(2,1)}, bf16[4096,1024]{1,0:T(8,128)(2,1)}) custom-call(bf16[1024,256]{1,0:T(8,128)(2,1)} %get-tuple-element.73.q_ref, bf16[1024,256]{1,0:T(8,128)(2,1)} %get-tuple-element.74.k_ref, ...), custom_call_target="tpu_custom_call", output_to_operand_aliasing={{1}: (3, {}), {2}: (4, {}), {3}: (5, {})} | custom-call | flops 4294967296 | bytes 2097152 | tf_op jit(solution)/shard_map/attend_left/pallas_call | solution.py:756
  197.7 100.2 %feed_forward.1 = (bf16[1280,1024]{1,0:T(8,128)(2,1)}, bf16[320,1024]{1,0:T(8,128)(2,1)}, bf16[320,1024]{1,0:T(8,128)(2,1)}, bf16[160,1024]{1,0:T(8,128)(2,1)}, ...) custom-call(bf16[1280,1024]{1,0:T(8,128)(2,1)} %get-tuple-element.62, ...), custom_call_target="tpu_custom_call", output_to_operand_aliasing={{8}: (12, {}), {9}: (13, {}), {10}: (14, {})} | custom-call | flops 42949672960 | bytes 25165824 | tf_op jit(solution)/shard_map/feed_forward/pallas_call | solution.py:1202
  297.9 1.9 slice.68
  299.8 1.8 dynamic-slice_bitcast_fusion.1
  301.6 3.6 collective-permute-start
  305.9 3.1 slice.67
  308.9 4.8 all-to-all-start
  315.1 1.5 fusion.3.pick_ref
  317.8 0.9 pad_maximum_fusion.7
  318.7 0.9 pad_maximum_fusion.9
  319.5 7.3 %back_left.1 = (bf16[1024,256]{1,0:T(8,128)(2,1)}, bf16[1024,256]{1,0:T(8,128)(2,1)}, bf16[1024,256]{1,0:T(8,128)(2,1)}) custom-call(bf16[1024,256]{1,0:T(8,128)(2,1)} %get-tuple-element.73.q_ref, bf16[160,256]{1,0:T(8,128)(2,1)} %get-tuple-element.91.g_ref, bf16[1024,256]{1,0:T(8,128)(2,1)} %get-tuple-element.74.k_ref, ...), custom_call_target="tpu_custom_call" | custom-call | flops 1006632960 | bytes 3145728 | tf_op jit(solution)/shard_map/back_left/pallas_call | solution.py:918
  326.8 27.4 %back_swap.1 = (bf16[1280,1024]{1,0:T(8,128)(2,1)}, bf16[1280,1024]{1,0:T(8,128)(2,1)}, bf16[1280,1024]{1,0:T(8,128)(2,1)}) custom-call(bf16[1280,1024]{1,0:T(8,128)(2,1)} %get-tuple-element.66.q_ref.q_all, bf16[160,1024]{1,0:T(8,128)(2,1)} %get-tuple-element.90.g_ref, bf16[1280,1024]{1,0:T(8,128)(2,1)} %get-tuple-element.67.k_ref.k_all, ...), custom_call_target="tpu_custom_call" | custom-call | flops 4026531840 | bytes 12582912 | tf_op jit(solution)/shard_map/back_swap/pallas_call | solution.py:981
  354.3 5.8 %fusion.21 = f32[800,1024]{1,0:T(8,128)} fusion(bf16[1024,1024]{1,0:T(8,128)(2,1)} %wg_ref.3, bf16[160,1024]{1,0:T(8,128)(2,1)} %bitcast.112, bf16[640,1024]{1,0:T(8,128)(2,1)} %bitcast.107), kind=kOutput, calls=%fused_computation.93 | convolution fusion | flops 1680998400 | bytes 7012352 | tf_op jit(solution)/shard_map/dot_general | solution.py:323
  360.1 3.5 fusion.22
  363.7 0.8 pad_maximum_fusion.6.pick_ref
  364.5 4.2 convolution_convert_fusion.2.gq_ref
  368.7 4.1 convolution_convert_fusion.1.gk_ref
  372.8 4.4 convolution_convert_fusion.gv_ref
  377.4 1.2 select_convert_fusion.1
  378.9 2.7 convolution_convert_fusion.3.go_ref
  381.7 1.9 fusion.1
  384.1 3.9 convolution_convert_fusion.5.gu_ref
  388.0 17.1 %token_back.1 = (bf16[1280,1024]{1,0:T(8,128)(2,1)}, f32[2,1024]{1,0:T(2,128)}) custom-call(bf16[1280,1024]{1,0:T(8,128)(2,1)} %get-tuple-element.62.x_ref.tok_ref, bf16[1280,1024]{1,0:T(8,128)(2,1)} %get-tuple-element.98.dq_ref, bf16[1280,1024]{1,0:T(8,128)(2,1)} %get-tuple-element.100.dk_ref, bf16[1280,1024]{1,0:T(8,128)(2,1)} %get-tuple-element.101.dv_ref, ...), custom_call_target="tpu_custom_call" | custom-call | flops 8053063680 | bytes 20971520 | tf_op jit(solution)/shard_map/token_back/pallas_call | solution.py:1274
  405.2 1.4 maximum_maximum_fusion.vec_ref
  406.7 6.9 %convolution_convert_fusion.4.gd_ref = bf16[1024,1024]{1,0:T(8,128)(2,1)} fusion(f32[800,1024]{1,0:T(8,128)} %fusion.22, bf16[160,1024]{1,0:T(8,128)(2,1)S(1)} %bitcast.94, bf16[640,1024]{1,0:T(8,128)(2,1)S(1)} %bitcast.92, f32[800,1024]{1,0:T(8,128)} %fusion.21), kind=kOutput, calls=%fused_computation.12 | convolution fusion | flops 1686962176 | bytes 10289152 | tf_op jit(solution)/shard_map/dot_general | solution.py:327
  413.6 4.8 convolution_convert_fusion.6.gg_ref
  418.3 110.3 %exchange_out.1 = (f32[4,256,128]{2,1,0:T(8,128)}, f32[3,1024,128]{2,1,0:T(8,128)}, bf16[10,128,1024]{2,1,0:T(8,128)(2,1)}, f32[8,1024]{1,0:T(8,128)}) custom-call(bf16[1024,1024]{1,0:T(8,128)(2,1)} %convolution_convert_fusion.3.go_ref, bf16[1024,1024]{1,0:T(8,128)(2,1)} %convolution_convert_fusion.2.gq_ref, ...), custom_call_target="tpu_custom_call" | custom-call | tf_op jit(solution)/shard_map/exchange_out/pallas_call | solution.py:1479
  528.6 1.9 slice_bitcast_fusion.3
  530.6 2.3 slice_bitcast_fusion
  532.8 3.0 convert_bitcast_fusion
  536.6 0.8 copy.39
  538.1 0.8 copy.41
  538.8 1.0 copy.42
  539.8 1.0 copy.43
  541.4 1.1 select_bitcast_fusion.1
  542.5 3.3 pad_maximum_fusion
  (92 shorter events, 8.2 us)
Async XLA Ops:
  2.8 0.8 copy-start.12
  6.8 85.6 %copy-start = (bf16[10,160,1024]{2,1,0:T(8,128)(2,1)S(1)}, bf16[10,160,1024]{2,1,0:T(8,128)(2,1)}, u32[]{:S(2)}) copy-start(bf16[10,160,1024]{2,1,0:T(8,128)(2,1)} %rows_ref.1) | copy-start | bytes 9830404
  87.9 5.9 %copy-start.10 = (s32[4,160]{1,0:T(4,128)}, s32[4,160]{1,0:T(4,128)S(1)}, u32[]{:S(2)}) copy-start(s32[4,160]{1,0:T(4,128)S(1)} %pad_add_fusion) | copy-start | bytes 7684
  88.0 5.9 %copy-start.9 = (s32[1,160]{1,0:T(1,128)}, s32[1,160]{1,0:T(1,128)S(1)}, u32[]{:S(2)}) copy-start(s32[1,160]{1,0:T(1,128)S(1)} %constant_dynamic-slice_fusion.5) | copy-start | bytes 1924
  91.4 1.1 copy-start.1
  301.6 239.8 %collective-permute-start = (bf16[128,1024]{1,0:T(8,128)(2,1)}, bf16[128,1024]{1,0:T(8,128)(2,1)}, u32[]{:S(2)}, u32[]{:S(2)}) collective-permute-start(bf16[128,1024]{1,0:T(8,128)(2,1)} %get-tuple-element.135), channel_id=1, source_target_pairs={{0,0},{1,1},{2,8},{3,9},{4,4},{5,5},{6,12},{7,13},{8,2},{9,3},{10,... | collective-permute-start | bytes 786440 | tf_op jit(solution)/shard_map/ppermute | solution.py:1642
  305.1 236.2 %collective-permute-start.1 = (bf16[128,1024]{1,0:T(8,128)(2,1)S(1)}, bf16[128,1024]{1,0:T(8,128)(2,1)}, u32[]{:S(2)}, u32[]{:S(2)}) collective-permute-start(bf16[128,1024]{1,0:T(8,128)(2,1)S(1)} %get-tuple-element.136), channel_id=1, source_target_pairs={{0,1},{1,0},{2,9},{3,8},{4,5},{5,4},{6,13},{7,12},{8,3},{9,2},{10,... | collective-permute-start | bytes 786440 | tf_op jit(solution)/shard_map/ppermute | solution.py:1642
  308.9 233.6 %all-to-all-start = ((bf16[8,128,1024]{2,1,0:T(8,128)(2,1)}), bf16[8,128,1024]{2,1,0:T(8,128)(2,1)}, u32[]{:S(2)}, u32[]{:S(2)}) async-start(bf16[8,128,1024]{2,1,0:T(8,128)(2,1)} %bitcast.87), calls=%async_computation | async-start | bytes 4194304 | tf_op jit(solution)/shard_map/all_to_all | solution.py:1630
  354.2 5.8 %copy-start.15 = (bf16[1024,1024]{1,0:T(8,128)(2,1)S(1)}, bf16[1024,1024]{1,0:T(8,128)(2,1)}, u32[]{:S(2)}) copy-start(bf16[1024,1024]{1,0:T(8,128)(2,1)} %wu_ref.3) | copy-start | bytes 6291460
  354.3 5.8 %copy-start.17 = (bf16[4,160,1024]{2,1,0:T(8,128)(2,1)S(1)}, bf16[4,160,1024]{2,1,0:T(8,128)(2,1)}, u32[]{:S(2)}) copy-start(bf16[4,160,1024]{2,1,0:T(8,128)(2,1)} %get-tuple-element.102) | copy-start | bytes 3932164
  354.3 5.8 %copy-start.20 = (bf16[4,40,1024]{2,1,0:T(8,128)(2,1)S(1)}, bf16[4,40,1024]{2,1,0:T(8,128)(2,1)}, u32[]{:S(2)}) copy-start(bf16[4,40,1024]{2,1,0:T(8,128)(2,1)} %get-tuple-element.103) | copy-start | bytes 983044
  360.1 3.6 copy-start.3
  360.1 3.6 copy-start.6
  360.1 4.3 copy-start.24
  360.1 4.3 copy-start.32
  364.5 4.2 copy-start.25
  368.7 4.1 copy-start.26
  372.8 4.4 copy-start.11
  372.8 5.7 %copy-start.14 = (pred[4,160]{1,0:T(4,128)(4,1)S(1)}, pred[4,160]{1,0:T(4,128)(4,1)}, u32[]{:S(2)}) copy-start(pred[4,160]{1,0:T(4,128)(4,1)} %fusion.10) | copy-start | bytes 1924
  377.3 1.7 copy-start.19
  377.3 1.7 copy-start.23
  378.5 3.1 copy-start.7
  378.9 2.7 copy-start.4
  378.9 2.7 copy-start.16
  381.6 1.9 copy-start.18
  381.6 1.9 copy-start.21
  381.7 2.4 copy-start.29
  384.1 3.9 copy-start.27
  388.0 17.2 %copy-start.13 = (f32[2,1024]{1,0:T(2,128)S(1)}, f32[2,1024]{1,0:T(2,128)}, u32[]{:S(2)}) copy-start(f32[2,1024]{1,0:T(2,128)} %get-tuple-element.106) | copy-start | bytes 24580
  388.0 18.6 %copy-start.5 = (bf16[4,160,1024]{2,1,0:T(8,128)(2,1)S(1)}, bf16[4,160,1024]{2,1,0:T(8,128)(2,1)}, u32[]{:S(2)}) copy-start(bf16[4,160,1024]{2,1,0:T(8,128)(2,1)} %copy-done.4) | copy-start | bytes 3932164
  388.0 18.6 %copy-start.8 = (bf16[4,40,1024]{2,1,0:T(8,128)(2,1)S(1)}, bf16[4,40,1024]{2,1,0:T(8,128)(2,1)}, u32[]{:S(2)}) copy-start(bf16[4,40,1024]{2,1,0:T(8,128)(2,1)} %copy-done.7) | copy-start | bytes 983044
  406.6 6.9 %copy-start.22 = (bf16[4,40,1024]{2,1,0:T(8,128)(2,1)S(1)}, bf16[4,40,1024]{2,1,0:T(8,128)(2,1)}, u32[]{:S(2)}) copy-start(bf16[4,40,1024]{2,1,0:T(8,128)(2,1)} %get-tuple-element.103) | copy-start | bytes 983044
  406.6 6.9 %copy-start.28 = (f32[800,1024]{1,0:T(8,128)S(1)}, f32[800,1024]{1,0:T(8,128)}, u32[]{:S(2)}) copy-start(f32[800,1024]{1,0:T(8,128)} %copy-done.27) | copy-start | bytes 9830404
  406.6 6.9 %copy-start.30 = (f32[800,1024]{1,0:T(8,128)S(1)}, f32[800,1024]{1,0:T(8,128)}, u32[]{:S(2)}) copy-start(f32[800,1024]{1,0:T(8,128)} %fusion.21) | copy-start | bytes 9830404
  406.7 6.9 %copy-start.31 = (f32[800,1024]{1,0:T(8,128)S(1)}, f32[800,1024]{1,0:T(8,128)}, u32[]{:S(2)}) copy-start(f32[800,1024]{1,0:T(8,128)} %fusion.22) | copy-start | bytes 9830404
  528.6 4.2 copy-start.2

commit v5 on v4

--- a/solution.py
+++ b/solution.py
@@ -386,11 +386,11 @@
         dp, sx, t = lax.axis_index("dp"), lax.axis_index("seq"), lax.axis_index("tensor")
         y, c = dp // 2, dp % 2
         gate_ref, up_ref, down_ref = gathered
-        self.refs, self.own = (gate_ref, up_ref, down_ref), own
+        self.refs, self.own = (gate_ref, up_ref, down_ref, down_ref), own
         self.width, self.units = gate_ref.shape[0], gate_ref.shape[1] // n_ten
         self.send, self.recv, self.c = send, recv, c
         s_xy, s_yx = c * 4 + y * 2 + sx, c * 4 + sx * 2 + y
-        self.slices = (s_xy, s_yx, s_xy)
+        self.slices = (s_xy, s_yx, s_xy, s_yx)
         self.x_peer, self.y_peer, self.c_peer = {"seq": 1 - sx}, {"dp": (dp + 2) % 4}, {"dp": 2 * y + 1 - c}
         side = t // 2
         middle = jnp.minimum(t, n_ten - 1 - t)
@@ -401,19 +401,19 @@
         self.t, self.middle, self.mirror = t, middle, mirror
 
     def shard(self, ref, k, first, count, which):
-        size, units = self.width // 8, self.units
+        size, cols, units = self.width // 8, self.width // 2, self.units
         rows = pl.multiple_of(first * (size if k < 2 else units // 8), 16)
         if k < 2:
             at = 0 if which is None else pl.multiple_of(which * units, units)
             return ref.at[pl.ds(rows, count * size), pl.ds(at, units)]
         at = rows if which is None else pl.multiple_of(which * units + rows, 16)
-        return ref.at[pl.ds(at, count * (units // 8)), :]
+        return ref.at[pl.ds(at, count * (units // 8)), pl.ds((k - 2) * cols, cols)]
 
     def along(self, which, to, slot, number, own=False):
         copies = []
-        for k in range(3):
+        for k in range(4):
             dst = self.shard(self.refs[k], k, self.slices[k], 1, which)
-            src = self.shard(self.own[k], k, self.slices[k], 1, None) if own else dst
+            src = self.shard(self.own[min(k, 2)], k, self.slices[k], 1, None) if own else dst
             copies.append(remote(src, dst, self.send.at[number, k], self.recv.at[slot, k], {"tensor": to}))
         return copies
 
@@ -437,8 +437,8 @@
 
     def hop(self, i, h):
         copies = []
-        for k in range(3):
-            xy = k != 1
+        for k in range(4):
+            xy = k % 2 == 0
             peer, first, count = (
                 (self.x_peer if xy else self.y_peer, self.slices[k], 1),
                 (self.y_peer if xy else self.x_peer, self.slices[k] // 2 * 2, 2),
@@ -460,7 +460,7 @@
 
 
 def route_sems():
-    return [pltpu.SemaphoreType.DMA((14, 3)), pltpu.SemaphoreType.DMA((13, 3))]
+    return [pltpu.SemaphoreType.DMA((14, 4)), pltpu.SemaphoreType.DMA((13, 4))]
 
 
 def exchange_in_kernel(
@@ -556,7 +556,7 @@
         pl.when(here)(near.start)
         pl.when(jnp.logical_not(here))(away.start)
     peer_rows = [
-        remote(rows_ref.at[i * half + n_ten], peer_rows_ref.at[i], rows_send.at[i], rows_recv.at[i], c_peer)
+        remote(rows_ref.at[i * half + n_ten], peer_rows_ref.at[2 * c + i], rows_send.at[i], rows_recv.at[i], c_peer)
         for i in range(n_seq)
     ]
     start_all(peer_rows)
@@ -568,6 +568,10 @@
     for i, (w_ref, out, s, by_rows) in enumerate(weights):
         local.append(pltpu.make_async_copy(w_ref, block(out, by_rows, 0, slices, t), local_sem.at[2 + i]))
     local.append(pltpu.make_async_copy(count_ref, counts_ref.at[dp], local_sem.at[6]))
+    for i in range(n_seq):
+        local.append(
+            pltpu.make_async_copy(rows_ref.at[i * half + n_ten], peer_rows_ref.at[2 * c + i], local_sem.at[7 + i])
+        )
     start_all(local)
     for k in range(1, 4):
         for earlier in stage[k - 1]:
@@ -602,7 +606,7 @@
         out_shape=[jax.ShapeDtypeStruct(((group + n_seq) * rows, width), BF)]
         + [square] * 4
         + [jax.ShapeDtypeStruct((n_dp,) + count.shape, count.dtype)]
-        + [jax.ShapeDtypeStruct((n_seq,) + out_grad.shape[1:], BF)],
+        + [jax.ShapeDtypeStruct((2 * n_seq,) + out_grad.shape[1:], BF)],
         scratch_shapes=[
             pltpu.SemaphoreType.DMA((group + 1,)),
             pltpu.SemaphoreType.DMA((group + 1,)),
@@ -612,7 +616,7 @@
             pltpu.SemaphoreType.DMA((3,)),
             pltpu.SemaphoreType.DMA((2,)),
             pltpu.SemaphoreType.DMA((2,)),
-            pltpu.SemaphoreType.DMA((7,)),
+            pltpu.SemaphoreType.DMA((9,)),
         ],
         compiler_params=pltpu.CompilerParams(collective_id=0, has_side_effects=True),
         name="exchange_in",
@@ -999,7 +1003,7 @@
 
 def feed_kernel(
     n_ten, tok_ref, att_ref, left_ref, wo_ref, gain_ref, bias_ref, pick_ref, part_pick_ref, cot_ref, wg_ref, wu_ref, wd_ref,
-    ag_in, au_in, ad_in, out_ref, att_m_ref, gr2_ref, gatt_ref, left_gatt_ref, vec_ref, all_own_ref, all_left_ref,
+    ag_in, au_in, ad_in, out_ref, out_left_ref, att_m_ref, gr2_ref, gatt_ref, left_gatt_ref, vec_ref, all_own_ref, all_left_ref,
     ag_ref, au_ref, ad_ref,
     x_ref, acc_ref, normed_ref, inv_ref, grad_ref, g_buf, u_buf, d_buf, rows_buf, rows_parts, own_m, left_m, gatt_buf, gatt_parts,
     buf_sem, small_send, small_recv, line_send, line_recv, local_sem, send, recv,
@@ -1180,7 +1184,10 @@
             [jnp.sum(grad * normed, axis=0, keepdims=True), jnp.sum(grad, axis=0, keepdims=True)], axis=0
         )
         start_all(gatt_copies)
-        out_ref[...] = acc_ref[...].astype(BF)
+        out_ref[...] = acc_ref[:length, :].astype(BF)
+        chunk = out_left_ref.shape[1]
+        for i in range(2):
+            out_left_ref[(i + route.t) % 2] = acc_ref[length + i * chunk : length + (i + 1) * chunk, :].astype(BF)
         sent_all(route.hop(2, 1) + route.hop(2, 2) + route.hop(3, 0) + route.hop(3, 1) + route.hop(3, 2))
         wait_all(gatt_copies)
         whole = gatt_buf[:, pl.ds(pl.multiple_of(place * hw, hw), hw)].astype(F32)
@@ -1205,17 +1212,18 @@
         in_specs=[once(x.shape) for x in (tok, att, left_att, w_out)]
         + [once((1, width)), once((1, width)), once(pick.shape), once(part_pick.shape), once(cot.shape)]
         + [any_spec()] * 6,
-        out_specs=[whole(rows, width), whole(masked, width), whole(masked, width), whole(slots, width), whole(slots, hw)]
+        out_specs=[whole(*att.shape), whole(2, left_att.shape[0] // 2, width)]
+        + [whole(masked, width), whole(masked, width), whole(slots, width), whole(slots, hw)]
         + [whole(2, width)]
         + [any_spec()] * 5,
         out_shape=[
-            jax.ShapeDtypeStruct((rows, width), BF), low, low,
+            jax.ShapeDtypeStruct(att.shape, BF), jax.ShapeDtypeStruct((2, left_att.shape[0] // 2, width), BF), low, low,
             jax.ShapeDtypeStruct((slots, width), BF), jax.ShapeDtypeStruct((slots, hw), BF),
             jax.ShapeDtypeStruct((2, width), F32),
             jax.ShapeDtypeStruct((n_ten, slots, width), BF), jax.ShapeDtypeStruct((n_ten, slots // QUAD, width), BF),
         ]
         + [jax.ShapeDtypeStruct(w.shape, BF) for w in gathered],
-        input_output_aliases={12: 8, 13: 9, 14: 10},
+        input_output_aliases={12: 9, 13: 10, 14: 11},
         scratch_shapes=[
             pltpu.VMEM((rows + masked, width), BF),
             pltpu.VMEM((rows, width), F32),
@@ -1244,7 +1252,7 @@
             flops=8 * rows * width * n_ten * units, bytes_accessed=6 * width * n_ten * units, transcendentals=rows * n_ten * units
         ),
         name="feed_forward",
-    )(tok, att, left_att, w_out, gain.reshape(1, width), bias.reshape(1, width), pick, part_pick, cot, *ffn, *gathered)[:8]
+    )(tok, att, left_att, w_out, gain.reshape(1, width), bias.reshape(1, width), pick, part_pick, cot, *ffn, *gathered)[:9]
 
 
 def token_back_kernel(
@@ -1308,7 +1316,7 @@
     greet([{"seq": a, "tensor": b} for a, b in others] + [y_peer, c_peer] + beside)
     grads = (go_ref, gq_ref, gk_ref, gv_ref, gg_ref, gu_ref, gd_ref)
     count, attn = len(grads), w_ref.shape[0]
-    x_first = (True, False, False, False, True, False, False)
+    x_first = (False, False, False, False, False, True, True)
     height = gq_ref.shape[0]
     hw = height // n_ten
 
@@ -1407,45 +1415,52 @@
     vec_hops[0][0].wait_recv()
     vec_sum[1] = vec_sum[0] + vec_buf[0]
     start_all(vec_hops[1])
-    stage3 = []
-    for a in range(count):
+    stage3, stage4 = {}, {}
+
+    def second(a):
         for copy in stage2[a]:
             copy.wait_recv()
         for b in range(2):
             own = buf1.at[a, b, sx] if x_first[a] else buf1.at[a, y, b]
             add_rows(buf2.at[a, b], own, buf2.at[a, b])
         src, peer = (buf2.at[a, 1 - y], y_peer) if x_first[a] else (buf2.at[a, 1 - sx], x_peer)
-        copy = remote(src, buf3.at[a], send3.at[a], recv3.at[a], peer)
-        copy.start()
-        stage3.append(copy)
+        stage3[a] = remote(src, buf3.at[a], send3.at[a], recv3.at[a], peer)
+        stage3[a].start()
+
+    def third(a):
+        stage3[a].wait_recv()
+        own = buf2.at[a, y] if x_first[a] else buf2.at[a, sx]
+        if a >= attn:
+
+            def final(i, carry):
+                at = pl.ds(pl.multiple_of(i * hw, hw), hw)
+                ffn_ref[a - attn, at, :] = own[at, :].astype(F32) + buf3[a, at, :].astype(F32)
+                return carry
+
+            lax.fori_loop(0, height // hw, final, 0)
+            return
+        add_rows(buf3.at[a], own, buf3.at[a])
+        stage4[a] = []
+        for j, peer in enumerate(z_peers):
+            to = (t + 1 + j) % n_ten
+            src = buf3.at[a, pl.ds(pl.multiple_of(to * hw, hw), hw), :]
+            stage4[a].append(remote(src, buf4.at[a, j], send4.at[a, j], recv4.at[a, j], peer))
+        start_all(stage4[a])
+
     vec_hops[1][0].wait_recv()
     vec_sum[2] = vec_sum[1] + vec_buf[1]
     start_all(vec_hops[2])
-    stage4 = []
-    for a in range(count):
-        stage3[a].wait_recv()
-        own = buf2.at[a, y] if x_first[a] else buf2.at[a, sx]
-        if a >= attn:
-
-            def final(i, carry, a=a, own=own):
-                at = pl.ds(pl.multiple_of(i * hw, hw), hw)
-                ffn_ref[a - attn, at, :] = own[at, :].astype(F32) + buf3[a, at, :].astype(F32)
-                return carry
-
-            lax.fori_loop(0, height // hw, final, 0)
-            continue
-        add_rows(buf3.at[a], own, buf3.at[a])
-        copies = []
-        for j, peer in enumerate(z_peers):
-            to = (t + 1 + j) % n_ten
-            src = buf3.at[a, pl.ds(pl.multiple_of(to * hw, hw), hw), :]
-            copies.append(remote(src, buf4.at[a, j], send4.at[a, j], recv4.at[a, j], peer))
-        start_all(copies)
-        stage4.append(copies)
+    for a in (0, 1, 2, 5, 3, 6):
+        second(a)
+    third(0)
+    third(1)
+    second(4)
+    for a in (2, 3, 5, 6, 4):
+        third(a)
     vec_hops[2][0].wait_recv()
     vec_sum[3] = vec_sum[2] + vec_buf[2]
     start_all(vec_hops[3])
-    for n, copies in enumerate(stage4):
+    for n, copies in stage4.items():
         total = buf3[n, pl.ds(pl.multiple_of(t * hw, hw), hw), :].astype(F32)
         for j, copy in enumerate(copies):
             copy.wait_recv()
@@ -1456,7 +1471,7 @@
         copy.wait_recv()
         total = total + vec_buf[3 + j]
     vec_out[...] = total
-    for copies in stage1 + stage2 + stage4 + [stage3] + vec_hops:
+    for copies in stage1 + stage2 + list(stage4.values()) + [list(stage3.values())] + vec_hops:
         for copy in copies:
             copy.wait_send()
     wait_all(local)
@@ -1555,7 +1570,7 @@
     coded = jnp.where(valid, masked_rows, length)
     info = jnp.concatenate([coded, jnp.full((1, slots), jnp.sum(valid.astype(jnp.int32)))], axis=0)
     info = jnp.pad(info, ((0, -(windows + 1) % 8), (0, -slots % LANES)))
-    both_tok, all_q, all_k, all_v, all_out, infos, peer_grad = exchange_in(
+    both_tok, all_q, all_k, all_v, all_out, infos, left_grad = exchange_in(
         jnp.swapaxes(tokens, 0, 1), w_query, w_key, w_value, w_out, info, out_grad, n_dp, n_seq, n_ten
     )
     loss_weight = LOSS_SCALE / jnp.sum(infos[:, windows, 0]).astype(F32)
@@ -1565,8 +1580,6 @@
     my_grad = lax.dynamic_slice_in_dim(out_grad, first_window, n_ten, 0)
     pair_infos = lax.dynamic_slice_in_dim(infos, dp_index - core, 2, 0)
     left_coded = jnp.stack([pair_infos[i // n_seq, i % n_seq * half + n_ten, :slots] for i in range(n_ten)])
-    own_left = jnp.stack([out_grad[i * half + n_ten] for i in range(n_seq)])
-    left_grad = jnp.where(core == 0, jnp.concatenate([own_left, peer_grad]), jnp.concatenate([peer_grad, own_left]))
     weigh = lambda grad, rows: jnp.where((rows < length)[..., None], grad.astype(F32) * loss_weight, 0.0)
 
     own_rows, left_rows = pick_one(my_coded, ten_index), pick_one(left_coded, ten_index)
@@ -1592,7 +1605,7 @@
     )
     own_att, left_q, left_k, left_v, *gathered = attend_swap(q, k, v, gathered, length, n_ten)
     left_att_part, *gathered = attend_left(left_q, left_k, left_v, gathered, n_ten)
-    out_both, att_m, gr2, own_gatt, left_gatt, grad_norm2, all_own, all_left = feed_forward(
+    own_out, left_chunks, att_m, gr2, own_gatt, left_gatt, grad_norm2, all_own, all_left = feed_forward(
         both_tok, own_att, left_att_part, all_out, norm2_gain, norm2_bias, own_pick, part_pick, my_cot, ffn, gathered, n_ten
     )
 
@@ -1628,9 +1641,8 @@
     )
 
     own_out = lax.all_to_all(
-        out_both[:length].reshape(n_seq * n_ten, rows_local, width), ("seq", "tensor"), 0, 0, tiled=True
+        own_out.reshape(n_seq * n_ten, rows_local, width), ("seq", "tensor"), 0, 0, tiled=True
     ).reshape(n_seq, n_ten, rows_local, width)
-    left_chunks = out_both[length:].reshape(n_seq, rows_local, width)
     left_out = []
     for turn in range(2):
         perm = []
@@ -1639,7 +1651,7 @@
                 for p in range(n_ten):
                     to = d // 2 * 2 + p // 2, sx, d % 2 * 2 + (p % 2 ^ turn)
                     perm.append(((d * n_seq + sx) * n_ten + p, (to[0] * n_seq + to[1]) * n_ten + to[2]))
-        left_out.append(lax.ppermute(pick_one(left_chunks, (ten_index + turn) % 2), ("dp", "seq", "tensor"), perm))
+        left_out.append(lax.ppermute(left_chunks[turn], ("dp", "seq", "tensor"), perm))
     even = ten_index % 2 == 0
     left_out = jnp.stack([jnp.where(even, left_out[0], left_out[1]), jnp.where(even, left_out[1], left_out[0])])
     output = jnp.concatenate([own_out, left_out[:, None]], axis=1).reshape(windows, rows_local, width)

time: 554 us -> 538 us (0.971)
  local copies, waits for them, and re-layouts: 22.5 us -> 14.7 us
    slice x3 -> x0, local copies, waits for them, and re-layouts: 6.88 us -> none  [the longest x1 3.07 us: window_shards(): out_both[:length].reshape(n_seq * n_ten, rows_local, width)]
  transfers between devices with their start and end apart: 3 -> 3, of which waited for: 0 -> 0; matrix products, arithmetic and copies ran while one was open for 13% -> 12% of each run, Pallas kernels for 30% -> 29%
where the time goes in v5:
time: 538 us; the launch traced here: 530 us
  Pallas kernels  438 us (81%)
  matrix products  43.2 us (8%)
  other arithmetic  22.4 us (4%)
  local copies, waits for them, and re-layouts  14.7 us (3%)
  starting transfers between devices  9.34 us (2%)
    pallas_call x1, Pallas kernels, exchange_out(): pl.pallas_call(functools.partial(exchange_out_kernel, (n_seq, n_ten, half...  107 us
    pallas_call x1, Pallas kernels, feed_forward(): pl.pallas_call(functools.partial(feed_kernel, n_ten), grid=(n_ten * units...  99.9 us
    pallas_call x1, Pallas kernels, exchange_in(): pl.pallas_call(functools.partial(exchange_in_kernel, (n_seq, n_ten, windo...  78.8 us
    pallas_call x1, Pallas kernels, attend_swap(): pl.pallas_call(functools.partial(attend_swap_kernel, n_ten, length), grid...  49.9 us
    pallas_call x1, Pallas kernels, norm_qkv(): pl.pallas_call(functools.partial(qkv_kernel, n_ten), grid=(rows // tile,)...  35 us
    dot_general x7, matrix products, t_dot(): lax.dot_general(a, b, (((0,), (0,)), ((), ())), preferred_element_type=F32)  32.1 us
    pallas_call x1, Pallas kernels, back_swap(): pl.pallas_call(back_swap_kernel, grid=(width // LANES,), in_specs=back_sp...  25.3 us
    pallas_call x1, Pallas kernels, attend_left(): pl.pallas_call(functools.partial(attend_left_kernel, n_ten), grid=(QUAD,...  18 us
  transfers between devices with their start and end apart: 3, of which 0 were waited for; matrix products, arithmetic and copies ran while one was open for 12% of the time, Pallas kernels for 29%

profile of v5, /device:TPU:0, one launch (start us, length us, event | category | flops | bytes accessed | tf_op | source)
XLA Modules:
  0.0 530.5 jit_solution(7556391847369831183)
XLA Ops:
  1.3 1.4 convert_reduce_fusion
  2.8 0.8 fusion.2.pick_ref
  3.6 1.3 select_select_fusion.count_ref
  4.9 78.8 %exchange_in.1 = (bf16[1280,1024]{1,0:T(8,128)(2,1)}, bf16[1024,1024]{1,0:T(8,128)(2,1)}, bf16[1024,1024]{1,0:T(8,128)(2,1)}, bf16[1024,1024]{1,0:T(8,128)(2,1)}...) custom-call(bf16[10,128,1024]{2,1,0:T(8,128)(2,1)} %bitcast.89, ...), custom_call_target="tpu_custom_call" | custom-call | tf_op jit(solution)/shard_map/exchange_in/pallas_call | solution.py:602
  83.7 1.4 slice_reduce_fusion
  85.1 0.8 fusion.13
  87.3 1.3 bitcast_select_fusion
  88.6 1.2 pad_maximum_fusion.3.cot_ref
  89.8 1.7 constant_dynamic-slice_fusion.7
  91.5 35.0 %norm_qkv.1 = (bf16[1280,1024]{1,0:T(8,128)(2,1)}, bf16[1280,1024]{1,0:T(8,128)(2,1)}, bf16[1280,1024]{1,0:T(8,128)(2,1)}, bf16[1280,1024]{1,0:T(8,128)(2,1)}, b...) custom-call(bf16[1280,1024]{1,0:T(8,128)(2,1)} %get-tuple-element.63.x_ref.tok_ref, ...), custom_call_target="tpu_custom_call" | custom-call | flops 8053063680 | bytes 20971520 | tf_op jit(solution)/shard_map/norm_qkv/pallas_call | solution.py:677
  126.5 49.9 %attend_swap.1 = (bf16[1024,1024]{1,0:T(8,128)(2,1)}, bf16[1024,256]{1,0:T(8,128)(2,1)}, bf16[1024,256]{1,0:T(8,128)(2,1)}, bf16[1024,256]{1,0:T(8,128)(2,1)}, b...) custom-call(bf16[1280,1024]{1,0:T(8,128)(2,1)} %get-tuple-element.67, ...), custom_call_target="tpu_custom_call", output_to_operand_aliasing={{4}: (6, {}), {5}: (7, {}), {6}: (8, {})} | custom-call | flops 17179869184 | bytes 8388608 | tf_op jit(solution)/shard_map/attend_swap/pallas_call | solution.py:848
  176.4 18.0 %attend_left.1 = (bf16[256,1024]{1,0:T(8,128)(2,1)}, bf16[1024,4096]{1,0:T(8,128)(2,1)}, bf16[1024,4096]{1,0:T(8,128)(2,1)}, bf16[4096,1024]{1,0:T(8,128)(2,1)}) custom-call(bf16[1024,256]{1,0:T(8,128)(2,1)} %get-tuple-element.74.q_ref, bf16[1024,256]{1,0:T(8,128)(2,1)} %get-tuple-element.75.k_ref, ...), custom_call_target="tpu_custom_call", output_to_operand_aliasing={{1}: (3, {}), {2}: (4, {}), {3}: (5, {})} | custom-call | flops 4294967296 | bytes 2097152 | tf_op jit(solution)/shard_map/attend_left/pallas_call | solution.py:760
  194.4 99.9 %feed_forward.1 = (bf16[1024,1024]{1,0:T(8,128)(2,1)}, bf16[2,128,1024]{2,1,0:T(8,128)(2,1)}, bf16[320,1024]{1,0:T(8,128)(2,1)}, bf16[320,1024]{1,0:T(8,128)(2,1...) custom-call(bf16[1280,1024]{1,0:T(8,128)(2,1)} %get-tuple-element.63, ...), custom_call_target="tpu_custom_call", output_to_operand_aliasing={{9}: (12, {}), {10}: (13, {}), {11}: (14, {})} | custom-call | flops 42949672960 | bytes 25165824 | tf_op jit(solution)/shard_map/feed_forward/pallas_call | solution.py:1209
  294.3 1.9 slice_bitcast_fusion.4
  296.2 3.6 collective-permute-start
  299.8 0.9 collective-permute-start.1
  300.7 4.9 all-to-all-start
  305.6 0.8 fusion.3.pick_ref
  307.1 0.9 pad_maximum_fusion.7
  308.0 0.9 pad_maximum_fusion.9
  308.8 7.3 %back_left.1 = (bf16[1024,256]{1,0:T(8,128)(2,1)}, bf16[1024,256]{1,0:T(8,128)(2,1)}, bf16[1024,256]{1,0:T(8,128)(2,1)}) custom-call(bf16[1024,256]{1,0:T(8,128)(2,1)} %get-tuple-element.74.q_ref, bf16[160,256]{1,0:T(8,128)(2,1)} %get-tuple-element.93.g_ref, bf16[1024,256]{1,0:T(8,128)(2,1)} %get-tuple-element.75.k_ref, ...), custom_call_target="tpu_custom_call" | custom-call | flops 1006632960 | bytes 3145728 | tf_op jit(solution)/shard_map/back_left/pallas_call | solution.py:922
  316.1 25.3 %back_swap.1 = (bf16[1280,1024]{1,0:T(8,128)(2,1)}, bf16[1280,1024]{1,0:T(8,128)(2,1)}, bf16[1280,1024]{1,0:T(8,128)(2,1)}) custom-call(bf16[1280,1024]{1,0:T(8,128)(2,1)} %get-tuple-element.67.q_ref.q_all, bf16[160,1024]{1,0:T(8,128)(2,1)} %get-tuple-element.92.g_ref, bf16[1280,1024]{1,0:T(8,128)(2,1)} %get-tuple-element.68.k_ref.k_all, ...), custom_call_target="tpu_custom_call" | custom-call | flops 4026531840 | bytes 12582912 | tf_op jit(solution)/shard_map/back_swap/pallas_call | solution.py:985
  341.5 5.7 %fusion.20 = f32[800,1024]{1,0:T(8,128)} fusion(bf16[1024,1024]{1,0:T(8,128)(2,1)} %wg_ref.3, bf16[160,1024]{1,0:T(8,128)(2,1)S(1)} %bitcast.113, bf16[640,1024]{1,0:T(8,128)(2,1)} %bitcast.108), kind=kOutput, calls=%fused_computation.91 | convolution fusion | flops 1680998400 | bytes 7012352 | tf_op jit(solution)/shard_map/dot_general | solution.py:323
  347.3 3.6 fusion.21
  350.8 0.8 pad_maximum_fusion.6.pick_ref
  351.6 4.1 convolution_convert_fusion.2.gq_ref
  355.8 4.2 convolution_convert_fusion.1.gk_ref
  359.9 4.4 convolution_convert_fusion.gv_ref
  364.4 1.1 select_convert_fusion.1
  365.5 1.8 select_convert_fusion
  367.4 4.0 convolution_convert_fusion.3.go_ref
  371.4 1.9 fusion.1
  373.8 3.8 convolution_convert_fusion.5.gu_ref
  377.7 17.0 %token_back.1 = (bf16[1280,1024]{1,0:T(8,128)(2,1)}, f32[2,1024]{1,0:T(2,128)}) custom-call(bf16[1280,1024]{1,0:T(8,128)(2,1)} %get-tuple-element.63.x_ref.tok_ref, bf16[1280,1024]{1,0:T(8,128)(2,1)} %get-tuple-element.100.dq_ref, bf16[1280,1024]{1,0:T(8,128)(2,1)} %get-tuple-element.102.dk_ref, bf16[1280,1024]{1,0:T(8,128)(2,1)} %get-tuple-element.103.dv_ref, ...), custom_call_target="tpu_custom_call" | custom-call | flops 8053063680 | bytes 20971520 | tf_op jit(solution)/shard_map/token_back/pallas_call | solution.py:1282
  394.8 1.4 maximum_maximum_fusion.vec_ref
  396.2 6.8 %convolution_convert_fusion.4.gd_ref = bf16[1024,1024]{1,0:T(8,128)(2,1)} fusion(f32[800,1024]{1,0:T(8,128)} %fusion.21, bf16[160,1024]{1,0:T(8,128)(2,1)} %bitcast.95, bf16[640,1024]{1,0:T(8,128)(2,1)S(1)} %bitcast.93, f32[800,1024]{1,0:T(8,128)} %fusion.20), kind=kOutput, calls=%fused_computation.12 | convolution fusion | flops 1686962176 | bytes 10289152 | tf_op jit(solution)/shard_map/dot_general | solution.py:327
  403.0 4.7 convolution_convert_fusion.6.gg_ref
  407.7 106.7 %exchange_out.1 = (f32[4,256,128]{2,1,0:T(8,128)}, f32[3,1024,128]{2,1,0:T(8,128)}, bf16[10,128,1024]{2,1,0:T(8,128)(2,1)}, f32[8,1024]{1,0:T(8,128)}) custom-call(bf16[1024,1024]{1,0:T(8,128)(2,1)} %convolution_convert_fusion.3.go_ref, bf16[1024,1024]{1,0:T(8,128)(2,1)} %convolution_convert_fusion.2.gq_ref, ...), custom_call_target="tpu_custom_call" | custom-call | tf_op jit(solution)/shard_map/exchange_out/pallas_call | solution.py:1494
  514.4 1.9 slice_bitcast_fusion.5
  516.4 2.3 slice_bitcast_fusion
  518.6 3.0 convert_bitcast_fusion
  522.4 0.8 copy.40
  523.1 0.8 copy.41
  523.9 0.8 copy.42
  524.7 1.0 copy.43
  525.7 1.0 copy.44
  527.2 1.1 select_bitcast_fusion.1
  528.3 1.7 pad_maximum_fusion
  (66 shorter events, 3.5 us)
Async XLA Ops:
  296.2 230.9 %collective-permute-start = (bf16[128,1024]{1,0:T(8,128)(2,1)}, bf16[128,1024]{1,0:T(8,128)(2,1)}, u32[]{:S(2)}, u32[]{:S(2)}) collective-permute-start(bf16[128,1024]{1,0:T(8,128)(2,1)} %get-tuple-element.135), channel_id=1, source_target_pairs={{0,0},{1,1},{2,8},{3,9},{4,4},{5,5},{6,12},{7,13},{8,2},{9,3},{10,... | collective-permute-start | bytes 786440 | tf_op jit(solution)/shard_map/ppermute | solution.py:1654
  299.8 227.4 %collective-permute-start.1 = (bf16[128,1024]{1,0:T(8,128)(2,1)}, bf16[128,1024]{1,0:T(8,128)(2,1)}, u32[]{:S(2)}, u32[]{:S(2)}) collective-permute-start(bf16[128,1024]{1,0:T(8,128)(2,1)} %get-tuple-element.136), channel_id=1, source_target_pairs={{0,1},{1,0},{2,9},{3,8},{4,5},{5,4},{6,13},{7,12},{8,3},{9,2},{10,... | collective-permute-start | bytes 786440 | tf_op jit(solution)/shard_map/ppermute | solution.py:1654
  300.7 227.6 %all-to-all-start = ((bf16[8,128,1024]{2,1,0:T(8,128)(2,1)}), bf16[8,128,1024]{2,1,0:T(8,128)(2,1)S(1)}, u32[]{:S(2)}, u32[]{:S(2)}) async-start(bf16[8,128,1024]{2,1,0:T(8,128)(2,1)} %bitcast.91), calls=%async_computation | async-start | bytes 4194304 | tf_op jit(solution)/shard_map/all_to_all | solution.py:1643
  316.1 25.4 %copy-start.10 = (bf16[4,40,1024]{2,1,0:T(8,128)(2,1)S(1)}, bf16[4,40,1024]{2,1,0:T(8,128)(2,1)}, u32[]{:S(2)}) copy-start(bf16[4,40,1024]{2,1,0:T(8,128)(2,1)} %get-tuple-element.105) | copy-start | bytes 983044
  341.5 5.7 %copy-start.5 = (bf16[1024,1024]{1,0:T(8,128)(2,1)S(1)}, bf16[1024,1024]{1,0:T(8,128)(2,1)}, u32[]{:S(2)}) copy-start(bf16[1024,1024]{1,0:T(8,128)(2,1)} %wu_ref.3) | copy-start | bytes 6291460
  341.5 5.7 %copy-start.7 = (bf16[4,160,1024]{2,1,0:T(8,128)(2,1)S(1)}, bf16[4,160,1024]{2,1,0:T(8,128)(2,1)}, u32[]{:S(2)}) copy-start(bf16[4,160,1024]{2,1,0:T(8,128)(2,1)} %get-tuple-element.104) | copy-start | bytes 3932164
  347.2 3.6 copy-start.1
  347.2 3.6 copy-start.2
  347.3 4.4 copy-start.13
  347.3 4.4 copy-start.21
  351.6 4.2 copy-start.14
  355.8 4.2 copy-start.15
  365.5 5.9 %copy-start.3 = (bf16[4,40,1024]{2,1,0:T(8,128)(2,1)}, bf16[4,40,1024]{2,1,0:T(8,128)(2,1)S(1)}, u32[]{:S(2)}) copy-start(bf16[4,40,1024]{2,1,0:T(8,128)(2,1)S(1)} %select_convert_fusion.1) | copy-start | bytes 983044
  367.3 4.1 copy-start.6
  371.4 1.9 copy-start.8
  371.4 1.9 copy-start.11
  371.4 2.4 copy-start.18
  373.8 3.8 copy-start.16
  377.7 17.1 %copy-start.4 = (f32[2,1024]{1,0:T(2,128)S(1)}, f32[2,1024]{1,0:T(2,128)}, u32[]{:S(2)}) copy-start(f32[2,1024]{1,0:T(2,128)} %get-tuple-element.108) | copy-start | bytes 24580
  396.2 6.8 %copy-start.9 = (bf16[4,160,1024]{2,1,0:T(8,128)(2,1)S(1)}, bf16[4,160,1024]{2,1,0:T(8,128)(2,1)}, u32[]{:S(2)}) copy-start(bf16[4,160,1024]{2,1,0:T(8,128)(2,1)} %get-tuple-element.104) | copy-start | bytes 3932164
  396.2 6.8 %copy-start.12 = (bf16[4,40,1024]{2,1,0:T(8,128)(2,1)S(1)}, bf16[4,40,1024]{2,1,0:T(8,128)(2,1)}, u32[]{:S(2)}) copy-start(bf16[4,40,1024]{2,1,0:T(8,128)(2,1)} %get-tuple-element.105) | copy-start | bytes 983044
  396.2 6.8 %copy-start.17 = (f32[800,1024]{1,0:T(8,128)S(1)}, f32[800,1024]{1,0:T(8,128)}, u32[]{:S(2)}) copy-start(f32[800,1024]{1,0:T(8,128)} %copy-done.16) | copy-start | bytes 9830404
  396.2 6.8 %copy-start.19 = (f32[800,1024]{1,0:T(8,128)S(1)}, f32[800,1024]{1,0:T(8,128)}, u32[]{:S(2)}) copy-start(f32[800,1024]{1,0:T(8,128)} %fusion.20) | copy-start | bytes 9830404
  396.2 6.8 %copy-start.20 = (f32[800,1024]{1,0:T(8,128)S(1)}, f32[800,1024]{1,0:T(8,128)}, u32[]{:S(2)}) copy-start(f32[800,1024]{1,0:T(8,128)} %fusion.21) | copy-start | bytes 9830404
  514.4 4.2 copy-start

commit v6 on v5

--- a/solution.py
+++ b/solution.py
@@ -624,20 +624,9 @@
 
 
 def qkv_kernel(
-    n_ten, x_ref, gain_ref, bias_ref, wq_ref, wk_ref, wv_ref, cos_ref, sin_ref, part_cos_ref, part_sin_ref,
-    wg_ref, wu_ref, wd_ref, first_ref, q_ref, k_ref, v_ref, ag_ref, au_ref, ad_ref, send, recv,
+    x_ref, gain_ref, bias_ref, wq_ref, wk_ref, wv_ref, cos_ref, sin_ref, part_cos_ref, part_sin_ref,
+    first_ref, q_ref, k_ref, v_ref,
 ):
-    route = WeightRoute((ag_ref, au_ref, ad_ref), (wg_ref, wu_ref, wd_ref), n_ten, send, recv)
-
-    @pl.when(pl.program_id(0) == 0)
-    def _():
-        greet([{"tensor": (route.t + j) % n_ten} for j in range(1, n_ten)])
-        start_all(route.to_in())
-
-        @pl.when(route.is_middle)
-        def _():
-            start_all(route.to_out())
-
     shared = pl.program_id(0) == pl.num_programs(0) - 1
     normed, _ = layer_stats(x_ref[...].astype(F32))
     first_ref[...] = (normed * gain_ref[...] + bias_ref[...]).astype(BF)
@@ -653,43 +642,26 @@
                     part = (part * cos + swap_halves(part) * sin) * scale
                 out_ref[:, at + c : at + c + LANES] = part.astype(BF)
 
-    @pl.when(shared)
-    def _():
-        route.arrived(1)
-        sent_all(route.to_in())
-
-        @pl.when(route.is_middle)
-        def _():
-            route.arrived(2)
-            sent_all(route.to_out())
-
 
 def once(shape):
     return pl.BlockSpec(shape, lambda *_: (0,) * len(shape), pipeline_mode=pl.Buffered(1))
 
 
-def norm_qkv(x, gain, bias, w_query, w_key, w_value, tables, part_tables, ffn, n_ten):
+def norm_qkv(x, gain, bias, w_query, w_key, w_value, tables, part_tables):
     rows, width = x.shape
     tile = 256
     row = pl.BlockSpec((tile, width), lambda r: (r, 0))
     own = tables[0].shape[0] // tile
     table = pl.BlockSpec((tile, LANES), lambda r: (jnp.minimum(r, own - 1), 0))
     return pl.pallas_call(
-        functools.partial(qkv_kernel, n_ten),
+        qkv_kernel,
         grid=(rows // tile,),
-        in_specs=[row, once((1, width)), once((1, width))] + [once((width, width))] * 3 + [table, table] + [once((tile, LANES))] * 2 + [any_spec()] * 3,
-        out_specs=[row] * 4 + [any_spec()] * 3,
-        out_shape=[jax.ShapeDtypeStruct((rows, width), BF)] * 4
-        + [
-            jax.ShapeDtypeStruct((width, n_ten * ffn[0].shape[1]), BF),
-            jax.ShapeDtypeStruct((width, n_ten * ffn[1].shape[1]), BF),
-            jax.ShapeDtypeStruct((n_ten * ffn[2].shape[0], width), BF),
-        ],
-        scratch_shapes=route_sems(),
-        compiler_params=pltpu.CompilerParams(collective_id=7, has_side_effects=True),
+        in_specs=[row, once((1, width)), once((1, width))] + [once((width, width))] * 3 + [table, table] + [once((tile, LANES))] * 2,
+        out_specs=[row] * 4,
+        out_shape=[jax.ShapeDtypeStruct((rows, width), BF)] * 4,
         cost_estimate=pl.CostEstimate(flops=6 * rows * width * width, bytes_accessed=16 * rows * width, transcendentals=0),
         name="norm_qkv",
-    )(x, gain.reshape(1, width), bias.reshape(1, width), w_query, w_key, w_value, *tables, *part_tables, *ffn)
+    )(x, gain.reshape(1, width), bias.reshape(1, width), w_query, w_key, w_value, *tables, *part_tables)
 
 
 def attend_body(q_ref, k_ref, v_ref):
@@ -732,8 +704,9 @@
 
     @pl.when((p == 0) & (r == 0))
     def _():
-        greet(quad_peers() + [route.y_peer])
+        greet(quad_peers() + [route.y_peer] + [{"tensor": (route.t + j) % n_ten} for j in range(1, n_ten)])
         start_all(hops)
+        pl.when(route.is_middle)(lambda: start_all(route.out_three()))
 
     buf[r, :, pl.ds(pl.multiple_of(p * LANES, LANES), LANES)] = attend_body(q_ref, k_ref, v_ref)
 
@@ -751,6 +724,8 @@
         wait_all([copy_to(j) for j in range(1, QUAD)])
         own.wait()
         wait_all(hops)
+        pl.when(route.is_middle)(lambda: sent_all(route.out_three()))
+        pl.when(route.is_end)(lambda: route.arrived(3))
 
 
 def attend_left(q, k, v, gathered, n_ten):
@@ -791,57 +766,56 @@
 
 
 def attend_swap_kernel(
-    n_ten, length, q_ref, k_ref, v_ref, q_all, k_all, v_all, ag_in, au_in, ad_in, o_ref, lq_ref, lk_ref, lv_ref,
+    n_ten, length, q_ref, k_ref, v_ref, q_all, k_all, v_all, wg_ref, wu_ref, wd_ref, o_ref, lq_ref, lk_ref, lv_ref,
     ag_ref, au_ref, ad_ref, send, recv, local_sem, route_send, route_recv,
 ):
     step = pl.program_id(0) * pl.num_programs(1) + pl.program_id(1)
     steps = pl.num_programs(0) * pl.num_programs(1)
     copies, local = swap_part((q_all, k_all, v_all), (lq_ref, lk_ref, lv_ref), send, recv, local_sem, length)
-    route = WeightRoute((ag_ref, au_ref, ad_ref), None, n_ten, route_send, route_recv)
+    route = WeightRoute((ag_ref, au_ref, ad_ref), (wg_ref, wu_ref, wd_ref), n_ten, route_send, route_recv)
 
     @pl.when(step == 0)
     def _():
         greet(quad_peers() + [route.y_peer] + [{"tensor": (route.t + j) % n_ten} for j in range(1, n_ten)])
+        start_all(route.to_in())
+        pl.when(route.is_middle)(lambda: start_all(route.to_out()))
+        start_all(copies + local)
+
+    o_ref[...] = attend_body(q_ref, k_ref, v_ref)
+
+    @pl.when(step == steps // 2)
+    def _():
+        route.arrived(1)
         start_all(route.hop(1, 0))
 
         @pl.when(route.is_middle)
         def _():
+            route.arrived(2)
             start_all(route.in_far())
             start_all(route.out_two())
 
-        start_all(copies + local)
-
-    o_ref[...] = attend_body(q_ref, k_ref, v_ref)
-
-    @pl.when(step == steps // 4)
+    @pl.when(step == steps * 3 // 4)
     def _():
         received(route.hop(1, 0))
         start_all(route.hop(1, 1))
 
-    @pl.when(step == steps // 2)
-    def _():
+    @pl.when(step == steps - 1)
+    def _():
+        wait_all(copies + local)
+        received(route.hop(1, 1))
+        sent_all(route.hop(1, 0) + route.hop(1, 1) + route.to_in())
+
         @pl.when(route.is_middle)
         def _():
             route.arrived(3)
-            start_all(route.out_three())
-
-    @pl.when(step == steps - 1)
-    def _():
-        wait_all(copies + local)
-        received(route.hop(1, 1))
-        sent_all(route.hop(1, 0) + route.hop(1, 1))
-
-        @pl.when(route.is_middle)
-        def _():
-            sent_all(route.in_far() + route.out_two() + route.out_three())
+            sent_all(route.to_out() + route.in_far() + route.out_two())
 
         @pl.when(route.is_end)
         def _():
             route.arrived(2)
-            route.arrived(3)
-
-
-def attend_swap(q, k, v, gathered, length, n_ten):
+
+
+def attend_swap(q, k, v, ffn, length, n_ten):
     width = q.shape[1]
     tile, pairs, hw = 512, width // LANES, width // QUAD
     left = jax.ShapeDtypeStruct((length, hw), BF)
@@ -851,8 +825,8 @@
         in_specs=attend_specs(length, tile) + [any_spec()] * 6,
         out_specs=[pl.BlockSpec((tile, LANES), lambda p, r: (r, p))] + [any_spec()] * 6,
         out_shape=[jax.ShapeDtypeStruct((length, width), BF), left, left, left]
-        + [jax.ShapeDtypeStruct(w.shape, BF) for w in gathered],
-        input_output_aliases={6: 4, 7: 5, 8: 6},
+        + [jax.ShapeDtypeStruct((width, n_ten * w.shape[1]), BF) for w in ffn[:2]]
+        + [jax.ShapeDtypeStruct((n_ten * ffn[2].shape[0], width), BF)],
         scratch_shapes=[
             pltpu.SemaphoreType.DMA((3, QUAD - 1)),
             pltpu.SemaphoreType.DMA((3, QUAD - 1)),
@@ -862,7 +836,7 @@
         compiler_params=pltpu.CompilerParams(collective_id=1, has_side_effects=True),
         cost_estimate=attend_cost(length, pairs),
         name="attend_swap",
-    )(q, k, v, q, k, v, *gathered)
+    )(q, k, v, q, k, v, *ffn)
 
 
 def back_body(q_ref, g_ref, k_ref, v_ref, pick_ref, cos_ref, sin_ref, qcos_ref, qsin_ref):
@@ -1135,7 +1109,7 @@
         start_all(line_copies[0])
         local[0].start()
 
-    @pl.when(step == 3)
+    @pl.when(step == 2 * per)
     def _():
         wait_all(rows_copies)
         whole = rows_buf[place].astype(F32)
@@ -1143,7 +1117,7 @@
             whole = whole + rows_parts[j].astype(F32)
         left_m[...] = whole.astype(BF)
 
-    @pl.when(step == 4)
+    @pl.when(step == 2 * per + 1)
     def _():
         start_all(line_copies[1])
         local[1].start()
@@ -1255,6 +1229,39 @@
     )(tok, att, left_att, w_out, gain.reshape(1, width), bias.reshape(1, width), pick, part_pick, cot, *ffn, *gathered)[:9]
 
 
+def feed_grads_kernel(own_ref, left_ref, cot_ref, wg_ref, wu_ref, wd_ref, gg_ref, gu_ref, gd_ref, x_ref):
+    @pl.when(pl.program_id(0) == 0)
+    def _():
+        x_ref[: own_ref.shape[0], :] = own_ref[...]
+        x_ref[own_ref.shape[0] :, :] = left_ref[...]
+
+    x, cot = x_ref[...], cot_ref[...]
+    gate, up, back = dot_n(x, wg_ref[...]), dot_n(x, wu_ref[...]), dot_t(cot, wd_ref[...])
+    sig = jax.nn.sigmoid(gate)
+    act = gate * sig
+    gg_ref[...] = t_dot((back * up * sig * (1.0 + gate * (1.0 - sig))).astype(BF), x).astype(BF)
+    gu_ref[...] = t_dot((back * act).astype(BF), x).astype(BF)
+    gd_ref[...] = t_dot((act * up).astype(BF), cot).astype(BF)
+
+
+def feed_grads(own, left, cot, w_gate, w_up, w_down):
+    rows, width = cot.shape
+    units = w_gate.shape[1]
+    unit = 256
+    columns = pl.BlockSpec((width, unit), lambda i: (0, i))
+    line = pl.BlockSpec((unit, width), lambda i: (i, 0))
+    return pl.pallas_call(
+        feed_grads_kernel,
+        grid=(units // unit,),
+        in_specs=[once(own.shape), once(left.shape), once(cot.shape), columns, columns, line],
+        out_specs=[line] * 3,
+        out_shape=[jax.ShapeDtypeStruct((units, width), BF)] * 3,
+        scratch_shapes=[pltpu.VMEM((rows, width), BF)],
+        cost_estimate=pl.CostEstimate(flops=12 * rows * width * units, bytes_accessed=12 * width * units, transcendentals=rows * units),
+        name="feed_grads",
+    )(own, left, cot, w_gate, w_up, w_down)
+
+
 def token_back_kernel(
     tok_ref, dq_ref, dk_ref, dv_ref, wq_ref, wk_ref, wv_ref, gain_ref, pick_ref, rows_ref, out_ref, vec_ref
 ):
@@ -1600,10 +1607,8 @@
     left_tables = tables + list(rotary_lanes(*rotary_tables(left_rows)))
 
     ffn = (w_gate, w_up, w_down)
-    first, q, k, v, *gathered = norm_qkv(
-        both_tok, norm1_gain, norm1_bias, all_q, all_k, all_v, tables, part_tables, ffn, n_ten
-    )
-    own_att, left_q, left_k, left_v, *gathered = attend_swap(q, k, v, gathered, length, n_ten)
+    first, q, k, v = norm_qkv(both_tok, norm1_gain, norm1_bias, all_q, all_k, all_v, tables, part_tables)
+    own_att, left_q, left_k, left_v, *gathered = attend_swap(q, k, v, ffn, length, n_ten)
     left_att_part, *gathered = attend_left(left_q, left_k, left_v, gathered, n_ten)
     own_out, left_chunks, att_m, gr2, own_gatt, left_gatt, grad_norm2, all_own, all_left = feed_forward(
         both_tok, own_att, left_att_part, all_out, norm2_gain, norm2_bias, own_pick, part_pick, my_cot, ffn, gathered, n_ten
@@ -1614,7 +1619,6 @@
     dq, dk, dv = back_swap(q, own_gatt, k, v, own_pick, own_tables, left_back)
     all_own, dq, dk, dv = lax.optimization_barrier((all_own, dq, dk, dv))
 
-    second = jnp.concatenate([all_own.reshape(-1, width), all_left.reshape(-1, width)], axis=0)
     part_of = lambda x: lax.dynamic_slice_in_dim(x, place * part, part, 1)
     down_in = jnp.concatenate(
         [
@@ -1623,17 +1627,7 @@
         ],
         axis=0,
     ).astype(BF)
-    gate = dot_n(second, w_gate)
-    up = dot_n(second, w_up)
-    grad_hidden = dot_t(down_in, w_down)
-    sig = jax.nn.sigmoid(gate)
-    silu = gate * sig
-    hidden_m = (silu * up).astype(BF)
-    grad_gate = (grad_hidden * up * sig * (1.0 + gate * (1.0 - sig))).astype(BF)
-    grad_up = (grad_hidden * silu).astype(BF)
-    grad_w_ffn = [
-        t_dot(grad_gate, second).astype(BF), t_dot(grad_up, second).astype(BF), t_dot(hidden_m, down_in).astype(BF)
-    ]
+    grad_w_ffn = feed_grads(all_own.reshape(-1, width), all_left.reshape(-1, width), down_in, *ffn)
     grad_w_attn = [grad_w_out] + [t_dot(d, first).astype(BF) for d in (dq, dk, dv)]
     grad_both, grad_norm1 = token_back(
         both_tok, (dq, dk, dv), (all_q, all_k, all_v), norm1_gain,

time: 538 us -> 525 us (0.976)
  matrix products: 43.2 us -> 19.4 us
  Pallas kernels: 438 us -> 447 us
    pallas_call x1, Pallas kernels: 49.9 us -> 62.7 us  [attend_swap(): pl.pallas_call(functools.partial(attend_swap_kernel, n_ten, length), grid...]
    dot_general x7 -> x4, matrix products: 32.1 us -> 19.4 us  [t_dot(): lax.dot_general(a, b, (((0,), (0,)), ((), ())), preferred_element_type=F32)]
    dot_general x3 -> x0, matrix products: 11.2 us -> none  [the longest x2 9.25 us: dot_n(): lax.dot_general(a, b, (((1,), (0,)), ((), ())), preferred_element_type=F32)]
    pallas_call x1, Pallas kernels: 99.9 us -> 90.4 us  [feed_forward(): pl.pallas_call(functools.partial(feed_kernel, n_ten), grid=(n_ten * units...]
    pallas_call x1 -> x2, Pallas kernels: 35 us -> 35.3 us  [the longest x1 20.5 us: feed_grads(): pl.pallas_call(feed_grads_kernel, grid=(units // unit,), in_specs=[once(o...]
  transfers between devices with their start and end apart: 3 -> 3, of which waited for: 0 -> 0; matrix products, arithmetic and copies ran while one was open for 12% -> 9% of each run, Pallas kernels for 29% -> 34%
where the time goes in v6:
time: 525 us; the launch traced here: 518 us
  Pallas kernels  447 us (85%)
  other arithmetic  25.3 us (5%)
  matrix products  19.4 us (4%)
  local copies, waits for them, and re-layouts  14.2 us (3%)
  starting transfers between devices  8.84 us (2%)
    pallas_call x1, Pallas kernels, exchange_out(): pl.pallas_call(functools.partial(exchange_out_kernel, (n_seq, n_ten, half...  104 us
    pallas_call x1, Pallas kernels, feed_forward(): pl.pallas_call(functools.partial(feed_kernel, n_ten), grid=(n_ten * units...  90.4 us
    pallas_call x1, Pallas kernels, exchange_in(): pl.pallas_call(functools.partial(exchange_in_kernel, (n_seq, n_ten, windo...  78.8 us
    pallas_call x1, Pallas kernels, attend_swap(): pl.pallas_call(functools.partial(attend_swap_kernel, n_ten, length), grid...  62.7 us
    pallas_call x1, Pallas kernels, back_swap(): pl.pallas_call(back_swap_kernel, grid=(width // LANES,), in_specs=back_sp...  28.6 us
    pallas_call x1, Pallas kernels, attend_left(): pl.pallas_call(functools.partial(attend_left_kernel, n_ten), grid=(QUAD,...  23.2 us
    pallas_call x1, Pallas kernels, feed_grads(): pl.pallas_call(feed_grads_kernel, grid=(units // unit,), in_specs=[once(o...  20.5 us
    dot_general x4, matrix products, t_dot(): lax.dot_general(a, b, (((0,), (0,)), ((), ())), preferred_element_type=F32)  19.4 us
  transfers between devices with their start and end apart: 3, of which 0 were waited for; matrix products, arithmetic and copies ran while one was open for 9% of the time, Pallas kernels for 34%

profile of v6, /device:TPU:0, one launch (start us, length us, event | category | flops | bytes accessed | tf_op | source)
XLA Modules:
  0.0 517.6 jit_solution(2444334251707239212)
XLA Ops:
  1.3 1.4 convert_reduce_fusion
  2.8 0.9 fusion.pick_ref
  3.7 1.3 select_select_fusion.count_ref
  4.9 78.8 %exchange_in.1 = (bf16[1280,1024]{1,0:T(8,128)(2,1)}, bf16[1024,1024]{1,0:T(8,128)(2,1)}, bf16[1024,1024]{1,0:T(8,128)(2,1)}, bf16[1024,1024]{1,0:T(8,128)(2,1)}...) custom-call(bf16[10,128,1024]{2,1,0:T(8,128)(2,1)} %bitcast.87, ...), custom_call_target="tpu_custom_call" | custom-call | tf_op jit(solution)/shard_map/exchange_in/pallas_call | solution.py:602
  83.8 1.4 slice_reduce_fusion
  85.1 0.8 fusion.9
  86.5 0.7 compare_reduce_fusion
  87.3 1.3 bitcast_select_fusion
  88.6 1.2 pad_maximum_fusion.2.cot_ref
  89.9 1.7 constant_dynamic-slice_fusion.7
  91.5 14.8 %norm_qkv.1 = (bf16[1280,1024]{1,0:T(8,128)(2,1)}, bf16[1280,1024]{1,0:T(8,128)(2,1)}, bf16[1280,1024]{1,0:T(8,128)(2,1)}, bf16[1280,1024]{1,0:T(8,128)(2,1)}) custom-call(bf16[1280,1024]{1,0:T(8,128)(2,1)} %get-tuple-element.63.x_ref.tok_ref, f32[1,1024]{1,0:T(1,128)} %bitcast.101, f32[1,1024]{1,0:T(1,128)} %bitcast.98, ...), custom_call_target="tpu_custom_call" | custom-call | flops 8053063680 | bytes 20971520 | tf_op jit(solution)/shard_map/norm_qkv/pallas_call | solution.py:656
  106.4 62.7 %attend_swap.1 = (bf16[1024,1024]{1,0:T(8,128)(2,1)}, bf16[1024,256]{1,0:T(8,128)(2,1)}, bf16[1024,256]{1,0:T(8,128)(2,1)}, bf16[1024,256]{1,0:T(8,128)(2,1)}, b...) custom-call(bf16[1280,1024]{1,0:T(8,128)(2,1)} %get-tuple-element.67.q_ref.q_all, ...), custom_call_target="tpu_custom_call" | custom-call | flops 17179869184 | bytes 8388608 | tf_op jit(solution)/shard_map/attend_swap/pallas_call | solution.py:822
  169.1 23.2 %attend_left.1 = (bf16[256,1024]{1,0:T(8,128)(2,1)}, bf16[1024,4096]{1,0:T(8,128)(2,1)}, bf16[1024,4096]{1,0:T(8,128)(2,1)}, bf16[4096,1024]{1,0:T(8,128)(2,1)}) custom-call(bf16[1024,256]{1,0:T(8,128)(2,1)} %get-tuple-element.71.q_ref, bf16[1024,256]{1,0:T(8,128)(2,1)} %get-tuple-element.72.k_ref, ...), custom_call_target="tpu_custom_call", output_to_operand_aliasing={{1}: (3, {}), {2}: (4, {}), {3}: (5, {})} | custom-call | flops 4294967296 | bytes 2097152 | tf_op jit(solution)/shard_map/attend_left/pallas_call | solution.py:735
  192.3 90.4 %feed_forward.1 = (bf16[1024,1024]{1,0:T(8,128)(2,1)}, bf16[2,128,1024]{2,1,0:T(8,128)(2,1)}, bf16[320,1024]{1,0:T(8,128)(2,1)}, bf16[320,1024]{1,0:T(8,128)(2,1...) custom-call(bf16[1280,1024]{1,0:T(8,128)(2,1)} %get-tuple-element.63, ...), custom_call_target="tpu_custom_call", output_to_operand_aliasing={{9}: (12, {}), {10}: (13, {}), {11}: (14, {})} | custom-call | flops 42949672960 | bytes 25165824 | tf_op jit(solution)/shard_map/feed_forward/pallas_call | solution.py:1183
  282.8 1.9 slice_bitcast_fusion.4
  284.7 3.6 collective-permute-start
  288.3 0.3 collective-permute-start.1
  288.6 5.0 all-to-all-start
  293.6 0.9 fusion.1.pick_ref
  294.5 0.8 pad_maximum_fusion.3.pick_ref
  295.3 0.6 fusion.3
  295.9 0.9 pad_maximum_fusion.4
  296.8 0.9 pad_maximum_fusion.6
  297.6 7.3 %back_left.1 = (bf16[1024,256]{1,0:T(8,128)(2,1)}, bf16[1024,256]{1,0:T(8,128)(2,1)}, bf16[1024,256]{1,0:T(8,128)(2,1)}) custom-call(bf16[1024,256]{1,0:T(8,128)(2,1)} %get-tuple-element.71.q_ref, bf16[160,256]{1,0:T(8,128)(2,1)} %get-tuple-element.90.g_ref, bf16[1024,256]{1,0:T(8,128)(2,1)} %get-tuple-element.72.k_ref, ...), custom_call_target="tpu_custom_call" | custom-call | flops 1006632960 | bytes 3145728 | tf_op jit(solution)/shard_map/back_left/pallas_call | solution.py:896
  305.0 28.6 %back_swap.1 = (bf16[1280,1024]{1,0:T(8,128)(2,1)}, bf16[1280,1024]{1,0:T(8,128)(2,1)}, bf16[1280,1024]{1,0:T(8,128)(2,1)}) custom-call(bf16[1280,1024]{1,0:T(8,128)(2,1)} %get-tuple-element.67.q_ref.q_all, bf16[160,1024]{1,0:T(8,128)(2,1)} %get-tuple-element.89.g_ref, bf16[1280,1024]{1,0:T(8,128)(2,1)} %get-tuple-element.68.k_ref.k_all, ...), custom_call_target="tpu_custom_call" | custom-call | flops 4026531840 | bytes 12582912 | tf_op jit(solution)/shard_map/back_swap/pallas_call | solution.py:959
  333.6 7.0 %convolution_convert_fusion.2.gq_ref = bf16[1024,1024]{1,0:T(8,128)(2,1)} fusion(bf16[1280,1024]{1,0:T(8,128)(2,1)} %get-tuple-element.97.dq_ref, bf16[1280,1024]{1,0:T(8,128)(2,1)} %get-tuple-element.98), kind=kOutput, calls=%fused_computation.5 | convolution fusion | flops 2685403136 | bytes 7340032 | tf_op jit(solution)/shard_map/dot_general | solution.py:327
  340.6 4.2 convolution_convert_fusion.1.gk_ref
  344.9 1.8 select_convert_fusion.1
  346.7 1.7 select_convert_fusion
  348.4 17.1 %token_back.1 = (bf16[1280,1024]{1,0:T(8,128)(2,1)}, f32[2,1024]{1,0:T(2,128)}) custom-call(bf16[1280,1024]{1,0:T(8,128)(2,1)} %get-tuple-element.63.x_ref.tok_ref, bf16[1280,1024]{1,0:T(8,128)(2,1)} %get-tuple-element.97.dq_ref, bf16[1280,1024]{1,0:T(8,128)(2,1)} %get-tuple-element.99.dk_ref, bf16[1280,1024]{1,0:T(8,128)(2,1)} %get-tuple-element.100.dv_ref, ...), custom_call_target="tpu_custom_call" | custom-call | flops 8053063680 | bytes 20971520 | tf_op jit(solution)/shard_map/token_back/pallas_call | solution.py:1289
  365.5 1.4 maximum_maximum_fusion.vec_ref
  366.9 2.3 pad_maximum_fusion.1.cot_ref
  369.2 4.1 convolution_convert_fusion.3.go_ref
  373.3 4.1 convolution_convert_fusion.gv_ref
  377.4 20.5 %feed_grads.1 = (bf16[1024,1024]{1,0:T(8,128)(2,1)}, bf16[1024,1024]{1,0:T(8,128)(2,1)}, bf16[1024,1024]{1,0:T(8,128)(2,1)}) custom-call(bf16[640,1024]{1,0:T(8,128)(2,1)} %bitcast.103, bf16[160,1024]{1,0:T(8,128)(2,1)} %bitcast.105, bf16[800,1024]{1,0:T(8,128)(2,1)} %pad_maximum_fusion.1.cot_ref, bf16[1024,1024]{1,0:T(8,128)(2,1)} %wg_ref.5, ...), custom_call_target="tpu_custom_call" | custom-call | flops 10066329600 | bytes 12582912 | tf_op jit(solution)/shard_map/feed_grads/pallas_call | solution.py:1253
  397.8 103.7 %exchange_out.1 = (f32[4,256,128]{2,1,0:T(8,128)}, f32[3,1024,128]{2,1,0:T(8,128)}, bf16[10,128,1024]{2,1,0:T(8,128)(2,1)}, f32[8,1024]{1,0:T(8,128)}) custom-call(bf16[1024,1024]{1,0:T(8,128)(2,1)} %convolution_convert_fusion.3.go_ref, bf16[1024,1024]{1,0:T(8,128)(2,1)} %convolution_convert_fusion.2.gq_ref, ...), custom_call_target="tpu_custom_call" | custom-call | tf_op jit(solution)/shard_map/exchange_out/pallas_call | solution.py:1501
  501.6 1.9 slice_bitcast_fusion.5
  503.5 2.3 slice_bitcast_fusion
  505.8 3.0 convert_bitcast_fusion
  508.8 0.8 constant_dynamic-slice_fusion.2
  509.5 0.8 copy.37
  510.3 0.8 copy.38
  511.0 0.8 copy.39
  511.8 1.0 copy.40
  512.8 1.0 copy.41
  513.8 0.5 slice_bitcast_fusion.9
  514.3 1.1 select_bitcast_fusion.1
  515.5 1.7 pad_maximum_fusion
  (34 shorter events, 0.3 us)
Async XLA Ops:
  282.8 11.7 %copy-start.1 = (bf16[160,1024]{1,0:T(8,128)(2,1)S(1)}, bf16[160,1024]{1,0:T(8,128)(2,1)}, u32[]{:S(2)}) copy-start(bf16[160,1024]{1,0:T(8,128)(2,1)} %fusion.pick_ref) | copy-start | bytes 983044
  282.8 11.7 %copy-start.2 = (bf16[160,256]{1,0:T(8,128)(2,1)S(1)}, bf16[160,256]{1,0:T(8,128)(2,1)}, u32[]{:S(2)}) copy-start(bf16[160,256]{1,0:T(8,128)(2,1)} %get-tuple-element.148.part_pick_ref) | copy-start | bytes 245764
  284.7 229.6 %collective-permute-start = (bf16[128,1024]{1,0:T(8,128)(2,1)}, bf16[128,1024]{1,0:T(8,128)(2,1)}, u32[]{:S(2)}, u32[]{:S(2)}) collective-permute-start(bf16[128,1024]{1,0:T(8,128)(2,1)} %get-tuple-element.135), channel_id=1, source_target_pairs={{0,0},{1,1},{2,8},{3,9},{4,4},{5,5},{6,12},{7,13},{8,2},{9,3},{10,... | collective-permute-start | bytes 786440 | tf_op jit(solution)/shard_map/ppermute | solution.py:1648
  288.3 226.0 %collective-permute-start.1 = (bf16[128,1024]{1,0:T(8,128)(2,1)}, bf16[128,1024]{1,0:T(8,128)(2,1)}, u32[]{:S(2)}, u32[]{:S(2)}) collective-permute-start(bf16[128,1024]{1,0:T(8,128)(2,1)} %get-tuple-element.136), channel_id=1, source_target_pairs={{0,1},{1,0},{2,9},{3,8},{4,5},{5,4},{6,13},{7,12},{8,3},{9,2},{10,... | collective-permute-start | bytes 786440 | tf_op jit(solution)/shard_map/ppermute | solution.py:1648
  288.6 226.9 %all-to-all-start = ((bf16[8,128,1024]{2,1,0:T(8,128)(2,1)}), bf16[8,128,1024]{2,1,0:T(8,128)(2,1)S(1)}, u32[]{:S(2)}, u32[]{:S(2)}) async-start(bf16[8,128,1024]{2,1,0:T(8,128)(2,1)} %bitcast.89), calls=%async_computation | async-start | bytes 4194304 | tf_op jit(solution)/shard_map/all_to_all | solution.py:1637
  333.6 7.1 %copy-start.5 = (bf16[1280,1024]{1,0:T(8,128)(2,1)S(1)}, bf16[1280,1024]{1,0:T(8,128)(2,1)}, u32[]{:S(2)}) copy-start(bf16[1280,1024]{1,0:T(8,128)(2,1)} %get-tuple-element.99.dk_ref) | copy-start | bytes 7864324
  333.6 7.0 %copy-start.6 = (bf16[1280,1024]{1,0:T(8,128)(2,1)S(1)}, bf16[1280,1024]{1,0:T(8,128)(2,1)}, u32[]{:S(2)}) copy-start(bf16[1280,1024]{1,0:T(8,128)(2,1)} %get-tuple-element.98) | copy-start | bytes 7864324
  348.4 17.1 %copy-start.3 = (f32[2,1024]{1,0:T(2,128)S(1)}, f32[2,1024]{1,0:T(2,128)}, u32[]{:S(2)}) copy-start(f32[2,1024]{1,0:T(2,128)} %get-tuple-element.108) | copy-start | bytes 24580
  369.2 4.1 copy-start.4
  369.2 4.1 copy-start.7
  501.6 4.2 copy-start

commit v7 on v6

--- a/solution.py
+++ b/solution.py
@@ -1247,7 +1247,7 @@
 def feed_grads(own, left, cot, w_gate, w_up, w_down):
     rows, width = cot.shape
     units = w_gate.shape[1]
-    unit = 256
+    unit = 512
     columns = pl.BlockSpec((width, unit), lambda i: (0, i))
     line = pl.BlockSpec((unit, width), lambda i: (i, 0))
     return pl.pallas_call(
@@ -1305,7 +1305,7 @@
 
 def exchange_out_kernel(
     sizes, go_ref, gq_ref, gk_ref, gv_ref, gg_ref, gu_ref, gd_ref, grad_ref, vec_ref, w_ref, ffn_ref, tok_ref, vec_out,
-    buf1, buf2, buf3, buf4, vec_buf, vec_sum,
+    mine, buf1, buf2, buf3, buf4, vec_buf, vec_sum, mine_sem,
     tok_send, tok_recv, send1, recv1, send2, recv2, send3, recv3, send4, recv4, vec_send, vec_recv, local_sem,
 ):
     n_seq, n_ten, half, rows = sizes
@@ -1351,6 +1351,18 @@
             ]
         )
     for copies in stage1:
+        start_all(copies)
+    kept = [
+        [
+            pltpu.make_async_copy(
+                grads[a].at[:, columns(b_y, c, b_x)], mine.at[a, b_y, b_x], mine_sem.at[a, 2 * b_y + b_x]
+            )
+            for b_y in range(2)
+            for b_x in range(2)
+        ]
+        for a in range(count)
+    ]
+    for copies in kept:
         start_all(copies)
 
     vec_hops = []
@@ -1408,11 +1420,12 @@
 
     stage2 = []
     for a in range(count):
+        wait_all(kept[a])
         for copy in stage1[a]:
             copy.wait_recv()
         for b_y in range(2):
             for b_x in range(2):
-                add_rows(buf1.at[a, b_y, b_x], grads[a].at[:, columns(b_y, c, b_x)], buf1.at[a, b_y, b_x])
+                add_rows(buf1.at[a, b_y, b_x], mine.at[a, b_y, b_x], buf1.at[a, b_y, b_x])
         copies = []
         for b in range(2):
             src, peer = (buf1.at[a, b, 1 - sx], x_peer) if x_first[a] else (buf1.at[a, 1 - y, b], y_peer)
@@ -1500,7 +1513,7 @@
     hops = 3 + n_ten - 1
     return pl.pallas_call(
         functools.partial(exchange_out_kernel, (n_seq, n_ten, half, rows)),
-        in_specs=[vmem] * (count + 2),
+        in_specs=[any_spec()] * (count + 1) + [vmem],
         out_specs=[vmem, vmem, any_spec(), vmem],
         out_shape=[
             jax.ShapeDtypeStruct((attn, hw, LANES), F32),
@@ -1510,11 +1523,13 @@
         ],
         scratch_shapes=[
             pltpu.VMEM((count, 2, 2, height, LANES), BF),
+            pltpu.VMEM((count, 2, 2, height, LANES), BF),
             pltpu.VMEM((count, 2, height, LANES), BF),
             pltpu.VMEM((count, height, LANES), BF),
             pltpu.VMEM((attn, n_ten - 1, hw, LANES), BF),
             pltpu.VMEM((hops,) + vectors.shape, F32),
             pltpu.VMEM((4,) + vectors.shape, F32),
+            dma((count, 4)),
             dma((group + 1,)), dma((group + 1,)),
             dma((count, 4)), dma((count, 4)),
             dma((count, 2)), dma((count, 2)),

time: 525 us -> 517 us (0.985)
  Pallas kernels: 447 us -> 439 us
  transfers between devices with their start and end apart: 3 -> 3, of which waited for: 0 -> 0; matrix products, arithmetic and copies ran while one was open for 9% -> 9% of each run, Pallas kernels for 34% -> 33%
where the time goes in v7:
time: 517 us; the launch traced here: 510 us
  Pallas kernels  439 us (85%)
  other arithmetic  25.3 us (5%)
  matrix products  19.4 us (4%)
  local copies, waits for them, and re-layouts  14.2 us (3%)
  starting transfers between devices  8.84 us (2%)
    pallas_call x1, Pallas kernels, exchange_out(): pl.pallas_call(functools.partial(exchange_out_kernel, (n_seq, n_ten, half...  98.9 us
    pallas_call x1, Pallas kernels, feed_forward(): pl.pallas_call(functools.partial(feed_kernel, n_ten), grid=(n_ten * units...  90.4 us
    pallas_call x1, Pallas kernels, exchange_in(): pl.pallas_call(functools.partial(exchange_in_kernel, (n_seq, n_ten, windo...  78.8 us
    pallas_call x1, Pallas kernels, attend_swap(): pl.pallas_call(functools.partial(attend_swap_kernel, n_ten, length), grid...  62.7 us
    pallas_call x1, Pallas kernels, back_swap(): pl.pallas_call(back_swap_kernel, grid=(width // LANES,), in_specs=back_sp...  28.6 us
    pallas_call x1, Pallas kernels, attend_left(): pl.pallas_call(functools.partial(attend_left_kernel, n_ten), grid=(QUAD,...  23.2 us
    dot_general x4, matrix products, t_dot(): lax.dot_general(a, b, (((0,), (0,)), ((), ())), preferred_element_type=F32)  19.4 us
    pallas_call x1, Pallas kernels, feed_grads(): pl.pallas_call(feed_grads_kernel, grid=(units // unit,), in_specs=[once(o...  17.5 us
  transfers between devices with their start and end apart: 3, of which 0 were waited for; matrix products, arithmetic and copies ran while one was open for 9% of the time, Pallas kernels for 33%

profile of v7, /device:TPU:0, one launch (start us, length us, event | category | flops | bytes accessed | tf_op | source)
XLA Modules:
  0.0 509.8 jit_solution(10998334825951350719)
XLA Ops:
  1.3 1.4 convert_reduce_fusion
  2.8 0.9 fusion.pick_ref
  3.7 1.3 select_select_fusion.count_ref
  4.9 78.8 %exchange_in.1 = (bf16[1280,1024]{1,0:T(8,128)(2,1)}, bf16[1024,1024]{1,0:T(8,128)(2,1)}, bf16[1024,1024]{1,0:T(8,128)(2,1)}, bf16[1024,1024]{1,0:T(8,128)(2,1)}...) custom-call(bf16[10,128,1024]{2,1,0:T(8,128)(2,1)} %bitcast.87, ...), custom_call_target="tpu_custom_call" | custom-call | tf_op jit(solution)/shard_map/exchange_in/pallas_call | solution.py:602
  83.8 1.4 slice_reduce_fusion
  85.1 0.8 fusion.9
  86.5 0.7 compare_reduce_fusion
  87.3 1.3 bitcast_select_fusion
  88.6 1.2 pad_maximum_fusion.2.cot_ref
  89.9 1.7 constant_dynamic-slice_fusion.7
  91.5 14.8 %norm_qkv.1 = (bf16[1280,1024]{1,0:T(8,128)(2,1)}, bf16[1280,1024]{1,0:T(8,128)(2,1)}, bf16[1280,1024]{1,0:T(8,128)(2,1)}, bf16[1280,1024]{1,0:T(8,128)(2,1)}) custom-call(bf16[1280,1024]{1,0:T(8,128)(2,1)} %get-tuple-element.63.x_ref.tok_ref, f32[1,1024]{1,0:T(1,128)} %bitcast.101, f32[1,1024]{1,0:T(1,128)} %bitcast.98, ...), custom_call_target="tpu_custom_call" | custom-call | flops 8053063680 | bytes 20971520 | tf_op jit(solution)/shard_map/norm_qkv/pallas_call | solution.py:656
  106.4 62.7 %attend_swap.1 = (bf16[1024,1024]{1,0:T(8,128)(2,1)}, bf16[1024,256]{1,0:T(8,128)(2,1)}, bf16[1024,256]{1,0:T(8,128)(2,1)}, bf16[1024,256]{1,0:T(8,128)(2,1)}, b...) custom-call(bf16[1280,1024]{1,0:T(8,128)(2,1)} %get-tuple-element.67.q_ref.q_all, ...), custom_call_target="tpu_custom_call" | custom-call | flops 17179869184 | bytes 8388608 | tf_op jit(solution)/shard_map/attend_swap/pallas_call | solution.py:822
  169.1 23.2 %attend_left.1 = (bf16[256,1024]{1,0:T(8,128)(2,1)}, bf16[1024,4096]{1,0:T(8,128)(2,1)}, bf16[1024,4096]{1,0:T(8,128)(2,1)}, bf16[4096,1024]{1,0:T(8,128)(2,1)}) custom-call(bf16[1024,256]{1,0:T(8,128)(2,1)} %get-tuple-element.71.q_ref, bf16[1024,256]{1,0:T(8,128)(2,1)} %get-tuple-element.72.k_ref, ...), custom_call_target="tpu_custom_call", output_to_operand_aliasing={{1}: (3, {}), {2}: (4, {}), {3}: (5, {})} | custom-call | flops 4294967296 | bytes 2097152 | tf_op jit(solution)/shard_map/attend_left/pallas_call | solution.py:735
  192.3 90.4 %feed_forward.1 = (bf16[1024,1024]{1,0:T(8,128)(2,1)}, bf16[2,128,1024]{2,1,0:T(8,128)(2,1)}, bf16[320,1024]{1,0:T(8,128)(2,1)}, bf16[320,1024]{1,0:T(8,128)(2,1...) custom-call(bf16[1280,1024]{1,0:T(8,128)(2,1)} %get-tuple-element.63, ...), custom_call_target="tpu_custom_call", output_to_operand_aliasing={{9}: (12, {}), {10}: (13, {}), {11}: (14, {})} | custom-call | flops 42949672960 | bytes 25165824 | tf_op jit(solution)/shard_map/feed_forward/pallas_call | solution.py:1183
  282.8 1.9 slice_bitcast_fusion.4
  284.7 3.6 collective-permute-start
  288.3 0.3 collective-permute-start.1
  288.6 5.0 all-to-all-start
  293.6 0.9 fusion.1.pick_ref
  294.5 0.8 pad_maximum_fusion.3.pick_ref
  295.3 0.6 fusion.3
  295.9 0.9 pad_maximum_fusion.4
  296.8 0.9 pad_maximum_fusion.6
  297.6 7.3 %back_left.1 = (bf16[1024,256]{1,0:T(8,128)(2,1)}, bf16[1024,256]{1,0:T(8,128)(2,1)}, bf16[1024,256]{1,0:T(8,128)(2,1)}) custom-call(bf16[1024,256]{1,0:T(8,128)(2,1)} %get-tuple-element.71.q_ref, bf16[160,256]{1,0:T(8,128)(2,1)} %get-tuple-element.90.g_ref, bf16[1024,256]{1,0:T(8,128)(2,1)} %get-tuple-element.72.k_ref, ...), custom_call_target="tpu_custom_call" | custom-call | flops 1006632960 | bytes 3145728 | tf_op jit(solution)/shard_map/back_left/pallas_call | solution.py:896
  305.0 28.6 %back_swap.1 = (bf16[1280,1024]{1,0:T(8,128)(2,1)}, bf16[1280,1024]{1,0:T(8,128)(2,1)}, bf16[1280,1024]{1,0:T(8,128)(2,1)}) custom-call(bf16[1280,1024]{1,0:T(8,128)(2,1)} %get-tuple-element.67.q_ref.q_all, bf16[160,1024]{1,0:T(8,128)(2,1)} %get-tuple-element.89.g_ref, bf16[1280,1024]{1,0:T(8,128)(2,1)} %get-tuple-element.68.k_ref.k_all, ...), custom_call_target="tpu_custom_call" | custom-call | flops 4026531840 | bytes 12582912 | tf_op jit(solution)/shard_map/back_swap/pallas_call | solution.py:959
  333.6 7.0 %convolution_convert_fusion.2.gq_ref = bf16[1024,1024]{1,0:T(8,128)(2,1)} fusion(bf16[1280,1024]{1,0:T(8,128)(2,1)} %get-tuple-element.97.dq_ref, bf16[1280,1024]{1,0:T(8,128)(2,1)} %get-tuple-element.98), kind=kOutput, calls=%fused_computation.5 | convolution fusion | flops 2685403136 | bytes 7340032 | tf_op jit(solution)/shard_map/dot_general | solution.py:327
  340.6 4.2 convolution_convert_fusion.1.gk_ref
  344.9 1.8 select_convert_fusion.1
  346.7 1.7 select_convert_fusion
  348.4 17.1 %token_back.1 = (bf16[1280,1024]{1,0:T(8,128)(2,1)}, f32[2,1024]{1,0:T(2,128)}) custom-call(bf16[1280,1024]{1,0:T(8,128)(2,1)} %get-tuple-element.63.x_ref.tok_ref, bf16[1280,1024]{1,0:T(8,128)(2,1)} %get-tuple-element.97.dq_ref, bf16[1280,1024]{1,0:T(8,128)(2,1)} %get-tuple-element.99.dk_ref, bf16[1280,1024]{1,0:T(8,128)(2,1)} %get-tuple-element.100.dv_ref, ...), custom_call_target="tpu_custom_call" | custom-call | flops 8053063680 | bytes 20971520 | tf_op jit(solution)/shard_map/token_back/pallas_call | solution.py:1289
  365.5 1.4 maximum_maximum_fusion.vec_ref
  366.9 2.3 pad_maximum_fusion.1.cot_ref
  369.2 4.1 convolution_convert_fusion.3.go_ref
  373.3 4.1 convolution_convert_fusion.gv_ref
  377.4 17.5 %feed_grads.1 = (bf16[1024,1024]{1,0:T(8,128)(2,1)}, bf16[1024,1024]{1,0:T(8,128)(2,1)}, bf16[1024,1024]{1,0:T(8,128)(2,1)}) custom-call(bf16[640,1024]{1,0:T(8,128)(2,1)} %bitcast.103, bf16[160,1024]{1,0:T(8,128)(2,1)} %bitcast.105, bf16[800,1024]{1,0:T(8,128)(2,1)} %pad_maximum_fusion.1.cot_ref, bf16[1024,1024]{1,0:T(8,128)(2,1)} %wg_ref.5, ...), custom_call_target="tpu_custom_call" | custom-call | flops 10066329600 | bytes 12582912 | tf_op jit(solution)/shard_map/feed_grads/pallas_call | solution.py:1253
  394.9 98.9 %exchange_out.1 = (f32[4,256,128]{2,1,0:T(8,128)}, f32[3,1024,128]{2,1,0:T(8,128)}, bf16[10,128,1024]{2,1,0:T(8,128)(2,1)}, f32[8,1024]{1,0:T(8,128)}) custom-call(bf16[1024,1024]{1,0:T(8,128)(2,1)} %convolution_convert_fusion.3.go_ref, bf16[1024,1024]{1,0:T(8,128)(2,1)} %convolution_convert_fusion.2.gq_ref, ...), custom_call_target="tpu_custom_call" | custom-call | tf_op jit(solution)/shard_map/exchange_out/pallas_call | solution.py:1514
  493.8 1.9 slice_bitcast_fusion.5
  495.7 2.3 slice_bitcast_fusion
  498.0 3.0 convert_bitcast_fusion
  501.0 0.8 constant_dynamic-slice_fusion.2
  501.7 0.8 copy.37
  502.5 0.8 copy.38
  503.3 0.8 copy.39
  504.0 1.0 copy.40
  505.0 1.0 copy.41
  506.0 0.5 slice_bitcast_fusion.9
  506.5 1.1 select_bitcast_fusion.1
  507.7 1.7 pad_maximum_fusion
  (34 shorter events, 0.3 us)
Async XLA Ops:
  282.8 11.7 %copy-start.1 = (bf16[160,1024]{1,0:T(8,128)(2,1)S(1)}, bf16[160,1024]{1,0:T(8,128)(2,1)}, u32[]{:S(2)}) copy-start(bf16[160,1024]{1,0:T(8,128)(2,1)} %fusion.pick_ref) | copy-start | bytes 983044
  282.8 11.7 %copy-start.2 = (bf16[160,256]{1,0:T(8,128)(2,1)S(1)}, bf16[160,256]{1,0:T(8,128)(2,1)}, u32[]{:S(2)}) copy-start(bf16[160,256]{1,0:T(8,128)(2,1)} %get-tuple-element.148.part_pick_ref) | copy-start | bytes 245764
  284.7 221.8 %collective-permute-start = (bf16[128,1024]{1,0:T(8,128)(2,1)}, bf16[128,1024]{1,0:T(8,128)(2,1)}, u32[]{:S(2)}, u32[]{:S(2)}) collective-permute-start(bf16[128,1024]{1,0:T(8,128)(2,1)} %get-tuple-element.135), channel_id=1, source_target_pairs={{0,0},{1,1},{2,8},{3,9},{4,4},{5,5},{6,12},{7,13},{8,2},{9,3},{10,... | collective-permute-start | bytes 786440 | tf_op jit(solution)/shard_map/ppermute | solution.py:1663
  288.3 218.2 %collective-permute-start.1 = (bf16[128,1024]{1,0:T(8,128)(2,1)}, bf16[128,1024]{1,0:T(8,128)(2,1)}, u32[]{:S(2)}, u32[]{:S(2)}) collective-permute-start(bf16[128,1024]{1,0:T(8,128)(2,1)} %get-tuple-element.136), channel_id=1, source_target_pairs={{0,1},{1,0},{2,9},{3,8},{4,5},{5,4},{6,13},{7,12},{8,3},{9,2},{10,... | collective-permute-start | bytes 786440 | tf_op jit(solution)/shard_map/ppermute | solution.py:1663
  288.6 219.1 %all-to-all-start = ((bf16[8,128,1024]{2,1,0:T(8,128)(2,1)}), bf16[8,128,1024]{2,1,0:T(8,128)(2,1)S(1)}, u32[]{:S(2)}, u32[]{:S(2)}) async-start(bf16[8,128,1024]{2,1,0:T(8,128)(2,1)} %bitcast.89), calls=%async_computation | async-start | bytes 4194304 | tf_op jit(solution)/shard_map/all_to_all | solution.py:1652
  333.6 7.1 %copy-start.5 = (bf16[1280,1024]{1,0:T(8,128)(2,1)S(1)}, bf16[1280,1024]{1,0:T(8,128)(2,1)}, u32[]{:S(2)}) copy-start(bf16[1280,1024]{1,0:T(8,128)(2,1)} %get-tuple-element.99.dk_ref) | copy-start | bytes 7864324
  333.6 7.0 %copy-start.6 = (bf16[1280,1024]{1,0:T(8,128)(2,1)S(1)}, bf16[1280,1024]{1,0:T(8,128)(2,1)}, u32[]{:S(2)}) copy-start(bf16[1280,1024]{1,0:T(8,128)(2,1)} %get-tuple-element.98) | copy-start | bytes 7864324
  348.4 17.1 %copy-start.3 = (f32[2,1024]{1,0:T(2,128)S(1)}, f32[2,1024]{1,0:T(2,128)}, u32[]{:S(2)}) copy-start(f32[2,1024]{1,0:T(2,128)} %get-tuple-element.108) | copy-start | bytes 24580
  369.2 4.1 copy-start.4
  369.2 4.1 copy-start.7
  493.8 4.2 copy-start

commit v8 on v7

--- a/solution.py
+++ b/solution.py
@@ -1632,7 +1632,7 @@
     grad_w_out = t_dot(att_m, gr2).astype(BF)
     left_back = back_left(left_q, left_gatt, left_k, left_v, left_pick, left_tables)
     dq, dk, dv = back_swap(q, own_gatt, k, v, own_pick, own_tables, left_back)
-    all_own, dq, dk, dv = lax.optimization_barrier((all_own, dq, dk, dv))
+    all_own, dq, dk, dv, own_out, left_chunks = lax.optimization_barrier((all_own, dq, dk, dv, own_out, left_chunks))
 
     part_of = lambda x: lax.dynamic_slice_in_dim(x, place * part, part, 1)
     down_in = jnp.concatenate(

time: 517 us -> 507 us (0.981)
  Pallas kernels: 439 us -> 431 us
    pallas_call x1, Pallas kernels: 98.9 us -> 93.3 us  [exchange_out(): pl.pallas_call(functools.partial(exchange_out_kernel, (n_seq, n_ten, half...]
  transfers between devices with their start and end apart: 3 -> 3, of which waited for: 0 -> 0; matrix products, arithmetic and copies ran while one was open for 9% -> 8% of each run, Pallas kernels for 33% -> 26%
where the time goes in v8:
time: 507 us; the launch traced here: 499 us
  Pallas kernels  431 us (85%)
  other arithmetic  25.4 us (5%)
  matrix products  19.3 us (4%)
  local copies, waits for them, and re-layouts  13.1 us (3%)
  starting transfers between devices  7.62 us (2%)
    pallas_call x1, Pallas kernels, exchange_out(): pl.pallas_call(functools.partial(exchange_out_kernel, (n_seq, n_ten, half...  93.3 us
    pallas_call x1, Pallas kernels, feed_forward(): pl.pallas_call(functools.partial(feed_kernel, n_ten), grid=(n_ten * units...  90.4 us
    pallas_call x1, Pallas kernels, exchange_in(): pl.pallas_call(functools.partial(exchange_in_kernel, (n_seq, n_ten, windo...  78.8 us
    pallas_call x1, Pallas kernels, attend_swap(): pl.pallas_call(functools.partial(attend_swap_kernel, n_ten, length), grid...  62.7 us
    pallas_call x1, Pallas kernels, back_swap(): pl.pallas_call(back_swap_kernel, grid=(width // LANES,), in_specs=back_sp...  25.4 us
    pallas_call x1, Pallas kernels, attend_left(): pl.pallas_call(functools.partial(attend_left_kernel, n_ten), grid=(QUAD,...  23.2 us
    dot_general x4, matrix products, t_dot(): lax.dot_general(a, b, (((0,), (0,)), ((), ())), preferred_element_type=F32)  19.3 us
    pallas_call x1, Pallas kernels, feed_grads(): pl.pallas_call(feed_grads_kernel, grid=(units // unit,), in_specs=[once(o...  17.7 us
  transfers between devices with their start and end apart: 3, of which 0 were waited for; matrix products, arithmetic and copies ran while one was open for 8% of the time, Pallas kernels for 26%

profile of v8, /device:TPU:0, one launch (start us, length us, event | category | flops | bytes accessed | tf_op | source)
XLA Modules:
  0.0 498.9 jit_solution(12020207495171326543)
XLA Ops:
  1.3 1.4 convert_reduce_fusion
  2.8 0.9 fusion.pick_ref
  3.7 1.3 select_select_fusion.count_ref
  4.9 78.8 %exchange_in.1 = (bf16[1280,1024]{1,0:T(8,128)(2,1)}, bf16[1024,1024]{1,0:T(8,128)(2,1)}, bf16[1024,1024]{1,0:T(8,128)(2,1)}, bf16[1024,1024]{1,0:T(8,128)(2,1)}...) custom-call(bf16[10,128,1024]{2,1,0:T(8,128)(2,1)} %bitcast.87, ...), custom_call_target="tpu_custom_call" | custom-call | tf_op jit(solution)/shard_map/exchange_in/pallas_call | solution.py:602
  83.8 1.4 slice_reduce_fusion
  85.1 0.8 fusion.9
  85.9 0.9 fusion.1.pick_ref
  86.8 0.7 compare_reduce_fusion
  88.2 1.3 bitcast_select_fusion
  89.5 1.2 pad_maximum_fusion.2.cot_ref
  90.7 1.7 constant_dynamic-slice_fusion.7
  92.4 0.6 fusion.3
  93.1 0.9 pad_maximum_fusion.4
  93.9 0.9 pad_maximum_fusion.6
  94.8 14.8 %norm_qkv.1 = (bf16[1280,1024]{1,0:T(8,128)(2,1)}, bf16[1280,1024]{1,0:T(8,128)(2,1)}, bf16[1280,1024]{1,0:T(8,128)(2,1)}, bf16[1280,1024]{1,0:T(8,128)(2,1)}) custom-call(bf16[1280,1024]{1,0:T(8,128)(2,1)} %get-tuple-element.65.x_ref.tok_ref, f32[1,1024]{1,0:T(1,128)} %bitcast.101, f32[1,1024]{1,0:T(1,128)} %bitcast.98, ...), custom_call_target="tpu_custom_call" | custom-call | flops 8053063680 | bytes 20971520 | tf_op jit(solution)/shard_map/norm_qkv/pallas_call | solution.py:656
  109.7 62.7 %attend_swap.1 = (bf16[1024,1024]{1,0:T(8,128)(2,1)}, bf16[1024,256]{1,0:T(8,128)(2,1)}, bf16[1024,256]{1,0:T(8,128)(2,1)}, bf16[1024,256]{1,0:T(8,128)(2,1)}, b...) custom-call(bf16[1280,1024]{1,0:T(8,128)(2,1)} %get-tuple-element.69.q_ref.q_all, ...), custom_call_target="tpu_custom_call" | custom-call | flops 17179869184 | bytes 8388608 | tf_op jit(solution)/shard_map/attend_swap/pallas_call | solution.py:822
  172.4 23.2 %attend_left.1 = (bf16[256,1024]{1,0:T(8,128)(2,1)}, bf16[1024,4096]{1,0:T(8,128)(2,1)}, bf16[1024,4096]{1,0:T(8,128)(2,1)}, bf16[4096,1024]{1,0:T(8,128)(2,1)}) custom-call(bf16[1024,256]{1,0:T(8,128)(2,1)} %get-tuple-element.73.q_ref, bf16[1024,256]{1,0:T(8,128)(2,1)} %get-tuple-element.74.k_ref, ...), custom_call_target="tpu_custom_call", output_to_operand_aliasing={{1}: (3, {}), {2}: (4, {}), {3}: (5, {})} | custom-call | flops 4294967296 | bytes 2097152 | tf_op jit(solution)/shard_map/attend_left/pallas_call | solution.py:735
  195.6 90.4 %feed_forward.1 = (bf16[1024,1024]{1,0:T(8,128)(2,1)}, bf16[2,128,1024]{2,1,0:T(8,128)(2,1)}, bf16[320,1024]{1,0:T(8,128)(2,1)}, bf16[320,1024]{1,0:T(8,128)(2,1...) custom-call(bf16[1280,1024]{1,0:T(8,128)(2,1)} %get-tuple-element.65, ...), custom_call_target="tpu_custom_call", output_to_operand_aliasing={{9}: (12, {}), {10}: (13, {}), {11}: (14, {})} | custom-call | flops 42949672960 | bytes 25165824 | tf_op jit(solution)/shard_map/feed_forward/pallas_call | solution.py:1183
  286.0 7.5 %back_left.1 = (bf16[1024,256]{1,0:T(8,128)(2,1)}, bf16[1024,256]{1,0:T(8,128)(2,1)}, bf16[1024,256]{1,0:T(8,128)(2,1)}) custom-call(bf16[1024,256]{1,0:T(8,128)(2,1)} %get-tuple-element.73.q_ref, bf16[160,256]{1,0:T(8,128)(2,1)} %get-tuple-element.88.g_ref, bf16[1024,256]{1,0:T(8,128)(2,1)} %get-tuple-element.74.k_ref, ...), custom_call_target="tpu_custom_call" | custom-call | flops 1006632960 | bytes 3145728 | tf_op jit(solution)/shard_map/back_left/pallas_call | solution.py:896
  293.6 25.4 %back_swap.1 = (bf16[1280,1024]{1,0:T(8,128)(2,1)}, bf16[1280,1024]{1,0:T(8,128)(2,1)}, bf16[1280,1024]{1,0:T(8,128)(2,1)}) custom-call(bf16[1280,1024]{1,0:T(8,128)(2,1)} %get-tuple-element.69.q_ref.q_all, bf16[160,1024]{1,0:T(8,128)(2,1)} %get-tuple-element.87.g_ref, bf16[1280,1024]{1,0:T(8,128)(2,1)} %get-tuple-element.70.k_ref.k_all, ...), custom_call_target="tpu_custom_call" | custom-call | flops 4026531840 | bytes 12582912 | tf_op jit(solution)/shard_map/back_swap/pallas_call | solution.py:959
  319.1 0.8 slice_bitcast_fusion.4
  319.9 3.6 collective-permute-start
  323.5 4.0 all-to-all-start
  327.5 0.8 pad_maximum_fusion.3.pick_ref
  328.3 7.0 %convolution_convert_fusion.2.gq_ref = bf16[1024,1024]{1,0:T(8,128)(2,1)} fusion(bf16[1280,1024]{1,0:T(8,128)(2,1)} %get-tuple-element.101.dq_ref, bf16[1280,1024]{1,0:T(8,128)(2,1)} %get-tuple-element.102), kind=kOutput, calls=%fused_computation.5 | convolution fusion | flops 2685403136 | bytes 7340032 | tf_op jit(solution)/shard_map/dot_general | solution.py:327
  335.4 4.2 convolution_convert_fusion.1.gk_ref
  339.5 0.1 fusion.6
  339.6 1.8 select_convert_fusion.1
  341.4 1.7 select_convert_fusion
  343.1 16.8 %token_back.1 = (bf16[1280,1024]{1,0:T(8,128)(2,1)}, f32[2,1024]{1,0:T(2,128)}) custom-call(bf16[1280,1024]{1,0:T(8,128)(2,1)} %get-tuple-element.65.x_ref.tok_ref, bf16[1280,1024]{1,0:T(8,128)(2,1)} %get-tuple-element.101.dq_ref, bf16[1280,1024]{1,0:T(8,128)(2,1)} %get-tuple-element.103.dk_ref, bf16[1280,1024]{1,0:T(8,128)(2,1)} %get-tuple-element.104.dv_ref, ...), custom_call_target="tpu_custom_call" | custom-call | flops 8053063680 | bytes 20971520 | tf_op jit(solution)/shard_map/token_back/pallas_call | solution.py:1289
  360.0 1.4 maximum_maximum_fusion.vec_ref
  361.3 2.3 pad_maximum_fusion.1.cot_ref
  363.7 4.0 convolution_convert_fusion.3.go_ref
  367.7 4.1 convolution_convert_fusion.gv_ref
  371.8 17.7 %feed_grads.1 = (bf16[1024,1024]{1,0:T(8,128)(2,1)}, bf16[1024,1024]{1,0:T(8,128)(2,1)}, bf16[1024,1024]{1,0:T(8,128)(2,1)}) custom-call(bf16[640,1024]{1,0:T(8,128)(2,1)} %bitcast.103, bf16[160,1024]{1,0:T(8,128)(2,1)} %bitcast.105, bf16[800,1024]{1,0:T(8,128)(2,1)} %pad_maximum_fusion.1.cot_ref, bf16[1024,1024]{1,0:T(8,128)(2,1)} %wg_ref.5, ...), custom_call_target="tpu_custom_call" | custom-call | flops 10066329600 | bytes 12582912 | tf_op jit(solution)/shard_map/feed_grads/pallas_call | solution.py:1253
  389.5 93.3 %exchange_out.1 = (f32[4,256,128]{2,1,0:T(8,128)}, f32[3,1024,128]{2,1,0:T(8,128)}, bf16[10,128,1024]{2,1,0:T(8,128)(2,1)}, f32[8,1024]{1,0:T(8,128)}) custom-call(bf16[1024,1024]{1,0:T(8,128)(2,1)} %convolution_convert_fusion.3.go_ref, bf16[1024,1024]{1,0:T(8,128)(2,1)} %convolution_convert_fusion.2.gq_ref, ...), custom_call_target="tpu_custom_call" | custom-call | tf_op jit(solution)/shard_map/exchange_out/pallas_call | solution.py:1514
  482.9 1.9 slice_bitcast_fusion.5
  484.8 2.3 slice_bitcast_fusion
  487.1 3.0 convert_bitcast_fusion
  490.1 0.8 constant_dynamic-slice_fusion.2
  490.8 0.8 copy.37
  491.6 0.8 copy.38
  492.4 0.8 copy.39
  493.1 1.0 copy.40
  494.1 1.0 copy.41
  495.1 0.5 slice_bitcast_fusion.9
  495.6 1.1 select_bitcast_fusion.1
  496.8 1.7 pad_maximum_fusion
  (36 shorter events, 0.3 us)
Async XLA Ops:
  293.6 25.5 %copy-start.2 = (bf16[2,128,1024]{2,1,0:T(8,128)(2,1)S(1)}, bf16[2,128,1024]{2,1,0:T(8,128)(2,1)}, u32[]{:S(2)}) copy-start(bf16[2,128,1024]{2,1,0:T(8,128)(2,1)} %get-tuple-element.98) | copy-start | bytes 1572868
  319.0 8.5 %copy-start.1 = (bf16[160,1024]{1,0:T(8,128)(2,1)S(1)}, bf16[160,1024]{1,0:T(8,128)(2,1)}, u32[]{:S(2)}) copy-start(bf16[160,1024]{1,0:T(8,128)(2,1)} %fusion.pick_ref) | copy-start | bytes 983044
  319.0 8.5 %copy-start.3 = (bf16[160,256]{1,0:T(8,128)(2,1)S(1)}, bf16[160,256]{1,0:T(8,128)(2,1)}, u32[]{:S(2)}) copy-start(bf16[160,256]{1,0:T(8,128)(2,1)} %get-tuple-element.152.part_pick_ref) | copy-start | bytes 245764
  319.9 175.7 %collective-permute-start = (bf16[128,1024]{1,0:T(8,128)(2,1)}, bf16[128,1024]{1,0:T(8,128)(2,1)}, u32[]{:S(2)}, u32[]{:S(2)}) collective-permute-start(bf16[128,1024]{1,0:T(8,128)(2,1)} %get-tuple-element.139), channel_id=1, source_target_pairs={{0,0},{1,1},{2,8},{3,9},{4,4},{5,5},{6,12},{7,13},{8,2},{9,3},{10,... | collective-permute-start | bytes 786440 | tf_op jit(solution)/shard_map/ppermute | solution.py:1663
  323.5 172.2 %collective-permute-start.1 = (bf16[128,1024]{1,0:T(8,128)(2,1)}, bf16[128,1024]{1,0:T(8,128)(2,1)}, u32[]{:S(2)}, u32[]{:S(2)}) collective-permute-start(bf16[128,1024]{1,0:T(8,128)(2,1)} %get-tuple-element.140), channel_id=1, source_target_pairs={{0,1},{1,0},{2,9},{3,8},{4,5},{5,4},{6,13},{7,12},{8,3},{9,2},{10,... | collective-permute-start | bytes 786440 | tf_op jit(solution)/shard_map/ppermute | solution.py:1663
  323.5 173.3 %all-to-all-start = ((bf16[8,128,1024]{2,1,0:T(8,128)(2,1)}), bf16[8,128,1024]{2,1,0:T(8,128)(2,1)S(1)}, u32[]{:S(2)}, u32[]{:S(2)}) async-start(bf16[8,128,1024]{2,1,0:T(8,128)(2,1)} %bitcast.89), calls=%async_computation | async-start | bytes 4194304 | tf_op jit(solution)/shard_map/all_to_all | solution.py:1652
  328.3 7.0 %copy-start.6 = (bf16[1280,1024]{1,0:T(8,128)(2,1)S(1)}, bf16[1280,1024]{1,0:T(8,128)(2,1)}, u32[]{:S(2)}) copy-start(bf16[1280,1024]{1,0:T(8,128)(2,1)} %get-tuple-element.103.dk_ref) | copy-start | bytes 7864324
  328.3 7.0 %copy-start.7 = (bf16[1280,1024]{1,0:T(8,128)(2,1)S(1)}, bf16[1280,1024]{1,0:T(8,128)(2,1)}, u32[]{:S(2)}) copy-start(bf16[1280,1024]{1,0:T(8,128)(2,1)} %get-tuple-element.102) | copy-start | bytes 7864324
  343.1 16.8 %copy-start.4 = (f32[2,1024]{1,0:T(2,128)S(1)}, f32[2,1024]{1,0:T(2,128)}, u32[]{:S(2)}) copy-start(f32[2,1024]{1,0:T(2,128)} %get-tuple-element.112) | copy-start | bytes 24580
  363.7 4.0 copy-start.5
  363.7 4.0 copy-start.8
  482.9 4.2 copy-start
